TPU v7x, 128 devices: a whole 4x4x4 slice. The times are simulated.
128 devices in a mesh: leaf: 8 (over x, core), front: 16 (over z, y).
Axes of the slice: x: 4, y: 4, z: 4, core: 2. Of those that a mesh axis runs over, the one named last changes fastest.
Arguments:
- front_matrix: float32 [8, 2048, 2048], P('leaf', 'front'), as said below
- child_blocks: float32 [128, 8, 3, 128, 128], P(('leaf', 'front')), may hold values from -0.046875 to 0.046875
- child_target: int32 [128, 8, 3], P(('leaf', 'front')), may hold values from 0 to 15, as said below
- child_count: int32 [128, 8], P(('leaf', 'front')), may hold values from 1 to 3, as said below
- shot_rhs: float32 [8, 64, 2048], P('leaf'), may hold values from -6 to 6
Outputs:
- factored: float32 [8, 2048, 2048], P('leaf', 'front')
- eliminated: float32 [8, 64, 2048], P('leaf')
Inputs may be any that keep to these rules, and one draw needn't show every extreme that they name: `child_target`: A bucket's code places its block on a row block that the receiving device (leaf index of the bucket, front index of the sender) holds, at a column block no later than that row block. Slots from child_count on are empty and hold no data. In every draw some leaf index receives 3 live blocks from every sender. `front_matrix`: after the child blocks are added, the symmetric matrix that each front's lower triangle defines is positive definite.
All inputs are finite; a program needn't handle non-finite values.
Results may differ from a plain program's by a relative error of at most 0.00013.
Values sent between devices are 32-bit elements; how exact they have to be, the bound alone decides.
No kernel may reach another device: no remote copies, remote signals or barrier semaphores. Data moves between devices by JAX's collectives and lax.ppermute only.
A program may use at most 64 MiB of HBM per device.

v0:
```python
import jax
import jax.numpy as jnp
from jax import lax
from jax.sharding import PartitionSpec as P

BLOCK = 128
PIVOTS = 1024


def spread(value, axis, source):
    kept = jnp.where(lax.axis_index(axis) == source, value, 0).astype(value.dtype)
    return lax.psum(kept, axis)


def lower_sym(square):
    return jnp.tril(square) + jnp.swapaxes(jnp.tril(square, -1), -1, -2)


def right_solve(factor, values):
    solved = jax.scipy.linalg.solve_triangular(factor, jnp.swapaxes(values, 1, 2), lower=True)
    return jnp.swapaxes(solved, 1, 2)


def local(front_matrix, child_blocks, child_target, child_count, shot_rhs):
    fronts_here, rows_local, order_here = front_matrix.shape
    leaf_count = lax.axis_size("leaf")
    capacity = child_blocks.shape[2]
    slot_ids = lax.broadcasted_iota(jnp.int32, child_target.shape, 2)
    live_code = jnp.where(slot_ids < child_count[:, :, None], child_target, -1)
    arrived, codes = (
        lax.all_to_all(child_blocks, "leaf", split_axis=1, concat_axis=1, tiled=True),
        lax.all_to_all(live_code, "leaf", split_axis=1, concat_axis=1, tiled=True),
    )
    count_in = leaf_count * capacity
    flat_blocks = arrived.reshape(count_in, BLOCK * BLOCK)
    flat_codes = codes.reshape(count_in)
    block_cols = order_here // BLOCK
    block_rows = rows_local // BLOCK
    slot_total = fronts_here * block_rows * block_cols
    one_hot = (
        lax.broadcasted_iota(jnp.int32, (slot_total, count_in), 0) == flat_codes[None, :]
    ).astype(jnp.float32)
    summed = jnp.dot(
        one_hot, flat_blocks, precision=lax.Precision.HIGHEST, preferred_element_type=jnp.float32
    )
    extended = summed.reshape(fronts_here, block_rows, block_cols, BLOCK, BLOCK)
    extended = extended.transpose(0, 1, 3, 2, 4).reshape(fronts_here, rows_local, order_here)
    matrix = front_matrix + extended
    my_index = lax.axis_index("front")
    row_global = my_index * rows_local + lax.broadcasted_iota(jnp.int32, (rows_local, 1), 0)
    current_rhs = shot_rhs
    left_parts = []
    diag_parts = []
    solved_parts = []
    for pivot_step in range(PIVOTS // BLOCK):
        start_col = pivot_step * BLOCK
        end_col = start_col + BLOCK
        column_panel = matrix[:, :, start_col:end_col]
        owner_index = start_col // rows_local
        owner_offset = start_col - owner_index * rows_local
        identity_mat = jnp.broadcast_to(jnp.eye(BLOCK, dtype=jnp.float32), column_panel.shape)
        safe_square = jnp.where(my_index == owner_index, lower_sym(column_panel), identity_mat)
        own_factor = jnp.linalg.cholesky(safe_square)
        pivot_factor = spread(own_factor, "front", owner_index)
        my_panel = right_solve(pivot_factor, column_panel)
        my_panel = jnp.where(row_global < start_col, jnp.float32(0.0), my_panel)
        placed = jnp.where(my_index == owner_index, pivot_factor, my_panel)
        my_panel = my_panel.at[:, owner_offset : owner_offset + BLOCK].set(placed)
        full_panel = lax.all_gather(my_panel, "front", axis=1, tiled=True)
        tail_panel = full_panel[:, end_col:]
        update = jnp.einsum(
            "frb,fcb->frc",
            my_panel,
            tail_panel,
            precision=lax.Precision.HIGHEST,
            preferred_element_type=jnp.float32,
        )
        matrix = matrix.at[:, :, end_col:].add(-update)
        zeta = right_solve(pivot_factor, current_rhs[:, :, start_col:end_col])
        rhs_update = jnp.einsum(
            "fnb,fcb->fnc",
            zeta,
            tail_panel,
            precision=lax.Precision.HIGHEST,
            preferred_element_type=jnp.float32,
        )
        current_rhs = current_rhs.at[:, :, end_col:].add(-rhs_update)
        pivots_now = jnp.diagonal(pivot_factor, axis1=1, axis2=2)
        left_parts.append(my_panel / pivots_now[:, None, :])
        diag_parts.append(pivots_now * pivots_now)
        solved_parts.append(zeta * pivots_now[:, None, :])
    col_global = lax.broadcasted_iota(jnp.int32, (1, order_here), 1)
    combined = jnp.concatenate(left_parts + [matrix[:, :, PIVOTS:]], axis=2)
    combined = jnp.where(row_global < col_global, jnp.float32(0.0), combined)
    diag_full = jnp.concatenate(
        diag_parts + [jnp.zeros((fronts_here, order_here - PIVOTS), jnp.float32)], axis=1
    )
    on_diagonal = (row_global == col_global) & (col_global < PIVOTS)
    factored = jnp.where(on_diagonal, diag_full[:, None, :], combined)
    eliminated = jnp.concatenate(solved_parts + [current_rhs[:, :, PIVOTS:]], axis=2)
    return (factored, eliminated)


def solution(mesh):
    return jax.shard_map(
        local,
        mesh=mesh,
        in_specs=(
            P("leaf", "front", None),
            P(("leaf", "front"), None, None, None, None),
            P(("leaf", "front"), None, None),
            P(("leaf", "front"), None),
            P("leaf", None, None),
        ),
        out_specs=(P("leaf", "front", None), P("leaf", None, None)),
        check_vma=False,
    )
```

profile of v0, /device:TPU:8, one launch (start us, length us, event | category | flops | bytes accessed | tf_op | source)
XLA Modules:
  0.0 1286.0 jit_solution(12583845993747838078)
XLA Ops:
  8.6 9.4 all_to_all.10
  18.0 3.6 all-to-all-start.1
  24.8 18.3 %all-to-all-done.1 = f32[1,8,3,128,128]{4,3,2,0,1:T(8,128)S(1)} async-done(((f32[1,8,3,128,128]{4,3,2,0,1:T(8,128)}), f32[1,8,3,128,128]{4,3,2,0,1:T(8,128)S(1)}, u32[]{:S(2)}, u32[]{:S(2)}) %all-to-all-start.1) | async-done | bytes 1572896 | tf_op jit(solution)/shard_map/all_to_all | solution.py:31
  43.1 2.6 fusion.31
  45.7 2.6 copy.268
  50.0 11.7 custom-call.46
  63.8 81.2 %all-reduce.9.cloned.1.call-done = f32[1,128,128]{2,1,0:T(8,128)} async-done(((f32[1,128,128]{2,1,0:T(8,128)}), f32[1,128,128]{2,1,0:T(8,128)}) %all-reduce.9.cloned.1.call-update) | async-done | bytes 65552 | tf_op jit(solution)/shard_map/psum | solution.py:12
  145.8 9.8 custom-call.47
  159.1 41.7 %all-gather.9.cloned.1.call-done = f32[1,2048,128]{2,1,0:T(8,128)} async-done(((f32[1,128,128]{2,1,0:T(8,128)}), f32[1,2048,128]{2,1,0:T(8,128)}) %all-gather.9.cloned.1.call-update) | async-done | bytes 1048592 | tf_op jit(solution)/shard_map/all_gather | solution.py:69
  200.8 2.2 fusion.13
  203.4 11.7 custom-call.48
  217.2 80.3 %all-reduce.11.cloned.1.call-done = f32[1,128,128]{2,1,0:T(8,128)} async-done(((f32[1,128,128]{2,1,0:T(8,128)}), f32[1,128,128]{2,1,0:T(8,128)}) %all-reduce.11.cloned.1.call-update) | async-done | bytes 65552 | tf_op jit(solution)/shard_map/psum | solution.py:12
  298.4 9.8 custom-call.49
  312.1 41.2 %all-gather.11.cloned.1.call-done = f32[1,2048,128]{2,1,0:T(8,128)} async-done(((f32[1,128,128]{2,1,0:T(8,128)}), f32[1,2048,128]{2,1,0:T(8,128)}) %all-gather.11.cloned.1.call-update) | async-done | bytes 1048592 | tf_op jit(solution)/shard_map/all_gather | solution.py:69
  353.3 2.1 fusion.12
  355.8 11.7 custom-call.50
  369.6 80.3 %all-reduce.13.cloned.1.call-done = f32[1,128,128]{2,1,0:T(8,128)} async-done(((f32[1,128,128]{2,1,0:T(8,128)}), f32[1,128,128]{2,1,0:T(8,128)}) %all-reduce.13.cloned.1.call-update) | async-done | bytes 65552 | tf_op jit(solution)/shard_map/psum | solution.py:12
  450.7 9.8 custom-call.51
  460.6 2.0 gather_fusion.2
  465.5 40.3 %all-gather.13.cloned.1.call-done = f32[1,2048,128]{2,1,0:T(8,128)} async-done(((f32[1,128,128]{2,1,0:T(8,128)}), f32[1,2048,128]{2,1,0:T(8,128)}) %all-gather.13.cloned.1.call-update) | async-done | bytes 1048592 | tf_op jit(solution)/shard_map/all_gather | solution.py:69
  505.8 2.0 fusion.11
  508.2 11.7 custom-call.52
  522.8 79.7 %all-reduce.15.cloned.1.call-done = f32[1,128,128]{1,2,0:T(8,128)} async-done(((f32[1,128,128]{1,2,0:T(8,128)}), f32[1,128,128]{1,2,0:T(8,128)}) %all-reduce.15.cloned.1.call-update) | async-done | bytes 65552 | tf_op jit(solution)/shard_map/psum | solution.py:12
  603.4 9.8 custom-call.53
  613.2 2.0 gather_fusion.3
  616.8 42.3 %all-gather.15.cloned.1.call-done = f32[1,2048,128]{1,2,0:T(8,128)} async-done(((f32[1,128,128]{1,2,0:T(8,128)}), f32[1,2048,128]{1,2,0:T(8,128)}) %all-gather.15.cloned.1.call-update) | async-done | bytes 1048592 | tf_op jit(solution)/shard_map/all_gather | solution.py:69
  659.1 2.0 fusion.7
  661.4 11.7 custom-call.54
  675.4 80.3 %all-reduce.17.cloned.1.call-done = f32[1,128,128]{1,2,0:T(8,128)} async-done(((f32[1,128,128]{1,2,0:T(8,128)}), f32[1,128,128]{1,2,0:T(8,128)}) %all-reduce.17.cloned.1.call-update) | async-done | bytes 65552 | tf_op jit(solution)/shard_map/psum | solution.py:12
  756.6 9.8 custom-call.55
  766.4 2.0 gather_fusion.4
  769.9 42.4 %all-gather.17.cloned.1.call-done = f32[1,2048,128]{1,2,0:T(8,128)} async-done(((f32[1,128,128]{1,2,0:T(8,128)}), f32[1,2048,128]{1,2,0:T(8,128)}) %all-gather.17.cloned.1.call-update) | async-done | bytes 1048592 | tf_op jit(solution)/shard_map/all_gather | solution.py:69
  814.6 11.7 custom-call.56
  828.5 80.3 %all-reduce.19.cloned.1.call-done = f32[1,128,128]{1,2,0:T(8,128)} async-done(((f32[1,128,128]{1,2,0:T(8,128)}), f32[1,128,128]{1,2,0:T(8,128)}) %all-reduce.19.cloned.1.call-update) | async-done | bytes 65552 | tf_op jit(solution)/shard_map/psum | solution.py:12
  909.7 9.8 custom-call.57
  919.5 2.0 gather_fusion.5
  928.0 37.4 %all-gather.19.cloned.1.call-done = f32[1,2048,128]{1,2,0:T(8,128)} async-done(((f32[1,128,128]{1,2,0:T(8,128)}), f32[1,2048,128]{1,2,0:T(8,128)}) %all-gather.19.cloned.1.call-update) | async-done | bytes 1048592 | tf_op jit(solution)/shard_map/all_gather | solution.py:69
  967.6 11.7 custom-call.58
  981.6 80.3 %all-reduce.21.cloned.1.call-done = f32[1,128,128]{1,2,0:T(8,128)} async-done(((f32[1,128,128]{1,2,0:T(8,128)}), f32[1,128,128]{1,2,0:T(8,128)}) %all-reduce.21.cloned.1.call-update) | async-done | bytes 65552 | tf_op jit(solution)/shard_map/psum | solution.py:12
  1062.8 9.8 custom-call.59
  1072.7 2.0 gather_fusion.6
  1082.1 37.1 %all-gather.21.cloned.1.call-done = f32[1,2048,128]{1,2,0:T(8,128)} async-done(((f32[1,128,128]{1,2,0:T(8,128)}), f32[1,2048,128]{1,2,0:T(8,128)}) %all-gather.21.cloned.1.call-update) | async-done | bytes 1048592 | tf_op jit(solution)/shard_map/all_gather | solution.py:69
  1119.1 2.2 fusion.1
  1121.7 11.7 custom-call.60
  1137.6 78.5 %all-reduce.23.cloned.1.call-done = f32[1,128,128]{2,1,0:T(8,128)} async-done(((f32[1,128,128]{2,1,0:T(8,128)}), f32[1,128,128]{2,1,0:T(8,128)}) %all-reduce.23.cloned.1.call-update) | async-done | bytes 65552 | tf_op jit(solution)/shard_map/psum | solution.py:12
  1217.0 9.8 custom-call.61
  1233.9 38.1 %all-gather.23.cloned.1.call-done = f32[1,2048,128]{2,1,0:T(8,128)} async-done(((f32[1,128,128]{2,1,0:T(8,128)}), f32[1,2048,128]{2,1,0:T(8,128)}) %all-gather.23.cloned.1.call-update) | async-done | bytes 1048592 | tf_op jit(solution)/shard_map/all_gather | solution.py:69
  1272.0 2.4 fusion.36
  (260 shorter events, 77.8 us)
Async XLA Ops:
  18.0 25.1 %all-to-all-start.1 = ((f32[1,8,3,128,128]{4,3,2,0,1:T(8,128)}), f32[1,8,3,128,128]{4,3,2,0,1:T(8,128)S(1)}, u32[]{:S(2)}, u32[]{:S(2)}) async-start(f32[1,8,3,128,128]{4,3,2,0,1:T(8,128)} %bitcast.595), calls=%async_computation.1 | async-start | bytes 3145728 | tf_op jit(solution)/shard_map/all_to_all | solution.py:31
  21.6 123.4 %all-reduce.9.cloned.1.call-start = ((), (), s32[]{:S(2)}) async-start(), calls=%async_computation.2 | async-start | bytes 131072 | tf_op jit(solution)/shard_map/psum | solution.py:12
  63.7 137.1 %all-gather.9.cloned.1.call-start = ((), (), s32[]{:S(2)}) async-start(), calls=%async_computation.3 | async-start | bytes 1114112 | tf_op jit(solution)/shard_map/all_gather | solution.py:69
  158.6 138.9 %all-reduce.11.cloned.1.call-start = ((), (), s32[]{:S(2)}) async-start(), calls=%async_computation.4 | async-start | bytes 131072 | tf_op jit(solution)/shard_map/psum | solution.py:12
  217.1 136.2 %all-gather.11.cloned.1.call-start = ((), (), s32[]{:S(2)}) async-start(), calls=%async_computation.5 | async-start | bytes 1114112 | tf_op jit(solution)/shard_map/all_gather | solution.py:69
  311.9 138.0 %all-reduce.13.cloned.1.call-start = ((), (), s32[]{:S(2)}) async-start(), calls=%async_computation.6 | async-start | bytes 131072 | tf_op jit(solution)/shard_map/psum | solution.py:12
  369.5 136.2 %all-gather.13.cloned.1.call-start = ((), (), s32[]{:S(2)}) async-start(), calls=%async_computation.7 | async-start | bytes 1114112 | tf_op jit(solution)/shard_map/all_gather | solution.py:69
  460.6 47.3 %copy-start.16 = (f32[1,128,128]{1,2,0:T(8,128)}, f32[1,128,128]{1,2,0:T(8,128)S(1)}, u32[]{:S(2)}) copy-start(f32[1,128,128]{1,2,0:T(8,128)S(1)} %custom-call.51) | copy-start | bytes 196612
  463.5 138.9 %all-reduce.15.cloned.1.call-start = ((), (), s32[]{:S(2)}) async-start(), calls=%async_computation.8 | async-start | bytes 131072 | tf_op jit(solution)/shard_map/psum | solution.py:12
  522.1 137.0 %all-gather.15.cloned.1.call-start = ((), (), s32[]{:S(2)}) async-start(), calls=%async_computation.9 | async-start | bytes 1114112 | tf_op jit(solution)/shard_map/all_gather | solution.py:69
  613.2 3.6 copy-start.18
  616.1 139.5 %all-reduce.17.cloned.1.call-start = ((), (), s32[]{:S(2)}) async-start(), calls=%async_computation.10 | async-start | bytes 131072 | tf_op jit(solution)/shard_map/psum | solution.py:12
  616.4 42.6 %copy-start.14 = (f32[1,128,128]{1,2,0:T(8,128)S(1)}, f32[1,128,128]{1,2,0:T(8,128)}, u32[]{:S(2)}) copy-start(f32[1,128,128]{1,2,0:T(8,128)} %get-tuple-element.372) | copy-start | bytes 196612
  675.3 137.0 %all-gather.17.cloned.1.call-start = ((), (), s32[]{:S(2)}) async-start(), calls=%async_computation.11 | async-start | bytes 1114112 | tf_op jit(solution)/shard_map/all_gather | solution.py:69
  766.4 47.8 %copy-start.22 = (f32[1,128,128]{1,2,0:T(8,128)}, f32[1,128,128]{1,2,0:T(8,128)S(1)}, u32[]{:S(2)}) copy-start(f32[1,128,128]{1,2,0:T(8,128)S(1)} %custom-call.55) | copy-start | bytes 196612
  769.4 139.4 %all-reduce.19.cloned.1.call-start = ((), (), s32[]{:S(2)}) async-start(), calls=%async_computation.12 | async-start | bytes 131072 | tf_op jit(solution)/shard_map/psum | solution.py:12
  814.2 110.1 %copy-start.15 = (f32[1,64,2048]{2,1,0:T(8,128)S(1)}, f32[1,64,2048]{2,1,0:T(8,128)}, u32[]{:S(2)}) copy-start(f32[1,64,2048]{2,1,0:T(8,128)} %param.78) | copy-start | bytes 1572868
  814.2 110.9 %copy-start = (f32[1,2048,128]{2,1,0:T(8,128)S(1)}, f32[1,2048,128]{2,1,0:T(8,128)}, u32[]{:S(2)}) copy-start(f32[1,2048,128]{2,1,0:T(8,128)} %all-gather.9.cloned.1.call-done) | copy-start | bytes 3145732
  828.4 137.0 %all-gather.19.cloned.1.call-start = ((), (), s32[]{:S(2)}) async-start(), calls=%async_computation.13 | async-start | bytes 1114112 | tf_op jit(solution)/shard_map/all_gather | solution.py:69
  919.5 6.8 copy-start.20
  922.5 42.9 %copy-start.13 = (f32[1,128,128]{1,2,0:T(8,128)S(1)}, f32[1,128,128]{1,2,0:T(8,128)}, u32[]{:S(2)}) copy-start(f32[1,128,128]{1,2,0:T(8,128)} %get-tuple-element.376) | copy-start | bytes 196612
  922.5 139.4 %all-reduce.21.cloned.1.call-start = ((), (), s32[]{:S(2)}) async-start(), calls=%async_computation.14 | async-start | bytes 131072 | tf_op jit(solution)/shard_map/psum | solution.py:12
  967.2 109.3 %copy-start.1 = (f32[1,2048,128]{2,1,0:T(8,128)S(1)}, f32[1,2048,128]{2,1,0:T(8,128)}, u32[]{:S(2)}) copy-start(f32[1,2048,128]{2,1,0:T(8,128)} %all-gather.11.cloned.1.call-done) | copy-start | bytes 3145732
  967.2 109.3 %copy-start.6 = (f32[1,64,1920]{2,1,0:T(8,128)S(1)}, f32[1,64,1920]{2,1,0:T(8,128)}, u32[]{:S(2)}) copy-start(f32[1,64,1920]{2,1,0:T(8,128)} %copy-done.5) | copy-start | bytes 1474564
  981.5 96.2 %copy-start.17 = (f32[1,128,128]{1,2,0:T(8,128)S(1)}, f32[1,128,128]{1,2,0:T(8,128)}, u32[]{:S(2)}) copy-start(f32[1,128,128]{1,2,0:T(8,128)} %copy-done.16) | copy-start | bytes 196612
  981.5 137.7 %all-gather.21.cloned.1.call-start = ((), (), s32[]{:S(2)}) async-start(), calls=%async_computation.15 | async-start | bytes 1114112 | tf_op jit(solution)/shard_map/all_gather | solution.py:69
  1062.7 15.7 %copy-start.2 = (f32[1,2048,128]{2,1,0:T(8,128)S(1)}, f32[1,2048,128]{2,1,0:T(8,128)}, u32[]{:S(2)}) copy-start(f32[1,2048,128]{2,1,0:T(8,128)} %all-gather.13.cloned.1.call-done) | copy-start | bytes 3145732
  1072.7 3.8 copy-start.24
  1074.6 3.8 copy-start.26
  1076.2 139.9 %all-reduce.23.cloned.1.call-start = ((), (), s32[]{:S(2)}) async-start(), calls=%async_computation.16 | async-start | bytes 131072 | tf_op jit(solution)/shard_map/psum | solution.py:12
  1076.5 3.1 copy-start.19
  1076.5 3.9 copy-start.3
  1078.5 2.5 copy-start.23
  1081.0 0.9 copy-start.8
  1081.0 38.2 %copy-start.11 = (f32[1,128,128]{1,2,0:T(8,128)S(1)}, f32[1,128,128]{1,2,0:T(8,128)}, u32[]{:S(2)}) copy-start(f32[1,128,128]{1,2,0:T(8,128)} %get-tuple-element.378) | copy-start | bytes 196612
  1082.1 54.0 %copy-start.4 = (f32[1,2048,128]{1,2,0:T(8,128)S(1)}, f32[1,2048,128]{1,2,0:T(8,128)}, u32[]{:S(2)}) copy-start(f32[1,2048,128]{1,2,0:T(8,128)} %all-gather.17.cloned.1.call-done) | copy-start | bytes 3145732
  1121.6 107.2 %copy-start.30 = (pred[128]{0:T(512)(128)(4,1)S(1)}, pred[128]{0:T(512)(128)(4,1)}, u32[]{:S(2)}) copy-start(pred[128]{0:T(512)(128)(4,1)} %broadcast_compare_fusion) | copy-start | bytes 388
  1121.7 108.0 %copy-start.21 = (f32[1,128,128]{1,2,0:T(8,128)S(1)}, f32[1,128,128]{1,2,0:T(8,128)}, u32[]{:S(2)}) copy-start(f32[1,128,128]{1,2,0:T(8,128)} %copy-done.20) | copy-start | bytes 196612
  1133.5 97.0 %copy-start.7 = (f32[1,2048,128]{1,2,0:T(8,128)S(1)}, f32[1,2048,128]{1,2,0:T(8,128)}, u32[]{:S(2)}) copy-start(f32[1,2048,128]{1,2,0:T(8,128)} %all-gather.19.cloned.1.call-done) | copy-start | bytes 3145732
  1135.8 136.2 %all-gather.23.cloned.1.call-start = ((), (), s32[]{:S(2)}) async-start(), calls=%async_computation.17 | async-start | bytes 1114112 | tf_op jit(solution)/shard_map/all_gather | solution.py:69
  1137.6 93.4 %copy-start.27 = (f32[128]{0:T(128)S(1)}, f32[128]{0:T(128)}, u32[]{:S(2)}) copy-start(f32[128]{0:T(128)} %copy-done.26) | copy-start | bytes 1540
  1137.6 93.4 %copy-start.25 = (f32[1,128,128]{1,2,0:T(8,128)S(1)}, f32[1,128,128]{1,2,0:T(8,128)}, u32[]{:S(2)}) copy-start(f32[1,128,128]{1,2,0:T(8,128)} %copy-done.24) | copy-start | bytes 196612
  1137.6 94.2 %copy-start.9 = (f32[1,2048,128]{1,2,0:T(8,128)S(1)}, f32[1,2048,128]{1,2,0:T(8,128)}, u32[]{:S(2)}) copy-start(f32[1,2048,128]{1,2,0:T(8,128)} %all-gather.21.cloned.1.call-done) | copy-start | bytes 3145732
  1230.5 41.5 %copy-start.12 = (f32[1,128,128]{2,1,0:T(8,128)S(1)}, f32[1,128,128]{2,1,0:T(8,128)}, u32[]{:S(2)}) copy-start(f32[1,128,128]{2,1,0:T(8,128)} %get-tuple-element.380) | copy-start | bytes 196612
  1231.8 42.6 %copy-start.31 = (s32[128]{0:T(128)S(1)}, s32[128]{0:T(128)}, u32[]{:S(2)}) copy-start(s32[128]{0:T(128)} %iota_add_fusion.1) | copy-start | bytes 1540
  1276.2 1.3 copy-start.10
  1276.2 1.6 copy-start.28
  1278.4 0.8 copy-start.29
  (1 other events, 0.8 us)
Sparse Core Ops, SparseCore 0:
  63.8 81.1 all-reduce.8
  158.7 42.1 all-gather.8
  217.2 80.2 all-reduce.10
  312.0 41.2 all-gather.10
  369.7 80.1 all-reduce.12
  463.6 42.1 all-gather.12
  522.2 80.1 all-reduce.14
  616.3 42.7 all-gather.14
  675.4 80.1 all-reduce.16
  769.5 42.7 all-gather.16
  828.5 80.2 all-reduce.18
  922.6 42.7 all-gather.18
  981.6 80.2 all-reduce.20
  1076.3 42.7 all-gather.20
  1135.9 80.2 all-reduce.22
  1229.8 42.1 all-gather.22
where the time goes:
time: 1300 us; the launch traced here: 1290 us
  waiting for transfers between devices  980 us (75%)
  other arithmetic  202 us (16%)
  matrix products  41.7 us (3%)
  local copies, waits for them, and re-layouts  31.6 us (2%)
  between operations  15.5 us (1%)
    psum x8, waiting for transfers between devices, spread(): return lax.psum(kept, axis)  641 us
    all_gather x8, waiting for transfers between devices, local(): full_panel = lax.all_gather(my_panel, 'front', axis=1, tiled=True)  321 us
    another operation x24, other arithmetic, local(): own_factor = jnp.linalg.cholesky(safe_square)  99.8 us
    another operation x16, other arithmetic, right_solve(): jax.scipy.linalg.solve_triangular(factor, jnp.swapaxes(values, 1, 2), low...  85.3 us
  transfers between devices with their start and end apart: 17, of which 17 were waited for; matrix products, arithmetic and copies ran while one was open for 2% of the time, Pallas kernels for 0%

commit v1 on v0

v1 whole, which is shorter than its diff:
```python
import jax
import jax.numpy as jnp
from jax import lax
from jax.experimental import pallas as pl
from jax.experimental.pallas import tpu as pltpu
from jax.sharding import PartitionSpec as P

B = 128
PIV = 1024
NP = PIV // B
F32 = jnp.float32
BF16 = jnp.bfloat16
VMEM_LIMIT = 56 * 1024 * 1024


def split(x):
    hi = x.astype(BF16)
    lo = (x - hi.astype(F32)).astype(BF16)
    return hi, lo


def dot_t(a, b):
    return lax.dot_general(a, b, (((1,), (1,)), ((), ())), preferred_element_type=F32)


def dot_n(a, b):
    return lax.dot_general(a, b, (((1,), (0,)), ((), ())), preferred_element_type=F32)


def dot3_t(ah, al, bh, bl):
    return dot_t(ah, bh) + dot_t(al, bh) + dot_t(ah, bl)


def dot3_n(ah, al, bh, bl):
    return dot_n(ah, bh) + dot_n(al, bh) + dot_n(ah, bl)


def assemble_kernel(code_ref, idx_ref, recv_ref, front_ref, out_ref):
    out_ref[...] = front_ref[...]
    for s in range(recv_ref.shape[0]):
        for j in range(code_ref.shape[1]):
            code = code_ref[s, j]

            @pl.when(code >= 0)
            def _(s=s, j=j, code=code):
                cols = pl.ds(pl.multiple_of(code * B, B), B)
                out_ref[:, cols] += recv_ref[s, j * B : (j + 1) * B, :]

    cols = pl.ds(pl.multiple_of(idx_ref[0] * B, B), B)
    square = out_ref[:, cols]
    row = lax.broadcasted_iota(jnp.int32, (B, B), 0)
    col = lax.broadcasted_iota(jnp.int32, (B, B), 1)
    out_ref[:, cols] = jnp.where(row >= col, square, square.T)


def assemble(codes, index, recv, front):
    return pl.pallas_call(
        assemble_kernel,
        out_shape=jax.ShapeDtypeStruct(front.shape, F32),
        in_specs=[
            pl.BlockSpec(memory_space=pltpu.SMEM),
            pl.BlockSpec(memory_space=pltpu.SMEM),
            pl.BlockSpec(memory_space=pltpu.VMEM),
            pl.BlockSpec(memory_space=pltpu.VMEM),
        ],
        out_specs=pl.BlockSpec(memory_space=pltpu.VMEM),
        compiler_params=pltpu.CompilerParams(vmem_limit_bytes=VMEM_LIMIT),
        name="assemble",
    )(codes, index, recv, front)


def chain(a_rows, e_rows, store):
    sub = lax.broadcasted_iota(jnp.int32, (8, B), 0)
    for g in range(16):
        ra, re = a_rows[g], e_rows[g]
        base = 8 * g
        b = [jnp.broadcast_to(ra[:, base + t : base + t + 1], (8, B)) for t in range(8)]
        ga, ge = ra, re
        fa, fe = ra, re
        rcps = []
        for t in range(8):
            piv = jnp.broadcast_to(b[t][t : t + 1, :], (8, B))
            r = 1.0 / piv
            rcps.append(r)
            m = b[t] * r
            mg = jnp.where(sub == t, 0.0, m)
            mf = jnp.where(sub > t, m, 0.0)
            for u in range(t + 1, 8):
                b[u] = b[u] - mg * jnp.broadcast_to(b[u][t : t + 1, :], (8, B))
            pa = jnp.broadcast_to(fa[t : t + 1, :], (8, B))
            pe = jnp.broadcast_to(fe[t : t + 1, :], (8, B))
            fa = fa - mf * pa
            fe = fe - mf * pe
            ga = ga - mg * pa
            ge = ge - mg * pe
        rc = rcps[0]
        for t in range(1, 8):
            rc = jnp.where(sub == t, rcps[t], rc)
        store(g, fa, fe, rc)
        ga = ga * rc
        ge = ge * rc
        if g < 15:
            gab = [jnp.broadcast_to(ga[t : t + 1, :], (8, B)) for t in range(8)]
            geb = [jnp.broadcast_to(ge[t : t + 1, :], (8, B)) for t in range(8)]
            for i in range(g + 1, 16):
                acc_a, acc_e = a_rows[i], e_rows[i]
                for t in range(8):
                    c = jnp.broadcast_to(a_rows[i][:, base + t : base + t + 1], (8, B))
                    acc_a = acc_a - c * gab[t]
                    acc_e = acc_e - c * geb[t]
                a_rows[i], e_rows[i] = acc_a, acc_e


def factor_kernel(idx_ref, a_ref, b_ref, lh_ref, ll_ref, t_ref, dinv_ref, y_ref, own_ref,
                  vh, vl, u_ref, lt_ref):
    me = idx_ref[0]
    vh[...] = jnp.zeros_like(vh)
    vl[...] = jnp.zeros_like(vl)
    lh_ref[...] = jnp.zeros_like(lh_ref)
    ll_ref[...] = jnp.zeros_like(ll_ref)
    own_ref[...] = jnp.zeros_like(own_ref)
    row = lax.broadcasted_iota(jnp.int32, (B, B), 0)
    col = lax.broadcasted_iota(jnp.int32, (B, B), 1)
    ri = lax.broadcasted_iota(jnp.int32, (8, B), 0)
    ci = lax.broadcasted_iota(jnp.int32, (8, B), 1)

    def panel(k, _):
        kcols = pl.ds(pl.multiple_of(k * B, B), B)
        krows = pl.ds(pl.multiple_of(k * B, B), B)
        chunks = (k + 1) // 2

        def updated(value, rows):
            def body(c, acc):
                cols = pl.ds(pl.multiple_of(c * 256, 256), 256)
                return acc - dot3_t(vh[rows, cols], vl[rows, cols], lh_ref[krows, cols], ll_ref[krows, cols])

            return lax.fori_loop(0, chunks, body, value)

        u_ref[...] = updated(a_ref[krows, kcols], krows)
        a_rows = [u_ref[8 * i : 8 * i + 8, :] for i in range(16)]
        e_rows = [jnp.where(ri + 8 * i == ci, 1.0, 0.0) for i in range(16)]
        diag = []

        def store(g, fa, fe, rc):
            own = ri + 8 * g == ci
            diag.append(jnp.where(own, fa, 0.0))
            lt_ref[8 * g : 8 * g + 8, :] = jnp.where(own, fa, jnp.where(ri + 8 * g < ci, fa * rc, 0.0))
            t_ref[k, 8 * g : 8 * g + 8, :] = fe

        chain(a_rows, e_rows, store)
        total = diag[0]
        for g in range(1, 16):
            total = total + diag[g]
        dinv = 1.0 / jnp.sum(total, axis=0, keepdims=True)
        dinv_ref[0:1, kcols] = dinv
        th, tl = split(t_ref[k])

        @pl.when(me == k)
        def _():
            own_ref[:, kcols] = lt_ref[...].T

        def rest(r, _):
            rows = pl.ds(pl.multiple_of(r * B, B), B)
            uh, ul = split(updated(a_ref[rows, kcols], rows))
            v = dot3_t(uh, ul, th, tl)
            vh[rows, kcols], vl[rows, kcols] = split(v)
            lower = v * dinv
            lh_ref[rows, kcols], ll_ref[rows, kcols] = split(lower)

            @pl.when(me == r)
            def _():
                own_ref[:, kcols] = lower

            return 0

        lax.fori_loop(k + 1, NP, rest, 0)
        rows = pl.ds(PIV, b_ref.shape[0])
        uh, ul = split(updated(b_ref[:, kcols], rows))
        v = dot3_t(uh, ul, th, tl)
        vh[rows, kcols], vl[rows, kcols] = split(v)
        y_ref[:, kcols] = v
        return 0

    lax.fori_loop(0, NP, panel, 0)


def factor(index, gathered, rhs):
    nrhs = rhs.shape[0]
    vmem = pl.BlockSpec(memory_space=pltpu.VMEM)
    return pl.pallas_call(
        factor_kernel,
        grid=(1,),
        out_shape=(
            jax.ShapeDtypeStruct((PIV, PIV), BF16),
            jax.ShapeDtypeStruct((PIV, PIV), BF16),
            jax.ShapeDtypeStruct((NP, B, B), F32),
            jax.ShapeDtypeStruct((8, PIV), F32),
            jax.ShapeDtypeStruct((nrhs, PIV), F32),
            jax.ShapeDtypeStruct((B, PIV), F32),
        ),
        in_specs=[
            pl.BlockSpec(memory_space=pltpu.SMEM),
            pl.BlockSpec((PIV, PIV), lambda i: (0, 0)),
            pl.BlockSpec((nrhs, PIV), lambda i: (0, 0)),
        ],
        out_specs=(
            pl.BlockSpec((PIV, PIV), lambda i: (0, 0)),
            pl.BlockSpec((PIV, PIV), lambda i: (0, 0)),
            pl.BlockSpec((NP, B, B), lambda i: (0, 0, 0)),
            pl.BlockSpec((8, PIV), lambda i: (0, 0)),
            pl.BlockSpec((nrhs, PIV), lambda i: (0, 0)),
            pl.BlockSpec((B, PIV), lambda i: (0, 0)),
        ),
        scratch_shapes=[
            pltpu.VMEM((PIV + nrhs, PIV), BF16),
            pltpu.VMEM((PIV + nrhs, PIV), BF16),
            pltpu.VMEM((B, B), F32),
            pltpu.VMEM((B, B), F32),
        ],
        compiler_params=pltpu.CompilerParams(vmem_limit_bytes=VMEM_LIMIT),
        name="factor",
    )(index, gathered, rhs)


def finish_kernel(idx_ref, a_ref, lh_ref, ll_ref, t_ref, dinv_ref, y_ref, own_ref, mine_ref, b_ref,
                  fac_ref, eli_ref, vh, vl, wh, wl, v32):
    me = idx_ref[0]
    order = fac_ref.shape[1]
    W2 = 2 * B
    for p in range(NP // 2):
        t0h, t0l = split(t_ref[2 * p])
        t1h, t1l = split(t_ref[2 * p + 1])
        r1 = slice((2 * p + 1) * B, (2 * p + 2) * B)
        c0 = slice(2 * p * B, (2 * p + 1) * B)
        xh, xl = split(dot3_n(lh_ref[r1, c0], ll_ref[r1, c0], t0h, t0l))
        xh, xl = split(-dot3_n(t1h, t1l, xh, xl))
        zero = jnp.zeros((B, B), BF16)
        tph = jnp.concatenate([jnp.concatenate([t0h, zero], 1), jnp.concatenate([xh, t1h], 1)], 0)
        tpl = jnp.concatenate([jnp.concatenate([t0l, zero], 1), jnp.concatenate([xl, t1l], 1)], 0)
        pc = slice(p * W2, (p + 1) * W2)
        dinv = dinv_ref[0:1, pc]

        def rows_body(r, _, p=p, pc=pc, tph=tph, tpl=tpl, dinv=dinv):
            rows = pl.ds(pl.multiple_of(r * W2, W2), W2)
            u = a_ref[rows, pc]
            if p:
                prev = slice(0, p * W2)
                u = u - dot3_t(vh[rows, prev], vl[rows, prev], lh_ref[pc, prev], ll_ref[pc, prev])
            uh, ul = split(u)
            v = dot3_t(uh, ul, tph, tpl)
            v32[rows, pc] = v
            vh[rows, pc], vl[rows, pc] = split(v)
            wh[rows, pc], wl[rows, pc] = split(v * dinv)
            return 0

        lax.fori_loop(0, (order - PIV) // W2, rows_body, 0)

    yh, yl = split(y_ref[...])
    eli_ref[:, :PIV] = y_ref[...]
    nblk = (order - PIV) // W2

    def b_body(c, _):
        rows = pl.ds(pl.multiple_of(c * W2, W2), W2)
        dst = pl.ds(pl.multiple_of(PIV + c * W2, W2), W2)
        eli_ref[:, dst] = b_ref[:, dst] - dot3_t(yh, yl, wh[rows, :], wl[rows, :])
        return 0

    lax.fori_loop(0, nblk, b_body, 0)

    @pl.when(me < NP)
    def _():
        fac_ref[:, :PIV] = own_ref[...]
        fac_ref[:, PIV:] = jnp.zeros((B, order - PIV), F32)

    @pl.when(me >= NP)
    def _():
        mine = pl.ds(pl.multiple_of((me - NP) * B, B), B)
        fac_ref[:, :PIV] = v32[mine, :] * dinv_ref[0:1, :]
        mh, ml = vh[mine, :], vl[mine, :]

        def s_body(c, _):
            rows = pl.ds(pl.multiple_of(c * W2, W2), W2)
            dst = pl.ds(pl.multiple_of(PIV + c * W2, W2), W2)
            s = mine_ref[:, dst] - dot3_t(mh, ml, wh[rows, :], wl[rows, :])
            row = me * B + lax.broadcasted_iota(jnp.int32, (B, W2), 0)
            col = PIV + c * W2 + lax.broadcasted_iota(jnp.int32, (B, W2), 1)
            fac_ref[:, dst] = jnp.where(row >= col, s, 0.0)
            return 0

        lax.fori_loop(0, nblk, s_body, 0)


def finish(index, gathered, lh, ll, t, dinv, y, own, mine, rhs):
    nrhs, order = rhs.shape
    low = order - PIV
    return pl.pallas_call(
        finish_kernel,
        grid=(1,),
        out_shape=(
            jax.ShapeDtypeStruct((B, order), F32),
            jax.ShapeDtypeStruct((nrhs, order), F32),
        ),
        in_specs=[
            pl.BlockSpec(memory_space=pltpu.SMEM),
            pl.BlockSpec((low, PIV), lambda i: (1, 0)),
            pl.BlockSpec((PIV, PIV), lambda i: (0, 0)),
            pl.BlockSpec((PIV, PIV), lambda i: (0, 0)),
            pl.BlockSpec((NP, B, B), lambda i: (0, 0, 0)),
            pl.BlockSpec((8, PIV), lambda i: (0, 0)),
            pl.BlockSpec((nrhs, PIV), lambda i: (0, 0)),
            pl.BlockSpec((B, PIV), lambda i: (0, 0)),
            pl.BlockSpec((B, order), lambda i: (0, 0)),
            pl.BlockSpec((nrhs, order), lambda i: (0, 0)),
        ],
        out_specs=(
            pl.BlockSpec((B, order), lambda i: (0, 0)),
            pl.BlockSpec((nrhs, order), lambda i: (0, 0)),
        ),
        scratch_shapes=[
            pltpu.VMEM((low, PIV), BF16),
            pltpu.VMEM((low, PIV), BF16),
            pltpu.VMEM((low, PIV), BF16),
            pltpu.VMEM((low, PIV), BF16),
            pltpu.VMEM((low, PIV), F32),
        ],
        compiler_params=pltpu.CompilerParams(vmem_limit_bytes=VMEM_LIMIT),
        name="finish",
    )(index, gathered, lh, ll, t, dinv, y, own, mine, rhs)


def local(front_matrix, child_blocks, child_target, child_count, shot_rhs):
    leaves, slots = child_blocks.shape[1:3]
    slot_ids = lax.broadcasted_iota(jnp.int32, (leaves, slots), 1)
    live_code = jnp.where(slot_ids < child_count[0][:, None], child_target[0], -1)
    code_rows = jnp.zeros((leaves, 8, B), F32).at[:, 0, :slots].set(live_code.astype(F32))
    payload = jnp.concatenate([child_blocks[0].reshape(leaves, slots * B, B), code_rows], axis=1)
    arrived = lax.all_to_all(payload, "leaf", split_axis=0, concat_axis=0, tiled=True)
    codes = arrived[:, slots * B, :slots].astype(jnp.int32)
    index = lax.axis_index("front").astype(jnp.int32).reshape(1)
    mine = assemble(codes, index, arrived, front_matrix[0])
    gathered = lax.all_gather(mine[:, :PIV], "front", axis=0, tiled=True)
    rhs = shot_rhs[0]
    lh, ll, t, dinv, y, own = factor(index, gathered, rhs)
    factored, eliminated = finish(index, gathered, lh, ll, t, dinv, y, own, mine, rhs)
    return factored[None], eliminated[None]


def solution(mesh):
    return jax.shard_map(
        local,
        mesh=mesh,
        in_specs=(
            P("leaf", "front", None),
            P(("leaf", "front"), None, None, None, None),
            P(("leaf", "front"), None, None),
            P(("leaf", "front"), None),
            P("leaf", None, None),
        ),
        out_specs=(P("leaf", "front", None), P("leaf", None, None)),
        check_vma=False,
    )
```

time: 1300 us -> 208 us (0.16)
  waiting for transfers between devices: 980 us -> 93.4 us
  other arithmetic: 202 us -> 4.03 us
  Pallas kernels: 0 us -> 86.8 us
  matrix products: 41.7 us -> 0 us
  local copies, waits for them, and re-layouts: 31.6 us -> 3.17 us
    psum x8 -> x0, waiting for transfers between devices: 641 us -> none  [spread(): return lax.psum(kept, axis)]
    all_gather x8 -> x1, waiting for transfers between devices: 321 us -> 71.5 us  [local(): gathered = lax.all_gather(mine[:, :PIV], 'front', axis=0, tiled=True)]
    another operation x40 -> x0, other arithmetic: 185 us -> none  [the longest x24 99.8 us: local(): own_factor = jnp.linalg.cholesky(safe_square)]
    pallas_call x0 -> x3, Pallas kernels: none -> 86.8 us  [the longest x1 63.4 us: factor(): pl.pallas_call(factor_kernel, grid=(1,), out_shape=(jax.ShapeDtypeStruct(...]
    dot_general x17 -> x0, matrix products: 26.3 us -> none  [the longest x8 16.7 us: local(): jnp.einsum('frb,fcb->frc', my_panel, tail_panel, precision=lax.Precision....]
    gather x8 -> x0, local copies, waits for them, and re-layouts: 15.7 us -> none  [local(): pivots_now = jnp.diagonal(pivot_factor, axis1=1, axis2=2)]
    another operation x16 -> x0, matrix products: 15.3 us -> none  [right_solve(): jax.scipy.linalg.solve_triangular(factor, jnp.swapaxes(values, 1, 2), low...]
  transfers between devices with their start and end apart: 17 -> 2, of which waited for: 17 -> 2; matrix products, arithmetic and copies ran while one was open for 2% -> 0% of each run, Pallas kernels for 0% -> 0%
where the time goes in v1:
time: 208 us; the launch traced here: 206 us
  waiting for transfers between devices  93.4 us (45%)
  Pallas kernels  86.8 us (42%)
  between operations  14 us (7%)
  starting transfers between devices  4.34 us (2%)
  other arithmetic  4.03 us (2%)
  local copies, waits for them, and re-layouts  3.17 us (2%)
    all_gather x1, waiting for transfers between devices, local(): gathered = lax.all_gather(mine[:, :PIV], 'front', axis=0, tiled=True)  71.5 us
    pallas_call x1, Pallas kernels, factor(): pl.pallas_call(factor_kernel, grid=(1,), out_shape=(jax.ShapeDtypeStruct(...  63.4 us
    all_to_all x1, waiting for transfers between devices, local(): lax.all_to_all(payload, 'leaf', split_axis=0, concat_axis=0, tiled=True)  21.9 us
    pallas_call x1, Pallas kernels, finish(): pl.pallas_call(finish_kernel, grid=(1,), out_shape=(jax.ShapeDtypeStruct(...  20.2 us
    all_to_all x1, starting transfers between devices, local(): lax.all_to_all(payload, 'leaf', split_axis=0, concat_axis=0, tiled=True)  4.3 us
  transfers between devices with their start and end apart: 2, of which 2 were waited for; matrix products, arithmetic and copies ran while one was open for 0% of the time, Pallas kernels for 0%

profile of v1, /device:TPU:8, one launch (start us, length us, event | category | flops | bytes accessed | tf_op | source)
XLA Modules:
  0.0 205.8 jit_solution(9657642526355212996)
XLA Ops:
  7.2 0.8 copy.10
  7.9 0.7 fusion
  8.6 2.7 %select_maximum_fusion = f32[8,392,128]{2,1,0:T(8,128)} fusion(f32[8,1,3]{2,1,0:T(1,128)S(1)} %fusion, f32[8,384,128]{2,1,0:T(8,128)} %bitcast.11), kind=kLoop, calls=%fused_computation | loop fusion | flops 1204224 | bytes 3178592 | tf_op jit(solution)/shard_map/concatenate | solution.py:336
  11.3 4.3 %all-to-all-start = ((f32[8,392,128]{2,1,0:T(8,128)}), f32[8,392,128]{2,1,0:T(8,128)S(1)}, u32[]{:S(2)}, u32[]{:S(2)}) async-start(f32[8,392,128]{2,1,0:T(8,128)} %select_maximum_fusion), calls=%async_computation | async-start | bytes 3211264 | tf_op jit(solution)/shard_map/all_to_all | solution.py:337
  15.6 0.0 all-gather.2.cloned.1.call-start
  15.7 21.9 %all-to-all-done.recv_ref = f32[8,392,128]{2,1,0:T(8,128)S(1)} async-done(((f32[8,392,128]{2,1,0:T(8,128)}), f32[8,392,128]{2,1,0:T(8,128)S(1)}, u32[]{:S(2)}, u32[]{:S(2)}) %all-to-all-start) | async-done | bytes 1605664 | tf_op jit(solution)/shard_map/all_to_all | solution.py:337
  37.6 0.0 copy-start
  37.6 0.6 slice_convert_fusion
  38.2 0.5 copy-done
  38.7 3.3 %assemble.1.mine_ref = f32[128,2048]{1,0:T(8,128)} custom-call(s32[8,3]{1,0:T(8,128)} %bitcast.13, s32[1]{0:T(128)} %bitcast.idx_ref, f32[8,392,128]{2,1,0:T(8,128)} %copy-done, f32[128,2048]{1,0:T(8,128)} %bitcast.12), custom_call_target="tpu_custom_call" | custom-call | tf_op jit(solution)/shard_map/assemble/pallas_call | solution.py:57
  42.0 1.9 slice.32
  43.9 0.0 all-gather.2.cloned.1.call-update
  43.9 71.5 %all-gather.2.cloned.1.call-done.a_ref = f32[2048,1024]{1,0:T(8,128)} async-done(((f32[128,1024]{1,0:T(8,128)}), f32[2048,1024]{1,0:T(8,128)}) %all-gather.2.cloned.1.call-update) | async-done | bytes 8388624 | tf_op jit(solution)/shard_map/all_gather | solution.py:341
  115.4 63.4 %factor.1 = (bf16[1024,1024]{1,0:T(8,128)(2,1)}, bf16[1024,1024]{1,0:T(8,128)(2,1)}, f32[8,128,128]{2,1,0:T(8,128)}, f32[8,1024]{1,0:T(8,128)}, f32[64,1024]{1,0:T(8,128)}, /*index=5*/f32[128,1024]{1,0:T(8,128)}) custom-call(s32[1]{0:T(128)} %bitcast.idx_ref, f32[2048,1024]{1,0:T(8,128)} %all-gather.2.cloned.1.call-done.a_ref, f32[64,2048]{1,0:T(8,128)} %bitcast.9), custom_call_target="tpu_custom_call" | custom-call | tf_op jit(solution)/shard_map/factor/pallas_call | solution.py:190
  178.8 20.2 %finish.1 = (f32[128,2048]{1,0:T(8,128)}, f32[64,2048]{1,0:T(8,128)}) custom-call(s32[1]{0:T(128)} %bitcast.idx_ref, f32[2048,1024]{1,0:T(8,128)} %all-gather.2.cloned.1.call-done.a_ref, bf16[1024,1024]{1,0:T(8,128)(2,1)} %get-tuple-element.22.lh_ref, bf16[1024,1024]{1,0:T(8,128)(2,1)} %get-tuple-element.23.ll_ref, f32[8,128,128]{2,1,0:T(8,128)} %get-tuple-element.24.t_ref, ...), custom_call_target="tpu_custom_call" | custom-call | tf_op jit(solution)/shard_map/finish/pallas_call | solution.py:296
Async XLA Ops:
  11.3 26.2 %all-to-all-start = ((f32[8,392,128]{2,1,0:T(8,128)}), f32[8,392,128]{2,1,0:T(8,128)S(1)}, u32[]{:S(2)}, u32[]{:S(2)}) async-start(f32[8,392,128]{2,1,0:T(8,128)} %select_maximum_fusion), calls=%async_computation | async-start | bytes 3211264 | tf_op jit(solution)/shard_map/all_to_all | solution.py:337
  15.6 99.8 %all-gather.2.cloned.1.call-start = ((), (), s32[]{:S(2)}) async-start(), calls=%async_computation.1 | async-start | bytes 8912896 | tf_op jit(solution)/shard_map/all_gather | solution.py:341
  37.6 1.2 copy-start
Sparse Core Ops, SparseCore 0:
  44.0 71.3 all-gather.1

commit v2 on v1

v2 whole, which is shorter than its diff:
```python
import jax
import jax.numpy as jnp
from jax import lax
from jax.experimental import pallas as pl
from jax.experimental.pallas import tpu as pltpu
from jax.sharding import PartitionSpec as P

B = 128
PIV = 1024
NP = PIV // B
F32 = jnp.float32
BF16 = jnp.bfloat16
VMEM_LIMIT = 56 * 1024 * 1024


def split(x):
    hi = x.astype(BF16)
    lo = (x - hi.astype(F32)).astype(BF16)
    return hi, lo


def dot_t(a, b):
    return lax.dot_general(a, b, (((1,), (1,)), ((), ())), preferred_element_type=F32)


def dot_n(a, b):
    return lax.dot_general(a, b, (((1,), (0,)), ((), ())), preferred_element_type=F32)


def dot3_t(ah, al, bh, bl):
    return dot_t(ah, bh) + dot_t(al, bh) + dot_t(ah, bl)


def dot3_n(ah, al, bh, bl):
    return dot_n(ah, bh) + dot_n(al, bh) + dot_n(ah, bl)


def assemble_kernel(code_ref, idx_ref, recv_ref, front_ref, out_ref):
    out_ref[...] = front_ref[...]
    for s in range(recv_ref.shape[0]):
        for j in range(code_ref.shape[1]):
            code = code_ref[s, j]

            @pl.when(code >= 0)
            def _(s=s, j=j, code=code):
                cols = pl.ds(pl.multiple_of(code * B, B), B)
                out_ref[:, cols] += recv_ref[s, j * B : (j + 1) * B, :]

    cols = pl.ds(pl.multiple_of(idx_ref[0] * B, B), B)
    square = out_ref[:, cols]
    row = lax.broadcasted_iota(jnp.int32, (B, B), 0)
    col = lax.broadcasted_iota(jnp.int32, (B, B), 1)
    out_ref[:, cols] = jnp.where(row >= col, square, square.T)


def assemble(codes, index, recv, front):
    return pl.pallas_call(
        assemble_kernel,
        out_shape=jax.ShapeDtypeStruct(front.shape, F32),
        in_specs=[
            pl.BlockSpec(memory_space=pltpu.SMEM),
            pl.BlockSpec(memory_space=pltpu.SMEM),
            pl.BlockSpec(memory_space=pltpu.VMEM),
            pl.BlockSpec(memory_space=pltpu.VMEM),
        ],
        out_specs=pl.BlockSpec(memory_space=pltpu.VMEM),
        compiler_params=pltpu.CompilerParams(vmem_limit_bytes=VMEM_LIMIT),
        name="assemble",
    )(codes, index, recv, front)


def chain(a_rows, e_rows, store, side):
    sub = lax.broadcasted_iota(jnp.int32, (8, B), 0)
    for g in range(16):
        if g < len(side):
            side[g]()
        ra, re = a_rows[g], e_rows[g]
        base = 8 * g
        b = [jnp.broadcast_to(ra[:, base + t : base + t + 1], (8, B)) for t in range(8)]
        ga, ge = ra, re
        fa, fe = ra, re
        rcps = []
        for t in range(8):
            piv = jnp.broadcast_to(b[t][t : t + 1, :], (8, B))
            r = 1.0 / piv
            rcps.append(r)
            m = b[t] * r
            mg = jnp.where(sub == t, 0.0, m)
            mf = jnp.where(sub > t, m, 0.0)
            for u in range(t + 1, 8):
                b[u] = b[u] - mg * jnp.broadcast_to(b[u][t : t + 1, :], (8, B))
            pa = jnp.broadcast_to(fa[t : t + 1, :], (8, B))
            pe = jnp.broadcast_to(fe[t : t + 1, :], (8, B))
            fa = fa - mf * pa
            fe = fe - mf * pe
            ga = ga - mg * pa
            ge = ge - mg * pe
        rc = rcps[0]
        for t in range(1, 8):
            rc = jnp.where(sub == t, rcps[t], rc)
        store(g, fa, fe, rc)
        ga = ga * rc
        ge = ge * rc
        if g < 15:
            gab = [jnp.broadcast_to(ga[t : t + 1, :], (8, B)) for t in range(8)]
            geb = [jnp.broadcast_to(ge[t : t + 1, :], (8, B)) for t in range(8)]
            for i in range(g + 1, 16):
                acc_a, acc_e = a_rows[i], e_rows[i]
                for t in range(8):
                    c = jnp.broadcast_to(a_rows[i][:, base + t : base + t + 1], (8, B))
                    acc_a = acc_a - c * gab[t]
                    acc_e = acc_e - c * geb[t]
                a_rows[i], e_rows[i] = acc_a, acc_e


HALF = PIV // 2
W2 = 2 * B


def cat_blocks(a, b, c, d):
    return jnp.concatenate([jnp.concatenate([a, b], 1), jnp.concatenate([c, d], 1)], 0)


def factor_panels(k0, k1, a_ref, b_ref, vh, vl, v32, lh, ll, t_ref, lt_ref, dinv_ref,
                  rest_ref, u_ref, part_ref, e_ref, extra):
    row0 = k0 * B
    na, nrhs = a_ref.shape[0], b_ref.shape[0]
    ri = lax.broadcasted_iota(jnp.int32, (8, B), 0)
    ci = lax.broadcasted_iota(jnp.int32, (8, B), 1)
    chunks = [(c * W2, W2) for c in range(na // W2)] + [(na, nrhs)]

    def settle(k, r0, n):
        rows, cols = slice(r0, r0 + n), pl.ds(pl.multiple_of(k * B, B), B)
        th, tl = split(t_ref[k])
        uh, ul = split(rest_ref[rows, :])
        v = dot3_t(uh, ul, th, tl)
        v32[rows, cols] = v
        vh[rows, cols], vl[rows, cols] = split(v)
        if r0 < na:
            lrows = slice(row0 + r0, row0 + r0 + n)
            lh[lrows, cols], ll[lrows, cols] = split(v * dinv_ref[0:1, cols])

    def panel(k, _):
        kcols = pl.ds(pl.multiple_of(k * B, B), B)
        acols = pl.ds(pl.multiple_of((k - k0) * B, B), B)
        prev = jnp.maximum(k - 1, k0)
        after = jnp.minimum(k + 1, k1 - 1)
        nabs = pl.ds(pl.multiple_of(after * B, B), B)
        nloc = pl.ds(pl.multiple_of((after - k0) * B, B), B)
        a_rows = [u_ref[8 * i : 8 * i + 8, :] for i in range(16)]
        e_rows = [jnp.where(ri + 8 * i == ci, 1.0, 0.0) for i in range(16)]
        diag = []

        def store(g, fa, fe, rc):
            own = ri + 8 * g == ci
            diag.append(jnp.where(own, fa, 0.0))
            lt_ref[k, 8 * g : 8 * g + 8, :] = jnp.where(own, fa, jnp.where(ri + 8 * g < ci, fa * rc, 0.0))
            e_ref[8 * g : 8 * g + 8, :] = fe

        def update(r0, n):
            rows = slice(r0, r0 + n)
            src = a_ref[rows, acols] if r0 < na else b_ref[:, acols]
            rest_ref[rows, :] = src - dot3_t(vh[rows, :], vl[rows, :], lh[kcols, :], ll[kcols, :])

        def partial():
            part_ref[...] = a_ref[nloc, nloc] - dot3_t(vh[nloc, :], vl[nloc, :], lh[nabs, :], ll[nabs, :])

        side = [lambda c=c: settle(prev, *c) for c in chunks]
        side += [lambda c=c: update(*c) for c in chunks]
        side += [partial] + extra(k)
        chain(a_rows, e_rows, store, side)
        total = diag[0]
        for g in range(1, 16):
            total = total + diag[g]
        dinv = 1.0 / jnp.sum(total, axis=0, keepdims=True)
        dinv_ref[0:1, kcols] = dinv
        t = e_ref[...]
        t_ref[k] = t
        th, tl = split(t)
        uh, ul = split(rest_ref[nloc, :])
        v = dot3_t(uh, ul, th, tl)
        v_h, v_l = split(v)
        l_h, l_l = split(v * dinv)
        u_ref[...] = part_ref[...] - dot3_t(v_h, v_l, l_h, l_l)
        return 0

    lax.fori_loop(k0, k1, panel, 0)
    for c in chunks:
        settle(k1 - 1, *c)


def first_kernel(idx_ref, y0_ref, y1_ref, y2_ref, y3_ref, b_ref,
                 vh, vl, lh, ll, t_ref, dinv_ref, y_ref, own_ref,
                 a_ref, v32, lt_ref, rest_ref, u_ref, part_ref, e_ref):
    me = idx_ref[0]
    ypos = lax.rem(me, 4)
    for d, ref in enumerate((y0_ref, y1_ref, y2_ref, y3_ref)):
        src = lax.rem(ypos + 4 - d, 4)
        for z in range(2):
            rows = pl.ds(pl.multiple_of((4 * z + src) * B, B), B)
            a_ref[rows, :] = ref[z * B : (z + 1) * B, :]
    for ref in (vh, vl, lh, ll, rest_ref, dinv_ref):
        ref[...] = jnp.zeros_like(ref)
    t_ref[0] = jnp.zeros((B, B), F32)
    u_ref[...] = a_ref[0:B, 0:B]
    factor_panels(0, NP // 2, a_ref, b_ref, vh, vl, v32, lh, ll, t_ref, lt_ref, dinv_ref,
                  rest_ref, u_ref, part_ref, e_ref, lambda k: [])
    nrhs = b_ref.shape[0]
    y_ref[...] = v32[PIV : PIV + nrhs, :]
    near = jnp.minimum(me, NP - 1)
    rows = pl.ds(pl.multiple_of(near * B, B), B)
    col = lax.broadcasted_iota(jnp.int32, (B, HALF), 1)
    own_ref[...] = jnp.where(col < near * B, v32[rows, :] * dinv_ref[0:1, :], 0.0)

    @pl.when(me < NP // 2)
    def _():
        own_ref[:, rows] = lt_ref[me].T


def whole(shape):
    zeros = (0,) * len(shape)
    return pl.BlockSpec(shape, lambda i: zeros)


def first(index, parts, rhs):
    nrhs = rhs.shape[0]
    outs = (
        ((PIV + nrhs, HALF), BF16),
        ((PIV + nrhs, HALF), BF16),
        ((PIV, HALF), BF16),
        ((PIV, HALF), BF16),
        ((NP // 2, B, B), F32),
        ((8, HALF), F32),
        ((nrhs, HALF), F32),
        ((B, HALF), F32),
    )
    return pl.pallas_call(
        first_kernel,
        grid=(1,),
        out_shape=tuple(jax.ShapeDtypeStruct(*o) for o in outs),
        in_specs=[pl.BlockSpec(memory_space=pltpu.SMEM)] + [whole((W2, HALF))] * 4 + [whole((nrhs, HALF))],
        out_specs=tuple(whole(o[0]) for o in outs),
        scratch_shapes=[
            pltpu.VMEM((PIV, HALF), F32),
            pltpu.VMEM((PIV + nrhs, HALF), F32),
            pltpu.VMEM((NP // 2, B, B), F32),
            pltpu.VMEM((PIV + nrhs, B), F32),
            pltpu.VMEM((B, B), F32),
            pltpu.VMEM((B, B), F32),
            pltpu.VMEM((B, B), F32),
        ],
        compiler_params=pltpu.CompilerParams(vmem_limit_bytes=VMEM_LIMIT),
        cost_estimate=pl.CostEstimate(flops=2 * 10**10, bytes_accessed=2 * 10**7, transcendentals=0),
        name="first",
    )(index, *parts, rhs)


def second_kernel(idx_ref, all_ref, vh0, vl0, lh0, ll0, t0, dinv0, y0, own0, mine_ref, b_ref,
                  fac_ref, eli_ref,
                  a_ref, a21, vh, vl, v32, lh, ll, t_ref, lt_ref, dinv_ref, rest_ref, u_ref, part_ref,
                  e_ref, xh, xl, x32, wh, wl, u21, tph_ref, tpl_ref, sem):
    me = idx_ref[0]
    nrhs, order = b_ref.shape
    low = order - PIV
    near_copy = pltpu.make_async_copy(all_ref.at[pl.ds(HALF, HALF), pl.ds(HALF, HALF)], a_ref, sem.at[0])
    far_copy = pltpu.make_async_copy(all_ref.at[pl.ds(PIV, low), :], a21, sem.at[1])
    near_copy.start()
    far_copy.start()
    for ref, src in ((vh, vh0), (vl, vl0)):
        ref[:, :HALF] = src[HALF:, :]
        ref[:, HALF:] = jnp.zeros((ref.shape[0], HALF), BF16)
    for ref, src in ((lh, lh0), (ll, ll0)):
        ref[:, :HALF] = src[...]
        ref[:, HALF:] = jnp.zeros((ref.shape[0], HALF), BF16)
    dinv_ref[...] = jnp.zeros_like(dinv_ref)
    dinv_ref[:, :HALF] = dinv0[...]
    t_ref[: NP // 2] = t0[...]
    t_ref[NP // 2 :] = jnp.zeros((NP // 2, B, B), F32)
    rest_ref[...] = jnp.zeros_like(rest_ref)
    xh[...] = jnp.zeros_like(xh)
    xl[...] = jnp.zeros_like(xl)
    near_copy.wait()
    u_ref[...] = a_ref[0:B, 0:B] - dot3_t(
        vh[0:B, :HALF], vl[0:B, :HALF], lh[HALF : HALF + B, :HALF], ll[HALF : HALF + B, :HALF]
    )
    far_copy.wait()

    def pair_inverse(i):
        t0h, t0l = split(t_ref[2 * i])
        t1h, t1l = split(t_ref[2 * i + 1])
        r1 = pl.ds(pl.multiple_of((2 * i + 1) * B, B), B)
        c0 = pl.ds(pl.multiple_of(2 * i * B, B), B)
        zh, zl = split(dot3_n(lh[r1, c0], ll[r1, c0], t0h, t0l))
        zh, zl = split(-dot3_n(t1h, t1l, zh, zl))
        zero = jnp.zeros((B, B), BF16)
        tph_ref[...] = cat_blocks(t0h, zero, zh, t1h)
        tpl_ref[...] = cat_blocks(t0l, zero, zl, t1l)

    def below_update(i, r0):
        rows, pc = slice(r0, r0 + W2), pl.ds(pl.multiple_of(i * W2, W2), W2)
        u21[rows, :] = a21[rows, pc] - dot3_t(xh[rows, :], xl[rows, :], lh[pc, :], ll[pc, :])

    def below_settle(i, r0):
        rows, pc = slice(r0, r0 + W2), pl.ds(pl.multiple_of(i * W2, W2), W2)
        uh, ul = split(u21[rows, :])
        v = dot3_t(uh, ul, tph_ref[...], tpl_ref[...])
        x32[rows, pc] = v
        xh[rows, pc], xl[rows, pc] = split(v)
        wh[rows, pc], wl[rows, pc] = split(v * dinv_ref[0:1, pc])

    starts = range(0, low, W2)

    def extra(k):
        i = k - NP // 2
        tasks = [lambda: pair_inverse(i)]
        for r0 in starts:
            tasks += [lambda r0=r0: (below_update(i, r0), below_settle(i, r0))]
        return tasks

    factor_panels(NP // 2, NP, a_ref, b_half(b_ref), vh, vl, v32, lh, ll, t_ref, lt_ref, dinv_ref,
                  rest_ref, u_ref, part_ref, e_ref, extra)
    last = NP // 2 - 1
    pair_inverse(last)
    for r0 in starts:
        below_settle(last, r0)

    y_late = v32[HALF : HALF + nrhs, HALF:]
    eli_ref[:, :HALF] = y0[...]
    eli_ref[:, HALF:PIV] = y_late
    mine = pl.ds(pl.multiple_of(jnp.maximum(me - NP, 0) * B, B), B)
    qh = jnp.concatenate([xh[mine, :], vh[HALF : HALF + nrhs, :]], 0)
    ql = jnp.concatenate([xl[mine, :], vl[HALF : HALF + nrhs, :]], 0)
    lower = me >= NP
    for c in range(low // W2):
        rows = slice(c * W2, (c + 1) * W2)
        dst = slice(PIV + c * W2, PIV + (c + 1) * W2)
        prod = dot3_t(qh, ql, wh[rows, :], wl[rows, :])
        row = me * B + lax.broadcasted_iota(jnp.int32, (B, W2), 0)
        col = PIV + c * W2 + lax.broadcasted_iota(jnp.int32, (B, W2), 1)
        fac_ref[:, dst] = jnp.where(row >= col, mine_ref[:, dst] - prod[:B], 0.0)
        eli_ref[:, dst] = b_ref[:, dst] - prod[B:]

    @pl.when(lower)
    def _():
        fac_ref[:, :PIV] = x32[mine, :] * dinv_ref[0:1, :]

    @pl.when(jnp.logical_not(lower))
    def _():
        fac_ref[:, :HALF] = own0[...]
        near = jnp.maximum(me - NP // 2, 0)
        rows = pl.ds(pl.multiple_of(near * B, B), B)
        col = HALF + lax.broadcasted_iota(jnp.int32, (B, HALF), 1)
        fac_ref[:, HALF:PIV] = jnp.where(col < me * B, v32[rows, HALF:] * dinv_ref[0:1, HALF:], 0.0)

    @pl.when((me >= NP // 2) & (me < NP))
    def _():
        fac_ref[:, pl.ds(pl.multiple_of(me * B, B), B)] = lt_ref[me].T


def b_half(b_ref):
    return b_ref.at[:, pl.ds(HALF, HALF)]


def second(index, gathered, state, mine, rhs):
    nrhs, order = rhs.shape
    low = order - PIV
    na = PIV - HALF
    return pl.pallas_call(
        second_kernel,
        grid=(1,),
        out_shape=(
            jax.ShapeDtypeStruct((B, order), F32),
            jax.ShapeDtypeStruct((nrhs, order), F32),
        ),
        in_specs=[pl.BlockSpec(memory_space=pltpu.SMEM), pl.BlockSpec(memory_space=pl.ANY)]
        + [whole(x.shape) for x in state]
        + [whole((B, order)), whole((nrhs, order))],
        out_specs=(whole((B, order)), whole((nrhs, order))),
        scratch_shapes=[
            pltpu.VMEM((na, na), F32),
            pltpu.VMEM((low, PIV), F32),
            pltpu.VMEM((na + nrhs, PIV), BF16),
            pltpu.VMEM((na + nrhs, PIV), BF16),
            pltpu.VMEM((na + nrhs, PIV), F32),
            pltpu.VMEM((PIV, PIV), BF16),
            pltpu.VMEM((PIV, PIV), BF16),
            pltpu.VMEM((NP, B, B), F32),
            pltpu.VMEM((NP, B, B), F32),
            pltpu.VMEM((8, PIV), F32),
            pltpu.VMEM((na + nrhs, B), F32),
            pltpu.VMEM((B, B), F32),
            pltpu.VMEM((B, B), F32),
            pltpu.VMEM((B, B), F32),
            pltpu.VMEM((low, PIV), BF16),
            pltpu.VMEM((low, PIV), BF16),
            pltpu.VMEM((low, PIV), F32),
            pltpu.VMEM((low, PIV), BF16),
            pltpu.VMEM((low, PIV), BF16),
            pltpu.VMEM((low, W2), F32),
            pltpu.VMEM((W2, W2), BF16),
            pltpu.VMEM((W2, W2), BF16),
            pltpu.SemaphoreType.DMA((2,)),
        ],
        compiler_params=pltpu.CompilerParams(vmem_limit_bytes=VMEM_LIMIT),
        name="second",
    )(index, gathered, *state, mine, rhs)


def shift_y(x, d):
    return lax.ppermute(x, "front", [(4 * z + y, 4 * z + (y + d) % 4) for z in range(4) for y in range(4)])


def planes(x, pairs):
    return lax.ppermute(x, "front", [(4 * a + y, 4 * b + y) for a, b in pairs for y in range(4)])


def gather_pivot_rows(x):
    z = lax.axis_index("front") // 4
    swap = planes(x, ((0, 1), (1, 0)))
    side = planes(x, ((1, 2), (0, 3)))
    far = planes(x, ((0, 2), (1, 3)))
    x0 = jnp.where(z == 0, x, jnp.where(z == 1, swap, jnp.where(z == 2, far, side)))
    x1 = jnp.where(z == 0, swap, jnp.where(z == 1, x, jnp.where(z == 2, side, far)))
    both = jnp.concatenate([x0, x1], 0)
    return [both] + [shift_y(both, d) for d in (1, 2, 3)]


def local(front_matrix, child_blocks, child_target, child_count, shot_rhs):
    leaves, slots = child_blocks.shape[1:3]
    slot_ids = lax.broadcasted_iota(jnp.int32, (leaves, slots), 1)
    live_code = jnp.where(slot_ids < child_count[0][:, None], child_target[0], -1)
    code_rows = jnp.zeros((leaves, 8, B), F32).at[:, 0, :slots].set(live_code.astype(F32))
    payload = jnp.concatenate([child_blocks[0].reshape(leaves, slots * B, B), code_rows], axis=1)
    arrived = lax.all_to_all(payload, "leaf", split_axis=0, concat_axis=0, tiled=True)
    codes = arrived[:, slots * B, :slots].astype(jnp.int32)
    index = lax.axis_index("front").astype(jnp.int32).reshape(1)
    mine = assemble(codes, index, arrived, front_matrix[0])
    gathered = lax.all_gather(mine[:, :PIV], "front", axis=0, tiled=True)
    rhs = shot_rhs[0]
    state = first(index, gather_pivot_rows(mine[:, :HALF]), rhs)
    factored, eliminated = second(index, gathered, state, mine, rhs)
    return factored[None], eliminated[None]


def solution(mesh):
    return jax.shard_map(
        local,
        mesh=mesh,
        in_specs=(
            P("leaf", "front", None),
            P(("leaf", "front"), None, None, None, None),
            P(("leaf", "front"), None, None),
            P(("leaf", "front"), None),
            P("leaf", None, None),
        ),
        out_specs=(P("leaf", "front", None), P("leaf", None, None)),
        check_vma=False,
    )
```

time: 208 us -> 176 us (0.85)
  waiting for transfers between devices: 93.4 us -> 65.5 us
  Pallas kernels: 86.8 us -> 68.7 us
  starting transfers between devices: 4.34 us -> 17.2 us
    all_gather x1, waiting for transfers between devices: 71.5 us -> 4.28 us  [local(): gathered = lax.all_gather(mine[:, :PIV], 'front', axis=0, tiled=True)]
    ppermute x0 -> x6, waiting for transfers between devices: none -> 39.3 us  [the longest x3 23.3 us: shift_y(): lax.ppermute(x, 'front', [(4 * z + y, 4 * z + (y + d) % 4) for z in range...]
    pallas_call x2, Pallas kernels: 83.6 us -> 65.5 us  [the longest x1 39.1 us: second(): pl.pallas_call(second_kernel, grid=(1,), out_shape=(jax.ShapeDtypeStruct(...]
    ppermute x0 -> x6, starting transfers between devices: none -> 12.9 us  [the longest x3 7.93 us: planes(): lax.ppermute(x, 'front', [(4 * a + y, 4 * b + y) for a, b in pairs for y...]
  transfers between devices with their start and end apart: 2 -> 8, of which waited for: 2 -> 8; matrix products, arithmetic and copies ran while one was open for 0% -> 0% of each run, Pallas kernels for 0% -> 15%
where the time goes in v2:
time: 176 us; the launch traced here: 174 us
  Pallas kernels  68.7 us (39%)
  waiting for transfers between devices  65.5 us (37%)
  starting transfers between devices  17.2 us (10%)
  between operations  14.1 us (8%)
  other arithmetic  4.19 us (2%)
  local copies, waits for them, and re-layouts  4.1 us (2%)
    pallas_call x1, Pallas kernels, second(): pl.pallas_call(second_kernel, grid=(1,), out_shape=(jax.ShapeDtypeStruct(...  39.1 us
    pallas_call x1, Pallas kernels, first(): pl.pallas_call(first_kernel, grid=(1,), out_shape=tuple((jax.ShapeDtypeSt...  26.3 us
    ppermute x3, waiting for transfers between devices, shift_y(): lax.ppermute(x, 'front', [(4 * z + y, 4 * z + (y + d) % 4) for z in range...  23.3 us
    all_to_all x1, waiting for transfers between devices, local(): lax.all_to_all(payload, 'leaf', split_axis=0, concat_axis=0, tiled=True)  21.9 us
    ppermute x3, waiting for transfers between devices, planes(): lax.ppermute(x, 'front', [(4 * a + y, 4 * b + y) for a, b in pairs for y...  16 us
    ppermute x3, starting transfers between devices, planes(): lax.ppermute(x, 'front', [(4 * a + y, 4 * b + y) for a, b in pairs for y...  7.93 us
    ppermute x3, starting transfers between devices, shift_y(): lax.ppermute(x, 'front', [(4 * z + y, 4 * z + (y + d) % 4) for z in range...  4.99 us
    all_to_all x1, starting transfers between devices, local(): lax.all_to_all(payload, 'leaf', split_axis=0, concat_axis=0, tiled=True)  4.3 us
  transfers between devices with their start and end apart: 8, of which 8 were waited for; matrix products, arithmetic and copies ran while one was open for 0% of the time, Pallas kernels for 15%

profile of v2, /device:TPU:8, one launch (start us, length us, event | category | flops | bytes accessed | tf_op | source)
XLA Modules:
  0.0 173.8 jit_solution(12900570800798606920)
XLA Ops:
  7.2 0.8 copy.10
  7.9 0.7 fusion
  8.6 2.7 %select_maximum_fusion = f32[8,392,128]{2,1,0:T(8,128)} fusion(f32[8,1,3]{2,1,0:T(1,128)S(1)} %fusion, f32[8,384,128]{2,1,0:T(8,128)} %bitcast.9), kind=kLoop, calls=%fused_computation | loop fusion | flops 1204224 | bytes 3178592 | tf_op jit(solution)/shard_map/concatenate | solution.py:433
  11.3 4.3 %all-to-all-start = ((f32[8,392,128]{2,1,0:T(8,128)}), f32[8,392,128]{2,1,0:T(8,128)S(1)}, u32[]{:S(2)}, u32[]{:S(2)}) async-start(f32[8,392,128]{2,1,0:T(8,128)} %select_maximum_fusion), calls=%async_computation | async-start | bytes 3211264 | tf_op jit(solution)/shard_map/all_to_all | solution.py:434
  15.6 0.0 all-gather.2.cloned.1.call-start
  15.7 21.9 %all-to-all-done.recv_ref = f32[8,392,128]{2,1,0:T(8,128)S(1)} async-done(((f32[8,392,128]{2,1,0:T(8,128)}), f32[8,392,128]{2,1,0:T(8,128)S(1)}, u32[]{:S(2)}, u32[]{:S(2)}) %all-to-all-start) | async-done | bytes 1605664 | tf_op jit(solution)/shard_map/all_to_all | solution.py:434
  37.6 0.0 copy-start.1
  37.6 0.6 slice_convert_fusion
  38.2 0.5 copy-done.1
  38.8 3.2 %assemble.1.mine_ref = f32[128,2048]{1,0:T(8,128)} custom-call(s32[8,3]{1,0:T(8,128)} %bitcast.13, s32[1]{0:T(128)} %bitcast.idx_ref, f32[8,392,128]{2,1,0:T(8,128)} %copy-done.1, f32[128,2048]{1,0:T(8,128)} %bitcast.10), custom_call_target="tpu_custom_call" | custom-call | tf_op jit(solution)/shard_map/assemble/pallas_call | solution.py:57
  42.0 0.0 copy-start
  42.0 2.0 %slice.36 = f32[128,1024]{1,0:T(8,128)} slice(f32[128,2048]{1,0:T(8,128)} %assemble.1.mine_ref), slice={[0:128], [0:1024]} | slice | bytes 1048576 | tf_op jit(solution)/shard_map/slice | solution.py:438
  43.9 0.0 all-gather.2.cloned.1.call-update
  44.0 0.0 copy-done
  44.0 3.8 %collective-permute-start = (f32[128,512]{1,0:T(8,128)S(1)}, f32[128,512]{1,0:T(8,128)S(1)}, u32[]{:S(2)}, u32[]{:S(2)}) collective-permute-start(f32[128,512]{1,0:T(8,128)S(1)} %slice.37), channel_id=1, source_target_pairs={{0,4},{1,5},{2,6},{3,7},{4,0},{5,1},{6,2},{7,3},{16,20},{17,21},{1... | collective-permute-start | bytes 786440 | tf_op jit(solution)/shard_map/ppermute | solution.py:414
  47.9 2.6 %collective-permute-start.1 = (f32[128,512]{1,0:T(8,128)S(1)}, f32[128,512]{1,0:T(8,128)S(1)}, u32[]{:S(2)}, u32[]{:S(2)}) collective-permute-start(f32[128,512]{1,0:T(8,128)S(1)} %slice.37), channel_id=1, source_target_pairs={{0,8},{1,9},{2,10},{3,11},{4,12},{5,13},{6,14},{7,15},{16,24},{17,... | collective-permute-start | bytes 786440 | tf_op jit(solution)/shard_map/ppermute | solution.py:414
  50.4 1.5 collective-permute-start.2
  52.0 3.1 %collective-permute-done = f32[128,512]{1,0:T(8,128)S(1)} collective-permute-done((f32[128,512]{1,0:T(8,128)S(1)}, f32[128,512]{1,0:T(8,128)S(1)}, u32[]{:S(2)}, u32[]{:S(2)}) %collective-permute-start) | collective-permute-done | bytes 262176 | tf_op jit(solution)/shard_map/ppermute | solution.py:414
  55.1 8.1 %collective-permute-done.1 = f32[128,512]{1,0:T(8,128)S(1)} collective-permute-done((f32[128,512]{1,0:T(8,128)S(1)}, f32[128,512]{1,0:T(8,128)S(1)}, u32[]{:S(2)}, u32[]{:S(2)}) %collective-permute-start.1) | collective-permute-done | bytes 262176 | tf_op jit(solution)/shard_map/ppermute | solution.py:414
  63.2 4.8 %collective-permute-done.2 = f32[128,512]{1,0:T(8,128)S(1)} collective-permute-done((f32[128,512]{1,0:T(8,128)S(1)}, f32[128,512]{1,0:T(8,128)S(1)}, u32[]{:S(2)}, u32[]{:S(2)}) %collective-permute-start.2) | collective-permute-done | bytes 262176 | tf_op jit(solution)/shard_map/ppermute | solution.py:414
  68.0 0.1 select_select_fusion.1
  68.1 0.0 copy-start.2
  68.1 1.6 collective-permute-start.3
  69.8 0.9 collective-permute-start.4
  70.7 2.4 %collective-permute-start.5 = (f32[256,512]{1,0:T(8,128)S(1)}, f32[256,512]{1,0:T(8,128)S(1)}, u32[]{:S(2)}, u32[]{:S(2)}) collective-permute-start(f32[256,512]{1,0:T(8,128)S(1)} %pad_maximum_fusion.y0_ref), channel_id=1, source_target_pairs={{0,3},{1,0},{2,1},{3,2},{4,7},{5,4},{6,5},{7,6},{8,11},{9,8},{10,9... | collective-permute-start | bytes 1572872 | tf_op jit(solution)/shard_map/ppermute | solution.py:410
  73.1 9.9 %collective-permute-done.3.y1_ref = f32[256,512]{1,0:T(8,128)S(1)} collective-permute-done((f32[256,512]{1,0:T(8,128)S(1)}, f32[256,512]{1,0:T(8,128)S(1)}, u32[]{:S(2)}, u32[]{:S(2)}) %collective-permute-start.3) | collective-permute-done | bytes 524320 | tf_op jit(solution)/shard_map/ppermute | solution.py:410
  83.1 0.0 copy-start.3
  83.1 3.1 %collective-permute-done.4.y2_ref = f32[256,512]{1,0:T(8,128)S(1)} collective-permute-done((f32[256,512]{1,0:T(8,128)S(1)}, f32[256,512]{1,0:T(8,128)S(1)}, u32[]{:S(2)}, u32[]{:S(2)}) %collective-permute-start.4) | collective-permute-done | bytes 524320 | tf_op jit(solution)/shard_map/ppermute | solution.py:410
  86.2 0.0 copy-start.4
  86.2 10.3 %collective-permute-done.5.y3_ref = f32[256,512]{1,0:T(8,128)S(1)} collective-permute-done((f32[256,512]{1,0:T(8,128)S(1)}, f32[256,512]{1,0:T(8,128)S(1)}, u32[]{:S(2)}, u32[]{:S(2)}) %collective-permute-start.5) | collective-permute-done | bytes 524320 | tf_op jit(solution)/shard_map/ppermute | solution.py:410
  96.4 0.0 copy-start.5
  96.4 0.0 copy-done.2
  96.4 0.0 copy-done.3
  96.4 0.0 copy-done.4
  96.4 0.8 copy-done.5
  97.2 26.3 %first.1 = (bf16[1088,512]{1,0:T(8,128)(2,1)}, bf16[1088,512]{1,0:T(8,128)(2,1)}, bf16[1024,512]{1,0:T(8,128)(2,1)}, bf16[1024,512]{1,0:T(8,128)(2,1)}, f32[4,12...) custom-call(s32[1]{0:T(128)} %bitcast.idx_ref, f32[256,512]{1,0:T(8,128)} %copy-done.2, ...), custom_call_target="tpu_custom_call" | custom-call | flops 20000000000 | bytes 20000000 | tf_op jit(solution)/shard_map/first/pallas_call | solution.py:237
  123.5 4.3 %all-gather.2.cloned.1.call-done.all_ref = f32[2048,1024]{1,0:T(8,128)} async-done(((f32[128,1024]{1,0:T(8,128)}), f32[2048,1024]{1,0:T(8,128)}) %all-gather.2.cloned.1.call-update) | async-done | bytes 8388624 | tf_op jit(solution)/shard_map/all_gather | solution.py:438
  127.8 39.1 %second.1 = (f32[128,2048]{1,0:T(8,128)}, f32[64,2048]{1,0:T(8,128)}) custom-call(s32[1]{0:T(128)} %bitcast.idx_ref, f32[2048,1024]{1,0:T(8,128)} %all-gather.2.cloned.1.call-done.all_ref, bf16[1088,512]{1,0:T(8,128)(2,1)} %get-tuple-element.24.vh0, bf16[1088,512]{1,0:T(8,128)(2,1)} %get-tuple-element.25.vl0, bf16[1024,512]{1,0:T(8,128)(2,1)} %get-tuple-element.26.lh0, ...), custom_call_target="tpu_custom_call" | custom-call | tf_op jit(solution)/shard_map/second/pallas_call | solution.py:368
  (2 shorter events, 0.1 us)
Async XLA Ops:
  11.3 26.2 %all-to-all-start = ((f32[8,392,128]{2,1,0:T(8,128)}), f32[8,392,128]{2,1,0:T(8,128)S(1)}, u32[]{:S(2)}, u32[]{:S(2)}) async-start(f32[8,392,128]{2,1,0:T(8,128)} %select_maximum_fusion), calls=%async_computation | async-start | bytes 3211264 | tf_op jit(solution)/shard_map/all_to_all | solution.py:434
  15.6 112.2 %all-gather.2.cloned.1.call-start = ((), (), s32[]{:S(2)}) async-start(), calls=%async_computation.1 | async-start | bytes 8912896 | tf_op jit(solution)/shard_map/all_gather | solution.py:438
  37.6 1.2 copy-start.1
  42.0 2.0 %copy-start = (f32[128,2048]{1,0:T(8,128)S(1)}, f32[128,2048]{1,0:T(8,128)}, u32[]{:S(2)}) copy-start(f32[128,2048]{1,0:T(8,128)} %assemble.1.mine_ref) | copy-start | bytes 3145732
  44.0 11.1 %collective-permute-start = (f32[128,512]{1,0:T(8,128)S(1)}, f32[128,512]{1,0:T(8,128)S(1)}, u32[]{:S(2)}, u32[]{:S(2)}) collective-permute-start(f32[128,512]{1,0:T(8,128)S(1)} %slice.37), channel_id=1, source_target_pairs={{0,4},{1,5},{2,6},{3,7},{4,0},{5,1},{6,2},{7,3},{16,20},{17,21},{1... | collective-permute-start | bytes 786440 | tf_op jit(solution)/shard_map/ppermute | solution.py:414
  47.9 15.4 %collective-permute-start.1 = (f32[128,512]{1,0:T(8,128)S(1)}, f32[128,512]{1,0:T(8,128)S(1)}, u32[]{:S(2)}, u32[]{:S(2)}) collective-permute-start(f32[128,512]{1,0:T(8,128)S(1)} %slice.37), channel_id=1, source_target_pairs={{0,8},{1,9},{2,10},{3,11},{4,12},{5,13},{6,14},{7,15},{16,24},{17,... | collective-permute-start | bytes 786440 | tf_op jit(solution)/shard_map/ppermute | solution.py:414
  50.4 17.5 %collective-permute-start.2 = (f32[128,512]{1,0:T(8,128)S(1)}, f32[128,512]{1,0:T(8,128)S(1)}, u32[]{:S(2)}, u32[]{:S(2)}) collective-permute-start(f32[128,512]{1,0:T(8,128)S(1)} %slice.37), channel_id=1, source_target_pairs={{4,8},{5,9},{6,10},{7,11},{0,12},{1,13},{2,14},{3,15},{20,24},{21,... | collective-permute-start | bytes 786440 | tf_op jit(solution)/shard_map/ppermute | solution.py:414
  68.1 28.3 %copy-start.2 = (f32[256,512]{1,0:T(8,128)}, f32[256,512]{1,0:T(8,128)S(1)}, u32[]{:S(2)}) copy-start(f32[256,512]{1,0:T(8,128)S(1)} %pad_maximum_fusion.y0_ref) | copy-start | bytes 1572868
  68.1 14.9 %collective-permute-start.3 = (f32[256,512]{1,0:T(8,128)S(1)}, f32[256,512]{1,0:T(8,128)S(1)}, u32[]{:S(2)}, u32[]{:S(2)}) collective-permute-start(f32[256,512]{1,0:T(8,128)S(1)} %pad_maximum_fusion.y0_ref), channel_id=1, source_target_pairs={{0,1},{1,2},{2,3},{3,0},{4,5},{5,6},{6,7},{7,4},{8,9},{9,10},{10,1... | collective-permute-start | bytes 1572872 | tf_op jit(solution)/shard_map/ppermute | solution.py:410
  69.8 16.4 %collective-permute-start.4 = (f32[256,512]{1,0:T(8,128)S(1)}, f32[256,512]{1,0:T(8,128)S(1)}, u32[]{:S(2)}, u32[]{:S(2)}) collective-permute-start(f32[256,512]{1,0:T(8,128)S(1)} %pad_maximum_fusion.y0_ref), channel_id=1, source_target_pairs={{0,2},{1,3},{2,0},{3,1},{4,6},{5,7},{6,4},{7,5},{8,10},{9,11},{10,... | collective-permute-start | bytes 1572872 | tf_op jit(solution)/shard_map/ppermute | solution.py:410
  70.7 25.7 %collective-permute-start.5 = (f32[256,512]{1,0:T(8,128)S(1)}, f32[256,512]{1,0:T(8,128)S(1)}, u32[]{:S(2)}, u32[]{:S(2)}) collective-permute-start(f32[256,512]{1,0:T(8,128)S(1)} %pad_maximum_fusion.y0_ref), channel_id=1, source_target_pairs={{0,3},{1,0},{2,1},{3,2},{4,7},{5,4},{6,5},{7,6},{8,11},{9,8},{10,9... | collective-permute-start | bytes 1572872 | tf_op jit(solution)/shard_map/ppermute | solution.py:410
  83.1 13.3 %copy-start.3 = (f32[256,512]{1,0:T(8,128)}, f32[256,512]{1,0:T(8,128)S(1)}, u32[]{:S(2)}) copy-start(f32[256,512]{1,0:T(8,128)S(1)} %collective-permute-done.3.y1_ref) | copy-start | bytes 1572868
  86.2 10.3 %copy-start.4 = (f32[256,512]{1,0:T(8,128)}, f32[256,512]{1,0:T(8,128)S(1)}, u32[]{:S(2)}) copy-start(f32[256,512]{1,0:T(8,128)S(1)} %collective-permute-done.4.y2_ref) | copy-start | bytes 1572868
  96.4 0.8 copy-start.5
Sparse Core Ops, SparseCore 0:
  44.1 83.6 all-gather.1

commit v3 on v2

--- a/solution.py
+++ b/solution.py
@@ -8,9 +8,10 @@
 B = 128
 PIV = 1024
 NP = PIV // B
+HALF = PIV // 2
+W2 = 2 * B
 F32 = jnp.float32
 BF16 = jnp.bfloat16
-VMEM_LIMIT = 56 * 1024 * 1024
 
 
 def split(x):
@@ -35,7 +36,7 @@
     return dot_n(ah, bh) + dot_n(al, bh) + dot_n(ah, bl)
 
 
-def assemble_kernel(code_ref, idx_ref, recv_ref, front_ref, out_ref):
+def assemble_kernel(code_ref, idx_ref, recv_ref, front_ref, late_ref, early_ref, pivot_ref, out_ref):
     out_ref[...] = front_ref[...]
     for s in range(recv_ref.shape[0]):
         for j in range(code_ref.shape[1]):
@@ -51,70 +52,99 @@
     row = lax.broadcasted_iota(jnp.int32, (B, B), 0)
     col = lax.broadcasted_iota(jnp.int32, (B, B), 1)
     out_ref[:, cols] = jnp.where(row >= col, square, square.T)
+    early_ref[...] = out_ref[:, :HALF]
+    pivot_ref[...] = out_ref[:, :PIV]
+    late_ref[...] = out_ref[:, PIV:]
 
 
 def assemble(codes, index, recv, front):
+    rows, order = front.shape
+    vmem = pl.BlockSpec(memory_space=pltpu.VMEM)
     return pl.pallas_call(
         assemble_kernel,
-        out_shape=jax.ShapeDtypeStruct(front.shape, F32),
-        in_specs=[
-            pl.BlockSpec(memory_space=pltpu.SMEM),
-            pl.BlockSpec(memory_space=pltpu.SMEM),
-            pl.BlockSpec(memory_space=pltpu.VMEM),
-            pl.BlockSpec(memory_space=pltpu.VMEM),
-        ],
-        out_specs=pl.BlockSpec(memory_space=pltpu.VMEM),
-        compiler_params=pltpu.CompilerParams(vmem_limit_bytes=VMEM_LIMIT),
+        out_shape=(
+            jax.ShapeDtypeStruct((rows, order - PIV), F32),
+            jax.ShapeDtypeStruct((rows, HALF), F32),
+            jax.ShapeDtypeStruct((rows, PIV), F32),
+        ),
+        in_specs=[pl.BlockSpec(memory_space=pltpu.SMEM)] * 2 + [vmem, vmem],
+        out_specs=(vmem, vmem, vmem),
+        scratch_shapes=[pltpu.VMEM((rows, order), F32)],
+        compiler_params=pltpu.CompilerParams(vmem_limit_bytes=8 * 1024 * 1024),
         name="assemble",
     )(codes, index, recv, front)
 
 
+def lane(x, c):
+    return jnp.broadcast_to(x[:, c : c + 1], (8, B))
+
+
+def sublane(x, t):
+    return jnp.broadcast_to(x[t : t + 1, :], (8, B))
+
+
 def chain(a_rows, e_rows, store, side):
     sub = lax.broadcasted_iota(jnp.int32, (8, B), 0)
+    ahead = None
     for g in range(16):
         if g < len(side):
             side[g]()
         ra, re = a_rows[g], e_rows[g]
         base = 8 * g
-        b = [jnp.broadcast_to(ra[:, base + t : base + t + 1], (8, B)) for t in range(8)]
+        b = ahead or [lane(ra, base + t) for t in range(8)]
+        more, far = g < 15, g < 14
+        if more:
+            na, ne = a_rows[g + 1], e_rows[g + 1]
+            c = [lane(na, base + t) for t in range(8)]
+            q = [lane(ra, base + 8 + t) for t in range(8)]
+            ahead = [lane(na, base + 8 + t) for t in range(8)]
         ga, ge = ra, re
         fa, fe = ra, re
         rcps = []
         for t in range(8):
-            piv = jnp.broadcast_to(b[t][t : t + 1, :], (8, B))
-            r = 1.0 / piv
+            r = 1.0 / sublane(b[t], t)
             rcps.append(r)
             m = b[t] * r
             mg = jnp.where(sub == t, 0.0, m)
             mf = jnp.where(sub > t, m, 0.0)
+            pa, pe = sublane(fa, t), sublane(fe, t)
+            if more:
+                mn = c[t] * r
             for u in range(t + 1, 8):
-                b[u] = b[u] - mg * jnp.broadcast_to(b[u][t : t + 1, :], (8, B))
-            pa = jnp.broadcast_to(fa[t : t + 1, :], (8, B))
-            pe = jnp.broadcast_to(fe[t : t + 1, :], (8, B))
+                w = sublane(b[u], t)
+                b[u] = b[u] - mg * w
+                if more:
+                    c[u] = c[u] - mn * w
+            if more:
+                for u in range(8):
+                    w = sublane(q[u], t)
+                    q[u] = q[u] - mf * w
+                    ahead[u] = ahead[u] - mn * w
+                na = na - mn * pa
+                ne = ne - mn * pe
             fa = fa - mf * pa
             fe = fe - mf * pe
-            ga = ga - mg * pa
-            ge = ge - mg * pe
+            if far:
+                ga = ga - mg * pa
+                ge = ge - mg * pe
         rc = rcps[0]
         for t in range(1, 8):
             rc = jnp.where(sub == t, rcps[t], rc)
         store(g, fa, fe, rc)
-        ga = ga * rc
-        ge = ge * rc
-        if g < 15:
-            gab = [jnp.broadcast_to(ga[t : t + 1, :], (8, B)) for t in range(8)]
-            geb = [jnp.broadcast_to(ge[t : t + 1, :], (8, B)) for t in range(8)]
-            for i in range(g + 1, 16):
+        if more:
+            a_rows[g + 1], e_rows[g + 1] = na, ne
+        if far:
+            ga = ga * rc
+            ge = ge * rc
+            gab = [sublane(ga, t) for t in range(8)]
+            geb = [sublane(ge, t) for t in range(8)]
+            for i in range(g + 2, 16):
                 acc_a, acc_e = a_rows[i], e_rows[i]
                 for t in range(8):
-                    c = jnp.broadcast_to(a_rows[i][:, base + t : base + t + 1], (8, B))
-                    acc_a = acc_a - c * gab[t]
-                    acc_e = acc_e - c * geb[t]
+                    cc = lane(a_rows[i], base + t)
+                    acc_a = acc_a - cc * gab[t]
+                    acc_e = acc_e - cc * geb[t]
                 a_rows[i], e_rows[i] = acc_a, acc_e
-
-
-HALF = PIV // 2
-W2 = 2 * B
 
 
 def cat_blocks(a, b, c, d):
@@ -127,18 +157,16 @@
     na, nrhs = a_ref.shape[0], b_ref.shape[0]
     ri = lax.broadcasted_iota(jnp.int32, (8, B), 0)
     ci = lax.broadcasted_iota(jnp.int32, (8, B), 1)
-    chunks = [(c * W2, W2) for c in range(na // W2)] + [(na, nrhs)]
-
-    def settle(k, r0, n):
-        rows, cols = slice(r0, r0 + n), pl.ds(pl.multiple_of(k * B, B), B)
+
+    def settle(k):
+        cols = pl.ds(pl.multiple_of(k * B, B), B)
         th, tl = split(t_ref[k])
-        uh, ul = split(rest_ref[rows, :])
+        uh, ul = split(rest_ref[...])
         v = dot3_t(uh, ul, th, tl)
-        v32[rows, cols] = v
-        vh[rows, cols], vl[rows, cols] = split(v)
-        if r0 < na:
-            lrows = slice(row0 + r0, row0 + r0 + n)
-            lh[lrows, cols], ll[lrows, cols] = split(v * dinv_ref[0:1, cols])
+        v32[:, cols] = v
+        vh[:, cols], vl[:, cols] = split(v)
+        lrows = slice(row0, row0 + na)
+        lh[lrows, cols], ll[lrows, cols] = split(v[:na] * dinv_ref[0:1, cols])
 
     def panel(k, _):
         kcols = pl.ds(pl.multiple_of(k * B, B), B)
@@ -157,17 +185,15 @@
             lt_ref[k, 8 * g : 8 * g + 8, :] = jnp.where(own, fa, jnp.where(ri + 8 * g < ci, fa * rc, 0.0))
             e_ref[8 * g : 8 * g + 8, :] = fe
 
-        def update(r0, n):
-            rows = slice(r0, r0 + n)
-            src = a_ref[rows, acols] if r0 < na else b_ref[:, acols]
-            rest_ref[rows, :] = src - dot3_t(vh[rows, :], vl[rows, :], lh[kcols, :], ll[kcols, :])
+        def update():
+            prod = dot3_t(vh[...], vl[...], lh[kcols, :], ll[kcols, :])
+            rest_ref[:na, :] = a_ref[:, acols] - prod[:na]
+            rest_ref[na:, :] = b_ref[:, acols] - prod[na:]
 
         def partial():
             part_ref[...] = a_ref[nloc, nloc] - dot3_t(vh[nloc, :], vl[nloc, :], lh[nabs, :], ll[nabs, :])
 
-        side = [lambda c=c: settle(prev, *c) for c in chunks]
-        side += [lambda c=c: update(*c) for c in chunks]
-        side += [partial] + extra(k)
+        side = [lambda: settle(prev), update, partial] + extra(k)
         chain(a_rows, e_rows, store, side)
         total = diag[0]
         for g in range(1, 16):
@@ -185,8 +211,7 @@
         return 0
 
     lax.fori_loop(k0, k1, panel, 0)
-    for c in chunks:
-        settle(k1 - 1, *c)
+    settle(k1 - 1)
 
 
 def first_kernel(idx_ref, y0_ref, y1_ref, y2_ref, y3_ref, b_ref,
@@ -203,7 +228,7 @@
         ref[...] = jnp.zeros_like(ref)
     t_ref[0] = jnp.zeros((B, B), F32)
     u_ref[...] = a_ref[0:B, 0:B]
-    factor_panels(0, NP // 2, a_ref, b_ref, vh, vl, v32, lh, ll, t_ref, lt_ref, dinv_ref,
+    factor_panels(0, NP // 2, a_ref, b_ref.at[:, pl.ds(0, HALF)], vh, vl, v32, lh, ll, t_ref, lt_ref, dinv_ref,
                   rest_ref, u_ref, part_ref, e_ref, lambda k: [])
     nrhs = b_ref.shape[0]
     y_ref[...] = v32[PIV : PIV + nrhs, :]
@@ -217,9 +242,7 @@
         own_ref[:, rows] = lt_ref[me].T
 
 
-def whole(shape):
-    zeros = (0,) * len(shape)
-    return pl.BlockSpec(shape, lambda i: zeros)
+VMEM_SPEC = pl.BlockSpec(memory_space=pltpu.VMEM)
 
 
 def first(index, parts, rhs):
@@ -236,10 +259,9 @@
     )
     return pl.pallas_call(
         first_kernel,
-        grid=(1,),
         out_shape=tuple(jax.ShapeDtypeStruct(*o) for o in outs),
-        in_specs=[pl.BlockSpec(memory_space=pltpu.SMEM)] + [whole((W2, HALF))] * 4 + [whole((nrhs, HALF))],
-        out_specs=tuple(whole(o[0]) for o in outs),
+        in_specs=[pl.BlockSpec(memory_space=pltpu.SMEM)] + [VMEM_SPEC] * 5,
+        out_specs=(VMEM_SPEC,) * len(outs),
         scratch_shapes=[
             pltpu.VMEM((PIV, HALF), F32),
             pltpu.VMEM((PIV + nrhs, HALF), F32),
@@ -249,7 +271,7 @@
             pltpu.VMEM((B, B), F32),
             pltpu.VMEM((B, B), F32),
         ],
-        compiler_params=pltpu.CompilerParams(vmem_limit_bytes=VMEM_LIMIT),
+        compiler_params=pltpu.CompilerParams(vmem_limit_bytes=20 * 1024 * 1024),
         cost_estimate=pl.CostEstimate(flops=2 * 10**10, bytes_accessed=2 * 10**7, transcendentals=0),
         name="first",
     )(index, *parts, rhs)
@@ -296,33 +318,27 @@
         tph_ref[...] = cat_blocks(t0h, zero, zh, t1h)
         tpl_ref[...] = cat_blocks(t0l, zero, zl, t1l)
 
-    def below_update(i, r0):
-        rows, pc = slice(r0, r0 + W2), pl.ds(pl.multiple_of(i * W2, W2), W2)
-        u21[rows, :] = a21[rows, pc] - dot3_t(xh[rows, :], xl[rows, :], lh[pc, :], ll[pc, :])
-
-    def below_settle(i, r0):
-        rows, pc = slice(r0, r0 + W2), pl.ds(pl.multiple_of(i * W2, W2), W2)
-        uh, ul = split(u21[rows, :])
+    def below_update(i):
+        pc = pl.ds(pl.multiple_of(i * W2, W2), W2)
+        u21[...] = a21[:, pc] - dot3_t(xh[...], xl[...], lh[pc, :], ll[pc, :])
+
+    def below_settle(i):
+        pc = pl.ds(pl.multiple_of(i * W2, W2), W2)
+        uh, ul = split(u21[...])
         v = dot3_t(uh, ul, tph_ref[...], tpl_ref[...])
-        x32[rows, pc] = v
-        xh[rows, pc], xl[rows, pc] = split(v)
-        wh[rows, pc], wl[rows, pc] = split(v * dinv_ref[0:1, pc])
-
-    starts = range(0, low, W2)
+        x32[:, pc] = v
+        xh[:, pc], xl[:, pc] = split(v)
+        wh[:, pc], wl[:, pc] = split(v * dinv_ref[0:1, pc])
 
     def extra(k):
         i = k - NP // 2
-        tasks = [lambda: pair_inverse(i)]
-        for r0 in starts:
-            tasks += [lambda r0=r0: (below_update(i, r0), below_settle(i, r0))]
-        return tasks
+        return [lambda: pair_inverse(i), lambda: below_update(i), lambda: below_settle(i)]
 
     factor_panels(NP // 2, NP, a_ref, b_half(b_ref), vh, vl, v32, lh, ll, t_ref, lt_ref, dinv_ref,
                   rest_ref, u_ref, part_ref, e_ref, extra)
     last = NP // 2 - 1
     pair_inverse(last)
-    for r0 in starts:
-        below_settle(last, r0)
+    below_settle(last)
 
     y_late = v32[HALF : HALF + nrhs, HALF:]
     eli_ref[:, :HALF] = y0[...]
@@ -337,7 +353,7 @@
         prod = dot3_t(qh, ql, wh[rows, :], wl[rows, :])
         row = me * B + lax.broadcasted_iota(jnp.int32, (B, W2), 0)
         col = PIV + c * W2 + lax.broadcasted_iota(jnp.int32, (B, W2), 1)
-        fac_ref[:, dst] = jnp.where(row >= col, mine_ref[:, dst] - prod[:B], 0.0)
+        fac_ref[:, dst] = jnp.where(row >= col, mine_ref[:, rows] - prod[:B], 0.0)
         eli_ref[:, dst] = b_ref[:, dst] - prod[B:]
 
     @pl.when(lower)
@@ -367,15 +383,13 @@
     na = PIV - HALF
     return pl.pallas_call(
         second_kernel,
-        grid=(1,),
         out_shape=(
             jax.ShapeDtypeStruct((B, order), F32),
             jax.ShapeDtypeStruct((nrhs, order), F32),
         ),
         in_specs=[pl.BlockSpec(memory_space=pltpu.SMEM), pl.BlockSpec(memory_space=pl.ANY)]
-        + [whole(x.shape) for x in state]
-        + [whole((B, order)), whole((nrhs, order))],
-        out_specs=(whole((B, order)), whole((nrhs, order))),
+        + [VMEM_SPEC] * (len(state) + 2),
+        out_specs=(VMEM_SPEC, VMEM_SPEC),
         scratch_shapes=[
             pltpu.VMEM((na, na), F32),
             pltpu.VMEM((low, PIV), F32),
@@ -401,7 +415,7 @@
             pltpu.VMEM((W2, W2), BF16),
             pltpu.SemaphoreType.DMA((2,)),
         ],
-        compiler_params=pltpu.CompilerParams(vmem_limit_bytes=VMEM_LIMIT),
+        compiler_params=pltpu.CompilerParams(vmem_limit_bytes=44 * 1024 * 1024),
         name="second",
     )(index, gathered, *state, mine, rhs)
 
@@ -434,11 +448,11 @@
     arrived = lax.all_to_all(payload, "leaf", split_axis=0, concat_axis=0, tiled=True)
     codes = arrived[:, slots * B, :slots].astype(jnp.int32)
     index = lax.axis_index("front").astype(jnp.int32).reshape(1)
-    mine = assemble(codes, index, arrived, front_matrix[0])
-    gathered = lax.all_gather(mine[:, :PIV], "front", axis=0, tiled=True)
+    late, early, pivots = assemble(codes, index, arrived, front_matrix[0])
+    gathered = lax.all_gather(pivots, "front", axis=0, tiled=True)
     rhs = shot_rhs[0]
-    state = first(index, gather_pivot_rows(mine[:, :HALF]), rhs)
-    factored, eliminated = second(index, gathered, state, mine, rhs)
+    state = first(index, gather_pivot_rows(early), rhs)
+    factored, eliminated = second(index, gathered, state, late, rhs)
     return factored[None], eliminated[None]
 
 

time: 176 us -> 168 us (0.955)
  Pallas kernels: 68.7 us -> 50.2 us
  local copies, waits for them, and re-layouts: 4.1 us -> 10.1 us
  waiting for transfers between devices: 65.5 us -> 70.5 us
    pallas_call x3, Pallas kernels: 68.7 us -> 50.2 us  [the longest x1 29.5 us: second(): pl.pallas_call(second_kernel, out_shape=(jax.ShapeDtypeStruct((B, order),...]
    unnamed x12 -> x22, local copies, waits for them, and re-layouts: 1.35 us -> 9.39 us
    all_gather x1, waiting for transfers between devices: 4.28 us -> 9.48 us  [local(): gathered = lax.all_gather(pivots, 'front', axis=0, tiled=True)]
    slice x2 -> x0, local copies, waits for them, and re-layouts: 1.99 us -> none  [the longest x1 1.97 us: local(): gathered = lax.all_gather(mine[:, :PIV], 'front', axis=0, tiled=True)]
  transfers between devices with their start and end apart: 8 -> 8, of which waited for: 8 -> 8; matrix products, arithmetic and copies ran while one was open for 0% -> 0% of each run, Pallas kernels for 15% -> 11%
where the time goes in v3:
time: 168 us; the launch traced here: 166 us
  waiting for transfers between devices  70.5 us (42%)
  Pallas kernels  50.2 us (30%)
  starting transfers between devices  17.4 us (10%)
  between operations  14.1 us (8%)
  local copies, waits for them, and re-layouts  10.1 us (6%)
  other arithmetic  3.57 us (2%)
    pallas_call x1, Pallas kernels, second(): pl.pallas_call(second_kernel, out_shape=(jax.ShapeDtypeStruct((B, order),...  29.5 us
    ppermute x3, waiting for transfers between devices, shift_y(): lax.ppermute(x, 'front', [(4 * z + y, 4 * z + (y + d) % 4) for z in range...  23.2 us
    all_to_all x1, waiting for transfers between devices, local(): lax.all_to_all(payload, 'leaf', split_axis=0, concat_axis=0, tiled=True)  21.9 us
    pallas_call x1, Pallas kernels, first(): pl.pallas_call(first_kernel, out_shape=tuple((jax.ShapeDtypeStruct(*o) fo...  18.7 us
    ppermute x3, waiting for transfers between devices, planes(): lax.ppermute(x, 'front', [(4 * a + y, 4 * b + y) for a, b in pairs for y...  15.9 us
    all_gather x1, waiting for transfers between devices, local(): gathered = lax.all_gather(pivots, 'front', axis=0, tiled=True)  9.48 us
    unnamed x22, local copies, waits for them, and re-layouts  9.39 us
    ppermute x3, starting transfers between devices, planes(): lax.ppermute(x, 'front', [(4 * a + y, 4 * b + y) for a, b in pairs for y...  7.95 us
  transfers between devices with their start and end apart: 8, of which 8 were waited for; matrix products, arithmetic and copies ran while one was open for 0% of the time, Pallas kernels for 11%

profile of v3, /device:TPU:8, one launch (start us, length us, event | category | flops | bytes accessed | tf_op | source)
XLA Modules:
  0.0 166.0 jit_solution(7890996029138695964)
XLA Ops:
  7.2 0.8 copy.10
  7.9 0.7 fusion
  8.6 2.7 %select_maximum_fusion = f32[8,392,128]{2,1,0:T(8,128)} fusion(f32[8,1,3]{2,1,0:T(1,128)S(1)} %fusion, f32[8,384,128]{2,1,0:T(8,128)} %bitcast.13), kind=kLoop, calls=%fused_computation | loop fusion | flops 1204224 | bytes 3178592 | tf_op jit(solution)/shard_map/concatenate | solution.py:447
  11.4 0.0 copy-start.2
  11.4 4.4 %all-to-all-start = ((f32[8,392,128]{2,1,0:T(8,128)}), f32[8,392,128]{2,1,0:T(8,128)S(1)}, u32[]{:S(2)}, u32[]{:S(2)}) async-start(f32[8,392,128]{2,1,0:T(8,128)} %select_maximum_fusion), calls=%async_computation | async-start | bytes 3211264 | tf_op jit(solution)/shard_map/all_to_all | solution.py:448
  15.8 0.0 all-gather.2.cloned.1.call-start
  15.8 21.9 %all-to-all-done.recv_ref = f32[8,392,128]{2,1,0:T(8,128)S(1)} async-done(((f32[8,392,128]{2,1,0:T(8,128)}), f32[8,392,128]{2,1,0:T(8,128)S(1)}, u32[]{:S(2)}, u32[]{:S(2)}) %all-to-all-start) | async-done | bytes 1605664 | tf_op jit(solution)/shard_map/all_to_all | solution.py:448
  37.7 0.0 copy-done.2
  37.7 1.9 %assemble.1 = (f32[128,1024]{1,0:T(8,128)S(1)}, f32[128,512]{1,0:T(8,128)S(1)}, f32[128,1024]{1,0:T(8,128)}) custom-call(s32[8,3]{1,0:T(8,128)S(1)} %bitcast.12, s32[1]{0:T(128)} %bitcast.idx_ref, f32[8,392,128]{2,1,0:T(8,128)S(1)} %all-to-all-done.recv_ref, f32[128,2048]{1,0:T(8,128)S(1)} %bitcast.9), custom_call_target="tpu_custom_call" | custom-call | tf_op jit(solution)/shard_map/assemble/pallas_call | solution.py:63
  39.7 0.0 copy-start.5
  39.7 0.9 copy-done.5
  40.5 0.0 all-gather.2.cloned.1.call-update
  40.6 3.8 %collective-permute-start = (f32[128,512]{1,0:T(8,128)S(1)}, f32[128,512]{1,0:T(8,128)S(1)}, u32[]{:S(2)}, u32[]{:S(2)}) collective-permute-start(f32[128,512]{1,0:T(8,128)S(1)} %get-tuple-element.28), channel_id=1, source_target_pairs={{0,4},{1,5},{2,6},{3,7},{4,0},{5,1},{6,2},{7,3},{16,20},{17,21},{1... | collective-permute-start | bytes 786440 | tf_op jit(solution)/shard_map/ppermute | solution.py:428
  44.4 2.7 %collective-permute-start.1 = (f32[128,512]{1,0:T(8,128)S(1)}, f32[128,512]{1,0:T(8,128)S(1)}, u32[]{:S(2)}, u32[]{:S(2)}) collective-permute-start(f32[128,512]{1,0:T(8,128)S(1)} %get-tuple-element.28), channel_id=1, source_target_pairs={{0,8},{1,9},{2,10},{3,11},{4,12},{5,13},{6,14},{7,15},{16,24},{17,... | collective-permute-start | bytes 786440 | tf_op jit(solution)/shard_map/ppermute | solution.py:428
  47.1 1.4 collective-permute-start.2
  48.6 3.1 %collective-permute-done = f32[128,512]{1,0:T(8,128)S(1)} collective-permute-done((f32[128,512]{1,0:T(8,128)S(1)}, f32[128,512]{1,0:T(8,128)S(1)}, u32[]{:S(2)}, u32[]{:S(2)}) %collective-permute-start) | collective-permute-done | bytes 262176 | tf_op jit(solution)/shard_map/ppermute | solution.py:428
  51.6 7.9 %collective-permute-done.1 = f32[128,512]{1,0:T(8,128)S(1)} collective-permute-done((f32[128,512]{1,0:T(8,128)S(1)}, f32[128,512]{1,0:T(8,128)S(1)}, u32[]{:S(2)}, u32[]{:S(2)}) %collective-permute-start.1) | collective-permute-done | bytes 262176 | tf_op jit(solution)/shard_map/ppermute | solution.py:428
  59.6 4.9 %collective-permute-done.2 = f32[128,512]{1,0:T(8,128)S(1)} collective-permute-done((f32[128,512]{1,0:T(8,128)S(1)}, f32[128,512]{1,0:T(8,128)S(1)}, u32[]{:S(2)}, u32[]{:S(2)}) %collective-permute-start.2) | collective-permute-done | bytes 262176 | tf_op jit(solution)/shard_map/ppermute | solution.py:428
  64.5 0.1 select_select_fusion.1
  64.6 1.7 %collective-permute-start.3 = (f32[256,512]{1,0:T(8,128)S(1)}, f32[256,512]{1,0:T(8,128)S(1)}, u32[]{:S(2)}, u32[]{:S(2)}) collective-permute-start(f32[256,512]{1,0:T(8,128)S(1)} %pad_maximum_fusion.y0_ref), channel_id=1, source_target_pairs={{0,1},{1,2},{2,3},{3,0},{4,5},{5,6},{6,7},{7,4},{8,9},{9,10},{10,1... | collective-permute-start | bytes 1572872 | tf_op jit(solution)/shard_map/ppermute | solution.py:424
  66.3 1.0 collective-permute-start.4
  67.3 2.4 %collective-permute-start.5 = (f32[256,512]{1,0:T(8,128)S(1)}, f32[256,512]{1,0:T(8,128)S(1)}, u32[]{:S(2)}, u32[]{:S(2)}) collective-permute-start(f32[256,512]{1,0:T(8,128)S(1)} %pad_maximum_fusion.y0_ref), channel_id=1, source_target_pairs={{0,3},{1,0},{2,1},{3,2},{4,7},{5,4},{6,5},{7,6},{8,11},{9,8},{10,9... | collective-permute-start | bytes 1572872 | tf_op jit(solution)/shard_map/ppermute | solution.py:424
  69.6 9.9 %collective-permute-done.3.y1_ref = f32[256,512]{1,0:T(8,128)S(1)} collective-permute-done((f32[256,512]{1,0:T(8,128)S(1)}, f32[256,512]{1,0:T(8,128)S(1)}, u32[]{:S(2)}, u32[]{:S(2)}) %collective-permute-start.3) | collective-permute-done | bytes 524320 | tf_op jit(solution)/shard_map/ppermute | solution.py:424
  79.5 3.1 %collective-permute-done.4.y2_ref = f32[256,512]{1,0:T(8,128)S(1)} collective-permute-done((f32[256,512]{1,0:T(8,128)S(1)}, f32[256,512]{1,0:T(8,128)S(1)}, u32[]{:S(2)}, u32[]{:S(2)}) %collective-permute-start.4) | collective-permute-done | bytes 524320 | tf_op jit(solution)/shard_map/ppermute | solution.py:424
  82.7 10.2 %collective-permute-done.5.y3_ref = f32[256,512]{1,0:T(8,128)S(1)} collective-permute-done((f32[256,512]{1,0:T(8,128)S(1)}, f32[256,512]{1,0:T(8,128)S(1)}, u32[]{:S(2)}, u32[]{:S(2)}) %collective-permute-start.5) | collective-permute-done | bytes 524320 | tf_op jit(solution)/shard_map/ppermute | solution.py:424
  92.8 0.0 copy-start.3
  92.8 1.0 copy-done.3
  93.9 18.7 %first.1 = (bf16[1088,512]{1,0:T(8,128)(2,1)S(1)}, bf16[1088,512]{1,0:T(8,128)(2,1)S(1)}, bf16[1024,512]{1,0:T(8,128)(2,1)S(1)}, bf16[1024,512]{1,0:T(8,128)(2,1...) custom-call(s32[1]{0:T(128)} %bitcast.idx_ref, ...), custom_call_target="tpu_custom_call" | custom-call | flops 20000000000 | bytes 20000000 | tf_op jit(solution)/shard_map/first/pallas_call | solution.py:260
  112.6 0.0 copy-start
  112.6 1.0 copy-done
  113.6 0.0 copy-start.7
  113.6 0.7 copy-done.7
  114.3 0.0 copy-start.9
  114.3 0.7 copy-done.9
  114.9 9.5 %all-gather.2.cloned.1.call-done.all_ref = f32[2048,1024]{1,0:T(8,128)} async-done(((f32[128,1024]{1,0:T(8,128)}), f32[2048,1024]{1,0:T(8,128)}) %all-gather.2.cloned.1.call-update) | async-done | bytes 8388624 | tf_op jit(solution)/shard_map/all_gather | solution.py:452
  124.4 0.0 copy-start.1
  124.4 1.2 copy-done.1
  125.6 0.0 copy-start.4
  125.6 1.0 copy-done.4
  126.7 0.0 copy-start.6
  126.7 1.0 copy-done.6
  127.7 0.0 copy-start.8
  127.7 0.9 copy-done.8
  128.7 0.0 copy-start.10
  128.7 0.9 copy-done.10
  129.6 29.5 %second.1 = (f32[128,2048]{1,0:T(8,128)}, f32[64,2048]{1,0:T(8,128)}) custom-call(s32[1]{0:T(128)} %bitcast.idx_ref, f32[2048,1024]{1,0:T(8,128)} %all-gather.2.cloned.1.call-done.all_ref, bf16[1088,512]{1,0:T(8,128)(2,1)S(1)} %get-tuple-element.29.vh0, bf16[1088,512]{1,0:T(8,128)(2,1)S(1)} %get-tuple-element.30.vl0, ...), custom_call_target="tpu_custom_call" | custom-call | tf_op jit(solution)/shard_map/second/pallas_call | solution.py:384
  (2 shorter events, 0.0 us)
Async XLA Ops:
  11.4 26.4 %copy-start.2 = (f32[1,128,2048]{2,1,0:T(8,128)S(1)}, f32[1,128,2048]{2,1,0:T(8,128)}, u32[]{:S(2)}) copy-start(f32[1,128,2048]{2,1,0:T(8,128)} %param.7) | copy-start | bytes 3145732
  11.4 26.4 %all-to-all-start = ((f32[8,392,128]{2,1,0:T(8,128)}), f32[8,392,128]{2,1,0:T(8,128)S(1)}, u32[]{:S(2)}, u32[]{:S(2)}) async-start(f32[8,392,128]{2,1,0:T(8,128)} %select_maximum_fusion), calls=%async_computation | async-start | bytes 3211264 | tf_op jit(solution)/shard_map/all_to_all | solution.py:448
  15.8 108.6 %all-gather.2.cloned.1.call-start = ((), (), s32[]{:S(2)}) async-start(), calls=%async_computation.1 | async-start | bytes 8912896 | tf_op jit(solution)/shard_map/all_gather | solution.py:452
  39.7 0.9 copy-start.5
  40.6 11.1 %collective-permute-start = (f32[128,512]{1,0:T(8,128)S(1)}, f32[128,512]{1,0:T(8,128)S(1)}, u32[]{:S(2)}, u32[]{:S(2)}) collective-permute-start(f32[128,512]{1,0:T(8,128)S(1)} %get-tuple-element.28), channel_id=1, source_target_pairs={{0,4},{1,5},{2,6},{3,7},{4,0},{5,1},{6,2},{7,3},{16,20},{17,21},{1... | collective-permute-start | bytes 786440 | tf_op jit(solution)/shard_map/ppermute | solution.py:428
  44.4 15.2 %collective-permute-start.1 = (f32[128,512]{1,0:T(8,128)S(1)}, f32[128,512]{1,0:T(8,128)S(1)}, u32[]{:S(2)}, u32[]{:S(2)}) collective-permute-start(f32[128,512]{1,0:T(8,128)S(1)} %get-tuple-element.28), channel_id=1, source_target_pairs={{0,8},{1,9},{2,10},{3,11},{4,12},{5,13},{6,14},{7,15},{16,24},{17,... | collective-permute-start | bytes 786440 | tf_op jit(solution)/shard_map/ppermute | solution.py:428
  47.1 17.4 %collective-permute-start.2 = (f32[128,512]{1,0:T(8,128)S(1)}, f32[128,512]{1,0:T(8,128)S(1)}, u32[]{:S(2)}, u32[]{:S(2)}) collective-permute-start(f32[128,512]{1,0:T(8,128)S(1)} %get-tuple-element.28), channel_id=1, source_target_pairs={{4,8},{5,9},{6,10},{7,11},{0,12},{1,13},{2,14},{3,15},{20,24},{21,... | collective-permute-start | bytes 786440 | tf_op jit(solution)/shard_map/ppermute | solution.py:428
  64.6 14.9 %collective-permute-start.3 = (f32[256,512]{1,0:T(8,128)S(1)}, f32[256,512]{1,0:T(8,128)S(1)}, u32[]{:S(2)}, u32[]{:S(2)}) collective-permute-start(f32[256,512]{1,0:T(8,128)S(1)} %pad_maximum_fusion.y0_ref), channel_id=1, source_target_pairs={{0,1},{1,2},{2,3},{3,0},{4,5},{5,6},{6,7},{7,4},{8,9},{9,10},{10,1... | collective-permute-start | bytes 1572872 | tf_op jit(solution)/shard_map/ppermute | solution.py:424
  66.3 16.4 %collective-permute-start.4 = (f32[256,512]{1,0:T(8,128)S(1)}, f32[256,512]{1,0:T(8,128)S(1)}, u32[]{:S(2)}, u32[]{:S(2)}) collective-permute-start(f32[256,512]{1,0:T(8,128)S(1)} %pad_maximum_fusion.y0_ref), channel_id=1, source_target_pairs={{0,2},{1,3},{2,0},{3,1},{4,6},{5,7},{6,4},{7,5},{8,10},{9,11},{10,... | collective-permute-start | bytes 1572872 | tf_op jit(solution)/shard_map/ppermute | solution.py:424
  67.3 25.6 %collective-permute-start.5 = (f32[256,512]{1,0:T(8,128)S(1)}, f32[256,512]{1,0:T(8,128)S(1)}, u32[]{:S(2)}, u32[]{:S(2)}) collective-permute-start(f32[256,512]{1,0:T(8,128)S(1)} %pad_maximum_fusion.y0_ref), channel_id=1, source_target_pairs={{0,3},{1,0},{2,1},{3,2},{4,7},{5,4},{6,5},{7,6},{8,11},{9,8},{10,9... | collective-permute-start | bytes 1572872 | tf_op jit(solution)/shard_map/ppermute | solution.py:424
  92.8 1.1 copy-start.3
  112.6 1.0 copy-start
  113.6 0.7 copy-start.7
  114.3 0.7 copy-start.9
  124.4 1.2 copy-start.1
  125.6 1.0 copy-start.4
  126.7 1.0 copy-start.6
  127.7 0.9 copy-start.8
  128.7 0.9 copy-start.10
Sparse Core Ops, SparseCore 0:
  40.7 83.6 all-gather.1

commit v4 on v3

--- a/solution.py
+++ b/solution.py
@@ -36,7 +36,7 @@
     return dot_n(ah, bh) + dot_n(al, bh) + dot_n(ah, bl)
 
 
-def assemble_kernel(code_ref, idx_ref, recv_ref, front_ref, late_ref, early_ref, pivot_ref, out_ref):
+def assemble_kernel(code_ref, idx_ref, recv_ref, front_ref, late_ref, pivot_ref, out_ref):
     out_ref[...] = front_ref[...]
     for s in range(recv_ref.shape[0]):
         for j in range(code_ref.shape[1]):
@@ -52,7 +52,6 @@
     row = lax.broadcasted_iota(jnp.int32, (B, B), 0)
     col = lax.broadcasted_iota(jnp.int32, (B, B), 1)
     out_ref[:, cols] = jnp.where(row >= col, square, square.T)
-    early_ref[...] = out_ref[:, :HALF]
     pivot_ref[...] = out_ref[:, :PIV]
     late_ref[...] = out_ref[:, PIV:]
 
@@ -64,11 +63,10 @@
         assemble_kernel,
         out_shape=(
             jax.ShapeDtypeStruct((rows, order - PIV), F32),
-            jax.ShapeDtypeStruct((rows, HALF), F32),
             jax.ShapeDtypeStruct((rows, PIV), F32),
         ),
         in_specs=[pl.BlockSpec(memory_space=pltpu.SMEM)] * 2 + [vmem, vmem],
-        out_specs=(vmem, vmem, vmem),
+        out_specs=(vmem, vmem),
         scratch_shapes=[pltpu.VMEM((rows, order), F32)],
         compiler_params=pltpu.CompilerParams(vmem_limit_bytes=8 * 1024 * 1024),
         name="assemble",
@@ -277,17 +275,25 @@
     )(index, *parts, rhs)
 
 
-def second_kernel(idx_ref, all_ref, vh0, vl0, lh0, ll0, t0, dinv0, y0, own0, mine_ref, b_ref,
+def second_kernel(idx_ref, near_ref, far_ref, p0_ref, p1_ref, p2_ref, p3_ref, vh0, vl0, lh0, ll0, t0, dinv0, y0, own0, mine_ref, b_ref,
                   fac_ref, eli_ref,
                   a_ref, a21, vh, vl, v32, lh, ll, t_ref, lt_ref, dinv_ref, rest_ref, u_ref, part_ref,
                   e_ref, xh, xl, x32, wh, wl, u21, tph_ref, tpl_ref, sem):
     me = idx_ref[0]
     nrhs, order = b_ref.shape
     low = order - PIV
-    near_copy = pltpu.make_async_copy(all_ref.at[pl.ds(HALF, HALF), pl.ds(HALF, HALF)], a_ref, sem.at[0])
-    far_copy = pltpu.make_async_copy(all_ref.at[pl.ds(PIV, low), :], a21, sem.at[1])
-    near_copy.start()
-    far_copy.start()
+    ypos, zpos = lax.rem(me, 4), jnp.maximum(me // 4 - 2, 0)
+    copies = []
+    for n, (ref, z) in enumerate(((near_ref, zpos), (far_ref, 1 - jnp.minimum(zpos, 1)))):
+        for d in range(4):
+            row = pl.multiple_of((4 * z + lax.rem(ypos + 4 - d, 4)) * B, B)
+            copies.append(pltpu.make_async_copy(
+                ref.at[pl.ds(d * B, B), :], a21.at[pl.ds(row, B), :], sem.at[4 * n + d]))
+    for copy in copies:
+        copy.start()
+    for d, ref in enumerate((p0_ref, p1_ref, p2_ref, p3_ref)):
+        rows = pl.ds(pl.multiple_of(lax.rem(ypos + 4 - d, 4) * B, B), B)
+        a_ref[rows, :] = ref[W2 : W2 + B, :]
     for ref, src in ((vh, vh0), (vl, vl0)):
         ref[:, :HALF] = src[HALF:, :]
         ref[:, HALF:] = jnp.zeros((ref.shape[0], HALF), BF16)
@@ -301,11 +307,11 @@
     rest_ref[...] = jnp.zeros_like(rest_ref)
     xh[...] = jnp.zeros_like(xh)
     xl[...] = jnp.zeros_like(xl)
-    near_copy.wait()
     u_ref[...] = a_ref[0:B, 0:B] - dot3_t(
         vh[0:B, :HALF], vl[0:B, :HALF], lh[HALF : HALF + B, :HALF], ll[HALF : HALF + B, :HALF]
     )
-    far_copy.wait()
+    for copy in copies:
+        copy.wait()
 
     def pair_inverse(i):
         t0h, t0l = split(t_ref[2 * i])
@@ -377,7 +383,7 @@
     return b_ref.at[:, pl.ds(HALF, HALF)]
 
 
-def second(index, gathered, state, mine, rhs):
+def second(index, near, far, parts, state, mine, rhs):
     nrhs, order = rhs.shape
     low = order - PIV
     na = PIV - HALF
@@ -387,8 +393,8 @@
             jax.ShapeDtypeStruct((B, order), F32),
             jax.ShapeDtypeStruct((nrhs, order), F32),
         ),
-        in_specs=[pl.BlockSpec(memory_space=pltpu.SMEM), pl.BlockSpec(memory_space=pl.ANY)]
-        + [VMEM_SPEC] * (len(state) + 2),
+        in_specs=[pl.BlockSpec(memory_space=pltpu.SMEM)]
+        + [VMEM_SPEC] * (len(parts) + len(state) + 4),
         out_specs=(VMEM_SPEC, VMEM_SPEC),
         scratch_shapes=[
             pltpu.VMEM((na, na), F32),
@@ -413,30 +419,34 @@
             pltpu.VMEM((low, W2), F32),
             pltpu.VMEM((W2, W2), BF16),
             pltpu.VMEM((W2, W2), BF16),
-            pltpu.SemaphoreType.DMA((2,)),
+            pltpu.SemaphoreType.DMA((8,)),
         ],
-        compiler_params=pltpu.CompilerParams(vmem_limit_bytes=44 * 1024 * 1024),
+        compiler_params=pltpu.CompilerParams(vmem_limit_bytes=36 * 1024 * 1024),
         name="second",
-    )(index, gathered, *state, mine, rhs)
-
-
-def shift_y(x, d):
-    return lax.ppermute(x, "front", [(4 * z + y, 4 * z + (y + d) % 4) for z in range(4) for y in range(4)])
+    )(index, near, far, *parts, *state, mine, rhs)
+
+
+def shift_y(x, d, zs=(0, 1, 2, 3)):
+    return lax.ppermute(x, "front", [(4 * z + y, 4 * z + (y + d) % 4) for z in zs for y in range(4)])
 
 
 def planes(x, pairs):
     return lax.ppermute(x, "front", [(4 * a + y, 4 * b + y) for a, b in pairs for y in range(4)])
 
 
-def gather_pivot_rows(x):
-    z = lax.axis_index("front") // 4
+def gather_pivot_rows(x, z):
     swap = planes(x, ((0, 1), (1, 0)))
     side = planes(x, ((1, 2), (0, 3)))
     far = planes(x, ((0, 2), (1, 3)))
-    x0 = jnp.where(z == 0, x, jnp.where(z == 1, swap, jnp.where(z == 2, far, side)))
+    x0 = jnp.where(z == 0, x, jnp.where(z == 1, swap, jnp.where(z == 2, far, side)))[:, :HALF]
     x1 = jnp.where(z == 0, swap, jnp.where(z == 1, x, jnp.where(z == 2, side, far)))
-    both = jnp.concatenate([x0, x1], 0)
-    return [both] + [shift_y(both, d) for d in (1, 2, 3)]
+    rows = jnp.concatenate([x0, x1[:, :HALF], x1[:, HALF:]], 0)
+    return [rows] + [shift_y(rows, d) for d in (1, 2, 3)]
+
+
+def gather_lower_rows(x):
+    near = jnp.concatenate([x] + [shift_y(x, d, (2, 3)) for d in (1, 2, 3)], 0)
+    return near, planes(near, ((2, 3), (3, 2)))
 
 
 def local(front_matrix, child_blocks, child_target, child_count, shot_rhs):
@@ -448,11 +458,16 @@
     arrived = lax.all_to_all(payload, "leaf", split_axis=0, concat_axis=0, tiled=True)
     codes = arrived[:, slots * B, :slots].astype(jnp.int32)
     index = lax.axis_index("front").astype(jnp.int32).reshape(1)
-    late, early, pivots = assemble(codes, index, arrived, front_matrix[0])
-    gathered = lax.all_gather(pivots, "front", axis=0, tiled=True)
+    late, pivots = assemble(codes, index, arrived, front_matrix[0])
+    z = lax.axis_index("front") // 4
+    near, far = gather_lower_rows(pivots)
+    parts = gather_pivot_rows(pivots, z)
     rhs = shot_rhs[0]
-    state = first(index, gather_pivot_rows(early), rhs)
-    factored, eliminated = second(index, gathered, state, late, rhs)
+    state = first(index, parts, rhs)
+    factored, eliminated = second(index, near, far, parts, state, late, rhs)
+    tail = eliminated[:, PIV:]
+    tail = jnp.where(z < 2, planes(tail, ((2, 0), (3, 1))), tail)
+    eliminated = jnp.concatenate([eliminated[:, :PIV], tail], 1)
     return factored[None], eliminated[None]
 
 

time: 168 us -> 169 us (level)
  waiting for transfers between devices: 70.5 us -> 86.2 us
  between operations: 14.1 us -> 0.88 us
  local copies, waits for them, and re-layouts: 10.1 us -> 1.74 us
  starting transfers between devices: 17.4 us -> 23.6 us
  Pallas kernels: 50.2 us -> 48.5 us
    ppermute x3 -> x5, waiting for transfers between devices: 15.9 us -> 33.3 us  [planes(): lax.ppermute(x, 'front', [(4 * a + y, 4 * b + y) for a, b in pairs for y...]
    all_gather x1 -> x0, waiting for transfers between devices: 9.48 us -> none  [local(): gathered = lax.all_gather(pivots, 'front', axis=0, tiled=True)]
    unnamed x22 -> x10, local copies, waits for them, and re-layouts: 9.39 us -> 0.88 us
    ppermute x3 -> x6, waiting for transfers between devices: 23.2 us -> 31 us  [shift_y(): lax.ppermute(x, 'front', [(4 * z + y, 4 * z + (y + d) % 4) for z in zs fo...]
    ppermute x3 -> x5, starting transfers between devices: 7.95 us -> 12.1 us  [planes(): lax.ppermute(x, 'front', [(4 * a + y, 4 * b + y) for a, b in pairs for y...]
    ppermute x3 -> x6, starting transfers between devices: 5.03 us -> 7.04 us  [shift_y(): lax.ppermute(x, 'front', [(4 * z + y, 4 * z + (y + d) % 4) for z in zs fo...]
  transfers between devices with their start and end apart: 8 -> 12, of which waited for: 8 -> 7; matrix products, arithmetic and copies ran while one was open for 0% -> 0% of each run, Pallas kernels for 11% -> 11%
where the time goes in v4:
time: 169 us; the launch traced here: 165 us
  waiting for transfers between devices  86.2 us (51%)
  Pallas kernels  48.5 us (29%)
  starting transfers between devices  23.6 us (14%)
  other arithmetic  4.61 us (3%)
  local copies, waits for them, and re-layouts  1.74 us (1%)
    ppermute x5, waiting for transfers between devices, planes(): lax.ppermute(x, 'front', [(4 * a + y, 4 * b + y) for a, b in pairs for y...  33.3 us
    ppermute x6, waiting for transfers between devices, shift_y(): lax.ppermute(x, 'front', [(4 * z + y, 4 * z + (y + d) % 4) for z in zs fo...  31 us
    pallas_call x1, Pallas kernels, second(): pl.pallas_call(second_kernel, out_shape=(jax.ShapeDtypeStruct((B, order),...  28.5 us
    all_to_all x1, waiting for transfers between devices, local(): lax.all_to_all(payload, 'leaf', split_axis=0, concat_axis=0, tiled=True)  21.9 us
    pallas_call x1, Pallas kernels, first(): pl.pallas_call(first_kernel, out_shape=tuple((jax.ShapeDtypeStruct(*o) fo...  18.7 us
    ppermute x5, starting transfers between devices, planes(): lax.ppermute(x, 'front', [(4 * a + y, 4 * b + y) for a, b in pairs for y...  12.1 us
    ppermute x6, starting transfers between devices, shift_y(): lax.ppermute(x, 'front', [(4 * z + y, 4 * z + (y + d) % 4) for z in zs fo...  7.04 us
    all_to_all x1, starting transfers between devices, local(): lax.all_to_all(payload, 'leaf', split_axis=0, concat_axis=0, tiled=True)  4.43 us
  transfers between devices with their start and end apart: 12, of which 7 were waited for; matrix products, arithmetic and copies ran while one was open for 0% of the time, Pallas kernels for 11%

profile of v4, /device:TPU:8, one launch (start us, length us, event | category | flops | bytes accessed | tf_op | source)
XLA Modules:
  0.0 165.5 jit_solution(14228338724381116992)
XLA Ops:
  0.6 0.8 copy.10
  1.4 0.7 fusion
  2.1 2.7 %select_maximum_fusion = f32[8,392,128]{2,1,0:T(8,128)} fusion(f32[8,1,3]{2,1,0:T(1,128)S(1)} %fusion, f32[8,384,128]{2,1,0:T(8,128)} %bitcast.14), kind=kLoop, calls=%fused_computation | loop fusion | flops 1204224 | bytes 3178592 | tf_op jit(solution)/shard_map/concatenate | solution.py:457
  4.8 0.0 copy-start
  4.8 4.4 %all-to-all-start = ((f32[8,392,128]{2,1,0:T(8,128)}), f32[8,392,128]{2,1,0:T(8,128)S(1)}, u32[]{:S(2)}, u32[]{:S(2)}) async-start(f32[8,392,128]{2,1,0:T(8,128)} %select_maximum_fusion), calls=%async_computation | async-start | bytes 3211264 | tf_op jit(solution)/shard_map/all_to_all | solution.py:458
  9.2 21.9 %all-to-all-done.recv_ref = f32[8,392,128]{2,1,0:T(8,128)S(1)} async-done(((f32[8,392,128]{2,1,0:T(8,128)}), f32[8,392,128]{2,1,0:T(8,128)S(1)}, u32[]{:S(2)}, u32[]{:S(2)}) %all-to-all-start) | async-done | bytes 1605664 | tf_op jit(solution)/shard_map/all_to_all | solution.py:458
  31.2 0.0 copy-done
  31.2 1.2 assemble.1
  32.4 0.0 copy-start.2
  32.4 0.8 copy-done.2
  33.2 6.0 %collective-permute-start.6 = (f32[128,1024]{1,0:T(8,128)S(1)}, f32[128,1024]{1,0:T(8,128)S(1)}, u32[]{:S(2)}, u32[]{:S(2)}) collective-permute-start(f32[128,1024]{1,0:T(8,128)S(1)} %get-tuple-element.26), channel_id=1, source_target_pairs={{4,8},{5,9},{6,10},{7,11},{0,12},{1,13},{2,14},{3,15},{20,24},{21,... | collective-permute-start | bytes 1572872 | tf_op jit(solution)/shard_map/ppermute | solution.py:434
  39.2 1.3 collective-permute-start.5
  40.5 2.7 %collective-permute-start.4 = (f32[128,1024]{1,0:T(8,128)S(1)}, f32[128,1024]{1,0:T(8,128)S(1)}, u32[]{:S(2)}, u32[]{:S(2)}) collective-permute-start(f32[128,1024]{1,0:T(8,128)S(1)} %get-tuple-element.26), channel_id=1, source_target_pairs={{0,4},{1,5},{2,6},{3,7},{4,0},{5,1},{6,2},{7,3},{16,20},{17,21},{1... | collective-permute-start | bytes 1572872 | tf_op jit(solution)/shard_map/ppermute | solution.py:434
  43.3 0.7 collective-permute-start.2
  44.0 0.7 collective-permute-start.1
  44.7 16.6 %collective-permute-done.6 = f32[128,1024]{1,0:T(8,128)S(1)} collective-permute-done((f32[128,1024]{1,0:T(8,128)S(1)}, f32[128,1024]{1,0:T(8,128)S(1)}, u32[]{:S(2)}, u32[]{:S(2)}) %collective-permute-start.6) | collective-permute-done | bytes 524320 | tf_op jit(solution)/shard_map/ppermute | solution.py:434
  61.3 0.7 collective-permute-start
  62.0 0.0 collective-permute-done.5
  62.0 2.0 %collective-permute-done.4 = f32[128,1024]{1,0:T(8,128)S(1)} collective-permute-done((f32[128,1024]{1,0:T(8,128)S(1)}, f32[128,1024]{1,0:T(8,128)S(1)}, u32[]{:S(2)}, u32[]{:S(2)}) %collective-permute-start.4) | collective-permute-done | bytes 524320 | tf_op jit(solution)/shard_map/ppermute | solution.py:434
  63.9 0.2 select_select_fusion
  64.1 0.1 slice_select_fusion
  64.3 0.1 pad_maximum_fusion.y0_ref.p0_ref
  64.3 0.0 copy-start.1
  64.3 0.5 collective-permute-start.9
  64.8 2.6 %collective-permute-start.8 = (f32[384,512]{1,0:T(8,128)S(1)}, f32[384,512]{1,0:T(8,128)S(1)}, u32[]{:S(2)}, u32[]{:S(2)}) collective-permute-start(f32[384,512]{1,0:T(8,128)S(1)} %pad_maximum_fusion.y0_ref.p0_ref), channel_id=1, source_target_pairs={{0,2},{1,3},{2,0},{3,1},{4,6},{5,7},{6,4},{7,5},{8,10},{9,11},{10,... | collective-permute-start | bytes 2359304 | tf_op jit(solution)/shard_map/ppermute | solution.py:430
  67.4 0.0 collective-permute-done
  67.4 1.9 %collective-permute-start.7 = (f32[384,512]{1,0:T(8,128)S(1)}, f32[384,512]{1,0:T(8,128)S(1)}, u32[]{:S(2)}, u32[]{:S(2)}) collective-permute-start(f32[384,512]{1,0:T(8,128)S(1)} %pad_maximum_fusion.y0_ref.p0_ref), channel_id=1, source_target_pairs={{0,1},{1,2},{2,3},{3,0},{4,5},{5,6},{6,7},{7,4},{8,9},{9,10},{10,1... | collective-permute-start | bytes 2359304 | tf_op jit(solution)/shard_map/ppermute | solution.py:430
  69.4 0.0 collective-permute-done.1
  69.4 0.0 collective-permute-done.2
  69.5 0.8 collective-permute-start.3
  70.3 13.7 %collective-permute-done.9.y3_ref.p3_ref = f32[384,512]{1,0:T(8,128)S(1)} collective-permute-done((f32[384,512]{1,0:T(8,128)S(1)}, f32[384,512]{1,0:T(8,128)S(1)}, u32[]{:S(2)}, u32[]{:S(2)}) %collective-permute-start.9) | collective-permute-done | bytes 786464 | tf_op jit(solution)/shard_map/ppermute | solution.py:430
  84.0 16.4 %collective-permute-done.8.y2_ref.p2_ref = f32[384,512]{1,0:T(8,128)S(1)} collective-permute-done((f32[384,512]{1,0:T(8,128)S(1)}, f32[384,512]{1,0:T(8,128)S(1)}, u32[]{:S(2)}, u32[]{:S(2)}) %collective-permute-start.8) | collective-permute-done | bytes 786464 | tf_op jit(solution)/shard_map/ppermute | solution.py:430
  100.3 0.9 collective-permute-done.7.y1_ref.p1_ref
  101.2 0.0 copy-done.1
  101.2 0.0 copy-start.3
  101.2 18.7 %first.1 = (bf16[1088,512]{1,0:T(8,128)(2,1)S(1)}, bf16[1088,512]{1,0:T(8,128)(2,1)S(1)}, bf16[1024,512]{1,0:T(8,128)(2,1)S(1)}, bf16[1024,512]{1,0:T(8,128)(2,1...) custom-call(s32[1]{0:T(128)} %bitcast.idx_ref, ...), custom_call_target="tpu_custom_call" | custom-call | flops 20000000000 | bytes 20000000 | tf_op jit(solution)/shard_map/first/pallas_call | solution.py:258
  120.0 0.0 collective-permute-done.3.far_ref
  120.0 0.0 copy-done.3
  120.0 28.5 %second.1 = (f32[128,2048]{1,0:T(8,128)}, f32[64,2048]{1,0:T(8,128)S(1)}) custom-call(s32[1]{0:T(128)} %bitcast.idx_ref, f32[512,1024]{1,0:T(8,128)S(1)} %constant_dynamic-update-slice_fusion.near_ref, f32[512,1024]{1,0:T(8,128)S(1)} %collective-permute-done.3.far_ref, f32[384,512]{1,0:T(8,128)S(1)} %pad_maximum_fusion.y0_ref.p0_ref, ...), custom_call_target="tpu_custom_call" | custom-call | tf_op jit(solution)/shard_map/second/pallas_call | solution.py:390
  148.6 1.3 collective-permute-start.10
  149.9 14.7 %collective-permute-done.10 = f32[64,1024]{1,0:T(8,128)S(1)} collective-permute-done((f32[64,1024]{1,0:T(8,128)S(1)}, f32[64,1024]{1,0:T(8,128)S(1)}, u32[]{:S(2)}, u32[]{:S(2)}) %collective-permute-start.10) | collective-permute-done | bytes 262176 | tf_op jit(solution)/shard_map/ppermute | solution.py:434
  164.6 0.1 fusion.1
  164.7 0.8 maximum_bitcast_fusion
  (6 shorter events, 0.2 us)
Async XLA Ops:
  4.8 26.4 %copy-start = (f32[1,128,2048]{2,1,0:T(8,128)S(1)}, f32[1,128,2048]{2,1,0:T(8,128)}, u32[]{:S(2)}) copy-start(f32[1,128,2048]{2,1,0:T(8,128)} %param.7) | copy-start | bytes 3145732
  4.8 26.4 %all-to-all-start = ((f32[8,392,128]{2,1,0:T(8,128)}), f32[8,392,128]{2,1,0:T(8,128)S(1)}, u32[]{:S(2)}, u32[]{:S(2)}) async-start(f32[8,392,128]{2,1,0:T(8,128)} %select_maximum_fusion), calls=%async_computation | async-start | bytes 3211264 | tf_op jit(solution)/shard_map/all_to_all | solution.py:458
  32.4 0.8 copy-start.2
  33.2 28.1 %collective-permute-start.6 = (f32[128,1024]{1,0:T(8,128)S(1)}, f32[128,1024]{1,0:T(8,128)S(1)}, u32[]{:S(2)}, u32[]{:S(2)}) collective-permute-start(f32[128,1024]{1,0:T(8,128)S(1)} %get-tuple-element.26), channel_id=1, source_target_pairs={{4,8},{5,9},{6,10},{7,11},{0,12},{1,13},{2,14},{3,15},{20,24},{21,... | collective-permute-start | bytes 1572872 | tf_op jit(solution)/shard_map/ppermute | solution.py:434
  39.2 22.8 %collective-permute-start.5 = (f32[128,1024]{1,0:T(8,128)S(1)}, f32[128,1024]{1,0:T(8,128)S(1)}, u32[]{:S(2)}, u32[]{:S(2)}) collective-permute-start(f32[128,1024]{1,0:T(8,128)S(1)} %get-tuple-element.26), channel_id=1, source_target_pairs={{0,8},{1,9},{2,10},{3,11},{4,12},{5,13},{6,14},{7,15},{16,24},{17,... | collective-permute-start | bytes 1572872 | tf_op jit(solution)/shard_map/ppermute | solution.py:434
  40.5 23.4 %collective-permute-start.4 = (f32[128,1024]{1,0:T(8,128)S(1)}, f32[128,1024]{1,0:T(8,128)S(1)}, u32[]{:S(2)}, u32[]{:S(2)}) collective-permute-start(f32[128,1024]{1,0:T(8,128)S(1)} %get-tuple-element.26), channel_id=1, source_target_pairs={{0,4},{1,5},{2,6},{3,7},{4,0},{5,1},{6,2},{7,3},{16,20},{17,21},{1... | collective-permute-start | bytes 1572872 | tf_op jit(solution)/shard_map/ppermute | solution.py:434
  43.3 26.1 %collective-permute-start.2 = (f32[128,1024]{1,0:T(8,128)S(1)}, f32[128,1024]{1,0:T(8,128)S(1)}, u32[]{:S(2)}, u32[]{:S(2)}) collective-permute-start(f32[128,1024]{1,0:T(8,128)S(1)} %get-tuple-element.26), channel_id=1, source_target_pairs={{8,11},{9,8},{10,9},{11,10},{12,15},{13,12},{14,13},{15,14},{24,27... | collective-permute-start | bytes 1572872 | tf_op jit(solution)/shard_map/ppermute | solution.py:430
  44.0 25.4 %collective-permute-start.1 = (f32[128,1024]{1,0:T(8,128)S(1)}, f32[128,1024]{1,0:T(8,128)S(1)}, u32[]{:S(2)}, u32[]{:S(2)}) collective-permute-start(f32[128,1024]{1,0:T(8,128)S(1)} %get-tuple-element.26), channel_id=1, source_target_pairs={{8,10},{9,11},{10,8},{11,9},{12,14},{13,15},{14,12},{15,13},{24,26... | collective-permute-start | bytes 1572872 | tf_op jit(solution)/shard_map/ppermute | solution.py:430
  61.3 6.1 %collective-permute-start = (f32[128,1024]{1,0:T(8,128)S(1)}, f32[128,1024]{1,0:T(8,128)S(1)}, u32[]{:S(2)}, u32[]{:S(2)}) collective-permute-start(f32[128,1024]{1,0:T(8,128)S(1)} %get-tuple-element.26), channel_id=1, source_target_pairs={{8,9},{9,10},{10,11},{11,8},{12,13},{13,14},{14,15},{15,12},{24,25... | collective-permute-start | bytes 1572872 | tf_op jit(solution)/shard_map/ppermute | solution.py:430
  64.3 36.9 %copy-start.1 = (f32[1,64,2048]{2,1,0:T(8,128)S(1)}, f32[1,64,2048]{2,1,0:T(8,128)}, u32[]{:S(2)}) copy-start(f32[1,64,2048]{2,1,0:T(8,128)} %param.11) | copy-start | bytes 1572868
  64.3 19.6 %collective-permute-start.9 = (f32[384,512]{1,0:T(8,128)S(1)}, f32[384,512]{1,0:T(8,128)S(1)}, u32[]{:S(2)}, u32[]{:S(2)}) collective-permute-start(f32[384,512]{1,0:T(8,128)S(1)} %pad_maximum_fusion.y0_ref.p0_ref), channel_id=1, source_target_pairs={{0,3},{1,0},{2,1},{3,2},{4,7},{5,4},{6,5},{7,6},{8,11},{9,8},{10,9... | collective-permute-start | bytes 2359304 | tf_op jit(solution)/shard_map/ppermute | solution.py:430
  64.8 35.5 %collective-permute-start.8 = (f32[384,512]{1,0:T(8,128)S(1)}, f32[384,512]{1,0:T(8,128)S(1)}, u32[]{:S(2)}, u32[]{:S(2)}) collective-permute-start(f32[384,512]{1,0:T(8,128)S(1)} %pad_maximum_fusion.y0_ref.p0_ref), channel_id=1, source_target_pairs={{0,2},{1,3},{2,0},{3,1},{4,6},{5,7},{6,4},{7,5},{8,10},{9,11},{10,... | collective-permute-start | bytes 2359304 | tf_op jit(solution)/shard_map/ppermute | solution.py:430
  67.4 33.8 %collective-permute-start.7 = (f32[384,512]{1,0:T(8,128)S(1)}, f32[384,512]{1,0:T(8,128)S(1)}, u32[]{:S(2)}, u32[]{:S(2)}) collective-permute-start(f32[384,512]{1,0:T(8,128)S(1)} %pad_maximum_fusion.y0_ref.p0_ref), channel_id=1, source_target_pairs={{0,1},{1,2},{2,3},{3,0},{4,5},{5,6},{6,7},{7,4},{8,9},{9,10},{10,1... | collective-permute-start | bytes 2359304 | tf_op jit(solution)/shard_map/ppermute | solution.py:430
  69.5 50.5 %collective-permute-start.3 = (f32[512,1024]{1,0:T(8,128)S(1)}, f32[512,1024]{1,0:T(8,128)S(1)}, u32[]{:S(2)}, u32[]{:S(2)}) collective-permute-start(f32[512,1024]{1,0:T(8,128)S(1)} %constant_dynamic-update-slice_fusion.near_ref), channel_id=1, source_target_pairs={{8,12},{9,13},{10,14},{11,15},{12,8},{13,9},{14,10},{15,11},{24,28... | collective-permute-start | bytes 6291464 | tf_op jit(solution)/shard_map/ppermute | solution.py:434
  101.2 18.7 %copy-start.3 = (f32[128,1024]{1,0:T(8,128)S(1)}, f32[128,1024]{1,0:T(8,128)}, u32[]{:S(2)}) copy-start(f32[128,1024]{1,0:T(8,128)} %copy-done.2) | copy-start | bytes 1572868
  148.6 16.0 %collective-permute-start.10 = (f32[64,1024]{1,0:T(8,128)S(1)}, f32[64,1024]{1,0:T(8,128)S(1)}, u32[]{:S(2)}, u32[]{:S(2)}) collective-permute-start(f32[64,1024]{1,0:T(8,128)S(1)} %slice.46), channel_id=1, source_target_pairs={{8,0},{9,1},{10,2},{11,3},{12,4},{13,5},{14,6},{15,7},{24,16},{25,... | collective-permute-start | bytes 786440 | tf_op jit(solution)/shard_map/ppermute | solution.py:434

commit v5 on v3

--- a/solution.py
+++ b/solution.py
@@ -36,7 +36,7 @@
     return dot_n(ah, bh) + dot_n(al, bh) + dot_n(ah, bl)
 
 
-def assemble_kernel(code_ref, idx_ref, recv_ref, front_ref, late_ref, early_ref, pivot_ref, out_ref):
+def assemble_kernel(code_ref, idx_ref, recv_ref, front_ref, tail_ref, early_ref, late_ref, out_ref):
     out_ref[...] = front_ref[...]
     for s in range(recv_ref.shape[0]):
         for j in range(code_ref.shape[1]):
@@ -53,8 +53,8 @@
     col = lax.broadcasted_iota(jnp.int32, (B, B), 1)
     out_ref[:, cols] = jnp.where(row >= col, square, square.T)
     early_ref[...] = out_ref[:, :HALF]
-    pivot_ref[...] = out_ref[:, :PIV]
-    late_ref[...] = out_ref[:, PIV:]
+    late_ref[...] = out_ref[:, HALF:PIV]
+    tail_ref[...] = out_ref[:, PIV:]
 
 
 def assemble(codes, index, recv, front):
@@ -65,7 +65,7 @@
         out_shape=(
             jax.ShapeDtypeStruct((rows, order - PIV), F32),
             jax.ShapeDtypeStruct((rows, HALF), F32),
-            jax.ShapeDtypeStruct((rows, PIV), F32),
+            jax.ShapeDtypeStruct((rows, HALF), F32),
         ),
         in_specs=[pl.BlockSpec(memory_space=pltpu.SMEM)] * 2 + [vmem, vmem],
         out_specs=(vmem, vmem, vmem),
@@ -152,7 +152,7 @@
 
 
 def factor_panels(k0, k1, a_ref, b_ref, vh, vl, v32, lh, ll, t_ref, lt_ref, dinv_ref,
-                  rest_ref, u_ref, part_ref, e_ref, extra):
+                  rest_ref, u_ref, part_ref, e_ref):
     row0 = k0 * B
     na, nrhs = a_ref.shape[0], b_ref.shape[0]
     ri = lax.broadcasted_iota(jnp.int32, (8, B), 0)
@@ -193,7 +193,7 @@
         def partial():
             part_ref[...] = a_ref[nloc, nloc] - dot3_t(vh[nloc, :], vl[nloc, :], lh[nabs, :], ll[nabs, :])
 
-        side = [lambda: settle(prev), update, partial] + extra(k)
+        side = [lambda: settle(prev), update, partial]
         chain(a_rows, e_rows, store, side)
         total = diag[0]
         for g in range(1, 16):
@@ -229,7 +229,7 @@
     t_ref[0] = jnp.zeros((B, B), F32)
     u_ref[...] = a_ref[0:B, 0:B]
     factor_panels(0, NP // 2, a_ref, b_ref.at[:, pl.ds(0, HALF)], vh, vl, v32, lh, ll, t_ref, lt_ref, dinv_ref,
-                  rest_ref, u_ref, part_ref, e_ref, lambda k: [])
+                  rest_ref, u_ref, part_ref, e_ref)
     nrhs = b_ref.shape[0]
     y_ref[...] = v32[PIV : PIV + nrhs, :]
     near = jnp.minimum(me, NP - 1)
@@ -277,84 +277,134 @@
     )(index, *parts, rhs)
 
 
-def second_kernel(idx_ref, all_ref, vh0, vl0, lh0, ll0, t0, dinv0, y0, own0, mine_ref, b_ref,
-                  fac_ref, eli_ref,
-                  a_ref, a21, vh, vl, v32, lh, ll, t_ref, lt_ref, dinv_ref, rest_ref, u_ref, part_ref,
-                  e_ref, xh, xl, x32, wh, wl, u21, tph_ref, tpl_ref, sem):
+def second_kernel(idx_ref, p0_ref, p1_ref, p2_ref, p3_ref, vh0, vl0, lh0, ll0, t0, dinv0, y0, own0, b_ref,
+                  lh, ll, t_ref, dinv_ref, y_ref, own_ref,
+                  a_ref, vh, vl, v32, lt_ref, rest_ref, u_ref, part_ref, e_ref):
     me = idx_ref[0]
-    nrhs, order = b_ref.shape
-    low = order - PIV
-    near_copy = pltpu.make_async_copy(all_ref.at[pl.ds(HALF, HALF), pl.ds(HALF, HALF)], a_ref, sem.at[0])
-    far_copy = pltpu.make_async_copy(all_ref.at[pl.ds(PIV, low), :], a21, sem.at[1])
-    near_copy.start()
-    far_copy.start()
+    nrhs = b_ref.shape[0]
+    ypos = lax.rem(me, 4)
+    for d, ref in enumerate((p0_ref, p1_ref, p2_ref, p3_ref)):
+        rows = pl.ds(pl.multiple_of(lax.rem(ypos + 4 - d, 4) * B, B), B)
+        a_ref[rows, :] = ref[...]
     for ref, src in ((vh, vh0), (vl, vl0)):
         ref[:, :HALF] = src[HALF:, :]
         ref[:, HALF:] = jnp.zeros((ref.shape[0], HALF), BF16)
     for ref, src in ((lh, lh0), (ll, ll0)):
         ref[:, :HALF] = src[...]
         ref[:, HALF:] = jnp.zeros((ref.shape[0], HALF), BF16)
-    dinv_ref[...] = jnp.zeros_like(dinv_ref)
     dinv_ref[:, :HALF] = dinv0[...]
+    dinv_ref[:, HALF:] = jnp.zeros((dinv_ref.shape[0], HALF), F32)
     t_ref[: NP // 2] = t0[...]
-    t_ref[NP // 2 :] = jnp.zeros((NP // 2, B, B), F32)
+    t_ref[NP // 2] = jnp.zeros((B, B), F32)
     rest_ref[...] = jnp.zeros_like(rest_ref)
-    xh[...] = jnp.zeros_like(xh)
-    xl[...] = jnp.zeros_like(xl)
-    near_copy.wait()
     u_ref[...] = a_ref[0:B, 0:B] - dot3_t(
         vh[0:B, :HALF], vl[0:B, :HALF], lh[HALF : HALF + B, :HALF], ll[HALF : HALF + B, :HALF]
     )
-    far_copy.wait()
-
-    def pair_inverse(i):
+    factor_panels(NP // 2, NP, a_ref, b_ref.at[:, pl.ds(HALF, HALF)], vh, vl, v32, lh, ll, t_ref, lt_ref,
+                  dinv_ref, rest_ref, u_ref, part_ref, e_ref)
+    y_ref[:, :HALF] = y0[...]
+    y_ref[:, HALF:] = v32[HALF : HALF + nrhs, HALF:]
+    own_ref[:, :HALF] = own0[...]
+    near = jnp.clip(me - NP // 2, 0, NP // 2 - 1)
+    rows = pl.ds(pl.multiple_of(near * B, B), B)
+    col = HALF + lax.broadcasted_iota(jnp.int32, (B, HALF), 1)
+    own_ref[:, HALF:] = jnp.where(col < me * B, v32[rows, HALF:] * dinv_ref[0:1, HALF:], 0.0)
+
+    @pl.when((me >= NP // 2) & (me < NP))
+    def _():
+        own_ref[:, pl.ds(pl.multiple_of(me * B, B), B)] = lt_ref[me].T
+
+
+def second(index, parts, state, rhs):
+    nrhs = rhs.shape[0]
+    na = PIV - HALF
+    outs = (
+        ((PIV, PIV), BF16),
+        ((PIV, PIV), BF16),
+        ((NP, B, B), F32),
+        ((8, PIV), F32),
+        ((nrhs, PIV), F32),
+        ((B, PIV), F32),
+    )
+    return pl.pallas_call(
+        second_kernel,
+        out_shape=tuple(jax.ShapeDtypeStruct(*o) for o in outs),
+        in_specs=[pl.BlockSpec(memory_space=pltpu.SMEM)] + [VMEM_SPEC] * (len(parts) + len(state) + 1),
+        out_specs=(VMEM_SPEC,) * len(outs),
+        scratch_shapes=[
+            pltpu.VMEM((na, na), F32),
+            pltpu.VMEM((na + nrhs, PIV), BF16),
+            pltpu.VMEM((na + nrhs, PIV), BF16),
+            pltpu.VMEM((na + nrhs, PIV), F32),
+            pltpu.VMEM((NP, B, B), F32),
+            pltpu.VMEM((na + nrhs, B), F32),
+            pltpu.VMEM((B, B), F32),
+            pltpu.VMEM((B, B), F32),
+            pltpu.VMEM((B, B), F32),
+        ],
+        compiler_params=pltpu.CompilerParams(vmem_limit_bytes=20 * 1024 * 1024),
+        cost_estimate=pl.CostEstimate(flops=2 * 10**10, bytes_accessed=2 * 10**7, transcendentals=0),
+        name="second",
+    )(index, *parts, *state, rhs)
+
+
+def third_kernel(idx_ref, h0, h1, h2, h3, near_ref, far_ref, lh, ll, t_ref, dinv_ref, y_ref, own_ref, tail_ref, b_ref,
+                 fac_ref, eli_ref, a21, xh, xl, x32, wh, wl, sem):
+    me = idx_ref[0]
+    nrhs, order = b_ref.shape
+    low = order - PIV
+    ypos, zpos = lax.rem(me, 4), jnp.clip(me // 4 - 2, 0, 1)
+    copies = []
+    for d, ref in enumerate((h0, h1, h2, h3)):
+        spot = lax.rem(ypos + 4 - d, 4)
+        for n, z in enumerate((zpos, 1 - zpos)):
+            rows = pl.ds(pl.multiple_of((4 * z + spot) * B, B), B)
+            src = (near_ref, far_ref)[n]
+            copies.append(pltpu.make_async_copy(
+                ref.at[pl.ds(n * B, B), :], a21.at[rows, pl.ds(0, HALF)], sem.at[2 * d + n]))
+            copies.append(pltpu.make_async_copy(
+                src.at[pl.ds(d * B, B), :], a21.at[rows, pl.ds(HALF, HALF)], sem.at[8 + 2 * d + n]))
+    for copy in copies:
+        copy.start()
+
+    inverses = []
+    for i in range(NP // 2):
         t0h, t0l = split(t_ref[2 * i])
         t1h, t1l = split(t_ref[2 * i + 1])
-        r1 = pl.ds(pl.multiple_of((2 * i + 1) * B, B), B)
-        c0 = pl.ds(pl.multiple_of(2 * i * B, B), B)
+        r1 = slice((2 * i + 1) * B, (2 * i + 2) * B)
+        c0 = slice(2 * i * B, (2 * i + 1) * B)
         zh, zl = split(dot3_n(lh[r1, c0], ll[r1, c0], t0h, t0l))
         zh, zl = split(-dot3_n(t1h, t1l, zh, zl))
         zero = jnp.zeros((B, B), BF16)
-        tph_ref[...] = cat_blocks(t0h, zero, zh, t1h)
-        tpl_ref[...] = cat_blocks(t0l, zero, zl, t1l)
-
-    def below_update(i):
-        pc = pl.ds(pl.multiple_of(i * W2, W2), W2)
-        u21[...] = a21[:, pc] - dot3_t(xh[...], xl[...], lh[pc, :], ll[pc, :])
-
-    def below_settle(i):
-        pc = pl.ds(pl.multiple_of(i * W2, W2), W2)
-        uh, ul = split(u21[...])
-        v = dot3_t(uh, ul, tph_ref[...], tpl_ref[...])
+        inverses.append((cat_blocks(t0h, zero, zh, t1h), cat_blocks(t0l, zero, zl, t1l)))
+    for copy in copies:
+        copy.wait()
+    for i in range(NP // 2):
+        pc, prev = slice(i * W2, (i + 1) * W2), slice(0, i * W2)
+        u = a21[:, pc]
+        if i:
+            u = u - dot3_t(xh[:, prev], xl[:, prev], lh[pc, prev], ll[pc, prev])
+        uh, ul = split(u)
+        v = dot3_t(uh, ul, *inverses[i])
         x32[:, pc] = v
         xh[:, pc], xl[:, pc] = split(v)
         wh[:, pc], wl[:, pc] = split(v * dinv_ref[0:1, pc])
 
-    def extra(k):
-        i = k - NP // 2
-        return [lambda: pair_inverse(i), lambda: below_update(i), lambda: below_settle(i)]
-
-    factor_panels(NP // 2, NP, a_ref, b_half(b_ref), vh, vl, v32, lh, ll, t_ref, lt_ref, dinv_ref,
-                  rest_ref, u_ref, part_ref, e_ref, extra)
-    last = NP // 2 - 1
-    pair_inverse(last)
-    below_settle(last)
-
-    y_late = v32[HALF : HALF + nrhs, HALF:]
-    eli_ref[:, :HALF] = y0[...]
-    eli_ref[:, HALF:PIV] = y_late
+    y = y_ref[...]
+    yh, yl = split(y)
+    eli_ref[:, :PIV] = y
     mine = pl.ds(pl.multiple_of(jnp.maximum(me - NP, 0) * B, B), B)
-    qh = jnp.concatenate([xh[mine, :], vh[HALF : HALF + nrhs, :]], 0)
-    ql = jnp.concatenate([xl[mine, :], vl[HALF : HALF + nrhs, :]], 0)
-    lower = me >= NP
+    qh = jnp.concatenate([xh[mine, :], yh], 0)
+    ql = jnp.concatenate([xl[mine, :], yl], 0)
     for c in range(low // W2):
         rows = slice(c * W2, (c + 1) * W2)
         dst = slice(PIV + c * W2, PIV + (c + 1) * W2)
         prod = dot3_t(qh, ql, wh[rows, :], wl[rows, :])
         row = me * B + lax.broadcasted_iota(jnp.int32, (B, W2), 0)
         col = PIV + c * W2 + lax.broadcasted_iota(jnp.int32, (B, W2), 1)
-        fac_ref[:, dst] = jnp.where(row >= col, mine_ref[:, rows] - prod[:B], 0.0)
+        fac_ref[:, dst] = jnp.where(row >= col, tail_ref[:, rows] - prod[:B], 0.0)
         eli_ref[:, dst] = b_ref[:, dst] - prod[B:]
+    lower = me >= NP
 
     @pl.when(lower)
     def _():
@@ -362,81 +412,48 @@
 
     @pl.when(jnp.logical_not(lower))
     def _():
-        fac_ref[:, :HALF] = own0[...]
-        near = jnp.maximum(me - NP // 2, 0)
-        rows = pl.ds(pl.multiple_of(near * B, B), B)
-        col = HALF + lax.broadcasted_iota(jnp.int32, (B, HALF), 1)
-        fac_ref[:, HALF:PIV] = jnp.where(col < me * B, v32[rows, HALF:] * dinv_ref[0:1, HALF:], 0.0)
-
-    @pl.when((me >= NP // 2) & (me < NP))
-    def _():
-        fac_ref[:, pl.ds(pl.multiple_of(me * B, B), B)] = lt_ref[me].T
-
-
-def b_half(b_ref):
-    return b_ref.at[:, pl.ds(HALF, HALF)]
-
-
-def second(index, gathered, state, mine, rhs):
+        fac_ref[:, :PIV] = own_ref[...]
+
+
+def third(index, lower, state, tail, rhs):
     nrhs, order = rhs.shape
     low = order - PIV
-    na = PIV - HALF
     return pl.pallas_call(
-        second_kernel,
+        third_kernel,
         out_shape=(
             jax.ShapeDtypeStruct((B, order), F32),
             jax.ShapeDtypeStruct((nrhs, order), F32),
         ),
-        in_specs=[pl.BlockSpec(memory_space=pltpu.SMEM), pl.BlockSpec(memory_space=pl.ANY)]
-        + [VMEM_SPEC] * (len(state) + 2),
+        in_specs=[pl.BlockSpec(memory_space=pltpu.SMEM)] + [VMEM_SPEC] * (len(lower) + len(state) + 2),
         out_specs=(VMEM_SPEC, VMEM_SPEC),
         scratch_shapes=[
-            pltpu.VMEM((na, na), F32),
             pltpu.VMEM((low, PIV), F32),
-            pltpu.VMEM((na + nrhs, PIV), BF16),
-            pltpu.VMEM((na + nrhs, PIV), BF16),
-            pltpu.VMEM((na + nrhs, PIV), F32),
-            pltpu.VMEM((PIV, PIV), BF16),
-            pltpu.VMEM((PIV, PIV), BF16),
-            pltpu.VMEM((NP, B, B), F32),
-            pltpu.VMEM((NP, B, B), F32),
-            pltpu.VMEM((8, PIV), F32),
-            pltpu.VMEM((na + nrhs, B), F32),
-            pltpu.VMEM((B, B), F32),
-            pltpu.VMEM((B, B), F32),
-            pltpu.VMEM((B, B), F32),
             pltpu.VMEM((low, PIV), BF16),
             pltpu.VMEM((low, PIV), BF16),
             pltpu.VMEM((low, PIV), F32),
             pltpu.VMEM((low, PIV), BF16),
             pltpu.VMEM((low, PIV), BF16),
-            pltpu.VMEM((low, W2), F32),
-            pltpu.VMEM((W2, W2), BF16),
-            pltpu.VMEM((W2, W2), BF16),
-            pltpu.SemaphoreType.DMA((2,)),
+            pltpu.SemaphoreType.DMA((16,)),
         ],
-        compiler_params=pltpu.CompilerParams(vmem_limit_bytes=44 * 1024 * 1024),
-        name="second",
-    )(index, gathered, *state, mine, rhs)
-
-
-def shift_y(x, d):
-    return lax.ppermute(x, "front", [(4 * z + y, 4 * z + (y + d) % 4) for z in range(4) for y in range(4)])
+        compiler_params=pltpu.CompilerParams(vmem_limit_bytes=34 * 1024 * 1024),
+        name="third",
+    )(index, *lower, *state, tail, rhs)
+
+
+def shift_y(x, d, zs=(0, 1, 2, 3)):
+    return lax.ppermute(x, "front", [(4 * z + y, 4 * z + (y + d) % 4) for z in zs for y in range(4)])
 
 
 def planes(x, pairs):
     return lax.ppermute(x, "front", [(4 * a + y, 4 * b + y) for a, b in pairs for y in range(4)])
 
 
-def gather_pivot_rows(x):
-    z = lax.axis_index("front") // 4
-    swap = planes(x, ((0, 1), (1, 0)))
-    side = planes(x, ((1, 2), (0, 3)))
-    far = planes(x, ((0, 2), (1, 3)))
-    x0 = jnp.where(z == 0, x, jnp.where(z == 1, swap, jnp.where(z == 2, far, side)))
-    x1 = jnp.where(z == 0, swap, jnp.where(z == 1, x, jnp.where(z == 2, side, far)))
-    both = jnp.concatenate([x0, x1], 0)
-    return [both] + [shift_y(both, d) for d in (1, 2, 3)]
+def pick(z, *values):
+    return jnp.where(z == 0, values[0], jnp.where(z == 1, values[1], jnp.where(z == 2, values[2], values[3])))
+
+
+def ring_y(x, zs=(0, 1, 2, 3)):
+    return [x] + [shift_y(x, d, zs) for d in (1, 2, 3)]
 
 
 def local(front_matrix, child_blocks, child_target, child_count, shot_rhs):
@@ -448,11 +465,26 @@
     arrived = lax.all_to_all(payload, "leaf", split_axis=0, concat_axis=0, tiled=True)
     codes = arrived[:, slots * B, :slots].astype(jnp.int32)
     index = lax.axis_index("front").astype(jnp.int32).reshape(1)
-    late, early, pivots = assemble(codes, index, arrived, front_matrix[0])
-    gathered = lax.all_gather(pivots, "front", axis=0, tiled=True)
+    tail, early, late = assemble(codes, index, arrived, front_matrix[0])
+    z = lax.axis_index("front") // 4
     rhs = shot_rhs[0]
-    state = first(index, gather_pivot_rows(early), rhs)
-    factored, eliminated = second(index, gathered, state, late, rhs)
+    swap = planes(early, ((0, 1), (1, 0), (2, 3), (3, 2)))
+    side = planes(early, ((1, 2), (0, 3)))
+    cross = planes(early, ((0, 2), (1, 3)))
+    near = jnp.concatenate(ring_y(late, (2, 3)), 0)
+    early_parts = ring_y(jnp.concatenate([pick(z, early, swap, cross, side), pick(z, swap, early, side, cross)], 0))
+    late_x, _ = lax.optimization_barrier((late, (swap, side, cross)))
+    to0, to2, to3 = (planes(late_x, ((1, d),)) for d in (0, 2, 3))
+    late_parts = ring_y(pick(z, to0, late_x, to2, to3))
+    far = planes(near, ((2, 3), (3, 2)))
+    state = first(index, early_parts, rhs)
+    pair, _ = lax.optimization_barrier((jnp.concatenate([early, swap], 0), state[6]))
+    below = ring_y(pair, (2, 3))
+    state = second(index, late_parts, state, rhs)
+    factored, eliminated = third(index, below + [near, far], state, tail, rhs)
+    tail = eliminated[:, PIV:]
+    tail = jnp.where(z < 2, planes(tail, ((2, 0), (3, 1))), tail)
+    eliminated = jnp.concatenate([eliminated[:, :PIV], tail], 1)
     return factored[None], eliminated[None]
 
 

time: 168 us -> 159 us (0.946)
  starting transfers between devices: 17.4 us -> 31.8 us
  between operations: 14.1 us -> 1 us
  local copies, waits for them, and re-layouts: 10.1 us -> 1.66 us
  waiting for transfers between devices: 70.5 us -> 67 us
    ppermute x3 -> x8, waiting for transfers between devices: 15.9 us -> 31.5 us  [planes(): lax.ppermute(x, 'front', [(4 * a + y, 4 * b + y) for a, b in pairs for y...]
    ppermute x3 -> x12, waiting for transfers between devices: 23.2 us -> 13.6 us  [shift_y(): lax.ppermute(x, 'front', [(4 * z + y, 4 * z + (y + d) % 4) for z in zs fo...]
    all_gather x1 -> x0, waiting for transfers between devices: 9.48 us -> none  [local(): gathered = lax.all_gather(pivots, 'front', axis=0, tiled=True)]
    ppermute x3 -> x12, starting transfers between devices: 5.03 us -> 14 us  [shift_y(): lax.ppermute(x, 'front', [(4 * z + y, 4 * z + (y + d) % 4) for z in zs fo...]
    unnamed x22 -> x11, local copies, waits for them, and re-layouts: 9.39 us -> 0.86 us
    ppermute x3 -> x8, starting transfers between devices: 7.95 us -> 13.4 us  [planes(): lax.ppermute(x, 'front', [(4 * a + y, 4 * b + y) for a, b in pairs for y...]
    pallas_call x1 -> x2, Pallas kernels: 29.5 us -> 30.7 us  [the longest x1 18.5 us: second(): pl.pallas_call(second_kernel, out_shape=tuple((jax.ShapeDtypeStruct(*o) f...]
  transfers between devices with their start and end apart: 8 -> 21, of which waited for: 8 -> 6; matrix products, arithmetic and copies ran while one was open for 0% -> 0% of each run, Pallas kernels for 11% -> 24%
where the time goes in v5:
time: 159 us; the launch traced here: 156 us
  waiting for transfers between devices  67 us (42%)
  Pallas kernels  50.4 us (32%)
  starting transfers between devices  31.8 us (20%)
  other arithmetic  4.58 us (3%)
  local copies, waits for them, and re-layouts  1.66 us (1%)
    ppermute x8, waiting for transfers between devices, planes(): lax.ppermute(x, 'front', [(4 * a + y, 4 * b + y) for a, b in pairs for y...  31.5 us
    all_to_all x1, waiting for transfers between devices, local(): lax.all_to_all(payload, 'leaf', split_axis=0, concat_axis=0, tiled=True)  21.9 us
    pallas_call x1, Pallas kernels, first(): pl.pallas_call(first_kernel, out_shape=tuple((jax.ShapeDtypeStruct(*o) fo...  18.5 us
    pallas_call x1, Pallas kernels, second(): pl.pallas_call(second_kernel, out_shape=tuple((jax.ShapeDtypeStruct(*o) f...  18.5 us
    ppermute x12, starting transfers between devices, shift_y(): lax.ppermute(x, 'front', [(4 * z + y, 4 * z + (y + d) % 4) for z in zs fo...  14 us
    ppermute x12, waiting for transfers between devices, shift_y(): lax.ppermute(x, 'front', [(4 * z + y, 4 * z + (y + d) % 4) for z in zs fo...  13.6 us
    ppermute x8, starting transfers between devices, planes(): lax.ppermute(x, 'front', [(4 * a + y, 4 * b + y) for a, b in pairs for y...  13.4 us
    pallas_call x1, Pallas kernels, third(): pl.pallas_call(third_kernel, out_shape=(jax.ShapeDtypeStruct((B, order),...  12.3 us
  transfers between devices with their start and end apart: 21, of which 6 were waited for; matrix products, arithmetic and copies ran while one was open for 0% of the time, Pallas kernels for 24%

profile of v5, /device:TPU:8, one launch (start us, length us, event | category | flops | bytes accessed | tf_op | source)
XLA Modules:
  0.0 156.5 jit_solution(3645299554306040459)
XLA Ops:
  0.6 0.8 copy.10
  1.4 0.7 fusion
  2.1 2.7 %select_maximum_fusion = f32[8,392,128]{2,1,0:T(8,128)} fusion(f32[8,1,3]{2,1,0:T(1,128)S(1)} %fusion, f32[8,384,128]{2,1,0:T(8,128)} %bitcast.15), kind=kLoop, calls=%fused_computation | loop fusion | flops 1204224 | bytes 3178592 | tf_op jit(solution)/shard_map/concatenate | solution.py:464
  4.8 4.4 %all-to-all-start = ((f32[8,392,128]{2,1,0:T(8,128)}), f32[8,392,128]{2,1,0:T(8,128)S(1)}, u32[]{:S(2)}, u32[]{:S(2)}) async-start(f32[8,392,128]{2,1,0:T(8,128)} %select_maximum_fusion), calls=%async_computation | async-start | bytes 3211264 | tf_op jit(solution)/shard_map/all_to_all | solution.py:465
  9.3 21.9 %all-to-all-done.recv_ref = f32[8,392,128]{2,1,0:T(8,128)S(1)} async-done(((f32[8,392,128]{2,1,0:T(8,128)}), f32[8,392,128]{2,1,0:T(8,128)S(1)}, u32[]{:S(2)}, u32[]{:S(2)}) %all-to-all-start) | async-done | bytes 1605664 | tf_op jit(solution)/shard_map/all_to_all | solution.py:465
  31.2 1.1 assemble.1
  32.4 0.0 copy-start.2
  32.4 0.8 copy-done.2
  33.1 1.9 %collective-permute-start = (f32[128,512]{1,0:T(8,128)S(1)}, f32[128,512]{1,0:T(8,128)S(1)}, u32[]{:S(2)}, u32[]{:S(2)}) collective-permute-start(f32[128,512]{1,0:T(8,128)S(1)} %get-tuple-element.35), channel_id=1, source_target_pairs={{0,4},{1,5},{2,6},{3,7},{4,0},{5,1},{6,2},{7,3},{8,12},{9,13},{10,... | collective-permute-start | bytes 786440 | tf_op jit(solution)/shard_map/ppermute | solution.py:448
  35.1 5.5 %collective-permute-start.1 = (f32[128,512]{1,0:T(8,128)S(1)}, f32[128,512]{1,0:T(8,128)S(1)}, u32[]{:S(2)}, u32[]{:S(2)}) collective-permute-start(f32[128,512]{1,0:T(8,128)S(1)} %get-tuple-element.35), channel_id=1, source_target_pairs={{0,8},{1,9},{2,10},{3,11},{4,12},{5,13},{6,14},{7,15},{16,24},{17,... | collective-permute-start | bytes 786440 | tf_op jit(solution)/shard_map/ppermute | solution.py:448
  40.6 1.3 collective-permute-start.2
  42.0 0.7 collective-permute-start.9
  42.6 0.7 collective-permute-start.10
  43.3 0.0 collective-permute-done
  43.4 0.7 collective-permute-start.11
  44.0 2.2 %collective-permute-done.1 = f32[128,512]{1,0:T(8,128)S(1)} collective-permute-done((f32[128,512]{1,0:T(8,128)S(1)}, f32[128,512]{1,0:T(8,128)S(1)}, u32[]{:S(2)}, u32[]{:S(2)}) %collective-permute-start.1) | collective-permute-done | bytes 262176 | tf_op jit(solution)/shard_map/ppermute | solution.py:448
  46.2 5.3 %collective-permute-done.2 = f32[128,512]{1,0:T(8,128)S(1)} collective-permute-done((f32[128,512]{1,0:T(8,128)S(1)}, f32[128,512]{1,0:T(8,128)S(1)}, u32[]{:S(2)}, u32[]{:S(2)}) %collective-permute-start.2) | collective-permute-done | bytes 262176 | tf_op jit(solution)/shard_map/ppermute | solution.py:448
  51.5 1.3 collective-permute-start.13
  52.8 0.7 collective-permute-start.14
  53.5 0.1 select_select_fusion.2
  53.6 0.0 collective-permute-done.9
  53.6 0.7 collective-permute-start.15
  54.3 0.0 copy-start.1
  54.4 0.0 collective-permute-done.10
  54.4 1.6 %collective-permute-start.3 = (f32[256,512]{1,0:T(8,128)S(1)}, f32[256,512]{1,0:T(8,128)S(1)}, u32[]{:S(2)}, u32[]{:S(2)}) collective-permute-start(f32[256,512]{1,0:T(8,128)S(1)} %pad_maximum_fusion.1.y0_ref), channel_id=1, source_target_pairs={{0,1},{1,2},{2,3},{3,0},{4,5},{5,6},{6,7},{7,4},{8,9},{9,10},{10,1... | collective-permute-start | bytes 1572872 | tf_op jit(solution)/shard_map/ppermute | solution.py:444
  56.0 0.9 collective-permute-start.4
  57.0 5.6 %collective-permute-done.13 = f32[128,512]{1,0:T(8,128)S(1)} collective-permute-done((f32[128,512]{1,0:T(8,128)S(1)}, f32[128,512]{1,0:T(8,128)S(1)}, u32[]{:S(2)}, u32[]{:S(2)}) %collective-permute-start.13) | collective-permute-done | bytes 262176 | tf_op jit(solution)/shard_map/ppermute | solution.py:448
  62.5 0.5 collective-permute-start.5
  63.1 0.0 collective-permute-done.14
  63.1 0.7 collective-permute-start.12
  63.8 0.0 collective-permute-done.15
  63.8 0.1 select_select_fusion.p0_ref
  63.9 1.6 %collective-permute-start.16 = (f32[128,512]{1,0:T(8,128)S(1)}, f32[128,512]{1,0:T(8,128)S(1)}, u32[]{:S(2)}, u32[]{:S(2)}) collective-permute-start(f32[128,512]{1,0:T(8,128)S(1)} %select_select_fusion.p0_ref), channel_id=1, source_target_pairs={{0,1},{1,2},{2,3},{3,0},{4,5},{5,6},{6,7},{7,4},{8,9},{9,10},{10,1... | collective-permute-start | bytes 786440 | tf_op jit(solution)/shard_map/ppermute | solution.py:444
  65.6 13.5 %collective-permute-done.3.y1_ref = f32[256,512]{1,0:T(8,128)S(1)} collective-permute-done((f32[256,512]{1,0:T(8,128)S(1)}, f32[256,512]{1,0:T(8,128)S(1)}, u32[]{:S(2)}, u32[]{:S(2)}) %collective-permute-start.3) | collective-permute-done | bytes 524320 | tf_op jit(solution)/shard_map/ppermute | solution.py:444
  79.1 0.0 collective-permute-start.17
  79.1 0.0 collective-permute-done.4.y2_ref
  79.1 5.0 %collective-permute-start.18 = (f32[128,512]{1,0:T(8,128)S(1)}, f32[128,512]{1,0:T(8,128)S(1)}, u32[]{:S(2)}, u32[]{:S(2)}) collective-permute-start(f32[128,512]{1,0:T(8,128)S(1)} %select_select_fusion.p0_ref), channel_id=1, source_target_pairs={{0,3},{1,0},{2,1},{3,2},{4,7},{5,4},{6,5},{7,6},{8,11},{9,8},{10,9... | collective-permute-start | bytes 786440 | tf_op jit(solution)/shard_map/ppermute | solution.py:444
  84.1 18.5 %first.1 = (bf16[1088,512]{1,0:T(8,128)(2,1)S(1)}, bf16[1088,512]{1,0:T(8,128)(2,1)S(1)}, bf16[1024,512]{1,0:T(8,128)(2,1)S(1)}, bf16[1024,512]{1,0:T(8,128)(2,1...) custom-call(s32[1]{0:T(128)} %bitcast.idx_ref, ...), custom_call_target="tpu_custom_call" | custom-call | flops 20000000000 | bytes 20000000 | tf_op jit(solution)/shard_map/first/pallas_call | solution.py:260
  102.6 0.7 collective-permute-start.6
  103.4 0.7 collective-permute-start.7
  104.1 0.0 collective-permute-done.17.p2_ref
  104.1 0.9 collective-permute-start.8
  105.0 0.0 copy-start.3
  105.0 18.5 %second.1 = (bf16[1024,1024]{1,0:T(8,128)(2,1)S(1)}, bf16[1024,1024]{1,0:T(8,128)(2,1)S(1)}, f32[8,128,128]{2,1,0:T(8,128)S(1)}, f32[8,1024]{1,0:T(8,128)S(1)}, ...) custom-call(s32[1]{0:T(128)} %bitcast.idx_ref, f32[128,512]{1,0:T(8,128)S(1)} %select_select_fusion.p0_ref, ...), custom_call_target="tpu_custom_call" | custom-call | flops 20000000000 | bytes 20000000 | tf_op jit(solution)/shard_map/second/pallas_call | solution.py:329
  123.5 12.3 %third.1 = (f32[128,2048]{1,0:T(8,128)}, f32[64,2048]{1,0:T(8,128)S(1)}) custom-call(s32[1]{0:T(128)} %bitcast.idx_ref, f32[256,512]{1,0:T(8,128)S(1)} %pad_maximum_fusion.h0, f32[256,512]{1,0:T(8,128)S(1)} %collective-permute-done.6.h1, f32[256,512]{1,0:T(8,128)S(1)} %collective-permute-done.7.h2, f32[256,512]{1,0:T(8,128)S(1)} %collective-permute-done.8.h3, ...), custom_call_target="tpu_custom_call" | custom-call | tf_op jit(solution)/shard_map/third/pallas_call | solution.py:421
  135.8 1.3 collective-permute-start.19
  137.1 18.5 %collective-permute-done.19 = f32[64,1024]{1,0:T(8,128)S(1)} collective-permute-done((f32[64,1024]{1,0:T(8,128)S(1)}, f32[64,1024]{1,0:T(8,128)S(1)}, u32[]{:S(2)}, u32[]{:S(2)}) %collective-permute-start.19) | collective-permute-done | bytes 262176 | tf_op jit(solution)/shard_map/ppermute | solution.py:448
  155.6 0.8 maximum_bitcast_fusion
  (21 shorter events, 0.3 us)
Async XLA Ops:
  4.8 26.4 %copy-start = (f32[1,128,2048]{2,1,0:T(8,128)S(1)}, f32[1,128,2048]{2,1,0:T(8,128)}, u32[]{:S(2)}) copy-start(f32[1,128,2048]{2,1,0:T(8,128)} %param.7) | copy-start | bytes 3145732
  4.8 26.4 %all-to-all-start = ((f32[8,392,128]{2,1,0:T(8,128)}), f32[8,392,128]{2,1,0:T(8,128)S(1)}, u32[]{:S(2)}, u32[]{:S(2)}) async-start(f32[8,392,128]{2,1,0:T(8,128)} %select_maximum_fusion), calls=%async_computation | async-start | bytes 3211264 | tf_op jit(solution)/shard_map/all_to_all | solution.py:465
  32.4 0.8 copy-start.2
  33.1 10.2 %collective-permute-start = (f32[128,512]{1,0:T(8,128)S(1)}, f32[128,512]{1,0:T(8,128)S(1)}, u32[]{:S(2)}, u32[]{:S(2)}) collective-permute-start(f32[128,512]{1,0:T(8,128)S(1)} %get-tuple-element.35), channel_id=1, source_target_pairs={{0,4},{1,5},{2,6},{3,7},{4,0},{5,1},{6,2},{7,3},{8,12},{9,13},{10,... | collective-permute-start | bytes 786440 | tf_op jit(solution)/shard_map/ppermute | solution.py:448
  35.1 11.1 %collective-permute-start.1 = (f32[128,512]{1,0:T(8,128)S(1)}, f32[128,512]{1,0:T(8,128)S(1)}, u32[]{:S(2)}, u32[]{:S(2)}) collective-permute-start(f32[128,512]{1,0:T(8,128)S(1)} %get-tuple-element.35), channel_id=1, source_target_pairs={{0,8},{1,9},{2,10},{3,11},{4,12},{5,13},{6,14},{7,15},{16,24},{17,... | collective-permute-start | bytes 786440 | tf_op jit(solution)/shard_map/ppermute | solution.py:448
  40.6 10.9 %collective-permute-start.2 = (f32[128,512]{1,0:T(8,128)S(1)}, f32[128,512]{1,0:T(8,128)S(1)}, u32[]{:S(2)}, u32[]{:S(2)}) collective-permute-start(f32[128,512]{1,0:T(8,128)S(1)} %get-tuple-element.35), channel_id=1, source_target_pairs={{4,8},{5,9},{6,10},{7,11},{0,12},{1,13},{2,14},{3,15},{20,24},{21,... | collective-permute-start | bytes 786440 | tf_op jit(solution)/shard_map/ppermute | solution.py:448
  42.0 11.6 %collective-permute-start.9 = (f32[128,512]{1,0:T(8,128)S(1)}, f32[128,512]{1,0:T(8,128)S(1)}, u32[]{:S(2)}, u32[]{:S(2)}) collective-permute-start(f32[128,512]{1,0:T(8,128)S(1)} %get-tuple-element.39), channel_id=1, source_target_pairs={{8,9},{9,10},{10,11},{11,8},{12,13},{13,14},{14,15},{15,12},{24,25... | collective-permute-start | bytes 786440 | tf_op jit(solution)/shard_map/ppermute | solution.py:444
  42.6 11.7 %collective-permute-start.10 = (f32[128,512]{1,0:T(8,128)S(1)}, f32[128,512]{1,0:T(8,128)S(1)}, u32[]{:S(2)}, u32[]{:S(2)}) collective-permute-start(f32[128,512]{1,0:T(8,128)S(1)} %get-tuple-element.39), channel_id=1, source_target_pairs={{8,10},{9,11},{10,8},{11,9},{12,14},{13,15},{14,12},{15,13},{24,26... | collective-permute-start | bytes 786440 | tf_op jit(solution)/shard_map/ppermute | solution.py:444
  43.4 12.7 %collective-permute-start.11 = (f32[128,512]{1,0:T(8,128)S(1)}, f32[128,512]{1,0:T(8,128)S(1)}, u32[]{:S(2)}, u32[]{:S(2)}) collective-permute-start(f32[128,512]{1,0:T(8,128)S(1)} %get-tuple-element.39), channel_id=1, source_target_pairs={{8,11},{9,8},{10,9},{11,10},{12,15},{13,12},{14,13},{15,14},{24,27... | collective-permute-start | bytes 786440 | tf_op jit(solution)/shard_map/ppermute | solution.py:444
  51.5 11.0 %collective-permute-start.13 = (f32[128,512]{1,0:T(8,128)S(1)}, f32[128,512]{1,0:T(8,128)S(1)}, u32[]{:S(2)}, u32[]{:S(2)}) collective-permute-start(f32[128,512]{1,0:T(8,128)S(1)} %get-tuple-element.39), channel_id=1, source_target_pairs={{4,0},{5,1},{6,2},{7,3},{20,16},{21,17},{22,18},{23,19},{36,32},{3... | collective-permute-start | bytes 786440 | tf_op jit(solution)/shard_map/ppermute | solution.py:448
  52.8 10.3 %collective-permute-start.14 = (f32[128,512]{1,0:T(8,128)S(1)}, f32[128,512]{1,0:T(8,128)S(1)}, u32[]{:S(2)}, u32[]{:S(2)}) collective-permute-start(f32[128,512]{1,0:T(8,128)S(1)} %get-tuple-element.39), channel_id=1, source_target_pairs={{4,8},{5,9},{6,10},{7,11},{20,24},{21,25},{22,26},{23,27},{36,40},... | collective-permute-start | bytes 786440 | tf_op jit(solution)/shard_map/ppermute | solution.py:448
  53.6 10.2 %collective-permute-start.15 = (f32[128,512]{1,0:T(8,128)S(1)}, f32[128,512]{1,0:T(8,128)S(1)}, u32[]{:S(2)}, u32[]{:S(2)}) collective-permute-start(f32[128,512]{1,0:T(8,128)S(1)} %get-tuple-element.39), channel_id=1, source_target_pairs={{4,12},{5,13},{6,14},{7,15},{20,28},{21,29},{22,30},{23,31},{36,44... | collective-permute-start | bytes 786440 | tf_op jit(solution)/shard_map/ppermute | solution.py:448
  54.3 29.8 %copy-start.1 = (f32[1,64,2048]{2,1,0:T(8,128)S(1)}, f32[1,64,2048]{2,1,0:T(8,128)}, u32[]{:S(2)}) copy-start(f32[1,64,2048]{2,1,0:T(8,128)} %param.11) | copy-start | bytes 1572868
  54.4 24.8 %collective-permute-start.3 = (f32[256,512]{1,0:T(8,128)S(1)}, f32[256,512]{1,0:T(8,128)S(1)}, u32[]{:S(2)}, u32[]{:S(2)}) collective-permute-start(f32[256,512]{1,0:T(8,128)S(1)} %pad_maximum_fusion.1.y0_ref), channel_id=1, source_target_pairs={{0,1},{1,2},{2,3},{3,0},{4,5},{5,6},{6,7},{7,4},{8,9},{9,10},{10,1... | collective-permute-start | bytes 1572872 | tf_op jit(solution)/shard_map/ppermute | solution.py:444
  56.0 23.1 %collective-permute-start.4 = (f32[256,512]{1,0:T(8,128)S(1)}, f32[256,512]{1,0:T(8,128)S(1)}, u32[]{:S(2)}, u32[]{:S(2)}) collective-permute-start(f32[256,512]{1,0:T(8,128)S(1)} %pad_maximum_fusion.1.y0_ref), channel_id=1, source_target_pairs={{0,2},{1,3},{2,0},{3,1},{4,6},{5,7},{6,4},{7,5},{8,10},{9,11},{10,... | collective-permute-start | bytes 1572872 | tf_op jit(solution)/shard_map/ppermute | solution.py:444
  62.5 21.6 %collective-permute-start.5 = (f32[256,512]{1,0:T(8,128)S(1)}, f32[256,512]{1,0:T(8,128)S(1)}, u32[]{:S(2)}, u32[]{:S(2)}) collective-permute-start(f32[256,512]{1,0:T(8,128)S(1)} %pad_maximum_fusion.1.y0_ref), channel_id=1, source_target_pairs={{0,3},{1,0},{2,1},{3,2},{4,7},{5,4},{6,5},{7,6},{8,11},{9,8},{10,9... | collective-permute-start | bytes 1572872 | tf_op jit(solution)/shard_map/ppermute | solution.py:444
  63.1 60.4 %collective-permute-start.12 = (f32[512,512]{1,0:T(8,128)S(1)}, f32[512,512]{1,0:T(8,128)S(1)}, u32[]{:S(2)}, u32[]{:S(2)}) collective-permute-start(f32[512,512]{1,0:T(8,128)S(1)} %constant_dynamic-update-slice_fusion.near_ref), channel_id=1, source_target_pairs={{8,12},{9,13},{10,14},{11,15},{12,8},{13,9},{14,10},{15,11},{24,28... | collective-permute-start | bytes 3145736 | tf_op jit(solution)/shard_map/ppermute | solution.py:448
  63.9 39.4 %collective-permute-start.16 = (f32[128,512]{1,0:T(8,128)S(1)}, f32[128,512]{1,0:T(8,128)S(1)}, u32[]{:S(2)}, u32[]{:S(2)}) collective-permute-start(f32[128,512]{1,0:T(8,128)S(1)} %select_select_fusion.p0_ref), channel_id=1, source_target_pairs={{0,1},{1,2},{2,3},{3,0},{4,5},{5,6},{6,7},{7,4},{8,9},{9,10},{10,1... | collective-permute-start | bytes 786440 | tf_op jit(solution)/shard_map/ppermute | solution.py:444
  79.1 24.9 %collective-permute-start.17 = (f32[128,512]{1,0:T(8,128)S(1)}, f32[128,512]{1,0:T(8,128)S(1)}, u32[]{:S(2)}, u32[]{:S(2)}) collective-permute-start(f32[128,512]{1,0:T(8,128)S(1)} %select_select_fusion.p0_ref), channel_id=1, source_target_pairs={{0,2},{1,3},{2,0},{3,1},{4,6},{5,7},{6,4},{7,5},{8,10},{9,11},{10,... | collective-permute-start | bytes 786440 | tf_op jit(solution)/shard_map/ppermute | solution.py:444
  79.1 25.8 %collective-permute-start.18 = (f32[128,512]{1,0:T(8,128)S(1)}, f32[128,512]{1,0:T(8,128)S(1)}, u32[]{:S(2)}, u32[]{:S(2)}) collective-permute-start(f32[128,512]{1,0:T(8,128)S(1)} %select_select_fusion.p0_ref), channel_id=1, source_target_pairs={{0,3},{1,0},{2,1},{3,2},{4,7},{5,4},{6,5},{7,6},{8,11},{9,8},{10,9... | collective-permute-start | bytes 786440 | tf_op jit(solution)/shard_map/ppermute | solution.py:444
  102.6 20.8 %collective-permute-start.6 = (f32[256,512]{1,0:T(8,128)S(1)}, f32[256,512]{1,0:T(8,128)S(1)}, u32[]{:S(2)}, u32[]{:S(2)}) collective-permute-start(f32[256,512]{1,0:T(8,128)S(1)} %pad_maximum_fusion.h0), channel_id=1, source_target_pairs={{8,9},{9,10},{10,11},{11,8},{12,13},{13,14},{14,15},{15,12},{24,25... | collective-permute-start | bytes 1572872 | tf_op jit(solution)/shard_map/ppermute | solution.py:444
  103.4 20.1 %collective-permute-start.7 = (f32[256,512]{1,0:T(8,128)S(1)}, f32[256,512]{1,0:T(8,128)S(1)}, u32[]{:S(2)}, u32[]{:S(2)}) collective-permute-start(f32[256,512]{1,0:T(8,128)S(1)} %pad_maximum_fusion.h0), channel_id=1, source_target_pairs={{8,10},{9,11},{10,8},{11,9},{12,14},{13,15},{14,12},{15,13},{24,26... | collective-permute-start | bytes 1572872 | tf_op jit(solution)/shard_map/ppermute | solution.py:444
  104.1 19.4 %collective-permute-start.8 = (f32[256,512]{1,0:T(8,128)S(1)}, f32[256,512]{1,0:T(8,128)S(1)}, u32[]{:S(2)}, u32[]{:S(2)}) collective-permute-start(f32[256,512]{1,0:T(8,128)S(1)} %pad_maximum_fusion.h0), channel_id=1, source_target_pairs={{8,11},{9,8},{10,9},{11,10},{12,15},{13,12},{14,13},{15,14},{24,27... | collective-permute-start | bytes 1572872 | tf_op jit(solution)/shard_map/ppermute | solution.py:444
  105.0 18.5 %copy-start.3 = (f32[128,1024]{1,0:T(8,128)S(1)}, f32[128,1024]{1,0:T(8,128)}, u32[]{:S(2)}) copy-start(f32[128,1024]{1,0:T(8,128)} %copy-done.2) | copy-start | bytes 1572868
  135.8 19.8 %collective-permute-start.19 = (f32[64,1024]{1,0:T(8,128)S(1)}, f32[64,1024]{1,0:T(8,128)S(1)}, u32[]{:S(2)}, u32[]{:S(2)}) collective-permute-start(f32[64,1024]{1,0:T(8,128)S(1)} %slice.34), channel_id=1, source_target_pairs={{8,0},{9,1},{10,2},{11,3},{12,4},{13,5},{14,6},{15,7},{24,16},{25,... | collective-permute-start | bytes 786440 | tf_op jit(solution)/shard_map/ppermute | solution.py:448

commit v6 on v5

--- a/solution.py
+++ b/solution.py
@@ -285,7 +285,7 @@
     ypos = lax.rem(me, 4)
     for d, ref in enumerate((p0_ref, p1_ref, p2_ref, p3_ref)):
         rows = pl.ds(pl.multiple_of(lax.rem(ypos + 4 - d, 4) * B, B), B)
-        a_ref[rows, :] = ref[...]
+        a_ref[rows, :] = ref[:B, :]
     for ref, src in ((vh, vh0), (vl, vl0)):
         ref[:, :HALF] = src[HALF:, :]
         ref[:, HALF:] = jnp.zeros((ref.shape[0], HALF), BF16)
@@ -348,22 +348,18 @@
     )(index, *parts, *state, rhs)
 
 
-def third_kernel(idx_ref, h0, h1, h2, h3, near_ref, far_ref, lh, ll, t_ref, dinv_ref, y_ref, own_ref, tail_ref, b_ref,
+def third_kernel(idx_ref, nf_ref, nl_ref, ff_ref, fl_ref, lh, ll, t_ref, dinv_ref, y_ref, own_ref, tail_ref, b_ref,
                  fac_ref, eli_ref, a21, xh, xl, x32, wh, wl, sem):
     me = idx_ref[0]
     nrhs, order = b_ref.shape
     low = order - PIV
     ypos, zpos = lax.rem(me, 4), jnp.clip(me // 4 - 2, 0, 1)
     copies = []
-    for d, ref in enumerate((h0, h1, h2, h3)):
-        spot = lax.rem(ypos + 4 - d, 4)
-        for n, z in enumerate((zpos, 1 - zpos)):
-            rows = pl.ds(pl.multiple_of((4 * z + spot) * B, B), B)
-            src = (near_ref, far_ref)[n]
+    for n, (ref, z, c) in enumerate(((nf_ref, zpos, 0), (ff_ref, 1 - zpos, 0), (nl_ref, zpos, HALF), (fl_ref, 1 - zpos, HALF))):
+        for d in range(4):
+            rows = pl.ds(pl.multiple_of((4 * z + lax.rem(ypos + 4 - d, 4)) * B, B), B)
             copies.append(pltpu.make_async_copy(
-                ref.at[pl.ds(n * B, B), :], a21.at[rows, pl.ds(0, HALF)], sem.at[2 * d + n]))
-            copies.append(pltpu.make_async_copy(
-                src.at[pl.ds(d * B, B), :], a21.at[rows, pl.ds(HALF, HALF)], sem.at[8 + 2 * d + n]))
+                ref.at[pl.ds(d * B, B), :], a21.at[rows, pl.ds(c, HALF)], sem.at[4 * n + d]))
     for copy in copies:
         copy.start()
 
@@ -468,22 +464,26 @@
     tail, early, late = assemble(codes, index, arrived, front_matrix[0])
     z = lax.axis_index("front") // 4
     rhs = shot_rhs[0]
-    swap = planes(early, ((0, 1), (1, 0), (2, 3), (3, 2)))
+    swap = planes(early, ((0, 1), (1, 0)))
     side = planes(early, ((1, 2), (0, 3)))
     cross = planes(early, ((0, 2), (1, 3)))
-    near = jnp.concatenate(ring_y(late, (2, 3)), 0)
+    near_last = jnp.concatenate(ring_y(late, (2, 3)), 0)
     early_parts = ring_y(jnp.concatenate([pick(z, early, swap, cross, side), pick(z, swap, early, side, cross)], 0))
-    late_x, _ = lax.optimization_barrier((late, (swap, side, cross)))
+    late_x, _ = lax.optimization_barrier((late, (swap, side, cross, near_last)))
     to0, to2, to3 = (planes(late_x, ((1, d),)) for d in (0, 2, 3))
-    late_parts = ring_y(pick(z, to0, late_x, to2, to3))
-    far = planes(near, ((2, 3), (3, 2)))
+    far_last = planes(near_last, ((2, 3), (3, 2)))
+    mixed = jnp.concatenate([pick(z, to0, late_x, to2, to3), early], 0)
+    mixed, _ = lax.optimization_barrier((mixed, early_parts))
+    late_parts = ring_y(mixed)
     state = first(index, early_parts, rhs)
-    pair, _ = lax.optimization_barrier((jnp.concatenate([early, swap], 0), state[6]))
-    below = ring_y(pair, (2, 3))
+    near_first = jnp.concatenate([part[B:] for part in late_parts], 0)
+    near_first, _ = lax.optimization_barrier((near_first, state[6]))
+    far_first = planes(near_first, ((2, 3), (3, 2)))
     state = second(index, late_parts, state, rhs)
-    factored, eliminated = third(index, below + [near, far], state, tail, rhs)
+    lower = [near_first, near_last, far_first, far_last]
+    factored, eliminated = third(index, lower, state, tail, rhs)
     tail = eliminated[:, PIV:]
-    tail = jnp.where(z < 2, planes(tail, ((2, 0), (3, 1))), tail)
+    tail = jnp.where(z < 2, planes(tail, ((2, 1), (3, 0))), tail)
     eliminated = jnp.concatenate([eliminated[:, :PIV], tail], 1)
     return factored[None], eliminated[None]
 

time: 159 us -> 161 us (1.013); the launches traced: 156 us -> 160 us
  starting transfers between devices: 31.8 us -> 41.6 us
  waiting for transfers between devices: 67 us -> 60.6 us
    ppermute x8 -> x9, waiting for transfers between devices: 31.5 us -> 22.9 us  [planes(): lax.ppermute(x, 'front', [(4 * a + y, 4 * b + y) for a, b in pairs for y...]
    ppermute x8 -> x9, starting transfers between devices: 13.4 us -> 22 us  [planes(): lax.ppermute(x, 'front', [(4 * a + y, 4 * b + y) for a, b in pairs for y...]
    ppermute x12 -> x9, waiting for transfers between devices: 13.6 us -> 15.8 us  [shift_y(): lax.ppermute(x, 'front', [(4 * z + y, 4 * z + (y + d) % 4) for z in zs fo...]
    ppermute x12 -> x9, starting transfers between devices: 14 us -> 15.2 us  [shift_y(): lax.ppermute(x, 'front', [(4 * z + y, 4 * z + (y + d) % 4) for z in zs fo...]
  transfers between devices with their start and end apart: 21 -> 19, of which waited for: 6 -> 7; matrix products, arithmetic and copies ran while one was open for 0% -> 0% of each run, Pallas kernels for 24% -> 23%
where the time goes in v6:
time: 161 us; the launch traced here: 160 us
  waiting for transfers between devices  60.6 us (38%)
  Pallas kernels  50.4 us (31%)
  starting transfers between devices  41.6 us (26%)
  other arithmetic  4.67 us (3%)
  local copies, waits for them, and re-layouts  1.73 us (1%)
    ppermute x9, waiting for transfers between devices, planes(): lax.ppermute(x, 'front', [(4 * a + y, 4 * b + y) for a, b in pairs for y...  22.9 us
    ppermute x9, starting transfers between devices, planes(): lax.ppermute(x, 'front', [(4 * a + y, 4 * b + y) for a, b in pairs for y...  22 us
    all_to_all x1, waiting for transfers between devices, local(): lax.all_to_all(payload, 'leaf', split_axis=0, concat_axis=0, tiled=True)  21.9 us
    pallas_call x1, Pallas kernels, first(): pl.pallas_call(first_kernel, out_shape=tuple((jax.ShapeDtypeStruct(*o) fo...  18.5 us
    pallas_call x1, Pallas kernels, second(): pl.pallas_call(second_kernel, out_shape=tuple((jax.ShapeDtypeStruct(*o) f...  18.5 us
    ppermute x9, waiting for transfers between devices, shift_y(): lax.ppermute(x, 'front', [(4 * z + y, 4 * z + (y + d) % 4) for z in zs fo...  15.8 us
    ppermute x9, starting transfers between devices, shift_y(): lax.ppermute(x, 'front', [(4 * z + y, 4 * z + (y + d) % 4) for z in zs fo...  15.2 us
    pallas_call x1, Pallas kernels, third(): pl.pallas_call(third_kernel, out_shape=(jax.ShapeDtypeStruct((B, order),...  12.2 us
  transfers between devices with their start and end apart: 19, of which 7 were waited for; matrix products, arithmetic and copies ran while one was open for 0% of the time, Pallas kernels for 23%

profile of v6, /device:TPU:8, one launch (start us, length us, event | category | flops | bytes accessed | tf_op | source)
XLA Modules:
  0.0 160.1 jit_solution(17402367246897909781)
XLA Ops:
  0.6 0.8 copy.10
  1.4 0.7 fusion
  2.1 2.7 %select_maximum_fusion = f32[8,392,128]{2,1,0:T(8,128)} fusion(f32[8,1,3]{2,1,0:T(1,128)S(1)} %fusion, f32[8,384,128]{2,1,0:T(8,128)} %bitcast.15), kind=kLoop, calls=%fused_computation | loop fusion | flops 1204224 | bytes 3178592 | tf_op jit(solution)/shard_map/concatenate | solution.py:460
  4.8 4.4 %all-to-all-start = ((f32[8,392,128]{2,1,0:T(8,128)}), f32[8,392,128]{2,1,0:T(8,128)S(1)}, u32[]{:S(2)}, u32[]{:S(2)}) async-start(f32[8,392,128]{2,1,0:T(8,128)} %select_maximum_fusion), calls=%async_computation | async-start | bytes 3211264 | tf_op jit(solution)/shard_map/all_to_all | solution.py:461
  9.3 21.9 %all-to-all-done.recv_ref = f32[8,392,128]{2,1,0:T(8,128)S(1)} async-done(((f32[8,392,128]{2,1,0:T(8,128)}), f32[8,392,128]{2,1,0:T(8,128)S(1)}, u32[]{:S(2)}, u32[]{:S(2)}) %all-to-all-start) | async-done | bytes 1605664 | tf_op jit(solution)/shard_map/all_to_all | solution.py:461
  31.2 1.1 assemble.1
  32.4 0.0 copy-start.2
  32.4 0.8 copy-done.2
  33.2 0.7 collective-permute-start.3
  33.8 0.7 collective-permute-start.4
  34.5 3.9 %collective-permute-start = (f32[128,512]{1,0:T(8,128)S(1)}, f32[128,512]{1,0:T(8,128)S(1)}, u32[]{:S(2)}, u32[]{:S(2)}) collective-permute-start(f32[128,512]{1,0:T(8,128)S(1)} %get-tuple-element.37), channel_id=1, source_target_pairs={{0,4},{1,5},{2,6},{3,7},{4,0},{5,1},{6,2},{7,3},{16,20},{17,21},{1... | collective-permute-start | bytes 786440 | tf_op jit(solution)/shard_map/ppermute | solution.py:444
  38.4 7.8 %collective-permute-start.1 = (f32[128,512]{1,0:T(8,128)S(1)}, f32[128,512]{1,0:T(8,128)S(1)}, u32[]{:S(2)}, u32[]{:S(2)}) collective-permute-start(f32[128,512]{1,0:T(8,128)S(1)} %get-tuple-element.37), channel_id=1, source_target_pairs={{4,8},{5,9},{6,10},{7,11},{0,12},{1,13},{2,14},{3,15},{20,24},{21,... | collective-permute-start | bytes 786440 | tf_op jit(solution)/shard_map/ppermute | solution.py:444
  46.2 0.7 collective-permute-start.5
  46.9 0.0 collective-permute-done.3
  46.9 4.8 %collective-permute-start.2 = (f32[128,512]{1,0:T(8,128)S(1)}, f32[128,512]{1,0:T(8,128)S(1)}, u32[]{:S(2)}, u32[]{:S(2)}) collective-permute-start(f32[128,512]{1,0:T(8,128)S(1)} %get-tuple-element.37), channel_id=1, source_target_pairs={{0,8},{1,9},{2,10},{3,11},{4,12},{5,13},{6,14},{7,15},{16,24},{17,... | collective-permute-start | bytes 786440 | tf_op jit(solution)/shard_map/ppermute | solution.py:444
  51.8 0.0 collective-permute-done.4
  51.8 0.0 collective-permute-done.5
  51.8 0.0 collective-permute-done
  51.9 4.3 %collective-permute-done.2 = f32[128,512]{1,0:T(8,128)S(1)} collective-permute-done((f32[128,512]{1,0:T(8,128)S(1)}, f32[128,512]{1,0:T(8,128)S(1)}, u32[]{:S(2)}, u32[]{:S(2)}) %collective-permute-start.2) | collective-permute-done | bytes 262176 | tf_op jit(solution)/shard_map/ppermute | solution.py:444
  56.2 1.3 collective-permute-start.6
  57.5 0.7 collective-permute-start.7
  58.2 0.7 collective-permute-start.8
  58.8 0.1 select_select_fusion.1
  59.0 0.0 copy-start.1
  59.0 3.1 %collective-permute-start.10 = (f32[256,512]{1,0:T(8,128)S(1)}, f32[256,512]{1,0:T(8,128)S(1)}, u32[]{:S(2)}, u32[]{:S(2)}) collective-permute-start(f32[256,512]{1,0:T(8,128)S(1)} %pad_maximum_fusion.2.y0_ref), channel_id=1, source_target_pairs={{0,2},{1,3},{2,0},{3,1},{4,6},{5,7},{6,4},{7,5},{8,10},{9,11},{10,... | collective-permute-start | bytes 1572872 | tf_op jit(solution)/shard_map/ppermute | solution.py:440
  62.1 2.7 %collective-permute-start.11 = (f32[256,512]{1,0:T(8,128)S(1)}, f32[256,512]{1,0:T(8,128)S(1)}, u32[]{:S(2)}, u32[]{:S(2)}) collective-permute-start(f32[256,512]{1,0:T(8,128)S(1)} %pad_maximum_fusion.2.y0_ref), channel_id=1, source_target_pairs={{0,3},{1,0},{2,1},{3,2},{4,7},{5,4},{6,5},{7,6},{8,11},{9,8},{10,9... | collective-permute-start | bytes 1572872 | tf_op jit(solution)/shard_map/ppermute | solution.py:440
  64.8 1.1 collective-permute-done.6
  65.9 3.3 %collective-permute-start.9 = (f32[256,512]{1,0:T(8,128)S(1)}, f32[256,512]{1,0:T(8,128)S(1)}, u32[]{:S(2)}, u32[]{:S(2)}) collective-permute-start(f32[256,512]{1,0:T(8,128)S(1)} %pad_maximum_fusion.2.y0_ref), channel_id=1, source_target_pairs={{0,1},{1,2},{2,3},{3,0},{4,5},{5,6},{6,7},{7,4},{8,9},{9,10},{10,1... | collective-permute-start | bytes 1572872 | tf_op jit(solution)/shard_map/ppermute | solution.py:440
  69.2 0.7 collective-permute-start.16
  69.9 0.0 collective-permute-done.8
  69.9 0.1 select_select_fusion.2
  70.1 5.4 %collective-permute-done.10.y2_ref = f32[256,512]{1,0:T(8,128)S(1)} collective-permute-done((f32[256,512]{1,0:T(8,128)S(1)}, f32[256,512]{1,0:T(8,128)S(1)}, u32[]{:S(2)}, u32[]{:S(2)}) %collective-permute-start.10) | collective-permute-done | bytes 524320 | tf_op jit(solution)/shard_map/ppermute | solution.py:440
  75.5 7.4 %collective-permute-done.11.y3_ref = f32[256,512]{1,0:T(8,128)S(1)} collective-permute-done((f32[256,512]{1,0:T(8,128)S(1)}, f32[256,512]{1,0:T(8,128)S(1)}, u32[]{:S(2)}, u32[]{:S(2)}) %collective-permute-start.11) | collective-permute-done | bytes 524320 | tf_op jit(solution)/shard_map/ppermute | solution.py:440
  82.8 0.0 collective-permute-done.9.y1_ref
  82.8 1.3 collective-permute-start.12
  84.1 2.9 %collective-permute-start.13 = (f32[256,512]{1,0:T(8,128)S(1)}, f32[256,512]{1,0:T(8,128)S(1)}, u32[]{:S(2)}, u32[]{:S(2)}) collective-permute-start(f32[256,512]{1,0:T(8,128)S(1)} %pad_maximum_fusion.1.p0_ref), channel_id=1, source_target_pairs={{0,2},{1,3},{2,0},{3,1},{4,6},{5,7},{6,4},{7,5},{8,10},{9,11},{10,... | collective-permute-start | bytes 1572872 | tf_op jit(solution)/shard_map/ppermute | solution.py:440
  87.0 0.0 collective-permute-start.14
  87.0 18.5 %first.1 = (bf16[1088,512]{1,0:T(8,128)(2,1)S(1)}, bf16[1088,512]{1,0:T(8,128)(2,1)S(1)}, bf16[1024,512]{1,0:T(8,128)(2,1)S(1)}, bf16[1024,512]{1,0:T(8,128)(2,1...) custom-call(s32[1]{0:T(128)} %bitcast.idx_ref, ...), custom_call_target="tpu_custom_call" | custom-call | flops 20000000000 | bytes 20000000 | tf_op jit(solution)/shard_map/first/pallas_call | solution.py:260
  105.5 0.0 collective-permute-done.12.p1_ref
  105.6 3.0 %collective-permute-done.14.p3_ref = f32[256,512]{1,0:T(8,128)S(1)} collective-permute-done((f32[256,512]{1,0:T(8,128)S(1)}, f32[256,512]{1,0:T(8,128)S(1)}, u32[]{:S(2)}, u32[]{:S(2)}) %collective-permute-start.14) | collective-permute-done | bytes 524320 | tf_op jit(solution)/shard_map/ppermute | solution.py:440
  108.6 0.1 pad_maximum_fusion.nf_ref
  108.7 0.9 collective-permute-start.15
  109.6 0.0 copy-start.3
  109.7 18.5 %second.1 = (bf16[1024,1024]{1,0:T(8,128)(2,1)S(1)}, bf16[1024,1024]{1,0:T(8,128)(2,1)S(1)}, f32[8,128,128]{2,1,0:T(8,128)S(1)}, f32[8,1024]{1,0:T(8,128)S(1)}, ...) custom-call(s32[1]{0:T(128)} %bitcast.idx_ref, f32[256,512]{1,0:T(8,128)S(1)} %pad_maximum_fusion.1.p0_ref, ...), custom_call_target="tpu_custom_call" | custom-call | flops 20000000000 | bytes 20000000 | tf_op jit(solution)/shard_map/second/pallas_call | solution.py:329
  128.2 12.2 %third.1 = (f32[128,2048]{1,0:T(8,128)}, f32[64,2048]{1,0:T(8,128)S(1)}) custom-call(s32[1]{0:T(128)} %bitcast.idx_ref, f32[512,512]{1,0:T(8,128)S(1)} %pad_maximum_fusion.nf_ref, f32[512,512]{1,0:T(8,128)S(1)} %constant_dynamic-update-slice_fusion.nl_ref, f32[512,512]{1,0:T(8,128)S(1)} %collective-permute-done.15.ff_ref, ...), custom_call_target="tpu_custom_call" | custom-call | tf_op jit(solution)/shard_map/third/pallas_call | solution.py:417
  140.5 1.3 collective-permute-start.17
  141.8 17.4 %collective-permute-done.17 = f32[64,1024]{1,0:T(8,128)S(1)} collective-permute-done((f32[64,1024]{1,0:T(8,128)S(1)}, f32[64,1024]{1,0:T(8,128)S(1)}, u32[]{:S(2)}, u32[]{:S(2)}) %collective-permute-start.17) | collective-permute-done | bytes 262176 | tf_op jit(solution)/shard_map/ppermute | solution.py:444
  159.2 0.8 maximum_bitcast_fusion
  (22 shorter events, 0.3 us)
Async XLA Ops:
  4.8 26.4 %copy-start = (f32[1,128,2048]{2,1,0:T(8,128)S(1)}, f32[1,128,2048]{2,1,0:T(8,128)}, u32[]{:S(2)}) copy-start(f32[1,128,2048]{2,1,0:T(8,128)} %param.7) | copy-start | bytes 3145732
  4.8 26.4 %all-to-all-start = ((f32[8,392,128]{2,1,0:T(8,128)}), f32[8,392,128]{2,1,0:T(8,128)S(1)}, u32[]{:S(2)}, u32[]{:S(2)}) async-start(f32[8,392,128]{2,1,0:T(8,128)} %select_maximum_fusion), calls=%async_computation | async-start | bytes 3211264 | tf_op jit(solution)/shard_map/all_to_all | solution.py:461
  32.4 0.8 copy-start.2
  33.2 13.7 %collective-permute-start.3 = (f32[128,512]{1,0:T(8,128)S(1)}, f32[128,512]{1,0:T(8,128)S(1)}, u32[]{:S(2)}, u32[]{:S(2)}) collective-permute-start(f32[128,512]{1,0:T(8,128)S(1)} %get-tuple-element.38), channel_id=1, source_target_pairs={{8,9},{9,10},{10,11},{11,8},{12,13},{13,14},{14,15},{15,12},{24,25... | collective-permute-start | bytes 786440 | tf_op jit(solution)/shard_map/ppermute | solution.py:440
  33.8 17.9 %collective-permute-start.4 = (f32[128,512]{1,0:T(8,128)S(1)}, f32[128,512]{1,0:T(8,128)S(1)}, u32[]{:S(2)}, u32[]{:S(2)}) collective-permute-start(f32[128,512]{1,0:T(8,128)S(1)} %get-tuple-element.38), channel_id=1, source_target_pairs={{8,10},{9,11},{10,8},{11,9},{12,14},{13,15},{14,12},{15,13},{24,26... | collective-permute-start | bytes 786440 | tf_op jit(solution)/shard_map/ppermute | solution.py:440
  34.5 17.3 %collective-permute-start = (f32[128,512]{1,0:T(8,128)S(1)}, f32[128,512]{1,0:T(8,128)S(1)}, u32[]{:S(2)}, u32[]{:S(2)}) collective-permute-start(f32[128,512]{1,0:T(8,128)S(1)} %get-tuple-element.37), channel_id=1, source_target_pairs={{0,4},{1,5},{2,6},{3,7},{4,0},{5,1},{6,2},{7,3},{16,20},{17,21},{1... | collective-permute-start | bytes 786440 | tf_op jit(solution)/shard_map/ppermute | solution.py:444
  38.4 13.4 %collective-permute-start.1 = (f32[128,512]{1,0:T(8,128)S(1)}, f32[128,512]{1,0:T(8,128)S(1)}, u32[]{:S(2)}, u32[]{:S(2)}) collective-permute-start(f32[128,512]{1,0:T(8,128)S(1)} %get-tuple-element.37), channel_id=1, source_target_pairs={{4,8},{5,9},{6,10},{7,11},{0,12},{1,13},{2,14},{3,15},{20,24},{21,... | collective-permute-start | bytes 786440 | tf_op jit(solution)/shard_map/ppermute | solution.py:444
  46.2 5.6 %collective-permute-start.5 = (f32[128,512]{1,0:T(8,128)S(1)}, f32[128,512]{1,0:T(8,128)S(1)}, u32[]{:S(2)}, u32[]{:S(2)}) collective-permute-start(f32[128,512]{1,0:T(8,128)S(1)} %get-tuple-element.38), channel_id=1, source_target_pairs={{8,11},{9,8},{10,9},{11,10},{12,15},{13,12},{14,13},{15,14},{24,27... | collective-permute-start | bytes 786440 | tf_op jit(solution)/shard_map/ppermute | solution.py:440
  46.9 9.3 %collective-permute-start.2 = (f32[128,512]{1,0:T(8,128)S(1)}, f32[128,512]{1,0:T(8,128)S(1)}, u32[]{:S(2)}, u32[]{:S(2)}) collective-permute-start(f32[128,512]{1,0:T(8,128)S(1)} %get-tuple-element.37), channel_id=1, source_target_pairs={{0,8},{1,9},{2,10},{3,11},{4,12},{5,13},{6,14},{7,15},{16,24},{17,... | collective-permute-start | bytes 786440 | tf_op jit(solution)/shard_map/ppermute | solution.py:444
  56.2 9.7 %collective-permute-start.6 = (f32[128,512]{1,0:T(8,128)S(1)}, f32[128,512]{1,0:T(8,128)S(1)}, u32[]{:S(2)}, u32[]{:S(2)}) collective-permute-start(f32[128,512]{1,0:T(8,128)S(1)} %get-tuple-element.38), channel_id=1, source_target_pairs={{4,0},{5,1},{6,2},{7,3},{20,16},{21,17},{22,18},{23,19},{36,32},{3... | collective-permute-start | bytes 786440 | tf_op jit(solution)/shard_map/ppermute | solution.py:444
  57.5 11.7 %collective-permute-start.7 = (f32[128,512]{1,0:T(8,128)S(1)}, f32[128,512]{1,0:T(8,128)S(1)}, u32[]{:S(2)}, u32[]{:S(2)}) collective-permute-start(f32[128,512]{1,0:T(8,128)S(1)} %get-tuple-element.38), channel_id=1, source_target_pairs={{4,8},{5,9},{6,10},{7,11},{20,24},{21,25},{22,26},{23,27},{36,40},... | collective-permute-start | bytes 786440 | tf_op jit(solution)/shard_map/ppermute | solution.py:444
  58.2 11.8 %collective-permute-start.8 = (f32[128,512]{1,0:T(8,128)S(1)}, f32[128,512]{1,0:T(8,128)S(1)}, u32[]{:S(2)}, u32[]{:S(2)}) collective-permute-start(f32[128,512]{1,0:T(8,128)S(1)} %get-tuple-element.38), channel_id=1, source_target_pairs={{4,12},{5,13},{6,14},{7,15},{20,28},{21,29},{22,30},{23,31},{36,44... | collective-permute-start | bytes 786440 | tf_op jit(solution)/shard_map/ppermute | solution.py:444
  59.0 28.0 %copy-start.1 = (f32[1,64,2048]{2,1,0:T(8,128)S(1)}, f32[1,64,2048]{2,1,0:T(8,128)}, u32[]{:S(2)}) copy-start(f32[1,64,2048]{2,1,0:T(8,128)} %param.11) | copy-start | bytes 1572868
  59.0 16.4 %collective-permute-start.10 = (f32[256,512]{1,0:T(8,128)S(1)}, f32[256,512]{1,0:T(8,128)S(1)}, u32[]{:S(2)}, u32[]{:S(2)}) collective-permute-start(f32[256,512]{1,0:T(8,128)S(1)} %pad_maximum_fusion.2.y0_ref), channel_id=1, source_target_pairs={{0,2},{1,3},{2,0},{3,1},{4,6},{5,7},{6,4},{7,5},{8,10},{9,11},{10,... | collective-permute-start | bytes 1572872 | tf_op jit(solution)/shard_map/ppermute | solution.py:440
  62.1 20.7 %collective-permute-start.11 = (f32[256,512]{1,0:T(8,128)S(1)}, f32[256,512]{1,0:T(8,128)S(1)}, u32[]{:S(2)}, u32[]{:S(2)}) collective-permute-start(f32[256,512]{1,0:T(8,128)S(1)} %pad_maximum_fusion.2.y0_ref), channel_id=1, source_target_pairs={{0,3},{1,0},{2,1},{3,2},{4,7},{5,4},{6,5},{7,6},{8,11},{9,8},{10,9... | collective-permute-start | bytes 1572872 | tf_op jit(solution)/shard_map/ppermute | solution.py:440
  65.9 16.9 %collective-permute-start.9 = (f32[256,512]{1,0:T(8,128)S(1)}, f32[256,512]{1,0:T(8,128)S(1)}, u32[]{:S(2)}, u32[]{:S(2)}) collective-permute-start(f32[256,512]{1,0:T(8,128)S(1)} %pad_maximum_fusion.2.y0_ref), channel_id=1, source_target_pairs={{0,1},{1,2},{2,3},{3,0},{4,5},{5,6},{6,7},{7,4},{8,9},{9,10},{10,1... | collective-permute-start | bytes 1572872 | tf_op jit(solution)/shard_map/ppermute | solution.py:440
  69.2 59.0 %collective-permute-start.16 = (f32[512,512]{1,0:T(8,128)S(1)}, f32[512,512]{1,0:T(8,128)S(1)}, u32[]{:S(2)}, u32[]{:S(2)}) collective-permute-start(f32[512,512]{1,0:T(8,128)S(1)} %constant_dynamic-update-slice_fusion.nl_ref), channel_id=1, source_target_pairs={{8,12},{9,13},{10,14},{11,15},{12,8},{13,9},{14,10},{15,11},{24,28... | collective-permute-start | bytes 3145736 | tf_op jit(solution)/shard_map/ppermute | solution.py:444
  82.8 22.7 %collective-permute-start.12 = (f32[256,512]{1,0:T(8,128)S(1)}, f32[256,512]{1,0:T(8,128)S(1)}, u32[]{:S(2)}, u32[]{:S(2)}) collective-permute-start(f32[256,512]{1,0:T(8,128)S(1)} %pad_maximum_fusion.1.p0_ref), channel_id=1, source_target_pairs={{0,1},{1,2},{2,3},{3,0},{4,5},{5,6},{6,7},{7,4},{8,9},{9,10},{10,1... | collective-permute-start | bytes 1572872 | tf_op jit(solution)/shard_map/ppermute | solution.py:440
  84.1 21.5 %collective-permute-start.13 = (f32[256,512]{1,0:T(8,128)S(1)}, f32[256,512]{1,0:T(8,128)S(1)}, u32[]{:S(2)}, u32[]{:S(2)}) collective-permute-start(f32[256,512]{1,0:T(8,128)S(1)} %pad_maximum_fusion.1.p0_ref), channel_id=1, source_target_pairs={{0,2},{1,3},{2,0},{3,1},{4,6},{5,7},{6,4},{7,5},{8,10},{9,11},{10,... | collective-permute-start | bytes 1572872 | tf_op jit(solution)/shard_map/ppermute | solution.py:440
  87.0 21.7 %collective-permute-start.14 = (f32[256,512]{1,0:T(8,128)S(1)}, f32[256,512]{1,0:T(8,128)S(1)}, u32[]{:S(2)}, u32[]{:S(2)}) collective-permute-start(f32[256,512]{1,0:T(8,128)S(1)} %pad_maximum_fusion.1.p0_ref), channel_id=1, source_target_pairs={{0,3},{1,0},{2,1},{3,2},{4,7},{5,4},{6,5},{7,6},{8,11},{9,8},{10,9... | collective-permute-start | bytes 1572872 | tf_op jit(solution)/shard_map/ppermute | solution.py:440
  108.7 19.4 %collective-permute-start.15 = (f32[512,512]{1,0:T(8,128)S(1)}, f32[512,512]{1,0:T(8,128)S(1)}, u32[]{:S(2)}, u32[]{:S(2)}) collective-permute-start(f32[512,512]{1,0:T(8,128)S(1)} %pad_maximum_fusion.nf_ref), channel_id=1, source_target_pairs={{8,12},{9,13},{10,14},{11,15},{12,8},{13,9},{14,10},{15,11},{24,28... | collective-permute-start | bytes 3145736 | tf_op jit(solution)/shard_map/ppermute | solution.py:444
  109.6 18.5 %copy-start.3 = (f32[128,1024]{1,0:T(8,128)S(1)}, f32[128,1024]{1,0:T(8,128)}, u32[]{:S(2)}) copy-start(f32[128,1024]{1,0:T(8,128)} %copy-done.2) | copy-start | bytes 1572868
  140.5 18.7 %collective-permute-start.17 = (f32[64,1024]{1,0:T(8,128)S(1)}, f32[64,1024]{1,0:T(8,128)S(1)}, u32[]{:S(2)}, u32[]{:S(2)}) collective-permute-start(f32[64,1024]{1,0:T(8,128)S(1)} %slice.50), channel_id=1, source_target_pairs={{8,4},{9,5},{10,6},{11,7},{12,0},{13,1},{14,2},{15,3},{24,20},{25,... | collective-permute-start | bytes 786440 | tf_op jit(solution)/shard_map/ppermute | solution.py:444

commit v7 on v5

--- a/solution.py
+++ b/solution.py
@@ -34,6 +34,31 @@
 
 def dot3_n(ah, al, bh, bl):
     return dot_n(ah, bh) + dot_n(al, bh) + dot_n(ah, bl)
+
+
+def pack_kernel(target_ref, count_ref, blocks_ref, out_ref):
+    leaves, slots = target_ref.shape[1:]
+    spot = lax.broadcasted_iota(jnp.int32, (8, B), 1)
+    out_ref[:, : slots * B, :] = blocks_ref[...]
+    for s in range(leaves):
+        codes = jnp.full((8, B), -1, jnp.int32)
+        for j in range(slots):
+            code = jnp.where(j < count_ref[0, s], target_ref[0, s, j], -1)
+            codes = jnp.where(spot == j, code, codes)
+        out_ref[s, slots * B :, :] = codes.astype(F32)
+
+
+def pack(target, count, blocks):
+    leaves, slots = target.shape[1:]
+    smem, vmem = pl.BlockSpec(memory_space=pltpu.SMEM), pl.BlockSpec(memory_space=pltpu.VMEM)
+    return pl.pallas_call(
+        pack_kernel,
+        out_shape=jax.ShapeDtypeStruct((leaves, slots * B + 8, B), F32),
+        in_specs=[smem, smem, vmem],
+        out_specs=vmem,
+        compiler_params=pltpu.CompilerParams(vmem_limit_bytes=8 * 1024 * 1024),
+        name="pack",
+    )(target, count, blocks.reshape(leaves, slots * B, B))
 
 
 def assemble_kernel(code_ref, idx_ref, recv_ref, front_ref, tail_ref, early_ref, late_ref, out_ref):
@@ -394,12 +419,14 @@
     yh, yl = split(y)
     eli_ref[:, :PIV] = y
     mine = pl.ds(pl.multiple_of(jnp.maximum(me - NP, 0) * B, B), B)
+    n = B + nrhs
     qh = jnp.concatenate([xh[mine, :], yh], 0)
-    ql = jnp.concatenate([xl[mine, :], yl], 0)
+    both = jnp.concatenate([qh, xl[mine, :], yl], 0)
     for c in range(low // W2):
         rows = slice(c * W2, (c + 1) * W2)
         dst = slice(PIV + c * W2, PIV + (c + 1) * W2)
-        prod = dot3_t(qh, ql, wh[rows, :], wl[rows, :])
+        prod = dot_t(both, wh[rows, :])
+        prod = prod[:n] + prod[n:] + dot_t(qh, wl[rows, :])
         row = me * B + lax.broadcasted_iota(jnp.int32, (B, W2), 0)
         col = PIV + c * W2 + lax.broadcasted_iota(jnp.int32, (B, W2), 1)
         fac_ref[:, dst] = jnp.where(row >= col, tail_ref[:, rows] - prod[:B], 0.0)
@@ -458,10 +485,7 @@
 
 def local(front_matrix, child_blocks, child_target, child_count, shot_rhs):
     leaves, slots = child_blocks.shape[1:3]
-    slot_ids = lax.broadcasted_iota(jnp.int32, (leaves, slots), 1)
-    live_code = jnp.where(slot_ids < child_count[0][:, None], child_target[0], -1)
-    code_rows = jnp.zeros((leaves, 8, B), F32).at[:, 0, :slots].set(live_code.astype(F32))
-    payload = jnp.concatenate([child_blocks[0].reshape(leaves, slots * B, B), code_rows], axis=1)
+    payload = pack(child_target, child_count, child_blocks)
     arrived = lax.all_to_all(payload, "leaf", split_axis=0, concat_axis=0, tiled=True)
     codes = arrived[:, slots * B, :slots].astype(jnp.int32)
     index = lax.axis_index("front").astype(jnp.int32).reshape(1)
@@ -483,7 +507,7 @@
     state = second(index, late_parts, state, rhs)
     factored, eliminated = third(index, below + [near, far], state, tail, rhs)
     tail = eliminated[:, PIV:]
-    tail = jnp.where(z < 2, planes(tail, ((2, 0), (3, 1))), tail)
+    tail = jnp.where(z < 2, planes(tail, ((2, 1), (3, 0))), tail)
     eliminated = jnp.concatenate([eliminated[:, :PIV], tail], 1)
     return factored[None], eliminated[None]
 

time: 159 us -> 157 us (0.987)
  other arithmetic: 4.58 us -> 1.16 us
  local copies, waits for them, and re-layouts: 1.66 us -> 3.72 us
    unnamed x11 -> x16, local copies, waits for them, and re-layouts: 0.86 us -> 3.68 us
    concatenate x1 -> x0, other arithmetic: 2.71 us -> none  [local(): jnp.concatenate([child_blocks[0].reshape(leaves, slots * B, B), code_rows...]
    pallas_call x0 -> x1, Pallas kernels: none -> 1.89 us  [pack(): pl.pallas_call(pack_kernel, out_shape=jax.ShapeDtypeStruct((leaves, slots...]
where the time goes in v7:
time: 157 us; the launch traced here: 156 us
  waiting for transfers between devices  66.5 us (42%)
  Pallas kernels  51.8 us (33%)
  starting transfers between devices  31.8 us (20%)
  local copies, waits for them, and re-layouts  3.72 us (2%)
    ppermute x8, waiting for transfers between devices, planes(): lax.ppermute(x, 'front', [(4 * a + y, 4 * b + y) for a, b in pairs for y...  30.9 us
    all_to_all x1, waiting for transfers between devices, local(): lax.all_to_all(payload, 'leaf', split_axis=0, concat_axis=0, tiled=True)  21.9 us
    pallas_call x1, Pallas kernels, first(): pl.pallas_call(first_kernel, out_shape=tuple((jax.ShapeDtypeStruct(*o) fo...  18.9 us
    pallas_call x1, Pallas kernels, second(): pl.pallas_call(second_kernel, out_shape=tuple((jax.ShapeDtypeStruct(*o) f...  18.3 us
    ppermute x12, starting transfers between devices, shift_y(): lax.ppermute(x, 'front', [(4 * z + y, 4 * z + (y + d) % 4) for z in zs fo...  14 us
    ppermute x12, waiting for transfers between devices, shift_y(): lax.ppermute(x, 'front', [(4 * z + y, 4 * z + (y + d) % 4) for z in zs fo...  13.6 us
    ppermute x8, starting transfers between devices, planes(): lax.ppermute(x, 'front', [(4 * a + y, 4 * b + y) for a, b in pairs for y...  13.4 us
    pallas_call x1, Pallas kernels, third(): pl.pallas_call(third_kernel, out_shape=(jax.ShapeDtypeStruct((B, order),...  11.5 us
  transfers between devices with their start and end apart: 21, of which 6 were waited for; matrix products, arithmetic and copies ran while one was open for 0% of the time, Pallas kernels for 24%

profile of v7, /device:TPU:8, one launch (start us, length us, event | category | flops | bytes accessed | tf_op | source)
XLA Modules:
  0.0 156.0 jit_solution(8161355996085999734)
XLA Ops:
  0.6 0.8 copy.10.target_ref
  1.4 1.4 copy-done
  2.8 0.7 copy-done.5
  3.4 1.9 %pack.1 = f32[8,392,128]{2,1,0:T(8,128)} custom-call(s32[1,8,3]{2,1,0:T(8,128)S(1)} %copy.10.target_ref, s32[1,8]{1,0:T(1,128)S(1)} %copy-done.5, f32[8,384,128]{2,1,0:T(8,128)S(1)} %bitcast.8), custom_call_target="tpu_custom_call" | custom-call | tf_op jit(solution)/shard_map/pack/pallas_call | solution.py:54
  5.3 4.4 %all-to-all-start = ((f32[8,392,128]{2,1,0:T(8,128)}), f32[8,392,128]{2,1,0:T(8,128)S(1)}, u32[]{:S(2)}, u32[]{:S(2)}) async-start(f32[8,392,128]{2,1,0:T(8,128)} %pack.1), calls=%async_computation | async-start | bytes 3211264 | tf_op jit(solution)/shard_map/all_to_all | solution.py:489
  9.8 21.9 %all-to-all-done.recv_ref = f32[8,392,128]{2,1,0:T(8,128)S(1)} async-done(((f32[8,392,128]{2,1,0:T(8,128)}), f32[8,392,128]{2,1,0:T(8,128)S(1)}, u32[]{:S(2)}, u32[]{:S(2)}) %all-to-all-start) | async-done | bytes 1605664 | tf_op jit(solution)/shard_map/all_to_all | solution.py:489
  31.7 1.2 assemble.1
  32.9 0.0 copy-start.3
  32.9 0.8 copy-done.3
  33.7 1.9 %collective-permute-start = (f32[128,512]{1,0:T(8,128)S(1)}, f32[128,512]{1,0:T(8,128)S(1)}, u32[]{:S(2)}, u32[]{:S(2)}) collective-permute-start(f32[128,512]{1,0:T(8,128)S(1)} %get-tuple-element.23), channel_id=1, source_target_pairs={{0,4},{1,5},{2,6},{3,7},{4,0},{5,1},{6,2},{7,3},{8,12},{9,13},{10,... | collective-permute-start | bytes 786440 | tf_op jit(solution)/shard_map/ppermute | solution.py:475
  35.6 5.5 %collective-permute-start.1 = (f32[128,512]{1,0:T(8,128)S(1)}, f32[128,512]{1,0:T(8,128)S(1)}, u32[]{:S(2)}, u32[]{:S(2)}) collective-permute-start(f32[128,512]{1,0:T(8,128)S(1)} %get-tuple-element.23), channel_id=1, source_target_pairs={{0,8},{1,9},{2,10},{3,11},{4,12},{5,13},{6,14},{7,15},{16,24},{17,... | collective-permute-start | bytes 786440 | tf_op jit(solution)/shard_map/ppermute | solution.py:475
  41.1 1.3 collective-permute-start.2
  42.4 0.7 collective-permute-start.9
  43.1 0.7 collective-permute-start.10
  43.9 0.7 collective-permute-start.11
  44.5 2.1 %collective-permute-done.1 = f32[128,512]{1,0:T(8,128)S(1)} collective-permute-done((f32[128,512]{1,0:T(8,128)S(1)}, f32[128,512]{1,0:T(8,128)S(1)}, u32[]{:S(2)}, u32[]{:S(2)}) %collective-permute-start.1) | collective-permute-done | bytes 262176 | tf_op jit(solution)/shard_map/ppermute | solution.py:475
  46.6 5.3 %collective-permute-done.2 = f32[128,512]{1,0:T(8,128)S(1)} collective-permute-done((f32[128,512]{1,0:T(8,128)S(1)}, f32[128,512]{1,0:T(8,128)S(1)}, u32[]{:S(2)}, u32[]{:S(2)}) %collective-permute-start.2) | collective-permute-done | bytes 262176 | tf_op jit(solution)/shard_map/ppermute | solution.py:475
  51.9 1.3 collective-permute-start.13
  53.2 0.7 collective-permute-start.14
  53.9 0.1 select_select_fusion.2
  54.0 0.7 collective-permute-start.15
  54.8 0.0 copy-start.2
  54.8 1.7 %collective-permute-start.3 = (f32[256,512]{1,0:T(8,128)S(1)}, f32[256,512]{1,0:T(8,128)S(1)}, u32[]{:S(2)}, u32[]{:S(2)}) collective-permute-start(f32[256,512]{1,0:T(8,128)S(1)} %pad_maximum_fusion.1.y0_ref), channel_id=1, source_target_pairs={{0,1},{1,2},{2,3},{3,0},{4,5},{5,6},{6,7},{7,4},{8,9},{9,10},{10,1... | collective-permute-start | bytes 1572872 | tf_op jit(solution)/shard_map/ppermute | solution.py:471
  56.5 0.0 collective-permute-done.11
  56.5 1.0 collective-permute-start.4
  57.4 5.5 %collective-permute-done.13 = f32[128,512]{1,0:T(8,128)S(1)} collective-permute-done((f32[128,512]{1,0:T(8,128)S(1)}, f32[128,512]{1,0:T(8,128)S(1)}, u32[]{:S(2)}, u32[]{:S(2)}) %collective-permute-start.13) | collective-permute-done | bytes 262176 | tf_op jit(solution)/shard_map/ppermute | solution.py:475
  63.0 0.5 collective-permute-start.5
  63.6 0.0 collective-permute-done.14
  63.6 0.7 collective-permute-start.12
  64.3 0.1 select_select_fusion.p0_ref
  64.4 1.6 %collective-permute-start.16 = (f32[128,512]{1,0:T(8,128)S(1)}, f32[128,512]{1,0:T(8,128)S(1)}, u32[]{:S(2)}, u32[]{:S(2)}) collective-permute-start(f32[128,512]{1,0:T(8,128)S(1)} %select_select_fusion.p0_ref), channel_id=1, source_target_pairs={{0,1},{1,2},{2,3},{3,0},{4,5},{5,6},{6,7},{7,4},{8,9},{9,10},{10,1... | collective-permute-start | bytes 786440 | tf_op jit(solution)/shard_map/ppermute | solution.py:471
  66.0 13.6 %collective-permute-done.3.y1_ref = f32[256,512]{1,0:T(8,128)S(1)} collective-permute-done((f32[256,512]{1,0:T(8,128)S(1)}, f32[256,512]{1,0:T(8,128)S(1)}, u32[]{:S(2)}, u32[]{:S(2)}) %collective-permute-start.3) | collective-permute-done | bytes 524320 | tf_op jit(solution)/shard_map/ppermute | solution.py:471
  79.6 0.0 collective-permute-start.17
  79.6 4.9 %collective-permute-start.18 = (f32[128,512]{1,0:T(8,128)S(1)}, f32[128,512]{1,0:T(8,128)S(1)}, u32[]{:S(2)}, u32[]{:S(2)}) collective-permute-start(f32[128,512]{1,0:T(8,128)S(1)} %select_select_fusion.p0_ref), channel_id=1, source_target_pairs={{0,3},{1,0},{2,1},{3,2},{4,7},{5,4},{6,5},{7,6},{8,11},{9,8},{10,9... | collective-permute-start | bytes 786440 | tf_op jit(solution)/shard_map/ppermute | solution.py:471
  84.6 0.0 collective-permute-done.5.y3_ref
  84.6 18.9 %first.1 = (bf16[1088,512]{1,0:T(8,128)(2,1)S(1)}, bf16[1088,512]{1,0:T(8,128)(2,1)S(1)}, bf16[1024,512]{1,0:T(8,128)(2,1)S(1)}, bf16[1024,512]{1,0:T(8,128)(2,1...) custom-call(s32[1]{0:T(128)} %bitcast.idx_ref, ...), custom_call_target="tpu_custom_call" | custom-call | flops 20000000000 | bytes 20000000 | tf_op jit(solution)/shard_map/first/pallas_call | solution.py:285
  103.4 0.7 collective-permute-start.6
  104.1 0.0 collective-permute-done.16.p1_ref
  104.1 0.7 collective-permute-start.7
  104.9 0.9 collective-permute-start.8
  105.7 0.0 copy-start.4
  105.8 18.3 %second.1 = (bf16[1024,1024]{1,0:T(8,128)(2,1)S(1)}, bf16[1024,1024]{1,0:T(8,128)(2,1)S(1)}, f32[8,128,128]{2,1,0:T(8,128)S(1)}, f32[8,1024]{1,0:T(8,128)S(1)}, ...) custom-call(s32[1]{0:T(128)} %bitcast.idx_ref, f32[128,512]{1,0:T(8,128)S(1)} %select_select_fusion.p0_ref, ...), custom_call_target="tpu_custom_call" | custom-call | flops 20000000000 | bytes 20000000 | tf_op jit(solution)/shard_map/second/pallas_call | solution.py:354
  124.1 0.0 collective-permute-done.12.far_ref
  124.2 11.5 %third.1 = (f32[128,2048]{1,0:T(8,128)}, f32[64,2048]{1,0:T(8,128)S(1)}) custom-call(s32[1]{0:T(128)} %bitcast.idx_ref, f32[256,512]{1,0:T(8,128)S(1)} %pad_maximum_fusion.h0, f32[256,512]{1,0:T(8,128)S(1)} %collective-permute-done.6.h1, f32[256,512]{1,0:T(8,128)S(1)} %collective-permute-done.7.h2, f32[256,512]{1,0:T(8,128)S(1)} %collective-permute-done.8.h3, ...), custom_call_target="tpu_custom_call" | custom-call | tf_op jit(solution)/shard_map/third/pallas_call | solution.py:448
  135.7 1.3 collective-permute-start.19
  137.0 18.0 %collective-permute-done.19 = f32[64,1024]{1,0:T(8,128)S(1)} collective-permute-done((f32[64,1024]{1,0:T(8,128)S(1)}, f32[64,1024]{1,0:T(8,128)S(1)}, u32[]{:S(2)}, u32[]{:S(2)}) %collective-permute-start.19) | collective-permute-done | bytes 262176 | tf_op jit(solution)/shard_map/ppermute | solution.py:475
  155.1 0.1 fusion
  155.1 0.8 maximum_bitcast_fusion
  (24 shorter events, 0.2 us)
Async XLA Ops:
  1.4 1.4 copy-start
  2.8 0.7 copy-start.5
  5.3 26.4 %copy-start.1 = (f32[1,128,2048]{2,1,0:T(8,128)S(1)}, f32[1,128,2048]{2,1,0:T(8,128)}, u32[]{:S(2)}) copy-start(f32[1,128,2048]{2,1,0:T(8,128)} %param.5) | copy-start | bytes 3145732
  5.3 26.4 %all-to-all-start = ((f32[8,392,128]{2,1,0:T(8,128)}), f32[8,392,128]{2,1,0:T(8,128)S(1)}, u32[]{:S(2)}, u32[]{:S(2)}) async-start(f32[8,392,128]{2,1,0:T(8,128)} %pack.1), calls=%async_computation | async-start | bytes 3211264 | tf_op jit(solution)/shard_map/all_to_all | solution.py:489
  32.9 0.8 copy-start.3
  33.7 10.2 %collective-permute-start = (f32[128,512]{1,0:T(8,128)S(1)}, f32[128,512]{1,0:T(8,128)S(1)}, u32[]{:S(2)}, u32[]{:S(2)}) collective-permute-start(f32[128,512]{1,0:T(8,128)S(1)} %get-tuple-element.23), channel_id=1, source_target_pairs={{0,4},{1,5},{2,6},{3,7},{4,0},{5,1},{6,2},{7,3},{8,12},{9,13},{10,... | collective-permute-start | bytes 786440 | tf_op jit(solution)/shard_map/ppermute | solution.py:475
  35.6 11.0 %collective-permute-start.1 = (f32[128,512]{1,0:T(8,128)S(1)}, f32[128,512]{1,0:T(8,128)S(1)}, u32[]{:S(2)}, u32[]{:S(2)}) collective-permute-start(f32[128,512]{1,0:T(8,128)S(1)} %get-tuple-element.23), channel_id=1, source_target_pairs={{0,8},{1,9},{2,10},{3,11},{4,12},{5,13},{6,14},{7,15},{16,24},{17,... | collective-permute-start | bytes 786440 | tf_op jit(solution)/shard_map/ppermute | solution.py:475
  41.1 10.8 %collective-permute-start.2 = (f32[128,512]{1,0:T(8,128)S(1)}, f32[128,512]{1,0:T(8,128)S(1)}, u32[]{:S(2)}, u32[]{:S(2)}) collective-permute-start(f32[128,512]{1,0:T(8,128)S(1)} %get-tuple-element.23), channel_id=1, source_target_pairs={{4,8},{5,9},{6,10},{7,11},{0,12},{1,13},{2,14},{3,15},{20,24},{21,... | collective-permute-start | bytes 786440 | tf_op jit(solution)/shard_map/ppermute | solution.py:475
  42.4 11.6 %collective-permute-start.9 = (f32[128,512]{1,0:T(8,128)S(1)}, f32[128,512]{1,0:T(8,128)S(1)}, u32[]{:S(2)}, u32[]{:S(2)}) collective-permute-start(f32[128,512]{1,0:T(8,128)S(1)} %get-tuple-element.27), channel_id=1, source_target_pairs={{8,9},{9,10},{10,11},{11,8},{12,13},{13,14},{14,15},{15,12},{24,25... | collective-permute-start | bytes 786440 | tf_op jit(solution)/shard_map/ppermute | solution.py:471
  43.1 11.6 %collective-permute-start.10 = (f32[128,512]{1,0:T(8,128)S(1)}, f32[128,512]{1,0:T(8,128)S(1)}, u32[]{:S(2)}, u32[]{:S(2)}) collective-permute-start(f32[128,512]{1,0:T(8,128)S(1)} %get-tuple-element.27), channel_id=1, source_target_pairs={{8,10},{9,11},{10,8},{11,9},{12,14},{13,15},{14,12},{15,13},{24,26... | collective-permute-start | bytes 786440 | tf_op jit(solution)/shard_map/ppermute | solution.py:471
  43.9 12.6 %collective-permute-start.11 = (f32[128,512]{1,0:T(8,128)S(1)}, f32[128,512]{1,0:T(8,128)S(1)}, u32[]{:S(2)}, u32[]{:S(2)}) collective-permute-start(f32[128,512]{1,0:T(8,128)S(1)} %get-tuple-element.27), channel_id=1, source_target_pairs={{8,11},{9,8},{10,9},{11,10},{12,15},{13,12},{14,13},{15,14},{24,27... | collective-permute-start | bytes 786440 | tf_op jit(solution)/shard_map/ppermute | solution.py:471
  51.9 11.0 %collective-permute-start.13 = (f32[128,512]{1,0:T(8,128)S(1)}, f32[128,512]{1,0:T(8,128)S(1)}, u32[]{:S(2)}, u32[]{:S(2)}) collective-permute-start(f32[128,512]{1,0:T(8,128)S(1)} %get-tuple-element.27), channel_id=1, source_target_pairs={{4,0},{5,1},{6,2},{7,3},{20,16},{21,17},{22,18},{23,19},{36,32},{3... | collective-permute-start | bytes 786440 | tf_op jit(solution)/shard_map/ppermute | solution.py:475
  53.2 10.4 %collective-permute-start.14 = (f32[128,512]{1,0:T(8,128)S(1)}, f32[128,512]{1,0:T(8,128)S(1)}, u32[]{:S(2)}, u32[]{:S(2)}) collective-permute-start(f32[128,512]{1,0:T(8,128)S(1)} %get-tuple-element.27), channel_id=1, source_target_pairs={{4,8},{5,9},{6,10},{7,11},{20,24},{21,25},{22,26},{23,27},{36,40},... | collective-permute-start | bytes 786440 | tf_op jit(solution)/shard_map/ppermute | solution.py:475
  54.0 10.3 %collective-permute-start.15 = (f32[128,512]{1,0:T(8,128)S(1)}, f32[128,512]{1,0:T(8,128)S(1)}, u32[]{:S(2)}, u32[]{:S(2)}) collective-permute-start(f32[128,512]{1,0:T(8,128)S(1)} %get-tuple-element.27), channel_id=1, source_target_pairs={{4,12},{5,13},{6,14},{7,15},{20,28},{21,29},{22,30},{23,31},{36,44... | collective-permute-start | bytes 786440 | tf_op jit(solution)/shard_map/ppermute | solution.py:475
  54.8 29.8 %copy-start.2 = (f32[1,64,2048]{2,1,0:T(8,128)S(1)}, f32[1,64,2048]{2,1,0:T(8,128)}, u32[]{:S(2)}) copy-start(f32[1,64,2048]{2,1,0:T(8,128)} %param.9) | copy-start | bytes 1572868
  54.8 24.8 %collective-permute-start.3 = (f32[256,512]{1,0:T(8,128)S(1)}, f32[256,512]{1,0:T(8,128)S(1)}, u32[]{:S(2)}, u32[]{:S(2)}) collective-permute-start(f32[256,512]{1,0:T(8,128)S(1)} %pad_maximum_fusion.1.y0_ref), channel_id=1, source_target_pairs={{0,1},{1,2},{2,3},{3,0},{4,5},{5,6},{6,7},{7,4},{8,9},{9,10},{10,1... | collective-permute-start | bytes 1572872 | tf_op jit(solution)/shard_map/ppermute | solution.py:471
  56.5 23.1 %collective-permute-start.4 = (f32[256,512]{1,0:T(8,128)S(1)}, f32[256,512]{1,0:T(8,128)S(1)}, u32[]{:S(2)}, u32[]{:S(2)}) collective-permute-start(f32[256,512]{1,0:T(8,128)S(1)} %pad_maximum_fusion.1.y0_ref), channel_id=1, source_target_pairs={{0,2},{1,3},{2,0},{3,1},{4,6},{5,7},{6,4},{7,5},{8,10},{9,11},{10,... | collective-permute-start | bytes 1572872 | tf_op jit(solution)/shard_map/ppermute | solution.py:471
  63.0 21.6 %collective-permute-start.5 = (f32[256,512]{1,0:T(8,128)S(1)}, f32[256,512]{1,0:T(8,128)S(1)}, u32[]{:S(2)}, u32[]{:S(2)}) collective-permute-start(f32[256,512]{1,0:T(8,128)S(1)} %pad_maximum_fusion.1.y0_ref), channel_id=1, source_target_pairs={{0,3},{1,0},{2,1},{3,2},{4,7},{5,4},{6,5},{7,6},{8,11},{9,8},{10,9... | collective-permute-start | bytes 1572872 | tf_op jit(solution)/shard_map/ppermute | solution.py:471
  63.6 60.5 %collective-permute-start.12 = (f32[512,512]{1,0:T(8,128)S(1)}, f32[512,512]{1,0:T(8,128)S(1)}, u32[]{:S(2)}, u32[]{:S(2)}) collective-permute-start(f32[512,512]{1,0:T(8,128)S(1)} %constant_dynamic-update-slice_fusion.near_ref), channel_id=1, source_target_pairs={{8,12},{9,13},{10,14},{11,15},{12,8},{13,9},{14,10},{15,11},{24,28... | collective-permute-start | bytes 3145736 | tf_op jit(solution)/shard_map/ppermute | solution.py:475
  64.4 39.7 %collective-permute-start.16 = (f32[128,512]{1,0:T(8,128)S(1)}, f32[128,512]{1,0:T(8,128)S(1)}, u32[]{:S(2)}, u32[]{:S(2)}) collective-permute-start(f32[128,512]{1,0:T(8,128)S(1)} %select_select_fusion.p0_ref), channel_id=1, source_target_pairs={{0,1},{1,2},{2,3},{3,0},{4,5},{5,6},{6,7},{7,4},{8,9},{9,10},{10,1... | collective-permute-start | bytes 786440 | tf_op jit(solution)/shard_map/ppermute | solution.py:471
  79.6 25.2 %collective-permute-start.17 = (f32[128,512]{1,0:T(8,128)S(1)}, f32[128,512]{1,0:T(8,128)S(1)}, u32[]{:S(2)}, u32[]{:S(2)}) collective-permute-start(f32[128,512]{1,0:T(8,128)S(1)} %select_select_fusion.p0_ref), channel_id=1, source_target_pairs={{0,2},{1,3},{2,0},{3,1},{4,6},{5,7},{6,4},{7,5},{8,10},{9,11},{10,... | collective-permute-start | bytes 786440 | tf_op jit(solution)/shard_map/ppermute | solution.py:471
  79.6 26.1 %collective-permute-start.18 = (f32[128,512]{1,0:T(8,128)S(1)}, f32[128,512]{1,0:T(8,128)S(1)}, u32[]{:S(2)}, u32[]{:S(2)}) collective-permute-start(f32[128,512]{1,0:T(8,128)S(1)} %select_select_fusion.p0_ref), channel_id=1, source_target_pairs={{0,3},{1,0},{2,1},{3,2},{4,7},{5,4},{6,5},{7,6},{8,11},{9,8},{10,9... | collective-permute-start | bytes 786440 | tf_op jit(solution)/shard_map/ppermute | solution.py:471
  103.4 20.7 %collective-permute-start.6 = (f32[256,512]{1,0:T(8,128)S(1)}, f32[256,512]{1,0:T(8,128)S(1)}, u32[]{:S(2)}, u32[]{:S(2)}) collective-permute-start(f32[256,512]{1,0:T(8,128)S(1)} %pad_maximum_fusion.h0), channel_id=1, source_target_pairs={{8,9},{9,10},{10,11},{11,8},{12,13},{13,14},{14,15},{15,12},{24,25... | collective-permute-start | bytes 1572872 | tf_op jit(solution)/shard_map/ppermute | solution.py:471
  104.1 20.0 %collective-permute-start.7 = (f32[256,512]{1,0:T(8,128)S(1)}, f32[256,512]{1,0:T(8,128)S(1)}, u32[]{:S(2)}, u32[]{:S(2)}) collective-permute-start(f32[256,512]{1,0:T(8,128)S(1)} %pad_maximum_fusion.h0), channel_id=1, source_target_pairs={{8,10},{9,11},{10,8},{11,9},{12,14},{13,15},{14,12},{15,13},{24,26... | collective-permute-start | bytes 1572872 | tf_op jit(solution)/shard_map/ppermute | solution.py:471
  104.9 19.3 %collective-permute-start.8 = (f32[256,512]{1,0:T(8,128)S(1)}, f32[256,512]{1,0:T(8,128)S(1)}, u32[]{:S(2)}, u32[]{:S(2)}) collective-permute-start(f32[256,512]{1,0:T(8,128)S(1)} %pad_maximum_fusion.h0), channel_id=1, source_target_pairs={{8,11},{9,8},{10,9},{11,10},{12,15},{13,12},{14,13},{15,14},{24,27... | collective-permute-start | bytes 1572872 | tf_op jit(solution)/shard_map/ppermute | solution.py:471
  105.7 18.4 %copy-start.4 = (f32[128,1024]{1,0:T(8,128)S(1)}, f32[128,1024]{1,0:T(8,128)}, u32[]{:S(2)}) copy-start(f32[128,1024]{1,0:T(8,128)} %copy-done.3) | copy-start | bytes 1572868
  135.7 19.3 %collective-permute-start.19 = (f32[64,1024]{1,0:T(8,128)S(1)}, f32[64,1024]{1,0:T(8,128)S(1)}, u32[]{:S(2)}, u32[]{:S(2)}) collective-permute-start(f32[64,1024]{1,0:T(8,128)S(1)} %slice.11), channel_id=1, source_target_pairs={{8,4},{9,5},{10,6},{11,7},{12,0},{13,1},{14,2},{15,3},{24,20},{25,... | collective-permute-start | bytes 786440 | tf_op jit(solution)/shard_map/ppermute | solution.py:475

commit v8 on v5

--- a/solution.py
+++ b/solution.py
@@ -285,7 +285,7 @@
     ypos = lax.rem(me, 4)
     for d, ref in enumerate((p0_ref, p1_ref, p2_ref, p3_ref)):
         rows = pl.ds(pl.multiple_of(lax.rem(ypos + 4 - d, 4) * B, B), B)
-        a_ref[rows, :] = ref[...]
+        a_ref[rows, :] = ref[:B, :]
     for ref, src in ((vh, vh0), (vl, vl0)):
         ref[:, :HALF] = src[HALF:, :]
         ref[:, HALF:] = jnp.zeros((ref.shape[0], HALF), BF16)
@@ -361,7 +361,7 @@
             rows = pl.ds(pl.multiple_of((4 * z + spot) * B, B), B)
             src = (near_ref, far_ref)[n]
             copies.append(pltpu.make_async_copy(
-                ref.at[pl.ds(n * B, B), :], a21.at[rows, pl.ds(0, HALF)], sem.at[2 * d + n]))
+                ref.at[pl.ds((n + 1) * B, B), :], a21.at[rows, pl.ds(0, HALF)], sem.at[2 * d + n]))
             copies.append(pltpu.make_async_copy(
                 src.at[pl.ds(d * B, B), :], a21.at[rows, pl.ds(HALF, HALF)], sem.at[8 + 2 * d + n]))
     for copy in copies:
@@ -394,12 +394,14 @@
     yh, yl = split(y)
     eli_ref[:, :PIV] = y
     mine = pl.ds(pl.multiple_of(jnp.maximum(me - NP, 0) * B, B), B)
+    n = B + nrhs
     qh = jnp.concatenate([xh[mine, :], yh], 0)
-    ql = jnp.concatenate([xl[mine, :], yl], 0)
+    both = jnp.concatenate([qh, xl[mine, :], yl], 0)
     for c in range(low // W2):
         rows = slice(c * W2, (c + 1) * W2)
         dst = slice(PIV + c * W2, PIV + (c + 1) * W2)
-        prod = dot3_t(qh, ql, wh[rows, :], wl[rows, :])
+        prod = dot_t(both, wh[rows, :])
+        prod = prod[:n] + prod[n:] + dot_t(qh, wl[rows, :])
         row = me * B + lax.broadcasted_iota(jnp.int32, (B, W2), 0)
         col = PIV + c * W2 + lax.broadcasted_iota(jnp.int32, (B, W2), 1)
         fac_ref[:, dst] = jnp.where(row >= col, tail_ref[:, rows] - prod[:B], 0.0)
@@ -475,15 +477,13 @@
     early_parts = ring_y(jnp.concatenate([pick(z, early, swap, cross, side), pick(z, swap, early, side, cross)], 0))
     late_x, _ = lax.optimization_barrier((late, (swap, side, cross)))
     to0, to2, to3 = (planes(late_x, ((1, d),)) for d in (0, 2, 3))
-    late_parts = ring_y(pick(z, to0, late_x, to2, to3))
+    late_parts = ring_y(jnp.concatenate([pick(z, to0, late_x, to2, to3), early, swap], 0))
     far = planes(near, ((2, 3), (3, 2)))
     state = first(index, early_parts, rhs)
-    pair, _ = lax.optimization_barrier((jnp.concatenate([early, swap], 0), state[6]))
-    below = ring_y(pair, (2, 3))
     state = second(index, late_parts, state, rhs)
-    factored, eliminated = third(index, below + [near, far], state, tail, rhs)
+    factored, eliminated = third(index, late_parts + [near, far], state, tail, rhs)
     tail = eliminated[:, PIV:]
-    tail = jnp.where(z < 2, planes(tail, ((2, 0), (3, 1))), tail)
+    tail = jnp.where(z < 2, planes(tail, ((2, 1), (3, 0))), tail)
     eliminated = jnp.concatenate([eliminated[:, :PIV], tail], 1)
     return factored[None], eliminated[None]
 

time: 159 us -> 158 us (level); the launches traced: 156 us -> 158 us
  waiting for transfers between devices: 67 us -> 71.4 us
  starting transfers between devices: 31.8 us -> 29.6 us
    ppermute x12 -> x9, waiting for transfers between devices: 13.6 us -> 26 us  [shift_y(): lax.ppermute(x, 'front', [(4 * z + y, 4 * z + (y + d) % 4) for z in zs fo...]
    ppermute x8, waiting for transfers between devices: 31.5 us -> 23.4 us  [planes(): lax.ppermute(x, 'front', [(4 * a + y, 4 * b + y) for a, b in pairs for y...]
    ppermute x12 -> x9, starting transfers between devices: 14 us -> 11.7 us  [shift_y(): lax.ppermute(x, 'front', [(4 * z + y, 4 * z + (y + d) % 4) for z in zs fo...]
  transfers between devices with their start and end apart: 21 -> 18, of which waited for: 6 -> 6; matrix products, arithmetic and copies ran while one was open for 0% -> 0% of each run, Pallas kernels for 24% -> 24%
where the time goes in v8:
time: 158 us
  waiting for transfers between devices  71.4 us (45%)
  Pallas kernels  49.9 us (32%)
  starting transfers between devices  29.6 us (19%)
  other arithmetic  4.63 us (3%)
  local copies, waits for them, and re-layouts  1.65 us (1%)
    ppermute x9, waiting for transfers between devices, shift_y(): lax.ppermute(x, 'front', [(4 * z + y, 4 * z + (y + d) % 4) for z in zs fo...  26 us
    ppermute x8, waiting for transfers between devices, planes(): lax.ppermute(x, 'front', [(4 * a + y, 4 * b + y) for a, b in pairs for y...  23.4 us
    all_to_all x1, waiting for transfers between devices, local(): lax.all_to_all(payload, 'leaf', split_axis=0, concat_axis=0, tiled=True)  21.9 us
    pallas_call x1, Pallas kernels, first(): pl.pallas_call(first_kernel, out_shape=tuple((jax.ShapeDtypeStruct(*o) fo...  18.7 us
    pallas_call x1, Pallas kernels, second(): pl.pallas_call(second_kernel, out_shape=tuple((jax.ShapeDtypeStruct(*o) f...  18.5 us
    ppermute x8, starting transfers between devices, planes(): lax.ppermute(x, 'front', [(4 * a + y, 4 * b + y) for a, b in pairs for y...  13.5 us
    ppermute x9, starting transfers between devices, shift_y(): lax.ppermute(x, 'front', [(4 * z + y, 4 * z + (y + d) % 4) for z in zs fo...  11.7 us
    pallas_call x1, Pallas kernels, third(): pl.pallas_call(third_kernel, out_shape=(jax.ShapeDtypeStruct((B, order),...  11.5 us
  transfers between devices with their start and end apart: 18, of which 6 were waited for; matrix products, arithmetic and copies ran while one was open for 0% of the time, Pallas kernels for 24%

profile of v8, /device:TPU:8, one launch (start us, length us, event | category | flops | bytes accessed | tf_op | source)
XLA Modules:
  0.0 158.0 jit_solution(3163923037414426223)
XLA Ops:
  0.6 0.8 copy.10
  1.4 0.7 fusion
  2.1 2.7 %select_maximum_fusion = f32[8,392,128]{2,1,0:T(8,128)} fusion(f32[8,1,3]{2,1,0:T(1,128)S(1)} %fusion, f32[8,384,128]{2,1,0:T(8,128)} %bitcast.15), kind=kLoop, calls=%fused_computation | loop fusion | flops 1204224 | bytes 3178592 | tf_op jit(solution)/shard_map/concatenate | solution.py:466
  4.8 4.4 %all-to-all-start = ((f32[8,392,128]{2,1,0:T(8,128)}), f32[8,392,128]{2,1,0:T(8,128)S(1)}, u32[]{:S(2)}, u32[]{:S(2)}) async-start(f32[8,392,128]{2,1,0:T(8,128)} %select_maximum_fusion), calls=%async_computation | async-start | bytes 3211264 | tf_op jit(solution)/shard_map/all_to_all | solution.py:467
  9.3 21.9 %all-to-all-done.recv_ref = f32[8,392,128]{2,1,0:T(8,128)S(1)} async-done(((f32[8,392,128]{2,1,0:T(8,128)}), f32[8,392,128]{2,1,0:T(8,128)S(1)}, u32[]{:S(2)}, u32[]{:S(2)}) %all-to-all-start) | async-done | bytes 1605664 | tf_op jit(solution)/shard_map/all_to_all | solution.py:467
  31.2 1.1 assemble.1
  32.4 0.0 copy-start.2
  32.4 0.8 copy-done.2
  33.2 1.9 %collective-permute-start = (f32[128,512]{1,0:T(8,128)S(1)}, f32[128,512]{1,0:T(8,128)S(1)}, u32[]{:S(2)}, u32[]{:S(2)}) collective-permute-start(f32[128,512]{1,0:T(8,128)S(1)} %get-tuple-element.35), channel_id=1, source_target_pairs={{0,4},{1,5},{2,6},{3,7},{4,0},{5,1},{6,2},{7,3},{8,12},{9,13},{10,... | collective-permute-start | bytes 786440 | tf_op jit(solution)/shard_map/ppermute | solution.py:450
  35.1 4.4 %collective-permute-start.1 = (f32[128,512]{1,0:T(8,128)S(1)}, f32[128,512]{1,0:T(8,128)S(1)}, u32[]{:S(2)}, u32[]{:S(2)}) collective-permute-start(f32[128,512]{1,0:T(8,128)S(1)} %get-tuple-element.35), channel_id=1, source_target_pairs={{4,8},{5,9},{6,10},{7,11},{0,12},{1,13},{2,14},{3,15},{20,24},{21,... | collective-permute-start | bytes 786440 | tf_op jit(solution)/shard_map/ppermute | solution.py:450
  39.5 2.4 %collective-permute-start.2 = (f32[128,512]{1,0:T(8,128)S(1)}, f32[128,512]{1,0:T(8,128)S(1)}, u32[]{:S(2)}, u32[]{:S(2)}) collective-permute-start(f32[128,512]{1,0:T(8,128)S(1)} %get-tuple-element.35), channel_id=1, source_target_pairs={{0,8},{1,9},{2,10},{3,11},{4,12},{5,13},{6,14},{7,15},{16,24},{17,... | collective-permute-start | bytes 786440 | tf_op jit(solution)/shard_map/ppermute | solution.py:450
  41.9 0.7 collective-permute-start.9
  42.6 0.7 collective-permute-start.10
  43.3 0.0 collective-permute-done
  43.3 0.7 collective-permute-start.11
  44.0 6.2 %collective-permute-done.1 = f32[128,512]{1,0:T(8,128)S(1)} collective-permute-done((f32[128,512]{1,0:T(8,128)S(1)}, f32[128,512]{1,0:T(8,128)S(1)}, u32[]{:S(2)}, u32[]{:S(2)}) %collective-permute-start.1) | collective-permute-done | bytes 262176 | tf_op jit(solution)/shard_map/ppermute | solution.py:450
  50.2 0.0 collective-permute-done.2
  50.2 1.3 collective-permute-start.3
  51.5 0.7 collective-permute-start.4
  52.2 0.1 select_select_fusion.1
  52.4 0.0 collective-permute-done.9
  52.4 0.7 collective-permute-start.5
  53.1 0.0 collective-permute-done.10
  53.1 1.7 %collective-permute-start.13 = (f32[256,512]{1,0:T(8,128)S(1)}, f32[256,512]{1,0:T(8,128)S(1)}, u32[]{:S(2)}, u32[]{:S(2)}) collective-permute-start(f32[256,512]{1,0:T(8,128)S(1)} %pad_maximum_fusion.1.y0_ref), channel_id=1, source_target_pairs={{0,1},{1,2},{2,3},{3,0},{4,5},{5,6},{6,7},{7,4},{8,9},{9,10},{10,1... | collective-permute-start | bytes 1572872 | tf_op jit(solution)/shard_map/ppermute | solution.py:446
  54.7 0.0 collective-permute-done.11
  54.7 0.9 collective-permute-start.14
  55.7 4.6 %collective-permute-done.3 = f32[128,512]{1,0:T(8,128)S(1)} collective-permute-done((f32[128,512]{1,0:T(8,128)S(1)}, f32[128,512]{1,0:T(8,128)S(1)}, u32[]{:S(2)}, u32[]{:S(2)}) %collective-permute-start.3) | collective-permute-done | bytes 262176 | tf_op jit(solution)/shard_map/ppermute | solution.py:450
  60.3 0.4 collective-permute-start.15
  60.6 0.0 copy-start.1
  60.7 0.0 collective-permute-done.4
  60.7 0.9 collective-permute-start.12
  61.6 0.0 collective-permute-done.5
  61.6 0.1 select_select_fusion.2
  61.7 0.1 pad_maximum_fusion.p0_ref.h0
  61.7 1.7 %collective-permute-start.6 = (f32[384,512]{1,0:T(8,128)S(1)}, f32[384,512]{1,0:T(8,128)S(1)}, u32[]{:S(2)}, u32[]{:S(2)}) collective-permute-start(f32[384,512]{1,0:T(8,128)S(1)} %pad_maximum_fusion.p0_ref.h0), channel_id=1, source_target_pairs={{0,1},{1,2},{2,3},{3,0},{4,5},{5,6},{6,7},{7,4},{8,9},{9,10},{10,1... | collective-permute-start | bytes 2359304 | tf_op jit(solution)/shard_map/ppermute | solution.py:446
  63.5 14.5 %collective-permute-done.13.y1_ref = f32[256,512]{1,0:T(8,128)S(1)} collective-permute-done((f32[256,512]{1,0:T(8,128)S(1)}, f32[256,512]{1,0:T(8,128)S(1)}, u32[]{:S(2)}, u32[]{:S(2)}) %collective-permute-start.13) | collective-permute-done | bytes 524320 | tf_op jit(solution)/shard_map/ppermute | solution.py:446
  77.9 0.0 collective-permute-start.7
  77.9 0.0 collective-permute-done.14.y2_ref
  78.0 5.0 %collective-permute-start.8 = (f32[384,512]{1,0:T(8,128)S(1)}, f32[384,512]{1,0:T(8,128)S(1)}, u32[]{:S(2)}, u32[]{:S(2)}) collective-permute-start(f32[384,512]{1,0:T(8,128)S(1)} %pad_maximum_fusion.p0_ref.h0), channel_id=1, source_target_pairs={{0,3},{1,0},{2,1},{3,2},{4,7},{5,4},{6,5},{7,6},{8,11},{9,8},{10,9... | collective-permute-start | bytes 2359304 | tf_op jit(solution)/shard_map/ppermute | solution.py:446
  82.9 0.0 collective-permute-done.15.y3_ref
  82.9 18.7 %first.1 = (bf16[1088,512]{1,0:T(8,128)(2,1)S(1)}, bf16[1088,512]{1,0:T(8,128)(2,1)S(1)}, bf16[1024,512]{1,0:T(8,128)(2,1)S(1)}, bf16[1024,512]{1,0:T(8,128)(2,1...) custom-call(s32[1]{0:T(128)} %bitcast.idx_ref, ...), custom_call_target="tpu_custom_call" | custom-call | flops 20000000000 | bytes 20000000 | tf_op jit(solution)/shard_map/first/pallas_call | solution.py:260
  101.7 11.5 %collective-permute-done.8.p3_ref.h3 = f32[384,512]{1,0:T(8,128)S(1)} collective-permute-done((f32[384,512]{1,0:T(8,128)S(1)}, f32[384,512]{1,0:T(8,128)S(1)}, u32[]{:S(2)}, u32[]{:S(2)}) %collective-permute-start.8) | collective-permute-done | bytes 786464 | tf_op jit(solution)/shard_map/ppermute | solution.py:446
  113.2 18.5 %second.1 = (bf16[1024,1024]{1,0:T(8,128)(2,1)S(1)}, bf16[1024,1024]{1,0:T(8,128)(2,1)S(1)}, f32[8,128,128]{2,1,0:T(8,128)S(1)}, f32[8,1024]{1,0:T(8,128)S(1)}, ...) custom-call(s32[1]{0:T(128)} %bitcast.idx_ref, f32[384,512]{1,0:T(8,128)S(1)} %pad_maximum_fusion.p0_ref.h0, ...), custom_call_target="tpu_custom_call" | custom-call | flops 20000000000 | bytes 20000000 | tf_op jit(solution)/shard_map/second/pallas_call | solution.py:329
  131.7 11.5 %third.1 = (f32[128,2048]{1,0:T(8,128)}, f32[64,2048]{1,0:T(8,128)S(1)}) custom-call(s32[1]{0:T(128)} %bitcast.idx_ref, f32[384,512]{1,0:T(8,128)S(1)} %pad_maximum_fusion.p0_ref.h0, f32[384,512]{1,0:T(8,128)S(1)} %collective-permute-done.6.p1_ref.h1, f32[384,512]{1,0:T(8,128)S(1)} %collective-permute-done.7.p2_ref.h2, ...), custom_call_target="tpu_custom_call" | custom-call | tf_op jit(solution)/shard_map/third/pallas_call | solution.py:423
  143.3 1.3 collective-permute-start.16
  144.6 12.6 %collective-permute-done.16 = f32[64,1024]{1,0:T(8,128)S(1)} collective-permute-done((f32[64,1024]{1,0:T(8,128)S(1)}, f32[64,1024]{1,0:T(8,128)S(1)}, u32[]{:S(2)}, u32[]{:S(2)}) %collective-permute-start.16) | collective-permute-done | bytes 262176 | tf_op jit(solution)/shard_map/ppermute | solution.py:450
  157.1 0.1 fusion.1
  157.2 0.8 maximum_bitcast_fusion
  (15 shorter events, 0.2 us)
Async XLA Ops:
  4.8 26.4 %copy-start = (f32[1,128,2048]{2,1,0:T(8,128)S(1)}, f32[1,128,2048]{2,1,0:T(8,128)}, u32[]{:S(2)}) copy-start(f32[1,128,2048]{2,1,0:T(8,128)} %param.7) | copy-start | bytes 3145732
  4.8 26.4 %all-to-all-start = ((f32[8,392,128]{2,1,0:T(8,128)}), f32[8,392,128]{2,1,0:T(8,128)S(1)}, u32[]{:S(2)}, u32[]{:S(2)}) async-start(f32[8,392,128]{2,1,0:T(8,128)} %select_maximum_fusion), calls=%async_computation | async-start | bytes 3211264 | tf_op jit(solution)/shard_map/all_to_all | solution.py:467
  32.4 0.8 copy-start.2
  33.2 10.1 %collective-permute-start = (f32[128,512]{1,0:T(8,128)S(1)}, f32[128,512]{1,0:T(8,128)S(1)}, u32[]{:S(2)}, u32[]{:S(2)}) collective-permute-start(f32[128,512]{1,0:T(8,128)S(1)} %get-tuple-element.35), channel_id=1, source_target_pairs={{0,4},{1,5},{2,6},{3,7},{4,0},{5,1},{6,2},{7,3},{8,12},{9,13},{10,... | collective-permute-start | bytes 786440 | tf_op jit(solution)/shard_map/ppermute | solution.py:450
  35.1 15.1 %collective-permute-start.1 = (f32[128,512]{1,0:T(8,128)S(1)}, f32[128,512]{1,0:T(8,128)S(1)}, u32[]{:S(2)}, u32[]{:S(2)}) collective-permute-start(f32[128,512]{1,0:T(8,128)S(1)} %get-tuple-element.35), channel_id=1, source_target_pairs={{4,8},{5,9},{6,10},{7,11},{0,12},{1,13},{2,14},{3,15},{20,24},{21,... | collective-permute-start | bytes 786440 | tf_op jit(solution)/shard_map/ppermute | solution.py:450
  39.5 10.7 %collective-permute-start.2 = (f32[128,512]{1,0:T(8,128)S(1)}, f32[128,512]{1,0:T(8,128)S(1)}, u32[]{:S(2)}, u32[]{:S(2)}) collective-permute-start(f32[128,512]{1,0:T(8,128)S(1)} %get-tuple-element.35), channel_id=1, source_target_pairs={{0,8},{1,9},{2,10},{3,11},{4,12},{5,13},{6,14},{7,15},{16,24},{17,... | collective-permute-start | bytes 786440 | tf_op jit(solution)/shard_map/ppermute | solution.py:450
  41.9 10.4 %collective-permute-start.9 = (f32[128,512]{1,0:T(8,128)S(1)}, f32[128,512]{1,0:T(8,128)S(1)}, u32[]{:S(2)}, u32[]{:S(2)}) collective-permute-start(f32[128,512]{1,0:T(8,128)S(1)} %get-tuple-element.36), channel_id=1, source_target_pairs={{8,9},{9,10},{10,11},{11,8},{12,13},{13,14},{14,15},{15,12},{24,25... | collective-permute-start | bytes 786440 | tf_op jit(solution)/shard_map/ppermute | solution.py:446
  42.6 10.5 %collective-permute-start.10 = (f32[128,512]{1,0:T(8,128)S(1)}, f32[128,512]{1,0:T(8,128)S(1)}, u32[]{:S(2)}, u32[]{:S(2)}) collective-permute-start(f32[128,512]{1,0:T(8,128)S(1)} %get-tuple-element.36), channel_id=1, source_target_pairs={{8,10},{9,11},{10,8},{11,9},{12,14},{13,15},{14,12},{15,13},{24,26... | collective-permute-start | bytes 786440 | tf_op jit(solution)/shard_map/ppermute | solution.py:446
  43.3 11.4 %collective-permute-start.11 = (f32[128,512]{1,0:T(8,128)S(1)}, f32[128,512]{1,0:T(8,128)S(1)}, u32[]{:S(2)}, u32[]{:S(2)}) collective-permute-start(f32[128,512]{1,0:T(8,128)S(1)} %get-tuple-element.36), channel_id=1, source_target_pairs={{8,11},{9,8},{10,9},{11,10},{12,15},{13,12},{14,13},{15,14},{24,27... | collective-permute-start | bytes 786440 | tf_op jit(solution)/shard_map/ppermute | solution.py:446
  50.2 10.0 %collective-permute-start.3 = (f32[128,512]{1,0:T(8,128)S(1)}, f32[128,512]{1,0:T(8,128)S(1)}, u32[]{:S(2)}, u32[]{:S(2)}) collective-permute-start(f32[128,512]{1,0:T(8,128)S(1)} %get-tuple-element.36), channel_id=1, source_target_pairs={{4,0},{5,1},{6,2},{7,3},{20,16},{21,17},{22,18},{23,19},{36,32},{3... | collective-permute-start | bytes 786440 | tf_op jit(solution)/shard_map/ppermute | solution.py:450
  51.5 9.2 %collective-permute-start.4 = (f32[128,512]{1,0:T(8,128)S(1)}, f32[128,512]{1,0:T(8,128)S(1)}, u32[]{:S(2)}, u32[]{:S(2)}) collective-permute-start(f32[128,512]{1,0:T(8,128)S(1)} %get-tuple-element.36), channel_id=1, source_target_pairs={{4,8},{5,9},{6,10},{7,11},{20,24},{21,25},{22,26},{23,27},{36,40},... | collective-permute-start | bytes 786440 | tf_op jit(solution)/shard_map/ppermute | solution.py:450
  52.4 9.2 %collective-permute-start.5 = (f32[128,512]{1,0:T(8,128)S(1)}, f32[128,512]{1,0:T(8,128)S(1)}, u32[]{:S(2)}, u32[]{:S(2)}) collective-permute-start(f32[128,512]{1,0:T(8,128)S(1)} %get-tuple-element.36), channel_id=1, source_target_pairs={{4,12},{5,13},{6,14},{7,15},{20,28},{21,29},{22,30},{23,31},{36,44... | collective-permute-start | bytes 786440 | tf_op jit(solution)/shard_map/ppermute | solution.py:450
  53.1 24.9 %collective-permute-start.13 = (f32[256,512]{1,0:T(8,128)S(1)}, f32[256,512]{1,0:T(8,128)S(1)}, u32[]{:S(2)}, u32[]{:S(2)}) collective-permute-start(f32[256,512]{1,0:T(8,128)S(1)} %pad_maximum_fusion.1.y0_ref), channel_id=1, source_target_pairs={{0,1},{1,2},{2,3},{3,0},{4,5},{5,6},{6,7},{7,4},{8,9},{9,10},{10,1... | collective-permute-start | bytes 1572872 | tf_op jit(solution)/shard_map/ppermute | solution.py:446
  54.7 23.2 %collective-permute-start.14 = (f32[256,512]{1,0:T(8,128)S(1)}, f32[256,512]{1,0:T(8,128)S(1)}, u32[]{:S(2)}, u32[]{:S(2)}) collective-permute-start(f32[256,512]{1,0:T(8,128)S(1)} %pad_maximum_fusion.1.y0_ref), channel_id=1, source_target_pairs={{0,2},{1,3},{2,0},{3,1},{4,6},{5,7},{6,4},{7,5},{8,10},{9,11},{10,... | collective-permute-start | bytes 1572872 | tf_op jit(solution)/shard_map/ppermute | solution.py:446
  60.3 22.7 %collective-permute-start.15 = (f32[256,512]{1,0:T(8,128)S(1)}, f32[256,512]{1,0:T(8,128)S(1)}, u32[]{:S(2)}, u32[]{:S(2)}) collective-permute-start(f32[256,512]{1,0:T(8,128)S(1)} %pad_maximum_fusion.1.y0_ref), channel_id=1, source_target_pairs={{0,3},{1,0},{2,1},{3,2},{4,7},{5,4},{6,5},{7,6},{8,11},{9,8},{10,9... | collective-permute-start | bytes 1572872 | tf_op jit(solution)/shard_map/ppermute | solution.py:446
  60.6 22.3 %copy-start.1 = (f32[1,64,2048]{2,1,0:T(8,128)S(1)}, f32[1,64,2048]{2,1,0:T(8,128)}, u32[]{:S(2)}) copy-start(f32[1,64,2048]{2,1,0:T(8,128)} %param.11) | copy-start | bytes 1572868
  60.7 71.0 %collective-permute-start.12 = (f32[512,512]{1,0:T(8,128)S(1)}, f32[512,512]{1,0:T(8,128)S(1)}, u32[]{:S(2)}, u32[]{:S(2)}) collective-permute-start(f32[512,512]{1,0:T(8,128)S(1)} %constant_dynamic-update-slice_fusion.near_ref), channel_id=1, source_target_pairs={{8,12},{9,13},{10,14},{11,15},{12,8},{13,9},{14,10},{15,11},{24,28... | collective-permute-start | bytes 3145736 | tf_op jit(solution)/shard_map/ppermute | solution.py:450
  61.7 39.9 %collective-permute-start.6 = (f32[384,512]{1,0:T(8,128)S(1)}, f32[384,512]{1,0:T(8,128)S(1)}, u32[]{:S(2)}, u32[]{:S(2)}) collective-permute-start(f32[384,512]{1,0:T(8,128)S(1)} %pad_maximum_fusion.p0_ref.h0), channel_id=1, source_target_pairs={{0,1},{1,2},{2,3},{3,0},{4,5},{5,6},{6,7},{7,4},{8,9},{9,10},{10,1... | collective-permute-start | bytes 2359304 | tf_op jit(solution)/shard_map/ppermute | solution.py:446
  77.9 23.7 %collective-permute-start.7 = (f32[384,512]{1,0:T(8,128)S(1)}, f32[384,512]{1,0:T(8,128)S(1)}, u32[]{:S(2)}, u32[]{:S(2)}) collective-permute-start(f32[384,512]{1,0:T(8,128)S(1)} %pad_maximum_fusion.p0_ref.h0), channel_id=1, source_target_pairs={{0,2},{1,3},{2,0},{3,1},{4,6},{5,7},{6,4},{7,5},{8,10},{9,11},{10,... | collective-permute-start | bytes 2359304 | tf_op jit(solution)/shard_map/ppermute | solution.py:446
  78.0 35.2 %collective-permute-start.8 = (f32[384,512]{1,0:T(8,128)S(1)}, f32[384,512]{1,0:T(8,128)S(1)}, u32[]{:S(2)}, u32[]{:S(2)}) collective-permute-start(f32[384,512]{1,0:T(8,128)S(1)} %pad_maximum_fusion.p0_ref.h0), channel_id=1, source_target_pairs={{0,3},{1,0},{2,1},{3,2},{4,7},{5,4},{6,5},{7,6},{8,11},{9,8},{10,9... | collective-permute-start | bytes 2359304 | tf_op jit(solution)/shard_map/ppermute | solution.py:446
  113.2 18.5 %copy-start.3 = (f32[128,1024]{1,0:T(8,128)S(1)}, f32[128,1024]{1,0:T(8,128)}, u32[]{:S(2)}) copy-start(f32[128,1024]{1,0:T(8,128)} %copy-done.2) | copy-start | bytes 1572868
  143.3 13.9 %collective-permute-start.16 = (f32[64,1024]{1,0:T(8,128)S(1)}, f32[64,1024]{1,0:T(8,128)S(1)}, u32[]{:S(2)}, u32[]{:S(2)}) collective-permute-start(f32[64,1024]{1,0:T(8,128)S(1)} %slice.34), channel_id=1, source_target_pairs={{8,4},{9,5},{10,6},{11,7},{12,0},{13,1},{14,2},{15,3},{24,20},{25,... | collective-permute-start | bytes 786440 | tf_op jit(solution)/shard_map/ppermute | solution.py:450

commit v9 on v6

--- a/solution.py
+++ b/solution.py
@@ -390,12 +390,14 @@
     yh, yl = split(y)
     eli_ref[:, :PIV] = y
     mine = pl.ds(pl.multiple_of(jnp.maximum(me - NP, 0) * B, B), B)
+    n = B + nrhs
     qh = jnp.concatenate([xh[mine, :], yh], 0)
-    ql = jnp.concatenate([xl[mine, :], yl], 0)
+    both = jnp.concatenate([qh, xl[mine, :], yl], 0)
     for c in range(low // W2):
         rows = slice(c * W2, (c + 1) * W2)
         dst = slice(PIV + c * W2, PIV + (c + 1) * W2)
-        prod = dot3_t(qh, ql, wh[rows, :], wl[rows, :])
+        prod = dot_t(both, wh[rows, :])
+        prod = prod[:n] + prod[n:] + dot_t(qh, wl[rows, :])
         row = me * B + lax.broadcasted_iota(jnp.int32, (B, W2), 0)
         col = PIV + c * W2 + lax.broadcasted_iota(jnp.int32, (B, W2), 1)
         fac_ref[:, dst] = jnp.where(row >= col, tail_ref[:, rows] - prod[:B], 0.0)
@@ -469,11 +471,10 @@
     cross = planes(early, ((0, 2), (1, 3)))
     near_last = jnp.concatenate(ring_y(late, (2, 3)), 0)
     early_parts = ring_y(jnp.concatenate([pick(z, early, swap, cross, side), pick(z, swap, early, side, cross)], 0))
-    late_x, _ = lax.optimization_barrier((late, (swap, side, cross, near_last)))
+    late_x, _ = lax.optimization_barrier((late, (swap, side, cross)))
     to0, to2, to3 = (planes(late_x, ((1, d),)) for d in (0, 2, 3))
     far_last = planes(near_last, ((2, 3), (3, 2)))
     mixed = jnp.concatenate([pick(z, to0, late_x, to2, to3), early], 0)
-    mixed, _ = lax.optimization_barrier((mixed, early_parts))
     late_parts = ring_y(mixed)
     state = first(index, early_parts, rhs)
     near_first = jnp.concatenate([part[B:] for part in late_parts], 0)

time: 161 us -> 153 us (0.950)
  starting transfers between devices: 41.6 us -> 30 us
  waiting for transfers between devices: 60.6 us -> 65 us
    ppermute x9, starting transfers between devices: 22 us -> 13.5 us  [planes(): lax.ppermute(x, 'front', [(4 * a + y, 4 * b + y) for a, b in pairs for y...]
    ppermute x9, waiting for transfers between devices: 22.9 us -> 28.4 us  [planes(): lax.ppermute(x, 'front', [(4 * a + y, 4 * b + y) for a, b in pairs for y...]
    ppermute x9, starting transfers between devices: 15.2 us -> 12.1 us  [shift_y(): lax.ppermute(x, 'front', [(4 * z + y, 4 * z + (y + d) % 4) for z in zs fo...]
  transfers between devices with their start and end apart: 19 -> 19, of which waited for: 7 -> 8; matrix products, arithmetic and copies ran while one was open for 0% -> 0% of each run, Pallas kernels for 23% -> 24%
where the time goes in v9:
time: 153 us; the launch traced here: 152 us
  waiting for transfers between devices  65 us (42%)
  Pallas kernels  49.7 us (32%)
  starting transfers between devices  30 us (20%)
  other arithmetic  4.66 us (3%)
  local copies, waits for them, and re-layouts  1.71 us (1%)
    ppermute x9, waiting for transfers between devices, planes(): lax.ppermute(x, 'front', [(4 * a + y, 4 * b + y) for a, b in pairs for y...  28.4 us
    all_to_all x1, waiting for transfers between devices, local(): lax.all_to_all(payload, 'leaf', split_axis=0, concat_axis=0, tiled=True)  21.9 us
    pallas_call x1, Pallas kernels, first(): pl.pallas_call(first_kernel, out_shape=tuple((jax.ShapeDtypeStruct(*o) fo...  18.5 us
    pallas_call x1, Pallas kernels, second(): pl.pallas_call(second_kernel, out_shape=tuple((jax.ShapeDtypeStruct(*o) f...  18.5 us
    ppermute x9, waiting for transfers between devices, shift_y(): lax.ppermute(x, 'front', [(4 * z + y, 4 * z + (y + d) % 4) for z in zs fo...  14.6 us
    ppermute x9, starting transfers between devices, planes(): lax.ppermute(x, 'front', [(4 * a + y, 4 * b + y) for a, b in pairs for y...  13.5 us
    ppermute x9, starting transfers between devices, shift_y(): lax.ppermute(x, 'front', [(4 * z + y, 4 * z + (y + d) % 4) for z in zs fo...  12.1 us
    pallas_call x1, Pallas kernels, third(): pl.pallas_call(third_kernel, out_shape=(jax.ShapeDtypeStruct((B, order),...  11.5 us
  transfers between devices with their start and end apart: 19, of which 8 were waited for; matrix products, arithmetic and copies ran while one was open for 0% of the time, Pallas kernels for 24%

profile of v9, /device:TPU:8, one launch (start us, length us, event | category | flops | bytes accessed | tf_op | source)
XLA Modules:
  0.0 152.0 jit_solution(10075873665652109609)
XLA Ops:
  0.6 0.8 copy.10
  1.4 0.7 fusion
  2.1 2.7 %select_maximum_fusion = f32[8,392,128]{2,1,0:T(8,128)} fusion(f32[8,1,3]{2,1,0:T(1,128)S(1)} %fusion, f32[8,384,128]{2,1,0:T(8,128)} %bitcast.15), kind=kLoop, calls=%fused_computation | loop fusion | flops 1204224 | bytes 3178592 | tf_op jit(solution)/shard_map/concatenate | solution.py:462
  4.8 4.4 %all-to-all-start = ((f32[8,392,128]{2,1,0:T(8,128)}), f32[8,392,128]{2,1,0:T(8,128)S(1)}, u32[]{:S(2)}, u32[]{:S(2)}) async-start(f32[8,392,128]{2,1,0:T(8,128)} %select_maximum_fusion), calls=%async_computation | async-start | bytes 3211264 | tf_op jit(solution)/shard_map/all_to_all | solution.py:463
  9.3 21.9 %all-to-all-done.recv_ref = f32[8,392,128]{2,1,0:T(8,128)S(1)} async-done(((f32[8,392,128]{2,1,0:T(8,128)}), f32[8,392,128]{2,1,0:T(8,128)S(1)}, u32[]{:S(2)}, u32[]{:S(2)}) %all-to-all-start) | async-done | bytes 1605664 | tf_op jit(solution)/shard_map/all_to_all | solution.py:463
  31.2 1.2 assemble.1
  32.4 0.0 copy-start.2
  32.4 0.8 copy-done.2
  33.2 3.8 %collective-permute-start = (f32[128,512]{1,0:T(8,128)S(1)}, f32[128,512]{1,0:T(8,128)S(1)}, u32[]{:S(2)}, u32[]{:S(2)}) collective-permute-start(f32[128,512]{1,0:T(8,128)S(1)} %get-tuple-element.35), channel_id=1, source_target_pairs={{0,4},{1,5},{2,6},{3,7},{4,0},{5,1},{6,2},{7,3},{16,20},{17,21},{1... | collective-permute-start | bytes 786440 | tf_op jit(solution)/shard_map/ppermute | solution.py:446
  37.0 2.8 %collective-permute-start.1 = (f32[128,512]{1,0:T(8,128)S(1)}, f32[128,512]{1,0:T(8,128)S(1)}, u32[]{:S(2)}, u32[]{:S(2)}) collective-permute-start(f32[128,512]{1,0:T(8,128)S(1)} %get-tuple-element.35), channel_id=1, source_target_pairs={{4,8},{5,9},{6,10},{7,11},{0,12},{1,13},{2,14},{3,15},{20,24},{21,... | collective-permute-start | bytes 786440 | tf_op jit(solution)/shard_map/ppermute | solution.py:446
  39.8 1.3 collective-permute-start.2
  41.2 0.7 collective-permute-start.12
  41.8 0.7 collective-permute-start.13
  42.6 1.5 collective-permute-done
  44.0 0.7 collective-permute-start.14
  44.7 6.1 %collective-permute-done.1 = f32[128,512]{1,0:T(8,128)S(1)} collective-permute-done((f32[128,512]{1,0:T(8,128)S(1)}, f32[128,512]{1,0:T(8,128)S(1)}, u32[]{:S(2)}, u32[]{:S(2)}) %collective-permute-start.1) | collective-permute-done | bytes 262176 | tf_op jit(solution)/shard_map/ppermute | solution.py:446
  50.8 0.0 collective-permute-done.2
  50.8 1.3 collective-permute-start.3
  52.1 0.7 collective-permute-start.4
  52.7 0.1 select_select_fusion.1
  52.9 0.0 collective-permute-done.12
  52.9 0.7 collective-permute-start.5
  53.6 0.0 copy-start.1
  53.6 0.0 collective-permute-done.13
  53.6 2.4 %collective-permute-start.10 = (f32[256,512]{1,0:T(8,128)S(1)}, f32[256,512]{1,0:T(8,128)S(1)}, u32[]{:S(2)}, u32[]{:S(2)}) collective-permute-start(f32[256,512]{1,0:T(8,128)S(1)} %pad_maximum_fusion.2.y0_ref), channel_id=1, source_target_pairs={{0,2},{1,3},{2,0},{3,1},{4,6},{5,7},{6,4},{7,5},{8,10},{9,11},{10,... | collective-permute-start | bytes 1572872 | tf_op jit(solution)/shard_map/ppermute | solution.py:442
  56.1 1.3 collective-permute-start.11
  57.4 3.7 %collective-permute-done.3 = f32[128,512]{1,0:T(8,128)S(1)} collective-permute-done((f32[128,512]{1,0:T(8,128)S(1)}, f32[128,512]{1,0:T(8,128)S(1)}, u32[]{:S(2)}, u32[]{:S(2)}) %collective-permute-start.3) | collective-permute-done | bytes 262176 | tf_op jit(solution)/shard_map/ppermute | solution.py:446
  61.1 1.6 %collective-permute-start.9 = (f32[256,512]{1,0:T(8,128)S(1)}, f32[256,512]{1,0:T(8,128)S(1)}, u32[]{:S(2)}, u32[]{:S(2)}) collective-permute-start(f32[256,512]{1,0:T(8,128)S(1)} %pad_maximum_fusion.2.y0_ref), channel_id=1, source_target_pairs={{0,1},{1,2},{2,3},{3,0},{4,5},{5,6},{6,7},{7,4},{8,9},{9,10},{10,1... | collective-permute-start | bytes 1572872 | tf_op jit(solution)/shard_map/ppermute | solution.py:442
  62.8 0.0 collective-permute-done.4
  62.8 0.7 collective-permute-start.16
  63.5 0.1 select_select_fusion.2
  63.7 1.4 collective-permute-start.6
  65.0 5.1 %collective-permute-done.10.y2_ref = f32[256,512]{1,0:T(8,128)S(1)} collective-permute-done((f32[256,512]{1,0:T(8,128)S(1)}, f32[256,512]{1,0:T(8,128)S(1)}, u32[]{:S(2)}, u32[]{:S(2)}) %collective-permute-start.10) | collective-permute-done | bytes 524320 | tf_op jit(solution)/shard_map/ppermute | solution.py:442
  70.1 2.3 %collective-permute-start.7 = (f32[256,512]{1,0:T(8,128)S(1)}, f32[256,512]{1,0:T(8,128)S(1)}, u32[]{:S(2)}, u32[]{:S(2)}) collective-permute-start(f32[256,512]{1,0:T(8,128)S(1)} %pad_maximum_fusion.1.p0_ref), channel_id=1, source_target_pairs={{0,2},{1,3},{2,0},{3,1},{4,6},{5,7},{6,4},{7,5},{8,10},{9,11},{10,... | collective-permute-start | bytes 1572872 | tf_op jit(solution)/shard_map/ppermute | solution.py:442
  72.4 8.8 %collective-permute-done.11.y3_ref = f32[256,512]{1,0:T(8,128)S(1)} collective-permute-done((f32[256,512]{1,0:T(8,128)S(1)}, f32[256,512]{1,0:T(8,128)S(1)}, u32[]{:S(2)}, u32[]{:S(2)}) %collective-permute-start.11) | collective-permute-done | bytes 524320 | tf_op jit(solution)/shard_map/ppermute | solution.py:442
  81.3 0.9 collective-permute-start.8
  82.2 18.5 %first.1 = (bf16[1088,512]{1,0:T(8,128)(2,1)S(1)}, bf16[1088,512]{1,0:T(8,128)(2,1)S(1)}, bf16[1024,512]{1,0:T(8,128)(2,1)S(1)}, bf16[1024,512]{1,0:T(8,128)(2,1...) custom-call(s32[1]{0:T(128)} %bitcast.idx_ref, ...), custom_call_target="tpu_custom_call" | custom-call | flops 20000000000 | bytes 20000000 | tf_op jit(solution)/shard_map/first/pallas_call | solution.py:260
  100.7 0.0 collective-permute-done.6.p1_ref
  100.8 0.7 collective-permute-done.8.p3_ref
  101.5 0.1 pad_maximum_fusion.nf_ref
  101.6 0.9 collective-permute-start.15
  102.5 0.0 copy-start.3
  102.6 18.5 %second.1 = (bf16[1024,1024]{1,0:T(8,128)(2,1)S(1)}, bf16[1024,1024]{1,0:T(8,128)(2,1)S(1)}, f32[8,128,128]{2,1,0:T(8,128)S(1)}, f32[8,1024]{1,0:T(8,128)S(1)}, ...) custom-call(s32[1]{0:T(128)} %bitcast.idx_ref, f32[256,512]{1,0:T(8,128)S(1)} %pad_maximum_fusion.1.p0_ref, ...), custom_call_target="tpu_custom_call" | custom-call | flops 20000000000 | bytes 20000000 | tf_op jit(solution)/shard_map/second/pallas_call | solution.py:329
  121.0 0.0 collective-permute-done.16.fl_ref
  121.1 11.5 %third.1 = (f32[128,2048]{1,0:T(8,128)}, f32[64,2048]{1,0:T(8,128)S(1)}) custom-call(s32[1]{0:T(128)} %bitcast.idx_ref, f32[512,512]{1,0:T(8,128)S(1)} %pad_maximum_fusion.nf_ref, f32[512,512]{1,0:T(8,128)S(1)} %constant_dynamic-update-slice_fusion.nl_ref, f32[512,512]{1,0:T(8,128)S(1)} %collective-permute-done.15.ff_ref, ...), custom_call_target="tpu_custom_call" | custom-call | tf_op jit(solution)/shard_map/third/pallas_call | solution.py:419
  132.6 1.3 collective-permute-start.17
  133.9 17.2 %collective-permute-done.17 = f32[64,1024]{1,0:T(8,128)S(1)} collective-permute-done((f32[64,1024]{1,0:T(8,128)S(1)}, f32[64,1024]{1,0:T(8,128)S(1)}, u32[]{:S(2)}, u32[]{:S(2)}) %collective-permute-start.17) | collective-permute-done | bytes 262176 | tf_op jit(solution)/shard_map/ppermute | solution.py:446
  151.2 0.8 maximum_bitcast_fusion
  (21 shorter events, 0.3 us)
Async XLA Ops:
  4.8 26.4 %copy-start = (f32[1,128,2048]{2,1,0:T(8,128)S(1)}, f32[1,128,2048]{2,1,0:T(8,128)}, u32[]{:S(2)}) copy-start(f32[1,128,2048]{2,1,0:T(8,128)} %param.7) | copy-start | bytes 3145732
  4.8 26.4 %all-to-all-start = ((f32[8,392,128]{2,1,0:T(8,128)}), f32[8,392,128]{2,1,0:T(8,128)S(1)}, u32[]{:S(2)}, u32[]{:S(2)}) async-start(f32[8,392,128]{2,1,0:T(8,128)} %select_maximum_fusion), calls=%async_computation | async-start | bytes 3211264 | tf_op jit(solution)/shard_map/all_to_all | solution.py:463
  32.4 0.8 copy-start.2
  33.2 10.8 %collective-permute-start = (f32[128,512]{1,0:T(8,128)S(1)}, f32[128,512]{1,0:T(8,128)S(1)}, u32[]{:S(2)}, u32[]{:S(2)}) collective-permute-start(f32[128,512]{1,0:T(8,128)S(1)} %get-tuple-element.35), channel_id=1, source_target_pairs={{0,4},{1,5},{2,6},{3,7},{4,0},{5,1},{6,2},{7,3},{16,20},{17,21},{1... | collective-permute-start | bytes 786440 | tf_op jit(solution)/shard_map/ppermute | solution.py:446
  37.0 13.8 %collective-permute-start.1 = (f32[128,512]{1,0:T(8,128)S(1)}, f32[128,512]{1,0:T(8,128)S(1)}, u32[]{:S(2)}, u32[]{:S(2)}) collective-permute-start(f32[128,512]{1,0:T(8,128)S(1)} %get-tuple-element.35), channel_id=1, source_target_pairs={{4,8},{5,9},{6,10},{7,11},{0,12},{1,13},{2,14},{3,15},{20,24},{21,... | collective-permute-start | bytes 786440 | tf_op jit(solution)/shard_map/ppermute | solution.py:446
  39.8 10.9 %collective-permute-start.2 = (f32[128,512]{1,0:T(8,128)S(1)}, f32[128,512]{1,0:T(8,128)S(1)}, u32[]{:S(2)}, u32[]{:S(2)}) collective-permute-start(f32[128,512]{1,0:T(8,128)S(1)} %get-tuple-element.35), channel_id=1, source_target_pairs={{0,8},{1,9},{2,10},{3,11},{4,12},{5,13},{6,14},{7,15},{16,24},{17,... | collective-permute-start | bytes 786440 | tf_op jit(solution)/shard_map/ppermute | solution.py:446
  41.2 11.7 %collective-permute-start.12 = (f32[128,512]{1,0:T(8,128)S(1)}, f32[128,512]{1,0:T(8,128)S(1)}, u32[]{:S(2)}, u32[]{:S(2)}) collective-permute-start(f32[128,512]{1,0:T(8,128)S(1)} %get-tuple-element.37), channel_id=1, source_target_pairs={{8,9},{9,10},{10,11},{11,8},{12,13},{13,14},{14,15},{15,12},{24,25... | collective-permute-start | bytes 786440 | tf_op jit(solution)/shard_map/ppermute | solution.py:442
  41.8 11.8 %collective-permute-start.13 = (f32[128,512]{1,0:T(8,128)S(1)}, f32[128,512]{1,0:T(8,128)S(1)}, u32[]{:S(2)}, u32[]{:S(2)}) collective-permute-start(f32[128,512]{1,0:T(8,128)S(1)} %get-tuple-element.37), channel_id=1, source_target_pairs={{8,10},{9,11},{10,8},{11,9},{12,14},{13,15},{14,12},{15,13},{24,26... | collective-permute-start | bytes 786440 | tf_op jit(solution)/shard_map/ppermute | solution.py:442
  44.0 12.0 %collective-permute-start.14 = (f32[128,512]{1,0:T(8,128)S(1)}, f32[128,512]{1,0:T(8,128)S(1)}, u32[]{:S(2)}, u32[]{:S(2)}) collective-permute-start(f32[128,512]{1,0:T(8,128)S(1)} %get-tuple-element.37), channel_id=1, source_target_pairs={{8,11},{9,8},{10,9},{11,10},{12,15},{13,12},{14,13},{15,14},{24,27... | collective-permute-start | bytes 786440 | tf_op jit(solution)/shard_map/ppermute | solution.py:442
  50.8 10.3 %collective-permute-start.3 = (f32[128,512]{1,0:T(8,128)S(1)}, f32[128,512]{1,0:T(8,128)S(1)}, u32[]{:S(2)}, u32[]{:S(2)}) collective-permute-start(f32[128,512]{1,0:T(8,128)S(1)} %get-tuple-element.37), channel_id=1, source_target_pairs={{4,0},{5,1},{6,2},{7,3},{20,16},{21,17},{22,18},{23,19},{36,32},{3... | collective-permute-start | bytes 786440 | tf_op jit(solution)/shard_map/ppermute | solution.py:446
  52.1 10.7 %collective-permute-start.4 = (f32[128,512]{1,0:T(8,128)S(1)}, f32[128,512]{1,0:T(8,128)S(1)}, u32[]{:S(2)}, u32[]{:S(2)}) collective-permute-start(f32[128,512]{1,0:T(8,128)S(1)} %get-tuple-element.37), channel_id=1, source_target_pairs={{4,8},{5,9},{6,10},{7,11},{20,24},{21,25},{22,26},{23,27},{36,40},... | collective-permute-start | bytes 786440 | tf_op jit(solution)/shard_map/ppermute | solution.py:446
  52.9 10.6 %collective-permute-start.5 = (f32[128,512]{1,0:T(8,128)S(1)}, f32[128,512]{1,0:T(8,128)S(1)}, u32[]{:S(2)}, u32[]{:S(2)}) collective-permute-start(f32[128,512]{1,0:T(8,128)S(1)} %get-tuple-element.37), channel_id=1, source_target_pairs={{4,12},{5,13},{6,14},{7,15},{20,28},{21,29},{22,30},{23,31},{36,44... | collective-permute-start | bytes 786440 | tf_op jit(solution)/shard_map/ppermute | solution.py:446
  53.6 28.6 %copy-start.1 = (f32[1,64,2048]{2,1,0:T(8,128)S(1)}, f32[1,64,2048]{2,1,0:T(8,128)}, u32[]{:S(2)}) copy-start(f32[1,64,2048]{2,1,0:T(8,128)} %param.11) | copy-start | bytes 1572868
  53.6 16.5 %collective-permute-start.10 = (f32[256,512]{1,0:T(8,128)S(1)}, f32[256,512]{1,0:T(8,128)S(1)}, u32[]{:S(2)}, u32[]{:S(2)}) collective-permute-start(f32[256,512]{1,0:T(8,128)S(1)} %pad_maximum_fusion.2.y0_ref), channel_id=1, source_target_pairs={{0,2},{1,3},{2,0},{3,1},{4,6},{5,7},{6,4},{7,5},{8,10},{9,11},{10,... | collective-permute-start | bytes 1572872 | tf_op jit(solution)/shard_map/ppermute | solution.py:442
  56.1 25.2 %collective-permute-start.11 = (f32[256,512]{1,0:T(8,128)S(1)}, f32[256,512]{1,0:T(8,128)S(1)}, u32[]{:S(2)}, u32[]{:S(2)}) collective-permute-start(f32[256,512]{1,0:T(8,128)S(1)} %pad_maximum_fusion.2.y0_ref), channel_id=1, source_target_pairs={{0,3},{1,0},{2,1},{3,2},{4,7},{5,4},{6,5},{7,6},{8,11},{9,8},{10,9... | collective-permute-start | bytes 1572872 | tf_op jit(solution)/shard_map/ppermute | solution.py:442
  61.1 21.1 %collective-permute-start.9 = (f32[256,512]{1,0:T(8,128)S(1)}, f32[256,512]{1,0:T(8,128)S(1)}, u32[]{:S(2)}, u32[]{:S(2)}) collective-permute-start(f32[256,512]{1,0:T(8,128)S(1)} %pad_maximum_fusion.2.y0_ref), channel_id=1, source_target_pairs={{0,1},{1,2},{2,3},{3,0},{4,5},{5,6},{6,7},{7,4},{8,9},{9,10},{10,1... | collective-permute-start | bytes 1572872 | tf_op jit(solution)/shard_map/ppermute | solution.py:442
  62.8 58.3 %collective-permute-start.16 = (f32[512,512]{1,0:T(8,128)S(1)}, f32[512,512]{1,0:T(8,128)S(1)}, u32[]{:S(2)}, u32[]{:S(2)}) collective-permute-start(f32[512,512]{1,0:T(8,128)S(1)} %constant_dynamic-update-slice_fusion.nl_ref), channel_id=1, source_target_pairs={{8,12},{9,13},{10,14},{11,15},{12,8},{13,9},{14,10},{15,11},{24,28... | collective-permute-start | bytes 3145736 | tf_op jit(solution)/shard_map/ppermute | solution.py:446
  63.7 37.1 %collective-permute-start.6 = (f32[256,512]{1,0:T(8,128)S(1)}, f32[256,512]{1,0:T(8,128)S(1)}, u32[]{:S(2)}, u32[]{:S(2)}) collective-permute-start(f32[256,512]{1,0:T(8,128)S(1)} %pad_maximum_fusion.1.p0_ref), channel_id=1, source_target_pairs={{0,1},{1,2},{2,3},{3,0},{4,5},{5,6},{6,7},{7,4},{8,9},{9,10},{10,1... | collective-permute-start | bytes 1572872 | tf_op jit(solution)/shard_map/ppermute | solution.py:442
  70.1 30.7 %collective-permute-start.7 = (f32[256,512]{1,0:T(8,128)S(1)}, f32[256,512]{1,0:T(8,128)S(1)}, u32[]{:S(2)}, u32[]{:S(2)}) collective-permute-start(f32[256,512]{1,0:T(8,128)S(1)} %pad_maximum_fusion.1.p0_ref), channel_id=1, source_target_pairs={{0,2},{1,3},{2,0},{3,1},{4,6},{5,7},{6,4},{7,5},{8,10},{9,11},{10,... | collective-permute-start | bytes 1572872 | tf_op jit(solution)/shard_map/ppermute | solution.py:442
  81.3 20.3 %collective-permute-start.8 = (f32[256,512]{1,0:T(8,128)S(1)}, f32[256,512]{1,0:T(8,128)S(1)}, u32[]{:S(2)}, u32[]{:S(2)}) collective-permute-start(f32[256,512]{1,0:T(8,128)S(1)} %pad_maximum_fusion.1.p0_ref), channel_id=1, source_target_pairs={{0,3},{1,0},{2,1},{3,2},{4,7},{5,4},{6,5},{7,6},{8,11},{9,8},{10,9... | collective-permute-start | bytes 1572872 | tf_op jit(solution)/shard_map/ppermute | solution.py:442
  101.6 19.4 %collective-permute-start.15 = (f32[512,512]{1,0:T(8,128)S(1)}, f32[512,512]{1,0:T(8,128)S(1)}, u32[]{:S(2)}, u32[]{:S(2)}) collective-permute-start(f32[512,512]{1,0:T(8,128)S(1)} %pad_maximum_fusion.nf_ref), channel_id=1, source_target_pairs={{8,12},{9,13},{10,14},{11,15},{12,8},{13,9},{14,10},{15,11},{24,28... | collective-permute-start | bytes 3145736 | tf_op jit(solution)/shard_map/ppermute | solution.py:446
  102.5 18.5 %copy-start.3 = (f32[128,1024]{1,0:T(8,128)S(1)}, f32[128,1024]{1,0:T(8,128)}, u32[]{:S(2)}) copy-start(f32[128,1024]{1,0:T(8,128)} %copy-done.2) | copy-start | bytes 1572868
  132.6 18.5 %collective-permute-start.17 = (f32[64,1024]{1,0:T(8,128)S(1)}, f32[64,1024]{1,0:T(8,128)S(1)}, u32[]{:S(2)}, u32[]{:S(2)}) collective-permute-start(f32[64,1024]{1,0:T(8,128)S(1)} %slice.46), channel_id=1, source_target_pairs={{8,4},{9,5},{10,6},{11,7},{12,0},{13,1},{14,2},{15,3},{24,20},{25,... | collective-permute-start | bytes 786440 | tf_op jit(solution)/shard_map/ppermute | solution.py:446

commit v10 on v9

--- a/solution.py
+++ b/solution.py
@@ -348,56 +348,98 @@
     )(index, *parts, *state, rhs)
 
 
-def third_kernel(idx_ref, nf_ref, nl_ref, ff_ref, fl_ref, lh, ll, t_ref, dinv_ref, y_ref, own_ref, tail_ref, b_ref,
-                 fac_ref, eli_ref, a21, xh, xl, x32, wh, wl, sem):
+def place_rows(me, near_ref, far_ref, a21, sem):
+    ypos, zpos = lax.rem(me, 4), jnp.clip(me // 4 - 2, 0, 1)
+    copies = []
+    for n, (ref, z) in enumerate(((near_ref, zpos), (far_ref, 1 - zpos))):
+        for d in range(4):
+            rows = pl.ds(pl.multiple_of((4 * z + lax.rem(ypos + 4 - d, 4)) * B, B), B)
+            copies.append(pltpu.make_async_copy(ref.at[pl.ds(d * B, B), :], a21.at[rows, :], sem.at[4 * n + d]))
+    for copy in copies:
+        copy.start()
+    return copies
+
+
+def pair_inverse(i, lh, ll, t_ref):
+    t0h, t0l = split(t_ref[2 * i])
+    t1h, t1l = split(t_ref[2 * i + 1])
+    r1 = slice((2 * i + 1) * B, (2 * i + 2) * B)
+    c0 = slice(2 * i * B, (2 * i + 1) * B)
+    zh, zl = split(dot3_n(lh[r1, c0], ll[r1, c0], t0h, t0l))
+    zh, zl = split(-dot3_n(t1h, t1l, zh, zl))
+    zero = jnp.zeros((B, B), BF16)
+    return cat_blocks(t0h, zero, zh, t1h), cat_blocks(t0l, zero, zl, t1l)
+
+
+def solve_half(half, inverses, a21, known, lh, ll, dinv_ref, xh, xl, x32, wh, wl):
+    base = half * HALF
+    for i in range(2):
+        lc, pc = slice(i * W2, (i + 1) * W2), slice(base + i * W2, base + (i + 1) * W2)
+        u = a21[:, lc]
+        if known:
+            u = u - dot3_t(known[0][...], known[1][...], lh[pc, :HALF], ll[pc, :HALF])
+        if i:
+            u = u - dot3_t(xh[:, :W2], xl[:, :W2], lh[pc, base : base + W2], ll[pc, base : base + W2])
+        uh, ul = split(u)
+        v = dot3_t(uh, ul, *inverses[i])
+        x32[:, lc] = v
+        xh[:, lc], xl[:, lc] = split(v)
+        wh[:, lc], wl[:, lc] = split(v * dinv_ref[0:1, pc])
+
+
+def third_kernel(idx_ref, near_ref, far_ref, lh, ll, t_ref, dinv_ref, xh, xl, wh, wl, own_ref, a21, x32, sem):
+    me = idx_ref[0]
+    copies = place_rows(me, near_ref, far_ref, a21, sem)
+    inverses = [pair_inverse(i, lh, ll, t_ref) for i in range(2)]
+    for copy in copies:
+        copy.wait()
+    solve_half(0, inverses, a21, None, lh, ll, dinv_ref, xh, xl, x32, wh, wl)
+    mine = pl.ds(pl.multiple_of(jnp.maximum(me - NP, 0) * B, B), B)
+    own_ref[...] = x32[mine, :] * dinv_ref[0:1, :HALF]
+
+
+def third(index, near, far, state):
+    low = 2 * near.shape[0]
+    outs = (((low, HALF), BF16),) * 4 + (((B, HALF), F32),)
+    return pl.pallas_call(
+        third_kernel,
+        out_shape=tuple(jax.ShapeDtypeStruct(*o) for o in outs),
+        in_specs=[pl.BlockSpec(memory_space=pltpu.SMEM)] + [VMEM_SPEC] * 6,
+        out_specs=(VMEM_SPEC,) * len(outs),
+        scratch_shapes=[
+            pltpu.VMEM((low, HALF), F32),
+            pltpu.VMEM((low, HALF), F32),
+            pltpu.SemaphoreType.DMA((8,)),
+        ],
+        compiler_params=pltpu.CompilerParams(vmem_limit_bytes=16 * 1024 * 1024),
+        cost_estimate=pl.CostEstimate(flops=5 * 10**9, bytes_accessed=10**7, transcendentals=0),
+        name="third",
+    )(index, near, far, *state[:4])
+
+
+def fourth_kernel(idx_ref, near_ref, far_ref, xh0, xl0, wh0, wl0, lown_ref, lh, ll, t_ref, dinv_ref, y_ref, own_ref,
+                  tail_ref, b_ref, fac_ref, eli_ref, a21, xh, xl, x32, wh, wl, sem):
     me = idx_ref[0]
     nrhs, order = b_ref.shape
     low = order - PIV
-    ypos, zpos = lax.rem(me, 4), jnp.clip(me // 4 - 2, 0, 1)
-    copies = []
-    for n, (ref, z, c) in enumerate(((nf_ref, zpos, 0), (ff_ref, 1 - zpos, 0), (nl_ref, zpos, HALF), (fl_ref, 1 - zpos, HALF))):
-        for d in range(4):
-            rows = pl.ds(pl.multiple_of((4 * z + lax.rem(ypos + 4 - d, 4)) * B, B), B)
-            copies.append(pltpu.make_async_copy(
-                ref.at[pl.ds(d * B, B), :], a21.at[rows, pl.ds(c, HALF)], sem.at[4 * n + d]))
-    for copy in copies:
-        copy.start()
-
-    inverses = []
-    for i in range(NP // 2):
-        t0h, t0l = split(t_ref[2 * i])
-        t1h, t1l = split(t_ref[2 * i + 1])
-        r1 = slice((2 * i + 1) * B, (2 * i + 2) * B)
-        c0 = slice(2 * i * B, (2 * i + 1) * B)
-        zh, zl = split(dot3_n(lh[r1, c0], ll[r1, c0], t0h, t0l))
-        zh, zl = split(-dot3_n(t1h, t1l, zh, zl))
-        zero = jnp.zeros((B, B), BF16)
-        inverses.append((cat_blocks(t0h, zero, zh, t1h), cat_blocks(t0l, zero, zl, t1l)))
+    copies = place_rows(me, near_ref, far_ref, a21, sem)
+    inverses = [pair_inverse(i, lh, ll, t_ref) for i in range(2, 4)]
     for copy in copies:
         copy.wait()
-    for i in range(NP // 2):
-        pc, prev = slice(i * W2, (i + 1) * W2), slice(0, i * W2)
-        u = a21[:, pc]
-        if i:
-            u = u - dot3_t(xh[:, prev], xl[:, prev], lh[pc, prev], ll[pc, prev])
-        uh, ul = split(u)
-        v = dot3_t(uh, ul, *inverses[i])
-        x32[:, pc] = v
-        xh[:, pc], xl[:, pc] = split(v)
-        wh[:, pc], wl[:, pc] = split(v * dinv_ref[0:1, pc])
-
+    solve_half(1, inverses, a21, (xh0, xl0), lh, ll, dinv_ref, xh, xl, x32, wh, wl)
     y = y_ref[...]
     yh, yl = split(y)
     eli_ref[:, :PIV] = y
     mine = pl.ds(pl.multiple_of(jnp.maximum(me - NP, 0) * B, B), B)
     n = B + nrhs
-    qh = jnp.concatenate([xh[mine, :], yh], 0)
-    both = jnp.concatenate([qh, xl[mine, :], yl], 0)
+    hi = [jnp.concatenate([x[mine, :], yh[:, c]], 0) for x, c in ((xh0, slice(0, HALF)), (xh, slice(HALF, PIV)))]
+    lo = [jnp.concatenate([x[mine, :], yl[:, c]], 0) for x, c in ((xl0, slice(0, HALF)), (xl, slice(HALF, PIV)))]
+    both = [jnp.concatenate([h, m], 0) for h, m in zip(hi, lo)]
     for c in range(low // W2):
         rows = slice(c * W2, (c + 1) * W2)
         dst = slice(PIV + c * W2, PIV + (c + 1) * W2)
-        prod = dot_t(both, wh[rows, :])
-        prod = prod[:n] + prod[n:] + dot_t(qh, wl[rows, :])
+        prod = dot_t(both[0], wh0[rows, :]) + dot_t(both[1], wh[rows, :])
+        prod = prod[:n] + prod[n:] + dot_t(hi[0], wl0[rows, :]) + dot_t(hi[1], wl[rows, :])
         row = me * B + lax.broadcasted_iota(jnp.int32, (B, W2), 0)
         col = PIV + c * W2 + lax.broadcasted_iota(jnp.int32, (B, W2), 1)
         fac_ref[:, dst] = jnp.where(row >= col, tail_ref[:, rows] - prod[:B], 0.0)
@@ -406,36 +448,37 @@
 
     @pl.when(lower)
     def _():
-        fac_ref[:, :PIV] = x32[mine, :] * dinv_ref[0:1, :]
+        fac_ref[:, :HALF] = lown_ref[...]
+        fac_ref[:, HALF:PIV] = x32[mine, :] * dinv_ref[0:1, HALF:]
 
     @pl.when(jnp.logical_not(lower))
     def _():
         fac_ref[:, :PIV] = own_ref[...]
 
 
-def third(index, lower, state, tail, rhs):
+def fourth(index, near, far, solved, state, tail, rhs):
     nrhs, order = rhs.shape
     low = order - PIV
     return pl.pallas_call(
-        third_kernel,
+        fourth_kernel,
         out_shape=(
             jax.ShapeDtypeStruct((B, order), F32),
             jax.ShapeDtypeStruct((nrhs, order), F32),
         ),
-        in_specs=[pl.BlockSpec(memory_space=pltpu.SMEM)] + [VMEM_SPEC] * (len(lower) + len(state) + 2),
+        in_specs=[pl.BlockSpec(memory_space=pltpu.SMEM)] + [VMEM_SPEC] * (len(solved) + len(state) + 4),
         out_specs=(VMEM_SPEC, VMEM_SPEC),
         scratch_shapes=[
-            pltpu.VMEM((low, PIV), F32),
-            pltpu.VMEM((low, PIV), BF16),
-            pltpu.VMEM((low, PIV), BF16),
-            pltpu.VMEM((low, PIV), F32),
-            pltpu.VMEM((low, PIV), BF16),
-            pltpu.VMEM((low, PIV), BF16),
-            pltpu.SemaphoreType.DMA((16,)),
+            pltpu.VMEM((low, HALF), F32),
+            pltpu.VMEM((low, HALF), BF16),
+            pltpu.VMEM((low, HALF), BF16),
+            pltpu.VMEM((low, HALF), F32),
+            pltpu.VMEM((low, HALF), BF16),
+            pltpu.VMEM((low, HALF), BF16),
+            pltpu.SemaphoreType.DMA((8,)),
         ],
-        compiler_params=pltpu.CompilerParams(vmem_limit_bytes=34 * 1024 * 1024),
-        name="third",
-    )(index, *lower, *state, tail, rhs)
+        compiler_params=pltpu.CompilerParams(vmem_limit_bytes=24 * 1024 * 1024),
+        name="fourth",
+    )(index, near, far, *solved, *state, tail, rhs)
 
 
 def shift_y(x, d, zs=(0, 1, 2, 3)):
@@ -469,20 +512,20 @@
     swap = planes(early, ((0, 1), (1, 0)))
     side = planes(early, ((1, 2), (0, 3)))
     cross = planes(early, ((0, 2), (1, 3)))
-    near_last = jnp.concatenate(ring_y(late, (2, 3)), 0)
+    near_first = jnp.concatenate(ring_y(early, (2, 3)), 0)
     early_parts = ring_y(jnp.concatenate([pick(z, early, swap, cross, side), pick(z, swap, early, side, cross)], 0))
     late_x, _ = lax.optimization_barrier((late, (swap, side, cross)))
     to0, to2, to3 = (planes(late_x, ((1, d),)) for d in (0, 2, 3))
-    far_last = planes(near_last, ((2, 3), (3, 2)))
-    mixed = jnp.concatenate([pick(z, to0, late_x, to2, to3), early], 0)
+    far_first = planes(near_first, ((2, 3), (3, 2)))
+    mixed = jnp.concatenate([pick(z, to0, late_x, to2, to3), late], 0)
     late_parts = ring_y(mixed)
     state = first(index, early_parts, rhs)
-    near_first = jnp.concatenate([part[B:] for part in late_parts], 0)
-    near_first, _ = lax.optimization_barrier((near_first, state[6]))
-    far_first = planes(near_first, ((2, 3), (3, 2)))
+    near_last = jnp.concatenate([part[B:] for part in late_parts], 0)
+    near_last, _ = lax.optimization_barrier((near_last, state[6]))
+    far_last = planes(near_last, ((2, 3), (3, 2)))
     state = second(index, late_parts, state, rhs)
-    lower = [near_first, near_last, far_first, far_last]
-    factored, eliminated = third(index, lower, state, tail, rhs)
+    solved = third(index, near_first, far_first, state)
+    factored, eliminated = fourth(index, near_last, far_last, solved, state, tail, rhs)
     tail = eliminated[:, PIV:]
     tail = jnp.where(z < 2, planes(tail, ((2, 1), (3, 0))), tail)
     eliminated = jnp.concatenate([eliminated[:, :PIV], tail], 1)

time: 153 us -> 151 us (0.987)
  waiting for transfers between devices: 65 us -> 61.9 us
    ppermute x9, waiting for transfers between devices: 28.4 us -> 23.6 us  [planes(): lax.ppermute(x, 'front', [(4 * a + y, 4 * b + y) for a, b in pairs for y...]
    ppermute x9, waiting for transfers between devices: 14.6 us -> 16.4 us  [shift_y(): lax.ppermute(x, 'front', [(4 * z + y, 4 * z + (y + d) % 4) for z in zs fo...]
    pallas_call x1 -> x2, Pallas kernels: 11.5 us -> 11.3 us  [the longest x1 8.47 us: fourth(): pl.pallas_call(fourth_kernel, out_shape=(jax.ShapeDtypeStruct((B, order),...]
  transfers between devices with their start and end apart: 19 -> 19, of which waited for: 8 -> 8; matrix products, arithmetic and copies ran while one was open for 0% -> 1% of each run, Pallas kernels for 24% -> 27%
where the time goes in v10:
time: 151 us; the launch traced here: 150 us
  waiting for transfers between devices  61.9 us (41%)
  Pallas kernels  50.1 us (33%)
  starting transfers between devices  30 us (20%)
  other arithmetic  5.62 us (4%)
    ppermute x9, waiting for transfers between devices, planes(): lax.ppermute(x, 'front', [(4 * a + y, 4 * b + y) for a, b in pairs for y...  23.6 us
    all_to_all x1, waiting for transfers between devices, local(): lax.all_to_all(payload, 'leaf', split_axis=0, concat_axis=0, tiled=True)  21.9 us
    pallas_call x1, Pallas kernels, first(): pl.pallas_call(first_kernel, out_shape=tuple((jax.ShapeDtypeStruct(*o) fo...  18.5 us
    pallas_call x1, Pallas kernels, second(): pl.pallas_call(second_kernel, out_shape=tuple((jax.ShapeDtypeStruct(*o) f...  18.5 us
    ppermute x9, waiting for transfers between devices, shift_y(): lax.ppermute(x, 'front', [(4 * z + y, 4 * z + (y + d) % 4) for z in zs fo...  16.4 us
    ppermute x9, starting transfers between devices, planes(): lax.ppermute(x, 'front', [(4 * a + y, 4 * b + y) for a, b in pairs for y...  13.5 us
    ppermute x9, starting transfers between devices, shift_y(): lax.ppermute(x, 'front', [(4 * z + y, 4 * z + (y + d) % 4) for z in zs fo...  12.1 us
    pallas_call x1, Pallas kernels, fourth(): pl.pallas_call(fourth_kernel, out_shape=(jax.ShapeDtypeStruct((B, order),...  8.47 us
  transfers between devices with their start and end apart: 19, of which 8 were waited for; matrix products, arithmetic and copies ran while one was open for 1% of the time, Pallas kernels for 27%

profile of v10, /device:TPU:8, one launch (start us, length us, event | category | flops | bytes accessed | tf_op | source)
XLA Modules:
  0.0 149.6 jit_solution(13464517649755630554)
XLA Ops:
  0.6 0.8 copy.10
  1.4 0.7 fusion
  2.1 2.7 %select_maximum_fusion = f32[8,392,128]{2,1,0:T(8,128)} fusion(f32[8,1,3]{2,1,0:T(1,128)S(1)} %fusion, f32[8,384,128]{2,1,0:T(8,128)} %bitcast.15), kind=kLoop, calls=%fused_computation | loop fusion | flops 1204224 | bytes 3178592 | tf_op jit(solution)/shard_map/concatenate | solution.py:505
  4.8 4.4 %all-to-all-start = ((f32[8,392,128]{2,1,0:T(8,128)}), f32[8,392,128]{2,1,0:T(8,128)S(1)}, u32[]{:S(2)}, u32[]{:S(2)}) async-start(f32[8,392,128]{2,1,0:T(8,128)} %select_maximum_fusion), calls=%async_computation | async-start | bytes 3211264 | tf_op jit(solution)/shard_map/all_to_all | solution.py:506
  9.3 21.9 %all-to-all-done.recv_ref = f32[8,392,128]{2,1,0:T(8,128)S(1)} async-done(((f32[8,392,128]{2,1,0:T(8,128)}), f32[8,392,128]{2,1,0:T(8,128)S(1)}, u32[]{:S(2)}, u32[]{:S(2)}) %all-to-all-start) | async-done | bytes 1605664 | tf_op jit(solution)/shard_map/all_to_all | solution.py:506
  31.2 1.8 %assemble.1 = (f32[128,1024]{1,0:T(8,128)S(1)}, f32[128,512]{1,0:T(8,128)}, f32[128,512]{1,0:T(8,128)S(1)}) custom-call(s32[8,3]{1,0:T(8,128)S(1)} %bitcast.14, s32[1]{0:T(128)} %bitcast.idx_ref, f32[8,392,128]{2,1,0:T(8,128)S(1)} %all-to-all-done.recv_ref, f32[128,2048]{1,0:T(8,128)S(1)} %bitcast.10), custom_call_target="tpu_custom_call" | custom-call | tf_op jit(solution)/shard_map/assemble/pallas_call | solution.py:63
  33.0 3.8 %collective-permute-start = (f32[128,512]{1,0:T(8,128)}, f32[128,512]{1,0:T(8,128)S(1)}, u32[]{:S(2)}, u32[]{:S(2)}) collective-permute-start(f32[128,512]{1,0:T(8,128)} %get-tuple-element.41), channel_id=1, source_target_pairs={{0,4},{1,5},{2,6},{3,7},{4,0},{5,1},{6,2},{7,3},{16,20},{17,21},{1... | collective-permute-start | bytes 786440 | tf_op jit(solution)/shard_map/ppermute | solution.py:489
  36.9 2.8 %collective-permute-start.1 = (f32[128,512]{1,0:T(8,128)}, f32[128,512]{1,0:T(8,128)S(1)}, u32[]{:S(2)}, u32[]{:S(2)}) collective-permute-start(f32[128,512]{1,0:T(8,128)} %get-tuple-element.41), channel_id=1, source_target_pairs={{4,8},{5,9},{6,10},{7,11},{0,12},{1,13},{2,14},{3,15},{20,24},{21,... | collective-permute-start | bytes 786440 | tf_op jit(solution)/shard_map/ppermute | solution.py:489
  39.7 1.3 collective-permute-start.2
  41.0 0.7 collective-permute-start.13
  41.7 0.7 collective-permute-start.14
  42.4 1.7 %collective-permute-done = f32[128,512]{1,0:T(8,128)S(1)} collective-permute-done((f32[128,512]{1,0:T(8,128)}, f32[128,512]{1,0:T(8,128)S(1)}, u32[]{:S(2)}, u32[]{:S(2)}) %collective-permute-start) | collective-permute-done | bytes 262176 | tf_op jit(solution)/shard_map/ppermute | solution.py:489
  44.1 0.7 collective-permute-start.15
  44.7 6.2 %collective-permute-done.1 = f32[128,512]{1,0:T(8,128)S(1)} collective-permute-done((f32[128,512]{1,0:T(8,128)}, f32[128,512]{1,0:T(8,128)S(1)}, u32[]{:S(2)}, u32[]{:S(2)}) %collective-permute-start.1) | collective-permute-done | bytes 262176 | tf_op jit(solution)/shard_map/ppermute | solution.py:489
  50.9 0.0 collective-permute-done.2
  50.9 1.3 collective-permute-start.3
  52.2 0.7 collective-permute-start.4
  52.9 1.1 select_select_fusion.1
  54.0 0.0 collective-permute-done.13
  54.0 0.7 collective-permute-start.5
  54.7 0.0 copy-start.1
  54.8 0.0 collective-permute-done.14
  54.8 2.4 %collective-permute-start.10 = (f32[256,512]{1,0:T(8,128)S(1)}, f32[256,512]{1,0:T(8,128)S(1)}, u32[]{:S(2)}, u32[]{:S(2)}) collective-permute-start(f32[256,512]{1,0:T(8,128)S(1)} %pad_maximum_fusion.2.y0_ref), channel_id=1, source_target_pairs={{0,2},{1,3},{2,0},{3,1},{4,6},{5,7},{6,4},{7,5},{8,10},{9,11},{10,... | collective-permute-start | bytes 1572872 | tf_op jit(solution)/shard_map/ppermute | solution.py:485
  57.2 0.0 collective-permute-done.15
  57.2 1.3 collective-permute-start.11
  58.5 1.9 %collective-permute-done.3 = f32[128,512]{1,0:T(8,128)S(1)} collective-permute-done((f32[128,512]{1,0:T(8,128)S(1)}, f32[128,512]{1,0:T(8,128)S(1)}, u32[]{:S(2)}, u32[]{:S(2)}) %collective-permute-start.3) | collective-permute-done | bytes 262176 | tf_op jit(solution)/shard_map/ppermute | solution.py:489
  60.4 1.7 %collective-permute-start.9 = (f32[256,512]{1,0:T(8,128)S(1)}, f32[256,512]{1,0:T(8,128)S(1)}, u32[]{:S(2)}, u32[]{:S(2)}) collective-permute-start(f32[256,512]{1,0:T(8,128)S(1)} %pad_maximum_fusion.2.y0_ref), channel_id=1, source_target_pairs={{0,1},{1,2},{2,3},{3,0},{4,5},{5,6},{6,7},{7,4},{8,9},{9,10},{10,1... | collective-permute-start | bytes 1572872 | tf_op jit(solution)/shard_map/ppermute | solution.py:485
  62.1 0.0 collective-permute-done.4
  62.1 0.7 collective-permute-start.16
  62.9 0.1 select_select_fusion.2
  63.0 1.4 collective-permute-start.6
  64.4 6.9 %collective-permute-done.10.y2_ref = f32[256,512]{1,0:T(8,128)S(1)} collective-permute-done((f32[256,512]{1,0:T(8,128)S(1)}, f32[256,512]{1,0:T(8,128)S(1)}, u32[]{:S(2)}, u32[]{:S(2)}) %collective-permute-start.10) | collective-permute-done | bytes 524320 | tf_op jit(solution)/shard_map/ppermute | solution.py:485
  71.2 2.3 %collective-permute-start.7 = (f32[256,512]{1,0:T(8,128)S(1)}, f32[256,512]{1,0:T(8,128)S(1)}, u32[]{:S(2)}, u32[]{:S(2)}) collective-permute-start(f32[256,512]{1,0:T(8,128)S(1)} %pad_maximum_fusion.1.p0_ref), channel_id=1, source_target_pairs={{0,2},{1,3},{2,0},{3,1},{4,6},{5,7},{6,4},{7,5},{8,10},{9,11},{10,... | collective-permute-start | bytes 1572872 | tf_op jit(solution)/shard_map/ppermute | solution.py:485
  73.6 8.8 %collective-permute-done.11.y3_ref = f32[256,512]{1,0:T(8,128)S(1)} collective-permute-done((f32[256,512]{1,0:T(8,128)S(1)}, f32[256,512]{1,0:T(8,128)S(1)}, u32[]{:S(2)}, u32[]{:S(2)}) %collective-permute-start.11) | collective-permute-done | bytes 524320 | tf_op jit(solution)/shard_map/ppermute | solution.py:485
  82.4 0.9 collective-permute-start.8
  83.3 0.0 collective-permute-done.9.y1_ref
  83.3 18.5 %first.1 = (bf16[1088,512]{1,0:T(8,128)(2,1)S(1)}, bf16[1088,512]{1,0:T(8,128)(2,1)S(1)}, bf16[1024,512]{1,0:T(8,128)(2,1)S(1)}, bf16[1024,512]{1,0:T(8,128)(2,1...) custom-call(s32[1]{0:T(128)} %bitcast.idx_ref, ...), custom_call_target="tpu_custom_call" | custom-call | flops 20000000000 | bytes 20000000 | tf_op jit(solution)/shard_map/first/pallas_call | solution.py:260
  101.9 0.0 collective-permute-done.6.p1_ref
  101.9 0.7 collective-permute-done.8.p3_ref
  102.7 0.1 pad_maximum_fusion.near_ref
  102.8 0.9 collective-permute-start.12
  103.7 18.5 %second.1 = (bf16[1024,1024]{1,0:T(8,128)(2,1)S(1)}, bf16[1024,1024]{1,0:T(8,128)(2,1)S(1)}, f32[8,128,128]{2,1,0:T(8,128)S(1)}, f32[8,1024]{1,0:T(8,128)S(1)}, ...) custom-call(s32[1]{0:T(128)} %bitcast.idx_ref, f32[256,512]{1,0:T(8,128)S(1)} %pad_maximum_fusion.1.p0_ref, ...), custom_call_target="tpu_custom_call" | custom-call | flops 20000000000 | bytes 20000000 | tf_op jit(solution)/shard_map/second/pallas_call | solution.py:329
  122.2 2.8 %third.1 = (bf16[1024,512]{1,0:T(8,128)(2,1)S(1)}, bf16[1024,512]{1,0:T(8,128)(2,1)S(1)}, bf16[1024,512]{1,0:T(8,128)(2,1)S(1)}, bf16[1024,512]{1,0:T(8,128)(2,1)S(1)}, f32[128,512]{1,0:T(8,128)S(1)}) custom-call(s32[1]{0:T(128)} %bitcast.idx_ref, f32[512,512]{1,0:T(8,128)S(1)} %constant_dynamic-update-slice_fusion.near_ref, ...), custom_call_target="tpu_custom_call" | custom-call | flops 5000000000 | bytes 10000000 | tf_op jit(solution)/shard_map/third/pallas_call | solution.py:404
  125.0 0.0 collective-permute-done.12.far_ref
  125.0 8.5 %fourth.1 = (f32[128,2048]{1,0:T(8,128)}, f32[64,2048]{1,0:T(8,128)S(1)}) custom-call(s32[1]{0:T(128)} %bitcast.idx_ref, f32[512,512]{1,0:T(8,128)S(1)} %pad_maximum_fusion.near_ref, f32[512,512]{1,0:T(8,128)S(1)} %collective-permute-done.12.far_ref, bf16[1024,512]{1,0:T(8,128)(2,1)S(1)} %get-tuple-element.56.xh0, ...), custom_call_target="tpu_custom_call" | custom-call | tf_op jit(solution)/shard_map/fourth/pallas_call | solution.py:462
  133.6 1.3 collective-permute-start.17
  134.9 13.8 %collective-permute-done.17 = f32[64,1024]{1,0:T(8,128)S(1)} collective-permute-done((f32[64,1024]{1,0:T(8,128)S(1)}, f32[64,1024]{1,0:T(8,128)S(1)}, u32[]{:S(2)}, u32[]{:S(2)}) %collective-permute-start.17) | collective-permute-done | bytes 262176 | tf_op jit(solution)/shard_map/ppermute | solution.py:489
  148.7 0.8 maximum_bitcast_fusion
  (17 shorter events, 0.3 us)
Async XLA Ops:
  4.8 26.4 %copy-start = (f32[1,128,2048]{2,1,0:T(8,128)S(1)}, f32[1,128,2048]{2,1,0:T(8,128)}, u32[]{:S(2)}) copy-start(f32[1,128,2048]{2,1,0:T(8,128)} %param.7) | copy-start | bytes 3145732
  4.8 26.4 %all-to-all-start = ((f32[8,392,128]{2,1,0:T(8,128)}), f32[8,392,128]{2,1,0:T(8,128)S(1)}, u32[]{:S(2)}, u32[]{:S(2)}) async-start(f32[8,392,128]{2,1,0:T(8,128)} %select_maximum_fusion), calls=%async_computation | async-start | bytes 3211264 | tf_op jit(solution)/shard_map/all_to_all | solution.py:506
  33.0 11.0 %collective-permute-start = (f32[128,512]{1,0:T(8,128)}, f32[128,512]{1,0:T(8,128)S(1)}, u32[]{:S(2)}, u32[]{:S(2)}) collective-permute-start(f32[128,512]{1,0:T(8,128)} %get-tuple-element.41), channel_id=1, source_target_pairs={{0,4},{1,5},{2,6},{3,7},{4,0},{5,1},{6,2},{7,3},{16,20},{17,21},{1... | collective-permute-start | bytes 786440 | tf_op jit(solution)/shard_map/ppermute | solution.py:489
  36.9 14.1 %collective-permute-start.1 = (f32[128,512]{1,0:T(8,128)}, f32[128,512]{1,0:T(8,128)S(1)}, u32[]{:S(2)}, u32[]{:S(2)}) collective-permute-start(f32[128,512]{1,0:T(8,128)} %get-tuple-element.41), channel_id=1, source_target_pairs={{4,8},{5,9},{6,10},{7,11},{0,12},{1,13},{2,14},{3,15},{20,24},{21,... | collective-permute-start | bytes 786440 | tf_op jit(solution)/shard_map/ppermute | solution.py:489
  39.7 11.3 %collective-permute-start.2 = (f32[128,512]{1,0:T(8,128)}, f32[128,512]{1,0:T(8,128)S(1)}, u32[]{:S(2)}, u32[]{:S(2)}) collective-permute-start(f32[128,512]{1,0:T(8,128)} %get-tuple-element.41), channel_id=1, source_target_pairs={{0,8},{1,9},{2,10},{3,11},{4,12},{5,13},{6,14},{7,15},{16,24},{17,... | collective-permute-start | bytes 786440 | tf_op jit(solution)/shard_map/ppermute | solution.py:489
  41.0 13.0 %collective-permute-start.13 = (f32[128,512]{1,0:T(8,128)}, f32[128,512]{1,0:T(8,128)S(1)}, u32[]{:S(2)}, u32[]{:S(2)}) collective-permute-start(f32[128,512]{1,0:T(8,128)} %get-tuple-element.41), channel_id=1, source_target_pairs={{8,9},{9,10},{10,11},{11,8},{12,13},{13,14},{14,15},{15,12},{24,25... | collective-permute-start | bytes 786440 | tf_op jit(solution)/shard_map/ppermute | solution.py:485
  41.7 13.1 %collective-permute-start.14 = (f32[128,512]{1,0:T(8,128)}, f32[128,512]{1,0:T(8,128)S(1)}, u32[]{:S(2)}, u32[]{:S(2)}) collective-permute-start(f32[128,512]{1,0:T(8,128)} %get-tuple-element.41), channel_id=1, source_target_pairs={{8,10},{9,11},{10,8},{11,9},{12,14},{13,15},{14,12},{15,13},{24,26... | collective-permute-start | bytes 786440 | tf_op jit(solution)/shard_map/ppermute | solution.py:485
  44.1 13.1 %collective-permute-start.15 = (f32[128,512]{1,0:T(8,128)}, f32[128,512]{1,0:T(8,128)S(1)}, u32[]{:S(2)}, u32[]{:S(2)}) collective-permute-start(f32[128,512]{1,0:T(8,128)} %get-tuple-element.41), channel_id=1, source_target_pairs={{8,11},{9,8},{10,9},{11,10},{12,15},{13,12},{14,13},{15,14},{24,27... | collective-permute-start | bytes 786440 | tf_op jit(solution)/shard_map/ppermute | solution.py:485
  50.9 9.5 %collective-permute-start.3 = (f32[128,512]{1,0:T(8,128)S(1)}, f32[128,512]{1,0:T(8,128)S(1)}, u32[]{:S(2)}, u32[]{:S(2)}) collective-permute-start(f32[128,512]{1,0:T(8,128)S(1)} %get-tuple-element.42), channel_id=1, source_target_pairs={{4,0},{5,1},{6,2},{7,3},{20,16},{21,17},{22,18},{23,19},{36,32},{3... | collective-permute-start | bytes 786440 | tf_op jit(solution)/shard_map/ppermute | solution.py:489
  52.2 9.9 %collective-permute-start.4 = (f32[128,512]{1,0:T(8,128)S(1)}, f32[128,512]{1,0:T(8,128)S(1)}, u32[]{:S(2)}, u32[]{:S(2)}) collective-permute-start(f32[128,512]{1,0:T(8,128)S(1)} %get-tuple-element.42), channel_id=1, source_target_pairs={{4,8},{5,9},{6,10},{7,11},{20,24},{21,25},{22,26},{23,27},{36,40},... | collective-permute-start | bytes 786440 | tf_op jit(solution)/shard_map/ppermute | solution.py:489
  54.0 8.8 %collective-permute-start.5 = (f32[128,512]{1,0:T(8,128)S(1)}, f32[128,512]{1,0:T(8,128)S(1)}, u32[]{:S(2)}, u32[]{:S(2)}) collective-permute-start(f32[128,512]{1,0:T(8,128)S(1)} %get-tuple-element.42), channel_id=1, source_target_pairs={{4,12},{5,13},{6,14},{7,15},{20,28},{21,29},{22,30},{23,31},{36,44... | collective-permute-start | bytes 786440 | tf_op jit(solution)/shard_map/ppermute | solution.py:489
  54.7 28.6 %copy-start.1 = (f32[1,64,2048]{2,1,0:T(8,128)S(1)}, f32[1,64,2048]{2,1,0:T(8,128)}, u32[]{:S(2)}) copy-start(f32[1,64,2048]{2,1,0:T(8,128)} %param.11) | copy-start | bytes 1572868
  54.8 16.5 %collective-permute-start.10 = (f32[256,512]{1,0:T(8,128)S(1)}, f32[256,512]{1,0:T(8,128)S(1)}, u32[]{:S(2)}, u32[]{:S(2)}) collective-permute-start(f32[256,512]{1,0:T(8,128)S(1)} %pad_maximum_fusion.2.y0_ref), channel_id=1, source_target_pairs={{0,2},{1,3},{2,0},{3,1},{4,6},{5,7},{6,4},{7,5},{8,10},{9,11},{10,... | collective-permute-start | bytes 1572872 | tf_op jit(solution)/shard_map/ppermute | solution.py:485
  57.2 25.2 %collective-permute-start.11 = (f32[256,512]{1,0:T(8,128)S(1)}, f32[256,512]{1,0:T(8,128)S(1)}, u32[]{:S(2)}, u32[]{:S(2)}) collective-permute-start(f32[256,512]{1,0:T(8,128)S(1)} %pad_maximum_fusion.2.y0_ref), channel_id=1, source_target_pairs={{0,3},{1,0},{2,1},{3,2},{4,7},{5,4},{6,5},{7,6},{8,11},{9,8},{10,9... | collective-permute-start | bytes 1572872 | tf_op jit(solution)/shard_map/ppermute | solution.py:485
  60.4 22.9 %collective-permute-start.9 = (f32[256,512]{1,0:T(8,128)S(1)}, f32[256,512]{1,0:T(8,128)S(1)}, u32[]{:S(2)}, u32[]{:S(2)}) collective-permute-start(f32[256,512]{1,0:T(8,128)S(1)} %pad_maximum_fusion.2.y0_ref), channel_id=1, source_target_pairs={{0,1},{1,2},{2,3},{3,0},{4,5},{5,6},{6,7},{7,4},{8,9},{9,10},{10,1... | collective-permute-start | bytes 1572872 | tf_op jit(solution)/shard_map/ppermute | solution.py:485
  62.1 60.1 %collective-permute-start.16 = (f32[512,512]{1,0:T(8,128)S(1)}, f32[512,512]{1,0:T(8,128)S(1)}, u32[]{:S(2)}, u32[]{:S(2)}) collective-permute-start(f32[512,512]{1,0:T(8,128)S(1)} %constant_dynamic-update-slice_fusion.near_ref), channel_id=1, source_target_pairs={{8,12},{9,13},{10,14},{11,15},{12,8},{13,9},{14,10},{15,11},{24,28... | collective-permute-start | bytes 3145736 | tf_op jit(solution)/shard_map/ppermute | solution.py:489
  63.0 38.9 %collective-permute-start.6 = (f32[256,512]{1,0:T(8,128)S(1)}, f32[256,512]{1,0:T(8,128)S(1)}, u32[]{:S(2)}, u32[]{:S(2)}) collective-permute-start(f32[256,512]{1,0:T(8,128)S(1)} %pad_maximum_fusion.1.p0_ref), channel_id=1, source_target_pairs={{0,1},{1,2},{2,3},{3,0},{4,5},{5,6},{6,7},{7,4},{8,9},{9,10},{10,1... | collective-permute-start | bytes 1572872 | tf_op jit(solution)/shard_map/ppermute | solution.py:485
  71.2 30.7 %collective-permute-start.7 = (f32[256,512]{1,0:T(8,128)S(1)}, f32[256,512]{1,0:T(8,128)S(1)}, u32[]{:S(2)}, u32[]{:S(2)}) collective-permute-start(f32[256,512]{1,0:T(8,128)S(1)} %pad_maximum_fusion.1.p0_ref), channel_id=1, source_target_pairs={{0,2},{1,3},{2,0},{3,1},{4,6},{5,7},{6,4},{7,5},{8,10},{9,11},{10,... | collective-permute-start | bytes 1572872 | tf_op jit(solution)/shard_map/ppermute | solution.py:485
  82.4 20.3 %collective-permute-start.8 = (f32[256,512]{1,0:T(8,128)S(1)}, f32[256,512]{1,0:T(8,128)S(1)}, u32[]{:S(2)}, u32[]{:S(2)}) collective-permute-start(f32[256,512]{1,0:T(8,128)S(1)} %pad_maximum_fusion.1.p0_ref), channel_id=1, source_target_pairs={{0,3},{1,0},{2,1},{3,2},{4,7},{5,4},{6,5},{7,6},{8,11},{9,8},{10,9... | collective-permute-start | bytes 1572872 | tf_op jit(solution)/shard_map/ppermute | solution.py:485
  102.8 22.3 %collective-permute-start.12 = (f32[512,512]{1,0:T(8,128)S(1)}, f32[512,512]{1,0:T(8,128)S(1)}, u32[]{:S(2)}, u32[]{:S(2)}) collective-permute-start(f32[512,512]{1,0:T(8,128)S(1)} %pad_maximum_fusion.near_ref), channel_id=1, source_target_pairs={{8,12},{9,13},{10,14},{11,15},{12,8},{13,9},{14,10},{15,11},{24,28... | collective-permute-start | bytes 3145736 | tf_op jit(solution)/shard_map/ppermute | solution.py:489
  133.6 15.1 %collective-permute-start.17 = (f32[64,1024]{1,0:T(8,128)S(1)}, f32[64,1024]{1,0:T(8,128)S(1)}, u32[]{:S(2)}, u32[]{:S(2)}) collective-permute-start(f32[64,1024]{1,0:T(8,128)S(1)} %slice.46), channel_id=1, source_target_pairs={{8,4},{9,5},{10,6},{11,7},{12,0},{13,1},{14,2},{15,3},{24,20},{25,... | collective-permute-start | bytes 786440 | tf_op jit(solution)/shard_map/ppermute | solution.py:489

commit v11 on v10

--- a/solution.py
+++ b/solution.py
@@ -10,6 +10,7 @@
 NP = PIV // B
 HALF = PIV // 2
 W2 = 2 * B
+AHEAD = HALF + B
 F32 = jnp.float32
 BF16 = jnp.bfloat16
 
@@ -36,7 +37,7 @@
     return dot_n(ah, bh) + dot_n(al, bh) + dot_n(ah, bl)
 
 
-def assemble_kernel(code_ref, idx_ref, recv_ref, front_ref, tail_ref, early_ref, late_ref, out_ref):
+def assemble_kernel(code_ref, idx_ref, recv_ref, front_ref, tail_ref, early_ref, late_ref, ahead_ref, out_ref):
     out_ref[...] = front_ref[...]
     for s in range(recv_ref.shape[0]):
         for j in range(code_ref.shape[1]):
@@ -54,6 +55,7 @@
     out_ref[:, cols] = jnp.where(row >= col, square, square.T)
     early_ref[...] = out_ref[:, :HALF]
     late_ref[...] = out_ref[:, HALF:PIV]
+    ahead_ref[...] = out_ref[:, :AHEAD]
     tail_ref[...] = out_ref[:, PIV:]
 
 
@@ -66,9 +68,10 @@
             jax.ShapeDtypeStruct((rows, order - PIV), F32),
             jax.ShapeDtypeStruct((rows, HALF), F32),
             jax.ShapeDtypeStruct((rows, HALF), F32),
+            jax.ShapeDtypeStruct((rows, AHEAD), F32),
         ),
         in_specs=[pl.BlockSpec(memory_space=pltpu.SMEM)] * 2 + [vmem, vmem],
-        out_specs=(vmem, vmem, vmem),
+        out_specs=(vmem, vmem, vmem, vmem),
         scratch_shapes=[pltpu.VMEM((rows, order), F32)],
         compiler_params=pltpu.CompilerParams(vmem_limit_bytes=8 * 1024 * 1024),
         name="assemble",
@@ -285,7 +288,7 @@
     ypos = lax.rem(me, 4)
     for d, ref in enumerate((p0_ref, p1_ref, p2_ref, p3_ref)):
         rows = pl.ds(pl.multiple_of(lax.rem(ypos + 4 - d, 4) * B, B), B)
-        a_ref[rows, :] = ref[:B, :]
+        a_ref[rows, :] = ref[:, :HALF]
     for ref, src in ((vh, vh0), (vl, vl0)):
         ref[:, :HALF] = src[HALF:, :]
         ref[:, HALF:] = jnp.zeros((ref.shape[0], HALF), BF16)
@@ -348,13 +351,15 @@
     )(index, *parts, *state, rhs)
 
 
-def place_rows(me, near_ref, far_ref, a21, sem):
+def place_rows(me, near_ref, far_ref, cols, a21, start, sem):
     ypos, zpos = lax.rem(me, 4), jnp.clip(me // 4 - 2, 0, 1)
+    dst = pl.ds(start, cols.size)
     copies = []
     for n, (ref, z) in enumerate(((near_ref, zpos), (far_ref, 1 - zpos))):
         for d in range(4):
             rows = pl.ds(pl.multiple_of((4 * z + lax.rem(ypos + 4 - d, 4)) * B, B), B)
-            copies.append(pltpu.make_async_copy(ref.at[pl.ds(d * B, B), :], a21.at[rows, :], sem.at[4 * n + d]))
+            copies.append(pltpu.make_async_copy(
+                ref.at[pl.ds(d * B, B), cols], a21.at[rows, dst], sem.at[4 * n + d]))
     for copy in copies:
         copy.start()
     return copies
@@ -389,7 +394,7 @@
 
 def third_kernel(idx_ref, near_ref, far_ref, lh, ll, t_ref, dinv_ref, xh, xl, wh, wl, own_ref, a21, x32, sem):
     me = idx_ref[0]
-    copies = place_rows(me, near_ref, far_ref, a21, sem)
+    copies = place_rows(me, near_ref, far_ref, pl.ds(0, HALF), a21, 0, sem)
     inverses = [pair_inverse(i, lh, ll, t_ref) for i in range(2)]
     for copy in copies:
         copy.wait()
@@ -417,12 +422,13 @@
     )(index, near, far, *state[:4])
 
 
-def fourth_kernel(idx_ref, near_ref, far_ref, xh0, xl0, wh0, wl0, lown_ref, lh, ll, t_ref, dinv_ref, y_ref, own_ref,
+def fourth_kernel(idx_ref, near0_ref, far0_ref, near_ref, far_ref, xh0, xl0, wh0, wl0, lown_ref, lh, ll, t_ref, dinv_ref, y_ref, own_ref,
                   tail_ref, b_ref, fac_ref, eli_ref, a21, xh, xl, x32, wh, wl, sem):
     me = idx_ref[0]
     nrhs, order = b_ref.shape
     low = order - PIV
-    copies = place_rows(me, near_ref, far_ref, a21, sem)
+    copies = place_rows(me, near0_ref, far0_ref, pl.ds(HALF, AHEAD - HALF), a21, 0, sem.at[0])
+    copies += place_rows(me, near_ref, far_ref, pl.ds(0, PIV - AHEAD), a21, AHEAD - HALF, sem.at[1])
     inverses = [pair_inverse(i, lh, ll, t_ref) for i in range(2, 4)]
     for copy in copies:
         copy.wait()
@@ -456,7 +462,7 @@
         fac_ref[:, :PIV] = own_ref[...]
 
 
-def fourth(index, near, far, solved, state, tail, rhs):
+def fourth(index, sent, solved, state, tail, rhs):
     nrhs, order = rhs.shape
     low = order - PIV
     return pl.pallas_call(
@@ -465,7 +471,7 @@
             jax.ShapeDtypeStruct((B, order), F32),
             jax.ShapeDtypeStruct((nrhs, order), F32),
         ),
-        in_specs=[pl.BlockSpec(memory_space=pltpu.SMEM)] + [VMEM_SPEC] * (len(solved) + len(state) + 4),
+        in_specs=[pl.BlockSpec(memory_space=pltpu.SMEM)] + [VMEM_SPEC] * (len(sent) + len(solved) + len(state) + 2),
         out_specs=(VMEM_SPEC, VMEM_SPEC),
         scratch_shapes=[
             pltpu.VMEM((low, HALF), F32),
@@ -474,11 +480,11 @@
             pltpu.VMEM((low, HALF), F32),
             pltpu.VMEM((low, HALF), BF16),
             pltpu.VMEM((low, HALF), BF16),
-            pltpu.SemaphoreType.DMA((8,)),
+            pltpu.SemaphoreType.DMA((2, 8)),
         ],
         compiler_params=pltpu.CompilerParams(vmem_limit_bytes=24 * 1024 * 1024),
         name="fourth",
-    )(index, near, far, *solved, *state, tail, rhs)
+    )(index, *sent, *solved, *state, tail, rhs)
 
 
 def shift_y(x, d, zs=(0, 1, 2, 3)):
@@ -506,26 +512,26 @@
     arrived = lax.all_to_all(payload, "leaf", split_axis=0, concat_axis=0, tiled=True)
     codes = arrived[:, slots * B, :slots].astype(jnp.int32)
     index = lax.axis_index("front").astype(jnp.int32).reshape(1)
-    tail, early, late = assemble(codes, index, arrived, front_matrix[0])
+    tail, early, late, ahead = assemble(codes, index, arrived, front_matrix[0])
     z = lax.axis_index("front") // 4
     rhs = shot_rhs[0]
     swap = planes(early, ((0, 1), (1, 0)))
     side = planes(early, ((1, 2), (0, 3)))
     cross = planes(early, ((0, 2), (1, 3)))
-    near_first = jnp.concatenate(ring_y(early, (2, 3)), 0)
+    near_first = jnp.concatenate(ring_y(ahead, (2, 3)), 0)
     early_parts = ring_y(jnp.concatenate([pick(z, early, swap, cross, side), pick(z, swap, early, side, cross)], 0))
     late_x, _ = lax.optimization_barrier((late, (swap, side, cross)))
     to0, to2, to3 = (planes(late_x, ((1, d),)) for d in (0, 2, 3))
     far_first = planes(near_first, ((2, 3), (3, 2)))
-    mixed = jnp.concatenate([pick(z, to0, late_x, to2, to3), late], 0)
+    mixed = jnp.concatenate([pick(z, to0, late_x, to2, to3), late[:, AHEAD - HALF :]], 1)
     late_parts = ring_y(mixed)
     state = first(index, early_parts, rhs)
-    near_last = jnp.concatenate([part[B:] for part in late_parts], 0)
+    near_last = jnp.concatenate([part[:, HALF:] for part in late_parts], 0)
     near_last, _ = lax.optimization_barrier((near_last, state[6]))
     far_last = planes(near_last, ((2, 3), (3, 2)))
     state = second(index, late_parts, state, rhs)
     solved = third(index, near_first, far_first, state)
-    factored, eliminated = fourth(index, near_last, far_last, solved, state, tail, rhs)
+    factored, eliminated = fourth(index, (near_first, far_first, near_last, far_last), solved, state, tail, rhs)
     tail = eliminated[:, PIV:]
     tail = jnp.where(z < 2, planes(tail, ((2, 1), (3, 0))), tail)
     eliminated = jnp.concatenate([eliminated[:, :PIV], tail], 1)

time: 151 us -> 158 us (1.046)
  waiting for transfers between devices: 61.9 us -> 68.2 us
  local copies, waits for them, and re-layouts: 0.9 us -> 2.64 us
    ppermute x9, waiting for transfers between devices: 23.6 us -> 30.2 us  [planes(): lax.ppermute(x, 'front', [(4 * a + y, 4 * b + y) for a, b in pairs for y...]
    unnamed x6 -> x9, local copies, waits for them, and re-layouts: 0.05 us -> 1.78 us
  transfers between devices with their start and end apart: 19 -> 19, of which waited for: 8 -> 6; matrix products, arithmetic and copies ran while one was open for 1% -> 2% of each run, Pallas kernels for 27% -> 25%
where the time goes in v11:
time: 158 us
  waiting for transfers between devices  68.2 us (43%)
  Pallas kernels  50.6 us (32%)
  starting transfers between devices  29.7 us (19%)
  other arithmetic  5.61 us (4%)
  local copies, waits for them, and re-layouts  2.64 us (2%)
    ppermute x9, waiting for transfers between devices, planes(): lax.ppermute(x, 'front', [(4 * a + y, 4 * b + y) for a, b in pairs for y...  30.2 us
    all_to_all x1, waiting for transfers between devices, local(): lax.all_to_all(payload, 'leaf', split_axis=0, concat_axis=0, tiled=True)  21.9 us
    pallas_call x1, Pallas kernels, first(): pl.pallas_call(first_kernel, out_shape=tuple((jax.ShapeDtypeStruct(*o) fo...  18.8 us
    pallas_call x1, Pallas kernels, second(): pl.pallas_call(second_kernel, out_shape=tuple((jax.ShapeDtypeStruct(*o) f...  18.3 us
    ppermute x9, waiting for transfers between devices, shift_y(): lax.ppermute(x, 'front', [(4 * z + y, 4 * z + (y + d) % 4) for z in zs fo...  16 us
    ppermute x9, starting transfers between devices, planes(): lax.ppermute(x, 'front', [(4 * a + y, 4 * b + y) for a, b in pairs for y...  13.6 us
    ppermute x9, starting transfers between devices, shift_y(): lax.ppermute(x, 'front', [(4 * z + y, 4 * z + (y + d) % 4) for z in zs fo...  11.7 us
    pallas_call x1, Pallas kernels, fourth(): pl.pallas_call(fourth_kernel, out_shape=(jax.ShapeDtypeStruct((B, order),...  8.69 us
  transfers between devices with their start and end apart: 19, of which 6 were waited for; matrix products, arithmetic and copies ran while one was open for 2% of the time, Pallas kernels for 25%

profile of v11, /device:TPU:8, one launch (start us, length us, event | category | flops | bytes accessed | tf_op | source)
XLA Modules:
  0.0 157.8 jit_solution(9655955191567837267)
XLA Ops:
  0.6 0.8 copy.10
  1.4 0.7 fusion
  2.1 2.7 %select_maximum_fusion = f32[8,392,128]{2,1,0:T(8,128)} fusion(f32[8,1,3]{2,1,0:T(1,128)S(1)} %fusion, f32[8,384,128]{2,1,0:T(8,128)} %bitcast.15), kind=kLoop, calls=%fused_computation | loop fusion | flops 1204224 | bytes 3178592 | tf_op jit(solution)/shard_map/concatenate | solution.py:511
  4.8 4.4 %all-to-all-start = ((f32[8,392,128]{2,1,0:T(8,128)}), f32[8,392,128]{2,1,0:T(8,128)S(1)}, u32[]{:S(2)}, u32[]{:S(2)}) async-start(f32[8,392,128]{2,1,0:T(8,128)} %select_maximum_fusion), calls=%async_computation | async-start | bytes 3211264 | tf_op jit(solution)/shard_map/all_to_all | solution.py:512
  9.3 21.9 %all-to-all-done.recv_ref = f32[8,392,128]{2,1,0:T(8,128)S(1)} async-done(((f32[8,392,128]{2,1,0:T(8,128)}), f32[8,392,128]{2,1,0:T(8,128)S(1)}, u32[]{:S(2)}, u32[]{:S(2)}) %all-to-all-start) | async-done | bytes 1605664 | tf_op jit(solution)/shard_map/all_to_all | solution.py:512
  31.2 1.9 %assemble.1 = (f32[128,1024]{1,0:T(8,128)S(1)}, f32[128,512]{1,0:T(8,128)}, f32[128,512]{1,0:T(8,128)S(1)}, f32[128,640]{1,0:T(8,128)S(1)}) custom-call(s32[8,3]{1,0:T(8,128)S(1)} %bitcast.14, s32[1]{0:T(128)} %bitcast.idx_ref, f32[8,392,128]{2,1,0:T(8,128)S(1)} %all-to-all-done.recv_ref, f32[128,2048]{1,0:T(8,128)S(1)} %bitcast.10), custom_call_target="tpu_custom_call" | custom-call | tf_op jit(solution)/shard_map/assemble/pallas_call | solution.py:65
  33.1 0.7 copy-done.2
  33.9 3.8 %collective-permute-start.4 = (f32[128,512]{1,0:T(8,128)}, f32[128,512]{1,0:T(8,128)S(1)}, u32[]{:S(2)}, u32[]{:S(2)}) collective-permute-start(f32[128,512]{1,0:T(8,128)} %get-tuple-element.43), channel_id=1, source_target_pairs={{0,4},{1,5},{2,6},{3,7},{4,0},{5,1},{6,2},{7,3},{16,20},{17,21},{1... | collective-permute-start | bytes 786440 | tf_op jit(solution)/shard_map/ppermute | solution.py:495
  37.7 2.8 %collective-permute-start.5 = (f32[128,512]{1,0:T(8,128)}, f32[128,512]{1,0:T(8,128)S(1)}, u32[]{:S(2)}, u32[]{:S(2)}) collective-permute-start(f32[128,512]{1,0:T(8,128)} %get-tuple-element.43), channel_id=1, source_target_pairs={{4,8},{5,9},{6,10},{7,11},{0,12},{1,13},{2,14},{3,15},{20,24},{21,... | collective-permute-start | bytes 786440 | tf_op jit(solution)/shard_map/ppermute | solution.py:495
  40.5 1.3 collective-permute-start.6
  41.8 0.7 collective-permute-start
  42.5 0.7 collective-permute-start.1
  43.2 1.0 constant_dynamic-update-slice_fusion.3
  44.2 0.6 collective-permute-done.4
  44.8 0.7 collective-permute-start.2
  45.5 6.2 %collective-permute-done.5 = f32[128,512]{1,0:T(8,128)S(1)} collective-permute-done((f32[128,512]{1,0:T(8,128)}, f32[128,512]{1,0:T(8,128)S(1)}, u32[]{:S(2)}, u32[]{:S(2)}) %collective-permute-start.5) | collective-permute-done | bytes 262176 | tf_op jit(solution)/shard_map/ppermute | solution.py:495
  51.7 0.0 collective-permute-done.6
  51.7 1.3 collective-permute-start.7
  53.0 0.7 collective-permute-start.8
  53.7 1.1 select_select_fusion.1
  54.8 0.7 collective-permute-start.9
  55.5 0.0 collective-permute-done.1
  55.5 1.6 %collective-permute-start.13 = (f32[256,512]{1,0:T(8,128)S(1)}, f32[256,512]{1,0:T(8,128)S(1)}, u32[]{:S(2)}, u32[]{:S(2)}) collective-permute-start(f32[256,512]{1,0:T(8,128)S(1)} %pad_maximum_fusion.1.y0_ref), channel_id=1, source_target_pairs={{0,1},{1,2},{2,3},{3,0},{4,5},{5,6},{6,7},{7,4},{8,9},{9,10},{10,1... | collective-permute-start | bytes 1572872 | tf_op jit(solution)/shard_map/ppermute | solution.py:491
  57.2 0.0 collective-permute-done.2
  57.2 0.9 collective-permute-start.14
  58.1 3.0 %collective-permute-done.7 = f32[128,512]{1,0:T(8,128)S(1)} collective-permute-done((f32[128,512]{1,0:T(8,128)S(1)}, f32[128,512]{1,0:T(8,128)S(1)}, u32[]{:S(2)}, u32[]{:S(2)}) %collective-permute-start.7) | collective-permute-done | bytes 262176 | tf_op jit(solution)/shard_map/ppermute | solution.py:495
  61.1 0.4 collective-permute-start.15
  61.5 0.0 copy-start.1
  61.6 0.0 collective-permute-done.8
  61.6 0.9 collective-permute-start.3
  62.5 0.1 select_select_fusion.2
  62.6 1.7 %collective-permute-start.10 = (f32[128,896]{1,0:T(8,128)S(1)}, f32[128,896]{1,0:T(8,128)S(1)}, u32[]{:S(2)}, u32[]{:S(2)}) collective-permute-start(f32[128,896]{1,0:T(8,128)S(1)} %pad_maximum_fusion.2.p0_ref), channel_id=1, source_target_pairs={{0,1},{1,2},{2,3},{3,0},{4,5},{5,6},{6,7},{7,4},{8,9},{9,10},{10,1... | collective-permute-start | bytes 1376264 | tf_op jit(solution)/shard_map/ppermute | solution.py:491
  64.3 16.0 %collective-permute-done.13.y1_ref = f32[256,512]{1,0:T(8,128)S(1)} collective-permute-done((f32[256,512]{1,0:T(8,128)S(1)}, f32[256,512]{1,0:T(8,128)S(1)}, u32[]{:S(2)}, u32[]{:S(2)}) %collective-permute-start.13) | collective-permute-done | bytes 524320 | tf_op jit(solution)/shard_map/ppermute | solution.py:491
  80.3 0.0 collective-permute-start.11
  80.3 0.0 collective-permute-done.14.y2_ref
  80.3 5.0 %collective-permute-start.12 = (f32[128,896]{1,0:T(8,128)S(1)}, f32[128,896]{1,0:T(8,128)S(1)}, u32[]{:S(2)}, u32[]{:S(2)}) collective-permute-start(f32[128,896]{1,0:T(8,128)S(1)} %pad_maximum_fusion.2.p0_ref), channel_id=1, source_target_pairs={{0,3},{1,0},{2,1},{3,2},{4,7},{5,4},{6,5},{7,6},{8,11},{9,8},{10,9... | collective-permute-start | bytes 1376264 | tf_op jit(solution)/shard_map/ppermute | solution.py:491
  85.3 0.0 collective-permute-done.15.y3_ref
  85.3 18.8 %first.1 = (bf16[1088,512]{1,0:T(8,128)(2,1)S(1)}, bf16[1088,512]{1,0:T(8,128)(2,1)S(1)}, bf16[1024,512]{1,0:T(8,128)(2,1)S(1)}, bf16[1024,512]{1,0:T(8,128)(2,1...) custom-call(s32[1]{0:T(128)} %bitcast.idx_ref, ...), custom_call_target="tpu_custom_call" | custom-call | flops 20000000000 | bytes 20000000 | tf_op jit(solution)/shard_map/first/pallas_call | solution.py:263
  104.2 0.0 collective-permute-done.10.p1_ref
  104.3 0.1 pad_maximum_fusion.near_ref
  104.3 0.9 collective-permute-start.16
  105.2 18.3 %second.1 = (bf16[1024,1024]{1,0:T(8,128)(2,1)S(1)}, bf16[1024,1024]{1,0:T(8,128)(2,1)S(1)}, f32[8,128,128]{2,1,0:T(8,128)S(1)}, f32[8,1024]{1,0:T(8,128)S(1)}, ...) custom-call(s32[1]{0:T(128)} %bitcast.idx_ref, f32[128,896]{1,0:T(8,128)S(1)} %pad_maximum_fusion.2.p0_ref, ...), custom_call_target="tpu_custom_call" | custom-call | flops 20000000000 | bytes 20000000 | tf_op jit(solution)/shard_map/second/pallas_call | solution.py:332
  123.6 2.9 %third.1 = (bf16[1024,512]{1,0:T(8,128)(2,1)S(1)}, bf16[1024,512]{1,0:T(8,128)(2,1)S(1)}, bf16[1024,512]{1,0:T(8,128)(2,1)S(1)}, bf16[1024,512]{1,0:T(8,128)(2,1)S(1)}, f32[128,512]{1,0:T(8,128)S(1)}) custom-call(s32[1]{0:T(128)} %bitcast.idx_ref, f32[512,640]{1,0:T(8,128)S(1)} %constant_dynamic-update-slice_fusion.near_ref.near0_ref, ...), custom_call_target="tpu_custom_call" | custom-call | flops 5000000000 | bytes 10000000 | tf_op jit(solution)/shard_map/third/pallas_call | solution.py:409
  126.5 8.7 %fourth.1 = (f32[128,2048]{1,0:T(8,128)}, f32[64,2048]{1,0:T(8,128)S(1)}) custom-call(s32[1]{0:T(128)} %bitcast.idx_ref, f32[512,640]{1,0:T(8,128)S(1)} %constant_dynamic-update-slice_fusion.near_ref.near0_ref, f32[512,640]{1,0:T(8,128)S(1)} %collective-permute-done.3.far_ref.far0_ref, f32[512,384]{1,0:T(8,128)S(1)} %pad_maximum_fusion.near_ref, ...), custom_call_target="tpu_custom_call" | custom-call | tf_op jit(solution)/shard_map/fourth/pallas_call | solution.py:468
  135.2 1.3 collective-permute-start.17
  136.5 20.4 %collective-permute-done.17 = f32[64,1024]{1,0:T(8,128)S(1)} collective-permute-done((f32[64,1024]{1,0:T(8,128)S(1)}, f32[64,1024]{1,0:T(8,128)S(1)}, u32[]{:S(2)}, u32[]{:S(2)}) %collective-permute-start.17) | collective-permute-done | bytes 262176 | tf_op jit(solution)/shard_map/ppermute | solution.py:495
  156.9 0.1 fusion.1
  156.9 0.8 maximum_bitcast_fusion
  (21 shorter events, 0.2 us)
Async XLA Ops:
  4.8 26.4 %copy-start = (f32[1,128,2048]{2,1,0:T(8,128)S(1)}, f32[1,128,2048]{2,1,0:T(8,128)}, u32[]{:S(2)}) copy-start(f32[1,128,2048]{2,1,0:T(8,128)} %param.7) | copy-start | bytes 3145732
  4.8 26.4 %all-to-all-start = ((f32[8,392,128]{2,1,0:T(8,128)}), f32[8,392,128]{2,1,0:T(8,128)S(1)}, u32[]{:S(2)}, u32[]{:S(2)}) async-start(f32[8,392,128]{2,1,0:T(8,128)} %select_maximum_fusion), calls=%async_computation | async-start | bytes 3211264 | tf_op jit(solution)/shard_map/all_to_all | solution.py:512
  33.1 0.7 copy-start.2
  33.9 10.9 %collective-permute-start.4 = (f32[128,512]{1,0:T(8,128)}, f32[128,512]{1,0:T(8,128)S(1)}, u32[]{:S(2)}, u32[]{:S(2)}) collective-permute-start(f32[128,512]{1,0:T(8,128)} %get-tuple-element.43), channel_id=1, source_target_pairs={{0,4},{1,5},{2,6},{3,7},{4,0},{5,1},{6,2},{7,3},{16,20},{17,21},{1... | collective-permute-start | bytes 786440 | tf_op jit(solution)/shard_map/ppermute | solution.py:495
  37.7 14.0 %collective-permute-start.5 = (f32[128,512]{1,0:T(8,128)}, f32[128,512]{1,0:T(8,128)S(1)}, u32[]{:S(2)}, u32[]{:S(2)}) collective-permute-start(f32[128,512]{1,0:T(8,128)} %get-tuple-element.43), channel_id=1, source_target_pairs={{4,8},{5,9},{6,10},{7,11},{0,12},{1,13},{2,14},{3,15},{20,24},{21,... | collective-permute-start | bytes 786440 | tf_op jit(solution)/shard_map/ppermute | solution.py:495
  40.5 11.2 %collective-permute-start.6 = (f32[128,512]{1,0:T(8,128)}, f32[128,512]{1,0:T(8,128)S(1)}, u32[]{:S(2)}, u32[]{:S(2)}) collective-permute-start(f32[128,512]{1,0:T(8,128)} %get-tuple-element.43), channel_id=1, source_target_pairs={{0,8},{1,9},{2,10},{3,11},{4,12},{5,13},{6,14},{7,15},{16,24},{17,... | collective-permute-start | bytes 786440 | tf_op jit(solution)/shard_map/ppermute | solution.py:495
  41.8 13.0 %collective-permute-start = (f32[128,640]{1,0:T(8,128)}, f32[128,640]{1,0:T(8,128)S(1)}, u32[]{:S(2)}, u32[]{:S(2)}) collective-permute-start(f32[128,640]{1,0:T(8,128)} %copy-done.2), channel_id=1, source_target_pairs={{8,9},{9,10},{10,11},{11,8},{12,13},{13,14},{14,15},{15,12},{24,25... | collective-permute-start | bytes 983048 | tf_op jit(solution)/shard_map/ppermute | solution.py:491
  42.5 13.0 %collective-permute-start.1 = (f32[128,640]{1,0:T(8,128)}, f32[128,640]{1,0:T(8,128)S(1)}, u32[]{:S(2)}, u32[]{:S(2)}) collective-permute-start(f32[128,640]{1,0:T(8,128)} %copy-done.2), channel_id=1, source_target_pairs={{8,10},{9,11},{10,8},{11,9},{12,14},{13,15},{14,12},{15,13},{24,26... | collective-permute-start | bytes 983048 | tf_op jit(solution)/shard_map/ppermute | solution.py:491
  44.8 12.4 %collective-permute-start.2 = (f32[128,640]{1,0:T(8,128)}, f32[128,640]{1,0:T(8,128)S(1)}, u32[]{:S(2)}, u32[]{:S(2)}) collective-permute-start(f32[128,640]{1,0:T(8,128)} %copy-done.2), channel_id=1, source_target_pairs={{8,11},{9,8},{10,9},{11,10},{12,15},{13,12},{14,13},{15,14},{24,27... | collective-permute-start | bytes 983048 | tf_op jit(solution)/shard_map/ppermute | solution.py:491
  51.7 9.4 %collective-permute-start.7 = (f32[128,512]{1,0:T(8,128)S(1)}, f32[128,512]{1,0:T(8,128)S(1)}, u32[]{:S(2)}, u32[]{:S(2)}) collective-permute-start(f32[128,512]{1,0:T(8,128)S(1)} %get-tuple-element.44), channel_id=1, source_target_pairs={{4,0},{5,1},{6,2},{7,3},{20,16},{21,17},{22,18},{23,19},{36,32},{3... | collective-permute-start | bytes 786440 | tf_op jit(solution)/shard_map/ppermute | solution.py:495
  53.0 8.6 %collective-permute-start.8 = (f32[128,512]{1,0:T(8,128)S(1)}, f32[128,512]{1,0:T(8,128)S(1)}, u32[]{:S(2)}, u32[]{:S(2)}) collective-permute-start(f32[128,512]{1,0:T(8,128)S(1)} %get-tuple-element.44), channel_id=1, source_target_pairs={{4,8},{5,9},{6,10},{7,11},{20,24},{21,25},{22,26},{23,27},{36,40},... | collective-permute-start | bytes 786440 | tf_op jit(solution)/shard_map/ppermute | solution.py:495
  54.8 7.7 %collective-permute-start.9 = (f32[128,512]{1,0:T(8,128)S(1)}, f32[128,512]{1,0:T(8,128)S(1)}, u32[]{:S(2)}, u32[]{:S(2)}) collective-permute-start(f32[128,512]{1,0:T(8,128)S(1)} %get-tuple-element.44), channel_id=1, source_target_pairs={{4,12},{5,13},{6,14},{7,15},{20,28},{21,29},{22,30},{23,31},{36,44... | collective-permute-start | bytes 786440 | tf_op jit(solution)/shard_map/ppermute | solution.py:495
  55.5 24.8 %collective-permute-start.13 = (f32[256,512]{1,0:T(8,128)S(1)}, f32[256,512]{1,0:T(8,128)S(1)}, u32[]{:S(2)}, u32[]{:S(2)}) collective-permute-start(f32[256,512]{1,0:T(8,128)S(1)} %pad_maximum_fusion.1.y0_ref), channel_id=1, source_target_pairs={{0,1},{1,2},{2,3},{3,0},{4,5},{5,6},{6,7},{7,4},{8,9},{9,10},{10,1... | collective-permute-start | bytes 1572872 | tf_op jit(solution)/shard_map/ppermute | solution.py:491
  57.2 23.2 %collective-permute-start.14 = (f32[256,512]{1,0:T(8,128)S(1)}, f32[256,512]{1,0:T(8,128)S(1)}, u32[]{:S(2)}, u32[]{:S(2)}) collective-permute-start(f32[256,512]{1,0:T(8,128)S(1)} %pad_maximum_fusion.1.y0_ref), channel_id=1, source_target_pairs={{0,2},{1,3},{2,0},{3,1},{4,6},{5,7},{6,4},{7,5},{8,10},{9,11},{10,... | collective-permute-start | bytes 1572872 | tf_op jit(solution)/shard_map/ppermute | solution.py:491
  61.1 24.2 %collective-permute-start.15 = (f32[256,512]{1,0:T(8,128)S(1)}, f32[256,512]{1,0:T(8,128)S(1)}, u32[]{:S(2)}, u32[]{:S(2)}) collective-permute-start(f32[256,512]{1,0:T(8,128)S(1)} %pad_maximum_fusion.1.y0_ref), channel_id=1, source_target_pairs={{0,3},{1,0},{2,1},{3,2},{4,7},{5,4},{6,5},{7,6},{8,11},{9,8},{10,9... | collective-permute-start | bytes 1572872 | tf_op jit(solution)/shard_map/ppermute | solution.py:491
  61.5 23.8 %copy-start.1 = (f32[1,64,2048]{2,1,0:T(8,128)S(1)}, f32[1,64,2048]{2,1,0:T(8,128)}, u32[]{:S(2)}) copy-start(f32[1,64,2048]{2,1,0:T(8,128)} %param.11) | copy-start | bytes 1572868
  61.6 62.0 %collective-permute-start.3 = (f32[512,640]{1,0:T(8,128)S(1)}, f32[512,640]{1,0:T(8,128)S(1)}, u32[]{:S(2)}, u32[]{:S(2)}) collective-permute-start(f32[512,640]{1,0:T(8,128)S(1)} %constant_dynamic-update-slice_fusion.near_ref.near0_ref), channel_id=1, source_target_pairs={{8,12},{9,13},{10,14},{11,15},{12,8},{13,9},{14,10},{15,11},{24,28... | collective-permute-start | bytes 3932168 | tf_op jit(solution)/shard_map/ppermute | solution.py:495
  62.6 41.6 %collective-permute-start.10 = (f32[128,896]{1,0:T(8,128)S(1)}, f32[128,896]{1,0:T(8,128)S(1)}, u32[]{:S(2)}, u32[]{:S(2)}) collective-permute-start(f32[128,896]{1,0:T(8,128)S(1)} %pad_maximum_fusion.2.p0_ref), channel_id=1, source_target_pairs={{0,1},{1,2},{2,3},{3,0},{4,5},{5,6},{6,7},{7,4},{8,9},{9,10},{10,1... | collective-permute-start | bytes 1376264 | tf_op jit(solution)/shard_map/ppermute | solution.py:491
  80.3 23.9 %collective-permute-start.11 = (f32[128,896]{1,0:T(8,128)S(1)}, f32[128,896]{1,0:T(8,128)S(1)}, u32[]{:S(2)}, u32[]{:S(2)}) collective-permute-start(f32[128,896]{1,0:T(8,128)S(1)} %pad_maximum_fusion.2.p0_ref), channel_id=1, source_target_pairs={{0,2},{1,3},{2,0},{3,1},{4,6},{5,7},{6,4},{7,5},{8,10},{9,11},{10,... | collective-permute-start | bytes 1376264 | tf_op jit(solution)/shard_map/ppermute | solution.py:491
  80.3 23.9 %collective-permute-start.12 = (f32[128,896]{1,0:T(8,128)S(1)}, f32[128,896]{1,0:T(8,128)S(1)}, u32[]{:S(2)}, u32[]{:S(2)}) collective-permute-start(f32[128,896]{1,0:T(8,128)S(1)} %pad_maximum_fusion.2.p0_ref), channel_id=1, source_target_pairs={{0,3},{1,0},{2,1},{3,2},{4,7},{5,4},{6,5},{7,6},{8,11},{9,8},{10,9... | collective-permute-start | bytes 1376264 | tf_op jit(solution)/shard_map/ppermute | solution.py:491
  104.3 22.1 %collective-permute-start.16 = (f32[512,384]{1,0:T(8,128)S(1)}, f32[512,384]{1,0:T(8,128)S(1)}, u32[]{:S(2)}, u32[]{:S(2)}) collective-permute-start(f32[512,384]{1,0:T(8,128)S(1)} %pad_maximum_fusion.near_ref), channel_id=1, source_target_pairs={{8,12},{9,13},{10,14},{11,15},{12,8},{13,9},{14,10},{15,11},{24,28... | collective-permute-start | bytes 2359304 | tf_op jit(solution)/shard_map/ppermute | solution.py:495
  135.2 21.7 %collective-permute-start.17 = (f32[64,1024]{1,0:T(8,128)S(1)}, f32[64,1024]{1,0:T(8,128)S(1)}, u32[]{:S(2)}, u32[]{:S(2)}) collective-permute-start(f32[64,1024]{1,0:T(8,128)S(1)} %slice.50), channel_id=1, source_target_pairs={{8,4},{9,5},{10,6},{11,7},{12,0},{13,1},{14,2},{15,3},{24,20},{25,... | collective-permute-start | bytes 786440 | tf_op jit(solution)/shard_map/ppermute | solution.py:495

commit v12 on v10

--- a/solution.py
+++ b/solution.py
@@ -376,8 +376,8 @@
     for i in range(2):
         lc, pc = slice(i * W2, (i + 1) * W2), slice(base + i * W2, base + (i + 1) * W2)
         u = a21[:, lc]
-        if known:
-            u = u - dot3_t(known[0][...], known[1][...], lh[pc, :HALF], ll[pc, :HALF])
+        if known is not None:
+            u = u - known[:, lc]
         if i:
             u = u - dot3_t(xh[:, :W2], xl[:, :W2], lh[pc, base : base + W2], ll[pc, base : base + W2])
         uh, ul = split(u)
@@ -387,37 +387,57 @@
         wh[:, lc], wl[:, lc] = split(v * dinv_ref[0:1, pc])
 
 
-def third_kernel(idx_ref, near_ref, far_ref, lh, ll, t_ref, dinv_ref, xh, xl, wh, wl, own_ref, a21, x32, sem):
+def products(mine, xh, xl, wh, wl, y):
+    yh, yl = split(y)
+    hi = jnp.concatenate([xh[mine, :], yh], 0)
+    both = jnp.concatenate([hi, xl[mine, :], yl], 0)
+    n = hi.shape[0]
+    for c in range(wh.shape[0] // W2):
+        rows = slice(c * W2, (c + 1) * W2)
+        prod = dot_t(both, wh[rows, :])
+        yield c, prod[:n] + prod[n:] + dot_t(hi, wl[rows, :])
+
+
+def third_kernel(idx_ref, near_ref, far_ref, lh, ll, t_ref, dinv_ref, y_ref, next_ref, prod_ref, own_ref,
+                 a21, xh, xl, x32, wh, wl, sem):
     me = idx_ref[0]
     copies = place_rows(me, near_ref, far_ref, a21, sem)
     inverses = [pair_inverse(i, lh, ll, t_ref) for i in range(2)]
     for copy in copies:
         copy.wait()
     solve_half(0, inverses, a21, None, lh, ll, dinv_ref, xh, xl, x32, wh, wl)
+    next_ref[...] = dot3_t(xh[...], xl[...], lh[HALF:, :HALF], ll[HALF:, :HALF])
     mine = pl.ds(pl.multiple_of(jnp.maximum(me - NP, 0) * B, B), B)
+    for c, prod in products(mine, xh, xl, wh, wl, y_ref[:, :HALF]):
+        prod_ref[:, c * W2 : (c + 1) * W2] = prod
     own_ref[...] = x32[mine, :] * dinv_ref[0:1, :HALF]
 
 
 def third(index, near, far, state):
     low = 2 * near.shape[0]
-    outs = (((low, HALF), BF16),) * 4 + (((B, HALF), F32),)
+    nrhs = state[4].shape[0]
+    outs = ((low, HALF), (B + nrhs, low), (B, HALF))
     return pl.pallas_call(
         third_kernel,
-        out_shape=tuple(jax.ShapeDtypeStruct(*o) for o in outs),
-        in_specs=[pl.BlockSpec(memory_space=pltpu.SMEM)] + [VMEM_SPEC] * 6,
+        out_shape=tuple(jax.ShapeDtypeStruct(o, F32) for o in outs),
+        in_specs=[pl.BlockSpec(memory_space=pltpu.SMEM)] + [VMEM_SPEC] * 7,
         out_specs=(VMEM_SPEC,) * len(outs),
         scratch_shapes=[
             pltpu.VMEM((low, HALF), F32),
+            pltpu.VMEM((low, HALF), BF16),
+            pltpu.VMEM((low, HALF), BF16),
             pltpu.VMEM((low, HALF), F32),
+            pltpu.VMEM((low, HALF), BF16),
+            pltpu.VMEM((low, HALF), BF16),
             pltpu.SemaphoreType.DMA((8,)),
         ],
-        compiler_params=pltpu.CompilerParams(vmem_limit_bytes=16 * 1024 * 1024),
+        compiler_params=pltpu.CompilerParams(vmem_limit_bytes=24 * 1024 * 1024),
         cost_estimate=pl.CostEstimate(flops=5 * 10**9, bytes_accessed=10**7, transcendentals=0),
         name="third",
-    )(index, near, far, *state[:4])
-
-
-def fourth_kernel(idx_ref, near_ref, far_ref, xh0, xl0, wh0, wl0, lown_ref, lh, ll, t_ref, dinv_ref, y_ref, own_ref,
+    )(index, near, far, *state[:5])
+
+
+def fourth_kernel(idx_ref, near_ref, far_ref, next_ref, prod_ref, lown_ref, lh, ll, t_ref, dinv_ref, y_ref, own_ref,
                   tail_ref, b_ref, fac_ref, eli_ref, a21, xh, xl, x32, wh, wl, sem):
     me = idx_ref[0]
     nrhs, order = b_ref.shape
@@ -426,20 +446,13 @@
     inverses = [pair_inverse(i, lh, ll, t_ref) for i in range(2, 4)]
     for copy in copies:
         copy.wait()
-    solve_half(1, inverses, a21, (xh0, xl0), lh, ll, dinv_ref, xh, xl, x32, wh, wl)
-    y = y_ref[...]
-    yh, yl = split(y)
-    eli_ref[:, :PIV] = y
+    solve_half(1, inverses, a21, next_ref, lh, ll, dinv_ref, xh, xl, x32, wh, wl)
+    eli_ref[:, :PIV] = y_ref[...]
     mine = pl.ds(pl.multiple_of(jnp.maximum(me - NP, 0) * B, B), B)
-    n = B + nrhs
-    hi = [jnp.concatenate([x[mine, :], yh[:, c]], 0) for x, c in ((xh0, slice(0, HALF)), (xh, slice(HALF, PIV)))]
-    lo = [jnp.concatenate([x[mine, :], yl[:, c]], 0) for x, c in ((xl0, slice(0, HALF)), (xl, slice(HALF, PIV)))]
-    both = [jnp.concatenate([h, m], 0) for h, m in zip(hi, lo)]
-    for c in range(low // W2):
+    for c, prod in products(mine, xh, xl, wh, wl, y_ref[:, HALF:]):
         rows = slice(c * W2, (c + 1) * W2)
         dst = slice(PIV + c * W2, PIV + (c + 1) * W2)
-        prod = dot_t(both[0], wh0[rows, :]) + dot_t(both[1], wh[rows, :])
-        prod = prod[:n] + prod[n:] + dot_t(hi[0], wl0[rows, :]) + dot_t(hi[1], wl[rows, :])
+        prod = prod + prod_ref[:, rows]
         row = me * B + lax.broadcasted_iota(jnp.int32, (B, W2), 0)
         col = PIV + c * W2 + lax.broadcasted_iota(jnp.int32, (B, W2), 1)
         fac_ref[:, dst] = jnp.where(row >= col, tail_ref[:, rows] - prod[:B], 0.0)

time: 151 us -> 149 us (0.987)
  waiting for transfers between devices: 61.9 us -> 59.7 us
    pallas_call x1, Pallas kernels: 8.47 us -> 5.13 us  [fourth(): pl.pallas_call(fourth_kernel, out_shape=(jax.ShapeDtypeStruct((B, order),...]
    pallas_call x1, Pallas kernels: 2.85 us -> 6 us  [third(): pl.pallas_call(third_kernel, out_shape=tuple((jax.ShapeDtypeStruct(o, F32...]
    ppermute x9, waiting for transfers between devices: 23.6 us -> 21.1 us  [planes(): lax.ppermute(x, 'front', [(4 * a + y, 4 * b + y) for a, b in pairs for y...]
  transfers between devices with their start and end apart: 19 -> 19, of which waited for: 8 -> 8; matrix products, arithmetic and copies ran while one was open for 1% -> 1% of each run, Pallas kernels for 27% -> 29%
where the time goes in v12:
time: 149 us; the launch traced here: 147 us
  waiting for transfers between devices  59.7 us (40%)
  Pallas kernels  50 us (34%)
  starting transfers between devices  29.6 us (20%)
  other arithmetic  5.63 us (4%)
    all_to_all x1, waiting for transfers between devices, local(): lax.all_to_all(payload, 'leaf', split_axis=0, concat_axis=0, tiled=True)  21.9 us
    ppermute x9, waiting for transfers between devices, planes(): lax.ppermute(x, 'front', [(4 * a + y, 4 * b + y) for a, b in pairs for y...  21.1 us
    pallas_call x1, Pallas kernels, first(): pl.pallas_call(first_kernel, out_shape=tuple((jax.ShapeDtypeStruct(*o) fo...  18.5 us
    pallas_call x1, Pallas kernels, second(): pl.pallas_call(second_kernel, out_shape=tuple((jax.ShapeDtypeStruct(*o) f...  18.5 us
    ppermute x9, waiting for transfers between devices, shift_y(): lax.ppermute(x, 'front', [(4 * z + y, 4 * z + (y + d) % 4) for z in zs fo...  16.7 us
    ppermute x9, starting transfers between devices, planes(): lax.ppermute(x, 'front', [(4 * a + y, 4 * b + y) for a, b in pairs for y...  13.5 us
    ppermute x9, starting transfers between devices, shift_y(): lax.ppermute(x, 'front', [(4 * z + y, 4 * z + (y + d) % 4) for z in zs fo...  11.8 us
    pallas_call x1, Pallas kernels, third(): pl.pallas_call(third_kernel, out_shape=tuple((jax.ShapeDtypeStruct(o, F32...  6 us
  transfers between devices with their start and end apart: 19, of which 8 were waited for; matrix products, arithmetic and copies ran while one was open for 1% of the time, Pallas kernels for 29%

profile of v12, /device:TPU:8, one launch (start us, length us, event | category | flops | bytes accessed | tf_op | source)
XLA Modules:
  0.0 146.9 jit_solution(2309296987411027768)
XLA Ops:
  0.6 0.8 copy.10
  1.4 0.7 fusion
  2.1 2.7 %select_maximum_fusion = f32[8,392,128]{2,1,0:T(8,128)} fusion(f32[8,1,3]{2,1,0:T(1,128)S(1)} %fusion, f32[8,384,128]{2,1,0:T(8,128)} %bitcast.15), kind=kLoop, calls=%fused_computation | loop fusion | flops 1204224 | bytes 3178592 | tf_op jit(solution)/shard_map/concatenate | solution.py:518
  4.8 4.4 %all-to-all-start = ((f32[8,392,128]{2,1,0:T(8,128)}), f32[8,392,128]{2,1,0:T(8,128)S(1)}, u32[]{:S(2)}, u32[]{:S(2)}) async-start(f32[8,392,128]{2,1,0:T(8,128)} %select_maximum_fusion), calls=%async_computation | async-start | bytes 3211264 | tf_op jit(solution)/shard_map/all_to_all | solution.py:519
  9.3 21.9 %all-to-all-done.recv_ref = f32[8,392,128]{2,1,0:T(8,128)S(1)} async-done(((f32[8,392,128]{2,1,0:T(8,128)}), f32[8,392,128]{2,1,0:T(8,128)S(1)}, u32[]{:S(2)}, u32[]{:S(2)}) %all-to-all-start) | async-done | bytes 1605664 | tf_op jit(solution)/shard_map/all_to_all | solution.py:519
  31.2 1.9 %assemble.1 = (f32[128,1024]{1,0:T(8,128)S(1)}, f32[128,512]{1,0:T(8,128)}, f32[128,512]{1,0:T(8,128)S(1)}) custom-call(s32[8,3]{1,0:T(8,128)S(1)} %bitcast.14, s32[1]{0:T(128)} %bitcast.idx_ref, f32[8,392,128]{2,1,0:T(8,128)S(1)} %all-to-all-done.recv_ref, f32[128,2048]{1,0:T(8,128)S(1)} %bitcast.10), custom_call_target="tpu_custom_call" | custom-call | tf_op jit(solution)/shard_map/assemble/pallas_call | solution.py:63
  33.1 3.8 %collective-permute-start = (f32[128,512]{1,0:T(8,128)}, f32[128,512]{1,0:T(8,128)S(1)}, u32[]{:S(2)}, u32[]{:S(2)}) collective-permute-start(f32[128,512]{1,0:T(8,128)} %get-tuple-element.39), channel_id=1, source_target_pairs={{0,4},{1,5},{2,6},{3,7},{4,0},{5,1},{6,2},{7,3},{16,20},{17,21},{1... | collective-permute-start | bytes 786440 | tf_op jit(solution)/shard_map/ppermute | solution.py:502
  36.9 2.8 %collective-permute-start.1 = (f32[128,512]{1,0:T(8,128)}, f32[128,512]{1,0:T(8,128)S(1)}, u32[]{:S(2)}, u32[]{:S(2)}) collective-permute-start(f32[128,512]{1,0:T(8,128)} %get-tuple-element.39), channel_id=1, source_target_pairs={{4,8},{5,9},{6,10},{7,11},{0,12},{1,13},{2,14},{3,15},{20,24},{21,... | collective-permute-start | bytes 786440 | tf_op jit(solution)/shard_map/ppermute | solution.py:502
  39.7 1.3 collective-permute-start.2
  41.0 0.7 collective-permute-start.13
  41.7 0.7 collective-permute-start.14
  42.4 1.6 %collective-permute-done = f32[128,512]{1,0:T(8,128)S(1)} collective-permute-done((f32[128,512]{1,0:T(8,128)}, f32[128,512]{1,0:T(8,128)S(1)}, u32[]{:S(2)}, u32[]{:S(2)}) %collective-permute-start) | collective-permute-done | bytes 262176 | tf_op jit(solution)/shard_map/ppermute | solution.py:502
  44.0 0.7 collective-permute-start.15
  44.7 6.3 %collective-permute-done.1 = f32[128,512]{1,0:T(8,128)S(1)} collective-permute-done((f32[128,512]{1,0:T(8,128)}, f32[128,512]{1,0:T(8,128)S(1)}, u32[]{:S(2)}, u32[]{:S(2)}) %collective-permute-start.1) | collective-permute-done | bytes 262176 | tf_op jit(solution)/shard_map/ppermute | solution.py:502
  51.0 0.0 collective-permute-done.2
  51.0 1.3 collective-permute-start.3
  52.3 0.7 collective-permute-start.4
  53.0 1.1 select_select_fusion.1
  54.1 0.0 collective-permute-done.13
  54.1 0.7 collective-permute-start.5
  54.8 0.0 copy-start.1
  54.8 0.0 collective-permute-done.14
  54.8 2.3 %collective-permute-start.10 = (f32[256,512]{1,0:T(8,128)S(1)}, f32[256,512]{1,0:T(8,128)S(1)}, u32[]{:S(2)}, u32[]{:S(2)}) collective-permute-start(f32[256,512]{1,0:T(8,128)S(1)} %pad_maximum_fusion.2.y0_ref), channel_id=1, source_target_pairs={{0,2},{1,3},{2,0},{3,1},{4,6},{5,7},{6,4},{7,5},{8,10},{9,11},{10,... | collective-permute-start | bytes 1572872 | tf_op jit(solution)/shard_map/ppermute | solution.py:498
  57.2 0.0 collective-permute-done.15
  57.2 1.3 collective-permute-start.11
  58.5 2.0 %collective-permute-done.3 = f32[128,512]{1,0:T(8,128)S(1)} collective-permute-done((f32[128,512]{1,0:T(8,128)S(1)}, f32[128,512]{1,0:T(8,128)S(1)}, u32[]{:S(2)}, u32[]{:S(2)}) %collective-permute-start.3) | collective-permute-done | bytes 262176 | tf_op jit(solution)/shard_map/ppermute | solution.py:502
  60.5 1.5 %collective-permute-start.9 = (f32[256,512]{1,0:T(8,128)S(1)}, f32[256,512]{1,0:T(8,128)S(1)}, u32[]{:S(2)}, u32[]{:S(2)}) collective-permute-start(f32[256,512]{1,0:T(8,128)S(1)} %pad_maximum_fusion.2.y0_ref), channel_id=1, source_target_pairs={{0,1},{1,2},{2,3},{3,0},{4,5},{5,6},{6,7},{7,4},{8,9},{9,10},{10,1... | collective-permute-start | bytes 1572872 | tf_op jit(solution)/shard_map/ppermute | solution.py:498
  62.1 0.0 collective-permute-done.4
  62.1 0.7 collective-permute-start.16
  62.8 0.1 select_select_fusion.2
  63.0 1.3 collective-permute-start.6
  64.3 7.0 %collective-permute-done.10.y2_ref = f32[256,512]{1,0:T(8,128)S(1)} collective-permute-done((f32[256,512]{1,0:T(8,128)S(1)}, f32[256,512]{1,0:T(8,128)S(1)}, u32[]{:S(2)}, u32[]{:S(2)}) %collective-permute-start.10) | collective-permute-done | bytes 524320 | tf_op jit(solution)/shard_map/ppermute | solution.py:498
  71.3 2.3 %collective-permute-start.7 = (f32[256,512]{1,0:T(8,128)S(1)}, f32[256,512]{1,0:T(8,128)S(1)}, u32[]{:S(2)}, u32[]{:S(2)}) collective-permute-start(f32[256,512]{1,0:T(8,128)S(1)} %pad_maximum_fusion.1.p0_ref), channel_id=1, source_target_pairs={{0,2},{1,3},{2,0},{3,1},{4,6},{5,7},{6,4},{7,5},{8,10},{9,11},{10,... | collective-permute-start | bytes 1572872 | tf_op jit(solution)/shard_map/ppermute | solution.py:498
  73.6 8.9 %collective-permute-done.11.y3_ref = f32[256,512]{1,0:T(8,128)S(1)} collective-permute-done((f32[256,512]{1,0:T(8,128)S(1)}, f32[256,512]{1,0:T(8,128)S(1)}, u32[]{:S(2)}, u32[]{:S(2)}) %collective-permute-start.11) | collective-permute-done | bytes 524320 | tf_op jit(solution)/shard_map/ppermute | solution.py:498
  82.4 0.9 collective-permute-start.8
  83.3 18.5 %first.1 = (bf16[1088,512]{1,0:T(8,128)(2,1)S(1)}, bf16[1088,512]{1,0:T(8,128)(2,1)S(1)}, bf16[1024,512]{1,0:T(8,128)(2,1)S(1)}, bf16[1024,512]{1,0:T(8,128)(2,1...) custom-call(s32[1]{0:T(128)} %bitcast.idx_ref, ...), custom_call_target="tpu_custom_call" | custom-call | flops 20000000000 | bytes 20000000 | tf_op jit(solution)/shard_map/first/pallas_call | solution.py:260
  101.8 0.0 collective-permute-done.6.p1_ref
  101.9 0.8 collective-permute-done.8.p3_ref
  102.8 0.1 pad_maximum_fusion.near_ref
  102.8 0.9 collective-permute-start.12
  103.8 18.5 %second.1 = (bf16[1024,1024]{1,0:T(8,128)(2,1)S(1)}, bf16[1024,1024]{1,0:T(8,128)(2,1)S(1)}, f32[8,128,128]{2,1,0:T(8,128)S(1)}, f32[8,1024]{1,0:T(8,128)S(1)}, ...) custom-call(s32[1]{0:T(128)} %bitcast.idx_ref, f32[256,512]{1,0:T(8,128)S(1)} %pad_maximum_fusion.1.p0_ref, ...), custom_call_target="tpu_custom_call" | custom-call | flops 20000000000 | bytes 20000000 | tf_op jit(solution)/shard_map/second/pallas_call | solution.py:329
  122.3 0.0 collective-permute-done.16.far_ref
  122.3 6.0 %third.1 = (f32[1024,512]{1,0:T(8,128)S(1)}, f32[192,1024]{1,0:T(8,128)S(1)}, f32[128,512]{1,0:T(8,128)S(1)}) custom-call(s32[1]{0:T(128)} %bitcast.idx_ref, f32[512,512]{1,0:T(8,128)S(1)} %constant_dynamic-update-slice_fusion.near_ref, f32[512,512]{1,0:T(8,128)S(1)} %collective-permute-done.16.far_ref, bf16[1024,1024]{1,0:T(8,128)(2,1)S(1)} %get-tuple-element.50.lh, ...), custom_call_target="tpu_custom_call" | custom-call | flops 5000000000 | bytes 10000000 | tf_op jit(solution)/shard_map/third/pallas_call | solution.py:420
  128.3 5.1 %fourth.1 = (f32[128,2048]{1,0:T(8,128)}, f32[64,2048]{1,0:T(8,128)S(1)}) custom-call(s32[1]{0:T(128)} %bitcast.idx_ref, f32[512,512]{1,0:T(8,128)S(1)} %pad_maximum_fusion.near_ref, f32[512,512]{1,0:T(8,128)S(1)} %collective-permute-done.12.far_ref, f32[1024,512]{1,0:T(8,128)S(1)} %get-tuple-element.55.next_ref, ...), custom_call_target="tpu_custom_call" | custom-call | tf_op jit(solution)/shard_map/fourth/pallas_call | solution.py:475
  133.4 1.3 collective-permute-start.17
  134.8 11.2 %collective-permute-done.17 = f32[64,1024]{1,0:T(8,128)S(1)} collective-permute-done((f32[64,1024]{1,0:T(8,128)S(1)}, f32[64,1024]{1,0:T(8,128)S(1)}, u32[]{:S(2)}, u32[]{:S(2)}) %collective-permute-start.17) | collective-permute-done | bytes 262176 | tf_op jit(solution)/shard_map/ppermute | solution.py:502
  146.0 0.1 fusion.1
  146.0 0.8 maximum_bitcast_fusion
  (17 shorter events, 0.2 us)
Async XLA Ops:
  4.8 26.4 %copy-start = (f32[1,128,2048]{2,1,0:T(8,128)S(1)}, f32[1,128,2048]{2,1,0:T(8,128)}, u32[]{:S(2)}) copy-start(f32[1,128,2048]{2,1,0:T(8,128)} %param.7) | copy-start | bytes 3145732
  4.8 26.4 %all-to-all-start = ((f32[8,392,128]{2,1,0:T(8,128)}), f32[8,392,128]{2,1,0:T(8,128)S(1)}, u32[]{:S(2)}, u32[]{:S(2)}) async-start(f32[8,392,128]{2,1,0:T(8,128)} %select_maximum_fusion), calls=%async_computation | async-start | bytes 3211264 | tf_op jit(solution)/shard_map/all_to_all | solution.py:519
  33.1 10.9 %collective-permute-start = (f32[128,512]{1,0:T(8,128)}, f32[128,512]{1,0:T(8,128)S(1)}, u32[]{:S(2)}, u32[]{:S(2)}) collective-permute-start(f32[128,512]{1,0:T(8,128)} %get-tuple-element.39), channel_id=1, source_target_pairs={{0,4},{1,5},{2,6},{3,7},{4,0},{5,1},{6,2},{7,3},{16,20},{17,21},{1... | collective-permute-start | bytes 786440 | tf_op jit(solution)/shard_map/ppermute | solution.py:502
  36.9 14.1 %collective-permute-start.1 = (f32[128,512]{1,0:T(8,128)}, f32[128,512]{1,0:T(8,128)S(1)}, u32[]{:S(2)}, u32[]{:S(2)}) collective-permute-start(f32[128,512]{1,0:T(8,128)} %get-tuple-element.39), channel_id=1, source_target_pairs={{4,8},{5,9},{6,10},{7,11},{0,12},{1,13},{2,14},{3,15},{20,24},{21,... | collective-permute-start | bytes 786440 | tf_op jit(solution)/shard_map/ppermute | solution.py:502
  39.7 11.3 %collective-permute-start.2 = (f32[128,512]{1,0:T(8,128)}, f32[128,512]{1,0:T(8,128)S(1)}, u32[]{:S(2)}, u32[]{:S(2)}) collective-permute-start(f32[128,512]{1,0:T(8,128)} %get-tuple-element.39), channel_id=1, source_target_pairs={{0,8},{1,9},{2,10},{3,11},{4,12},{5,13},{6,14},{7,15},{16,24},{17,... | collective-permute-start | bytes 786440 | tf_op jit(solution)/shard_map/ppermute | solution.py:502
  41.0 13.0 %collective-permute-start.13 = (f32[128,512]{1,0:T(8,128)}, f32[128,512]{1,0:T(8,128)S(1)}, u32[]{:S(2)}, u32[]{:S(2)}) collective-permute-start(f32[128,512]{1,0:T(8,128)} %get-tuple-element.39), channel_id=1, source_target_pairs={{8,9},{9,10},{10,11},{11,8},{12,13},{13,14},{14,15},{15,12},{24,25... | collective-permute-start | bytes 786440 | tf_op jit(solution)/shard_map/ppermute | solution.py:498
  41.7 13.1 %collective-permute-start.14 = (f32[128,512]{1,0:T(8,128)}, f32[128,512]{1,0:T(8,128)S(1)}, u32[]{:S(2)}, u32[]{:S(2)}) collective-permute-start(f32[128,512]{1,0:T(8,128)} %get-tuple-element.39), channel_id=1, source_target_pairs={{8,10},{9,11},{10,8},{11,9},{12,14},{13,15},{14,12},{15,13},{24,26... | collective-permute-start | bytes 786440 | tf_op jit(solution)/shard_map/ppermute | solution.py:498
  44.0 13.2 %collective-permute-start.15 = (f32[128,512]{1,0:T(8,128)}, f32[128,512]{1,0:T(8,128)S(1)}, u32[]{:S(2)}, u32[]{:S(2)}) collective-permute-start(f32[128,512]{1,0:T(8,128)} %get-tuple-element.39), channel_id=1, source_target_pairs={{8,11},{9,8},{10,9},{11,10},{12,15},{13,12},{14,13},{15,14},{24,27... | collective-permute-start | bytes 786440 | tf_op jit(solution)/shard_map/ppermute | solution.py:498
  51.0 9.5 %collective-permute-start.3 = (f32[128,512]{1,0:T(8,128)S(1)}, f32[128,512]{1,0:T(8,128)S(1)}, u32[]{:S(2)}, u32[]{:S(2)}) collective-permute-start(f32[128,512]{1,0:T(8,128)S(1)} %get-tuple-element.40), channel_id=1, source_target_pairs={{4,0},{5,1},{6,2},{7,3},{20,16},{21,17},{22,18},{23,19},{36,32},{3... | collective-permute-start | bytes 786440 | tf_op jit(solution)/shard_map/ppermute | solution.py:502
  52.3 9.8 %collective-permute-start.4 = (f32[128,512]{1,0:T(8,128)S(1)}, f32[128,512]{1,0:T(8,128)S(1)}, u32[]{:S(2)}, u32[]{:S(2)}) collective-permute-start(f32[128,512]{1,0:T(8,128)S(1)} %get-tuple-element.40), channel_id=1, source_target_pairs={{4,8},{5,9},{6,10},{7,11},{20,24},{21,25},{22,26},{23,27},{36,40},... | collective-permute-start | bytes 786440 | tf_op jit(solution)/shard_map/ppermute | solution.py:502
  54.1 8.7 %collective-permute-start.5 = (f32[128,512]{1,0:T(8,128)S(1)}, f32[128,512]{1,0:T(8,128)S(1)}, u32[]{:S(2)}, u32[]{:S(2)}) collective-permute-start(f32[128,512]{1,0:T(8,128)S(1)} %get-tuple-element.40), channel_id=1, source_target_pairs={{4,12},{5,13},{6,14},{7,15},{20,28},{21,29},{22,30},{23,31},{36,44... | collective-permute-start | bytes 786440 | tf_op jit(solution)/shard_map/ppermute | solution.py:502
  54.8 28.5 %copy-start.1 = (f32[1,64,2048]{2,1,0:T(8,128)S(1)}, f32[1,64,2048]{2,1,0:T(8,128)}, u32[]{:S(2)}) copy-start(f32[1,64,2048]{2,1,0:T(8,128)} %param.11) | copy-start | bytes 1572868
  54.8 16.5 %collective-permute-start.10 = (f32[256,512]{1,0:T(8,128)S(1)}, f32[256,512]{1,0:T(8,128)S(1)}, u32[]{:S(2)}, u32[]{:S(2)}) collective-permute-start(f32[256,512]{1,0:T(8,128)S(1)} %pad_maximum_fusion.2.y0_ref), channel_id=1, source_target_pairs={{0,2},{1,3},{2,0},{3,1},{4,6},{5,7},{6,4},{7,5},{8,10},{9,11},{10,... | collective-permute-start | bytes 1572872 | tf_op jit(solution)/shard_map/ppermute | solution.py:498
  57.2 25.3 %collective-permute-start.11 = (f32[256,512]{1,0:T(8,128)S(1)}, f32[256,512]{1,0:T(8,128)S(1)}, u32[]{:S(2)}, u32[]{:S(2)}) collective-permute-start(f32[256,512]{1,0:T(8,128)S(1)} %pad_maximum_fusion.2.y0_ref), channel_id=1, source_target_pairs={{0,3},{1,0},{2,1},{3,2},{4,7},{5,4},{6,5},{7,6},{8,11},{9,8},{10,9... | collective-permute-start | bytes 1572872 | tf_op jit(solution)/shard_map/ppermute | solution.py:498
  60.5 22.8 %collective-permute-start.9 = (f32[256,512]{1,0:T(8,128)S(1)}, f32[256,512]{1,0:T(8,128)S(1)}, u32[]{:S(2)}, u32[]{:S(2)}) collective-permute-start(f32[256,512]{1,0:T(8,128)S(1)} %pad_maximum_fusion.2.y0_ref), channel_id=1, source_target_pairs={{0,1},{1,2},{2,3},{3,0},{4,5},{5,6},{6,7},{7,4},{8,9},{9,10},{10,1... | collective-permute-start | bytes 1572872 | tf_op jit(solution)/shard_map/ppermute | solution.py:498
  62.1 60.2 %collective-permute-start.16 = (f32[512,512]{1,0:T(8,128)S(1)}, f32[512,512]{1,0:T(8,128)S(1)}, u32[]{:S(2)}, u32[]{:S(2)}) collective-permute-start(f32[512,512]{1,0:T(8,128)S(1)} %constant_dynamic-update-slice_fusion.near_ref), channel_id=1, source_target_pairs={{8,12},{9,13},{10,14},{11,15},{12,8},{13,9},{14,10},{15,11},{24,28... | collective-permute-start | bytes 3145736 | tf_op jit(solution)/shard_map/ppermute | solution.py:502
  63.0 38.9 %collective-permute-start.6 = (f32[256,512]{1,0:T(8,128)S(1)}, f32[256,512]{1,0:T(8,128)S(1)}, u32[]{:S(2)}, u32[]{:S(2)}) collective-permute-start(f32[256,512]{1,0:T(8,128)S(1)} %pad_maximum_fusion.1.p0_ref), channel_id=1, source_target_pairs={{0,1},{1,2},{2,3},{3,0},{4,5},{5,6},{6,7},{7,4},{8,9},{9,10},{10,1... | collective-permute-start | bytes 1572872 | tf_op jit(solution)/shard_map/ppermute | solution.py:498
  71.3 30.6 %collective-permute-start.7 = (f32[256,512]{1,0:T(8,128)S(1)}, f32[256,512]{1,0:T(8,128)S(1)}, u32[]{:S(2)}, u32[]{:S(2)}) collective-permute-start(f32[256,512]{1,0:T(8,128)S(1)} %pad_maximum_fusion.1.p0_ref), channel_id=1, source_target_pairs={{0,2},{1,3},{2,0},{3,1},{4,6},{5,7},{6,4},{7,5},{8,10},{9,11},{10,... | collective-permute-start | bytes 1572872 | tf_op jit(solution)/shard_map/ppermute | solution.py:498
  82.4 20.3 %collective-permute-start.8 = (f32[256,512]{1,0:T(8,128)S(1)}, f32[256,512]{1,0:T(8,128)S(1)}, u32[]{:S(2)}, u32[]{:S(2)}) collective-permute-start(f32[256,512]{1,0:T(8,128)S(1)} %pad_maximum_fusion.1.p0_ref), channel_id=1, source_target_pairs={{0,3},{1,0},{2,1},{3,2},{4,7},{5,4},{6,5},{7,6},{8,11},{9,8},{10,9... | collective-permute-start | bytes 1572872 | tf_op jit(solution)/shard_map/ppermute | solution.py:498
  102.8 25.4 %collective-permute-start.12 = (f32[512,512]{1,0:T(8,128)S(1)}, f32[512,512]{1,0:T(8,128)S(1)}, u32[]{:S(2)}, u32[]{:S(2)}) collective-permute-start(f32[512,512]{1,0:T(8,128)S(1)} %pad_maximum_fusion.near_ref), channel_id=1, source_target_pairs={{8,12},{9,13},{10,14},{11,15},{12,8},{13,9},{14,10},{15,11},{24,28... | collective-permute-start | bytes 3145736 | tf_op jit(solution)/shard_map/ppermute | solution.py:502
  133.4 12.5 %collective-permute-start.17 = (f32[64,1024]{1,0:T(8,128)S(1)}, f32[64,1024]{1,0:T(8,128)S(1)}, u32[]{:S(2)}, u32[]{:S(2)}) collective-permute-start(f32[64,1024]{1,0:T(8,128)S(1)} %slice.46), channel_id=1, source_target_pairs={{8,4},{9,5},{10,6},{11,7},{12,0},{13,1},{14,2},{15,3},{24,20},{25,... | collective-permute-start | bytes 786440 | tf_op jit(solution)/shard_map/ppermute | solution.py:502

commit v13 on v12

--- a/solution.py
+++ b/solution.py
@@ -29,6 +29,8 @@
 
 
 def dot3_t(ah, al, bh, bl):
+    if ah.shape[1] == B:
+        return dot_t(jnp.concatenate([ah, al, ah], 1), jnp.concatenate([bh, bh, bl], 1))
     return dot_t(ah, bh) + dot_t(al, bh) + dot_t(ah, bl)
 
 

time: 149 us -> 149 us (level)
  no operation moved by 1% of the time
where the time goes in v13:
time: 149 us; the launch traced here: 146 us
  waiting for transfers between devices  59.7 us (40%)
  Pallas kernels  49.5 us (33%)
  starting transfers between devices  29.7 us (20%)
  other arithmetic  5.63 us (4%)
    all_to_all x1, waiting for transfers between devices, local(): lax.all_to_all(payload, 'leaf', split_axis=0, concat_axis=0, tiled=True)  21.9 us
    ppermute x9, waiting for transfers between devices, planes(): lax.ppermute(x, 'front', [(4 * a + y, 4 * b + y) for a, b in pairs for y...  21 us
    pallas_call x1, Pallas kernels, first(): pl.pallas_call(first_kernel, out_shape=tuple((jax.ShapeDtypeStruct(*o) fo...  18.5 us
    pallas_call x1, Pallas kernels, second(): pl.pallas_call(second_kernel, out_shape=tuple((jax.ShapeDtypeStruct(*o) f...  18.1 us
    ppermute x9, waiting for transfers between devices, shift_y(): lax.ppermute(x, 'front', [(4 * z + y, 4 * z + (y + d) % 4) for z in zs fo...  16.7 us
    ppermute x9, starting transfers between devices, planes(): lax.ppermute(x, 'front', [(4 * a + y, 4 * b + y) for a, b in pairs for y...  13.5 us
    ppermute x9, starting transfers between devices, shift_y(): lax.ppermute(x, 'front', [(4 * z + y, 4 * z + (y + d) % 4) for z in zs fo...  11.8 us
    pallas_call x1, Pallas kernels, third(): pl.pallas_call(third_kernel, out_shape=tuple((jax.ShapeDtypeStruct(o, F32...  6 us
  transfers between devices with their start and end apart: 19, of which 8 were waited for; matrix products, arithmetic and copies ran while one was open for 1% of the time, Pallas kernels for 29%

profile of v13, /device:TPU:8, one launch (start us, length us, event | category | flops | bytes accessed | tf_op | source)
XLA Modules:
  0.0 146.4 jit_solution(3131225398730341155)
XLA Ops:
  0.6 0.8 copy.10
  1.4 0.7 fusion
  2.1 2.7 %select_maximum_fusion = f32[8,392,128]{2,1,0:T(8,128)} fusion(f32[8,1,3]{2,1,0:T(1,128)S(1)} %fusion, f32[8,384,128]{2,1,0:T(8,128)} %bitcast.15), kind=kLoop, calls=%fused_computation | loop fusion | flops 1204224 | bytes 3178592 | tf_op jit(solution)/shard_map/concatenate | solution.py:520
  4.8 4.4 %all-to-all-start = ((f32[8,392,128]{2,1,0:T(8,128)}), f32[8,392,128]{2,1,0:T(8,128)S(1)}, u32[]{:S(2)}, u32[]{:S(2)}) async-start(f32[8,392,128]{2,1,0:T(8,128)} %select_maximum_fusion), calls=%async_computation | async-start | bytes 3211264 | tf_op jit(solution)/shard_map/all_to_all | solution.py:521
  9.3 21.9 %all-to-all-done.recv_ref = f32[8,392,128]{2,1,0:T(8,128)S(1)} async-done(((f32[8,392,128]{2,1,0:T(8,128)}), f32[8,392,128]{2,1,0:T(8,128)S(1)}, u32[]{:S(2)}, u32[]{:S(2)}) %all-to-all-start) | async-done | bytes 1605664 | tf_op jit(solution)/shard_map/all_to_all | solution.py:521
  31.2 1.9 %assemble.1 = (f32[128,1024]{1,0:T(8,128)S(1)}, f32[128,512]{1,0:T(8,128)}, f32[128,512]{1,0:T(8,128)S(1)}) custom-call(s32[8,3]{1,0:T(8,128)S(1)} %bitcast.14, s32[1]{0:T(128)} %bitcast.idx_ref, f32[8,392,128]{2,1,0:T(8,128)S(1)} %all-to-all-done.recv_ref, f32[128,2048]{1,0:T(8,128)S(1)} %bitcast.10), custom_call_target="tpu_custom_call" | custom-call | tf_op jit(solution)/shard_map/assemble/pallas_call | solution.py:65
  33.1 3.8 %collective-permute-start = (f32[128,512]{1,0:T(8,128)}, f32[128,512]{1,0:T(8,128)S(1)}, u32[]{:S(2)}, u32[]{:S(2)}) collective-permute-start(f32[128,512]{1,0:T(8,128)} %get-tuple-element.39), channel_id=1, source_target_pairs={{0,4},{1,5},{2,6},{3,7},{4,0},{5,1},{6,2},{7,3},{16,20},{17,21},{1... | collective-permute-start | bytes 786440 | tf_op jit(solution)/shard_map/ppermute | solution.py:504
  36.9 2.8 %collective-permute-start.1 = (f32[128,512]{1,0:T(8,128)}, f32[128,512]{1,0:T(8,128)S(1)}, u32[]{:S(2)}, u32[]{:S(2)}) collective-permute-start(f32[128,512]{1,0:T(8,128)} %get-tuple-element.39), channel_id=1, source_target_pairs={{4,8},{5,9},{6,10},{7,11},{0,12},{1,13},{2,14},{3,15},{20,24},{21,... | collective-permute-start | bytes 786440 | tf_op jit(solution)/shard_map/ppermute | solution.py:504
  39.7 1.3 collective-permute-start.2
  41.0 0.7 collective-permute-start.13
  41.7 0.7 collective-permute-start.14
  42.4 1.6 %collective-permute-done = f32[128,512]{1,0:T(8,128)S(1)} collective-permute-done((f32[128,512]{1,0:T(8,128)}, f32[128,512]{1,0:T(8,128)S(1)}, u32[]{:S(2)}, u32[]{:S(2)}) %collective-permute-start) | collective-permute-done | bytes 262176 | tf_op jit(solution)/shard_map/ppermute | solution.py:504
  44.1 0.7 collective-permute-start.15
  44.7 6.2 %collective-permute-done.1 = f32[128,512]{1,0:T(8,128)S(1)} collective-permute-done((f32[128,512]{1,0:T(8,128)}, f32[128,512]{1,0:T(8,128)S(1)}, u32[]{:S(2)}, u32[]{:S(2)}) %collective-permute-start.1) | collective-permute-done | bytes 262176 | tf_op jit(solution)/shard_map/ppermute | solution.py:504
  51.0 0.0 collective-permute-done.2
  51.0 1.3 collective-permute-start.3
  52.3 0.7 collective-permute-start.4
  52.9 1.1 select_select_fusion.1
  54.1 0.0 collective-permute-done.13
  54.1 0.7 collective-permute-start.5
  54.8 0.0 copy-start.1
  54.8 2.3 %collective-permute-start.10 = (f32[256,512]{1,0:T(8,128)S(1)}, f32[256,512]{1,0:T(8,128)S(1)}, u32[]{:S(2)}, u32[]{:S(2)}) collective-permute-start(f32[256,512]{1,0:T(8,128)S(1)} %pad_maximum_fusion.2.y0_ref), channel_id=1, source_target_pairs={{0,2},{1,3},{2,0},{3,1},{4,6},{5,7},{6,4},{7,5},{8,10},{9,11},{10,... | collective-permute-start | bytes 1572872 | tf_op jit(solution)/shard_map/ppermute | solution.py:500
  57.1 0.0 collective-permute-done.15
  57.1 1.4 collective-permute-start.11
  58.5 1.9 %collective-permute-done.3 = f32[128,512]{1,0:T(8,128)S(1)} collective-permute-done((f32[128,512]{1,0:T(8,128)S(1)}, f32[128,512]{1,0:T(8,128)S(1)}, u32[]{:S(2)}, u32[]{:S(2)}) %collective-permute-start.3) | collective-permute-done | bytes 262176 | tf_op jit(solution)/shard_map/ppermute | solution.py:504
  60.4 1.6 %collective-permute-start.9 = (f32[256,512]{1,0:T(8,128)S(1)}, f32[256,512]{1,0:T(8,128)S(1)}, u32[]{:S(2)}, u32[]{:S(2)}) collective-permute-start(f32[256,512]{1,0:T(8,128)S(1)} %pad_maximum_fusion.2.y0_ref), channel_id=1, source_target_pairs={{0,1},{1,2},{2,3},{3,0},{4,5},{5,6},{6,7},{7,4},{8,9},{9,10},{10,1... | collective-permute-start | bytes 1572872 | tf_op jit(solution)/shard_map/ppermute | solution.py:500
  62.1 0.7 collective-permute-start.16
  62.9 0.0 collective-permute-done.5
  62.9 0.1 select_select_fusion.2
  63.0 1.3 collective-permute-start.6
  64.3 7.0 %collective-permute-done.10.y2_ref = f32[256,512]{1,0:T(8,128)S(1)} collective-permute-done((f32[256,512]{1,0:T(8,128)S(1)}, f32[256,512]{1,0:T(8,128)S(1)}, u32[]{:S(2)}, u32[]{:S(2)}) %collective-permute-start.10) | collective-permute-done | bytes 524320 | tf_op jit(solution)/shard_map/ppermute | solution.py:500
  71.3 2.3 %collective-permute-start.7 = (f32[256,512]{1,0:T(8,128)S(1)}, f32[256,512]{1,0:T(8,128)S(1)}, u32[]{:S(2)}, u32[]{:S(2)}) collective-permute-start(f32[256,512]{1,0:T(8,128)S(1)} %pad_maximum_fusion.1.p0_ref), channel_id=1, source_target_pairs={{0,2},{1,3},{2,0},{3,1},{4,6},{5,7},{6,4},{7,5},{8,10},{9,11},{10,... | collective-permute-start | bytes 1572872 | tf_op jit(solution)/shard_map/ppermute | solution.py:500
  73.5 8.9 %collective-permute-done.11.y3_ref = f32[256,512]{1,0:T(8,128)S(1)} collective-permute-done((f32[256,512]{1,0:T(8,128)S(1)}, f32[256,512]{1,0:T(8,128)S(1)}, u32[]{:S(2)}, u32[]{:S(2)}) %collective-permute-start.11) | collective-permute-done | bytes 524320 | tf_op jit(solution)/shard_map/ppermute | solution.py:500
  82.4 0.9 collective-permute-start.8
  83.3 0.0 collective-permute-done.9.y1_ref
  83.3 18.5 %first.1 = (bf16[1088,512]{1,0:T(8,128)(2,1)S(1)}, bf16[1088,512]{1,0:T(8,128)(2,1)S(1)}, bf16[1024,512]{1,0:T(8,128)(2,1)S(1)}, bf16[1024,512]{1,0:T(8,128)(2,1...) custom-call(s32[1]{0:T(128)} %bitcast.idx_ref, ...), custom_call_target="tpu_custom_call" | custom-call | flops 20000000000 | bytes 20000000 | tf_op jit(solution)/shard_map/first/pallas_call | solution.py:262
  101.7 0.0 collective-permute-done.6.p1_ref
  101.8 0.9 collective-permute-done.8.p3_ref
  102.7 0.1 pad_maximum_fusion.near_ref
  102.8 0.9 collective-permute-start.12
  103.7 18.1 %second.1 = (bf16[1024,1024]{1,0:T(8,128)(2,1)S(1)}, bf16[1024,1024]{1,0:T(8,128)(2,1)S(1)}, f32[8,128,128]{2,1,0:T(8,128)S(1)}, f32[8,1024]{1,0:T(8,128)S(1)}, ...) custom-call(s32[1]{0:T(128)} %bitcast.idx_ref, f32[256,512]{1,0:T(8,128)S(1)} %pad_maximum_fusion.1.p0_ref, ...), custom_call_target="tpu_custom_call" | custom-call | flops 20000000000 | bytes 20000000 | tf_op jit(solution)/shard_map/second/pallas_call | solution.py:331
  121.8 6.0 %third.1 = (f32[1024,512]{1,0:T(8,128)S(1)}, f32[192,1024]{1,0:T(8,128)S(1)}, f32[128,512]{1,0:T(8,128)S(1)}) custom-call(s32[1]{0:T(128)} %bitcast.idx_ref, f32[512,512]{1,0:T(8,128)S(1)} %constant_dynamic-update-slice_fusion.near_ref, f32[512,512]{1,0:T(8,128)S(1)} %collective-permute-done.16.far_ref, bf16[1024,1024]{1,0:T(8,128)(2,1)S(1)} %get-tuple-element.50.lh, ...), custom_call_target="tpu_custom_call" | custom-call | flops 5000000000 | bytes 10000000 | tf_op jit(solution)/shard_map/third/pallas_call | solution.py:422
  127.8 0.0 collective-permute-done.12.far_ref
  127.8 5.1 %fourth.1 = (f32[128,2048]{1,0:T(8,128)}, f32[64,2048]{1,0:T(8,128)S(1)}) custom-call(s32[1]{0:T(128)} %bitcast.idx_ref, f32[512,512]{1,0:T(8,128)S(1)} %pad_maximum_fusion.near_ref, f32[512,512]{1,0:T(8,128)S(1)} %collective-permute-done.12.far_ref, f32[1024,512]{1,0:T(8,128)S(1)} %get-tuple-element.55.next_ref, ...), custom_call_target="tpu_custom_call" | custom-call | tf_op jit(solution)/shard_map/fourth/pallas_call | solution.py:477
  133.0 1.3 collective-permute-start.17
  134.3 11.2 %collective-permute-done.17 = f32[64,1024]{1,0:T(8,128)S(1)} collective-permute-done((f32[64,1024]{1,0:T(8,128)S(1)}, f32[64,1024]{1,0:T(8,128)S(1)}, u32[]{:S(2)}, u32[]{:S(2)}) %collective-permute-start.17) | collective-permute-done | bytes 262176 | tf_op jit(solution)/shard_map/ppermute | solution.py:504
  145.5 0.1 fusion.1
  145.6 0.8 maximum_bitcast_fusion
  (17 shorter events, 0.2 us)
Async XLA Ops:
  4.8 26.4 %copy-start = (f32[1,128,2048]{2,1,0:T(8,128)S(1)}, f32[1,128,2048]{2,1,0:T(8,128)}, u32[]{:S(2)}) copy-start(f32[1,128,2048]{2,1,0:T(8,128)} %param.7) | copy-start | bytes 3145732
  4.8 26.4 %all-to-all-start = ((f32[8,392,128]{2,1,0:T(8,128)}), f32[8,392,128]{2,1,0:T(8,128)S(1)}, u32[]{:S(2)}, u32[]{:S(2)}) async-start(f32[8,392,128]{2,1,0:T(8,128)} %select_maximum_fusion), calls=%async_computation | async-start | bytes 3211264 | tf_op jit(solution)/shard_map/all_to_all | solution.py:521
  33.1 11.0 %collective-permute-start = (f32[128,512]{1,0:T(8,128)}, f32[128,512]{1,0:T(8,128)S(1)}, u32[]{:S(2)}, u32[]{:S(2)}) collective-permute-start(f32[128,512]{1,0:T(8,128)} %get-tuple-element.39), channel_id=1, source_target_pairs={{0,4},{1,5},{2,6},{3,7},{4,0},{5,1},{6,2},{7,3},{16,20},{17,21},{1... | collective-permute-start | bytes 786440 | tf_op jit(solution)/shard_map/ppermute | solution.py:504
  36.9 14.1 %collective-permute-start.1 = (f32[128,512]{1,0:T(8,128)}, f32[128,512]{1,0:T(8,128)S(1)}, u32[]{:S(2)}, u32[]{:S(2)}) collective-permute-start(f32[128,512]{1,0:T(8,128)} %get-tuple-element.39), channel_id=1, source_target_pairs={{4,8},{5,9},{6,10},{7,11},{0,12},{1,13},{2,14},{3,15},{20,24},{21,... | collective-permute-start | bytes 786440 | tf_op jit(solution)/shard_map/ppermute | solution.py:504
  39.7 11.3 %collective-permute-start.2 = (f32[128,512]{1,0:T(8,128)}, f32[128,512]{1,0:T(8,128)S(1)}, u32[]{:S(2)}, u32[]{:S(2)}) collective-permute-start(f32[128,512]{1,0:T(8,128)} %get-tuple-element.39), channel_id=1, source_target_pairs={{0,8},{1,9},{2,10},{3,11},{4,12},{5,13},{6,14},{7,15},{16,24},{17,... | collective-permute-start | bytes 786440 | tf_op jit(solution)/shard_map/ppermute | solution.py:504
  41.0 13.0 %collective-permute-start.13 = (f32[128,512]{1,0:T(8,128)}, f32[128,512]{1,0:T(8,128)S(1)}, u32[]{:S(2)}, u32[]{:S(2)}) collective-permute-start(f32[128,512]{1,0:T(8,128)} %get-tuple-element.39), channel_id=1, source_target_pairs={{8,9},{9,10},{10,11},{11,8},{12,13},{13,14},{14,15},{15,12},{24,25... | collective-permute-start | bytes 786440 | tf_op jit(solution)/shard_map/ppermute | solution.py:500
  41.7 13.1 %collective-permute-start.14 = (f32[128,512]{1,0:T(8,128)}, f32[128,512]{1,0:T(8,128)S(1)}, u32[]{:S(2)}, u32[]{:S(2)}) collective-permute-start(f32[128,512]{1,0:T(8,128)} %get-tuple-element.39), channel_id=1, source_target_pairs={{8,10},{9,11},{10,8},{11,9},{12,14},{13,15},{14,12},{15,13},{24,26... | collective-permute-start | bytes 786440 | tf_op jit(solution)/shard_map/ppermute | solution.py:500
  44.1 13.1 %collective-permute-start.15 = (f32[128,512]{1,0:T(8,128)}, f32[128,512]{1,0:T(8,128)S(1)}, u32[]{:S(2)}, u32[]{:S(2)}) collective-permute-start(f32[128,512]{1,0:T(8,128)} %get-tuple-element.39), channel_id=1, source_target_pairs={{8,11},{9,8},{10,9},{11,10},{12,15},{13,12},{14,13},{15,14},{24,27... | collective-permute-start | bytes 786440 | tf_op jit(solution)/shard_map/ppermute | solution.py:500
  51.0 9.5 %collective-permute-start.3 = (f32[128,512]{1,0:T(8,128)S(1)}, f32[128,512]{1,0:T(8,128)S(1)}, u32[]{:S(2)}, u32[]{:S(2)}) collective-permute-start(f32[128,512]{1,0:T(8,128)S(1)} %get-tuple-element.40), channel_id=1, source_target_pairs={{4,0},{5,1},{6,2},{7,3},{20,16},{21,17},{22,18},{23,19},{36,32},{3... | collective-permute-start | bytes 786440 | tf_op jit(solution)/shard_map/ppermute | solution.py:504
  52.3 9.9 %collective-permute-start.4 = (f32[128,512]{1,0:T(8,128)S(1)}, f32[128,512]{1,0:T(8,128)S(1)}, u32[]{:S(2)}, u32[]{:S(2)}) collective-permute-start(f32[128,512]{1,0:T(8,128)S(1)} %get-tuple-element.40), channel_id=1, source_target_pairs={{4,8},{5,9},{6,10},{7,11},{20,24},{21,25},{22,26},{23,27},{36,40},... | collective-permute-start | bytes 786440 | tf_op jit(solution)/shard_map/ppermute | solution.py:504
  54.1 8.8 %collective-permute-start.5 = (f32[128,512]{1,0:T(8,128)S(1)}, f32[128,512]{1,0:T(8,128)S(1)}, u32[]{:S(2)}, u32[]{:S(2)}) collective-permute-start(f32[128,512]{1,0:T(8,128)S(1)} %get-tuple-element.40), channel_id=1, source_target_pairs={{4,12},{5,13},{6,14},{7,15},{20,28},{21,29},{22,30},{23,31},{36,44... | collective-permute-start | bytes 786440 | tf_op jit(solution)/shard_map/ppermute | solution.py:504
  54.8 28.5 %copy-start.1 = (f32[1,64,2048]{2,1,0:T(8,128)S(1)}, f32[1,64,2048]{2,1,0:T(8,128)}, u32[]{:S(2)}) copy-start(f32[1,64,2048]{2,1,0:T(8,128)} %param.11) | copy-start | bytes 1572868
  54.8 16.5 %collective-permute-start.10 = (f32[256,512]{1,0:T(8,128)S(1)}, f32[256,512]{1,0:T(8,128)S(1)}, u32[]{:S(2)}, u32[]{:S(2)}) collective-permute-start(f32[256,512]{1,0:T(8,128)S(1)} %pad_maximum_fusion.2.y0_ref), channel_id=1, source_target_pairs={{0,2},{1,3},{2,0},{3,1},{4,6},{5,7},{6,4},{7,5},{8,10},{9,11},{10,... | collective-permute-start | bytes 1572872 | tf_op jit(solution)/shard_map/ppermute | solution.py:500
  57.1 25.3 %collective-permute-start.11 = (f32[256,512]{1,0:T(8,128)S(1)}, f32[256,512]{1,0:T(8,128)S(1)}, u32[]{:S(2)}, u32[]{:S(2)}) collective-permute-start(f32[256,512]{1,0:T(8,128)S(1)} %pad_maximum_fusion.2.y0_ref), channel_id=1, source_target_pairs={{0,3},{1,0},{2,1},{3,2},{4,7},{5,4},{6,5},{7,6},{8,11},{9,8},{10,9... | collective-permute-start | bytes 1572872 | tf_op jit(solution)/shard_map/ppermute | solution.py:500
  60.4 22.9 %collective-permute-start.9 = (f32[256,512]{1,0:T(8,128)S(1)}, f32[256,512]{1,0:T(8,128)S(1)}, u32[]{:S(2)}, u32[]{:S(2)}) collective-permute-start(f32[256,512]{1,0:T(8,128)S(1)} %pad_maximum_fusion.2.y0_ref), channel_id=1, source_target_pairs={{0,1},{1,2},{2,3},{3,0},{4,5},{5,6},{6,7},{7,4},{8,9},{9,10},{10,1... | collective-permute-start | bytes 1572872 | tf_op jit(solution)/shard_map/ppermute | solution.py:500
  62.1 59.7 %collective-permute-start.16 = (f32[512,512]{1,0:T(8,128)S(1)}, f32[512,512]{1,0:T(8,128)S(1)}, u32[]{:S(2)}, u32[]{:S(2)}) collective-permute-start(f32[512,512]{1,0:T(8,128)S(1)} %constant_dynamic-update-slice_fusion.near_ref), channel_id=1, source_target_pairs={{8,12},{9,13},{10,14},{11,15},{12,8},{13,9},{14,10},{15,11},{24,28... | collective-permute-start | bytes 3145736 | tf_op jit(solution)/shard_map/ppermute | solution.py:504
  63.0 38.7 %collective-permute-start.6 = (f32[256,512]{1,0:T(8,128)S(1)}, f32[256,512]{1,0:T(8,128)S(1)}, u32[]{:S(2)}, u32[]{:S(2)}) collective-permute-start(f32[256,512]{1,0:T(8,128)S(1)} %pad_maximum_fusion.1.p0_ref), channel_id=1, source_target_pairs={{0,1},{1,2},{2,3},{3,0},{4,5},{5,6},{6,7},{7,4},{8,9},{9,10},{10,1... | collective-permute-start | bytes 1572872 | tf_op jit(solution)/shard_map/ppermute | solution.py:500
  71.3 30.5 %collective-permute-start.7 = (f32[256,512]{1,0:T(8,128)S(1)}, f32[256,512]{1,0:T(8,128)S(1)}, u32[]{:S(2)}, u32[]{:S(2)}) collective-permute-start(f32[256,512]{1,0:T(8,128)S(1)} %pad_maximum_fusion.1.p0_ref), channel_id=1, source_target_pairs={{0,2},{1,3},{2,0},{3,1},{4,6},{5,7},{6,4},{7,5},{8,10},{9,11},{10,... | collective-permute-start | bytes 1572872 | tf_op jit(solution)/shard_map/ppermute | solution.py:500
  82.4 20.3 %collective-permute-start.8 = (f32[256,512]{1,0:T(8,128)S(1)}, f32[256,512]{1,0:T(8,128)S(1)}, u32[]{:S(2)}, u32[]{:S(2)}) collective-permute-start(f32[256,512]{1,0:T(8,128)S(1)} %pad_maximum_fusion.1.p0_ref), channel_id=1, source_target_pairs={{0,3},{1,0},{2,1},{3,2},{4,7},{5,4},{6,5},{7,6},{8,11},{9,8},{10,9... | collective-permute-start | bytes 1572872 | tf_op jit(solution)/shard_map/ppermute | solution.py:500
  102.8 25.0 %collective-permute-start.12 = (f32[512,512]{1,0:T(8,128)S(1)}, f32[512,512]{1,0:T(8,128)S(1)}, u32[]{:S(2)}, u32[]{:S(2)}) collective-permute-start(f32[512,512]{1,0:T(8,128)S(1)} %pad_maximum_fusion.near_ref), channel_id=1, source_target_pairs={{8,12},{9,13},{10,14},{11,15},{12,8},{13,9},{14,10},{15,11},{24,28... | collective-permute-start | bytes 3145736 | tf_op jit(solution)/shard_map/ppermute | solution.py:504
  133.0 12.5 %collective-permute-start.17 = (f32[64,1024]{1,0:T(8,128)S(1)}, f32[64,1024]{1,0:T(8,128)S(1)}, u32[]{:S(2)}, u32[]{:S(2)}) collective-permute-start(f32[64,1024]{1,0:T(8,128)S(1)} %slice.46), channel_id=1, source_target_pairs={{8,4},{9,5},{10,6},{11,7},{12,0},{13,1},{14,2},{15,3},{24,20},{25,... | collective-permute-start | bytes 786440 | tf_op jit(solution)/shard_map/ppermute | solution.py:504
